TPU v7x, 32 devices: a whole 2x2x4 slice. The times are simulated.
32 devices in a mesh: grp: 4 (over y, x), fsdp: 8 (over z, core).
Axes of the slice: x: 2, y: 2, z: 4, core: 2. Of those that a mesh axis runs over, the one named last changes fastest.
Arguments:
- content_in: bfloat16 [2, 12288, 768], P(None, ('grp', 'fsdp')), may hold values from -6 to 6
- query_in: bfloat16 [2, 1792, 768], P(None, ('grp', 'fsdp')), may hold values from -6 to 6
- pred_order: int32 [2, 32, 56], P(None, ('grp', 'fsdp')), may hold values from 0 to 383, as said below
- cont_prompt: int32 [2, 4, 4], P(None, 'grp'), may hold values from 0 to 1
- rel_bucket: int32 [128], replicated, may hold values from 0 to 31
- w_query: bfloat16 [768, 768], P('fsdp'), may hold values from -0.21875 to 0.21875
- b_query: bfloat16 [768], P('fsdp'), may hold values from -3 to 3
- w_key: bfloat16 [768, 768], P('fsdp'), may hold values from -0.21875 to 0.21875
- w_value: bfloat16 [768, 768], P('fsdp'), may hold values from -0.21875 to 0.21875
- b_value: bfloat16 [768], P('fsdp'), may hold values from -1.1953125 to 1.1953125
- w_out: bfloat16 [768, 768], P('fsdp'), may hold values from -3.5 to 3.5
- b_out: bfloat16 [768], P('fsdp'), may hold values from -3 to 3
- ln1_gain: bfloat16 [768], P('fsdp'), may hold values from 0.5 to 1.5
- ln1_bias: bfloat16 [768], P('fsdp'), may hold values from -2 to 2
- w_up: bfloat16 [768, 3072], P('fsdp'), may hold values from -0.21875 to 0.21875
- b_up: bfloat16 [3072], P('fsdp'), may hold values from -3 to 3
- w_down: bfloat16 [3072, 768], P('fsdp'), may hold values from -0.109375 to 0.109375
- b_down: bfloat16 [768], P('fsdp'), may hold values from -3 to 3
- ln2_gain: bfloat16 [768], P('fsdp'), may hold values from 0.5 to 1.5
- ln2_bias: bfloat16 [768], P('fsdp'), may hold values from -2 to 2
- bias_table: bfloat16 [32, 12], replicated, may hold values from -4 to 4
- cot_content: bfloat16 [2, 12288, 768], P(None, ('grp', 'fsdp')), may hold values from -6 to 6
- cot_query: bfloat16 [2, 1792, 768], P(None, ('grp', 'fsdp')), may hold values from -6 to 6
Outputs:
- content_out: float32 [2, 12288, 768], P(None, ('grp', 'fsdp'))
- query_out: float32 [2, 1792, 768], P(None, ('grp', 'fsdp'))
- content_grad: float32 [2, 12288, 768], P(None, ('grp', 'fsdp'))
- query_grad: float32 [2, 1792, 768], P(None, ('grp', 'fsdp'))
- grad_w_query: float32 [768, 768], P('fsdp')
- grad_b_query: float32 [768], P('fsdp')
- grad_w_key: float32 [768, 768], P('fsdp')
- grad_w_value: float32 [768, 768], P('fsdp')
- grad_b_value: float32 [768], P('fsdp')
- grad_w_out: float32 [768, 768], P('fsdp')
- grad_b_out: float32 [768], P('fsdp')
- grad_ln1_gain: float32 [768], P('fsdp')
- grad_ln1_bias: float32 [768], P('fsdp')
- grad_w_up: float32 [768, 3072], P('fsdp')
- grad_b_up: float32 [3072], P('fsdp')
- grad_w_down: float32 [3072, 768], P('fsdp')
- grad_b_down: float32 [768], P('fsdp')
- grad_ln2_gain: float32 [768], P('fsdp')
- grad_ln2_bias: float32 [768], P('fsdp')
- grad_bias_table: float32 [32, 12], P('fsdp')
Inputs may be any that keep to these rules, and one draw needn't show every extreme that they name: `pred_order`: each row of 56 entries names distinct content rows of one device.
All inputs are finite; a program needn't handle non-finite values.
Results may differ from a plain program's by a relative error of at most 0.025.
Values may be sent and summed in bfloat16 or wider, within the bound.
A program may use at most 320 MiB of HBM per device.

v0:
```python
import jax
import jax.numpy as jnp
from jax import lax
from jax.sharding import PartitionSpec as P

D = 768
PD = 128
CH = 256
MICRO = 2
TD = 384


PRECISE = lax.Precision.HIGHEST
MASKED = -1e30


def from_partner(block, axis, distance):
    count = lax.axis_size(axis)
    route = []
    for low in range(count):
        high = low | 1 << distance
        if high != low and high < count:
            route += [(low, high), (high, low)]
    return lax.ppermute(block, axis, route)


def layer_norm(value, gain, shift):
    centred = value - jnp.mean(value, axis=-1, keepdims=True)
    inverse = lax.rsqrt(jnp.mean(centred * centred, axis=-1, keepdims=True) + 1e-05)
    normed = centred * inverse
    return (normed * gain + shift, normed, inverse)


def norm_back(upstream, normed, inverse, gain):
    scaled = upstream * gain
    inner = (
        scaled
        - jnp.mean(scaled, axis=-1, keepdims=True)
        - normed * jnp.mean(scaled * normed, axis=-1, keepdims=True)
    )
    return (inverse * inner, jnp.sum(upstream * normed, axis=0), jnp.sum(upstream, axis=0))


def gelu_slope(hidden):
    return (
        0.5 * (1.0 + lax.erf(hidden * 0.7071067811865476))
        + hidden * jnp.exp(-0.5 * hidden * hidden) * 0.3989422804014327
    )


def distance_hot(query_pos, pos_block, reach):
    relative = jnp.clip(query_pos[:, None] - pos_block[None, :], 0, reach - 1)
    return (relative[:, :, None] == jnp.arange(reach, dtype=jnp.int32)[None, None, :]).astype(
        jnp.bfloat16
    )


def block_scores(queries, key_block, pos_block, query_pos, limits, dist_low):
    raw = jnp.einsum("qhd,khd->hqk", queries, key_block, preferred_element_type=jnp.float32) * 0.125
    hot = distance_hot(query_pos, pos_block, dist_low.shape[1])
    bias = jnp.einsum("qkr,hr->hqk", hot, dist_low, preferred_element_type=jnp.float32)
    visible = pos_block[None, :] < limits[:, None]
    return (jnp.where(visible[None], raw + bias, MASKED), hot)


def attend(queries, key_heads, value_heads, key_pos, query_pos, limits, dist_low, block):
    blocks = key_heads.shape[0] // block
    heads = queries.shape[1]
    key_blocks = key_heads.reshape(blocks, block, heads, -1)
    value_blocks = value_heads.reshape(blocks, block, heads, -1)
    pos_blocks = key_pos.reshape(blocks, block)

    def gather_stats(carry, item):
        running, total = carry
        key_block, pos_block = item
        scores, _ = block_scores(queries, key_block, pos_block, query_pos, limits, dist_low)
        peak = jnp.maximum(running, jnp.max(scores, axis=2))
        total = total * jnp.exp(running - peak) + jnp.sum(
            jnp.exp(scores - peak[:, :, None]), axis=2
        )
        return ((peak, total), None)

    start = (
        jnp.full((heads, queries.shape[0]), MASKED, jnp.float32),
        jnp.zeros((heads, queries.shape[0]), jnp.float32),
    )
    (running, total), _ = lax.scan(gather_stats, start, (key_blocks, pos_blocks))
    log_total = running + jnp.log(total)

    def mix(context, item):
        key_block, value_block, pos_block = item
        scores, _ = block_scores(queries, key_block, pos_block, query_pos, limits, dist_low)
        chance = jnp.exp(scores - log_total[:, :, None]).astype(jnp.bfloat16)
        return (
            context
            + jnp.einsum("hqk,khd->qhd", chance, value_block, preferred_element_type=jnp.float32),
            None,
        )

    context, _ = lax.scan(
        mix, jnp.zeros(queries.shape, jnp.float32), (key_blocks, value_blocks, pos_blocks)
    )
    return (context, log_total)


def attend_back(
    queries,
    key_heads,
    value_heads,
    key_pos,
    query_pos,
    limits,
    dist_low,
    block,
    log_total,
    context,
    dcontext,
):
    blocks = key_heads.shape[0] // block
    heads = queries.shape[1]
    key_blocks = key_heads.reshape(blocks, block, heads, -1)
    value_blocks = value_heads.reshape(blocks, block, heads, -1)
    pos_blocks = key_pos.reshape(blocks, block)
    delta = jnp.einsum("qhd,qhd->hq", dcontext.astype(jnp.float32), context)

    def step_back(carry, item):
        dquery, dist_sum = carry
        key_block, value_block, pos_block = item
        scores, hot = block_scores(queries, key_block, pos_block, query_pos, limits, dist_low)
        chance = jnp.exp(scores - log_total[:, :, None])
        dchance = jnp.einsum(
            "qhd,khd->hqk", dcontext, value_block, preferred_element_type=jnp.float32
        )
        dscore = chance * (dchance - delta[:, :, None])
        dscore_b = dscore.astype(jnp.bfloat16)
        dscore_rest = (dscore - dscore_b.astype(jnp.float32)).astype(jnp.bfloat16)
        dquery = (
            dquery
            + jnp.einsum("hqk,khd->qhd", dscore_b, key_block, preferred_element_type=jnp.float32)
            * 0.125
        )
        dkey = (
            jnp.einsum("hqk,qhd->khd", dscore_b, queries, preferred_element_type=jnp.float32)
            * 0.125
        )
        dvalue = jnp.einsum(
            "hqk,qhd->khd",
            chance.astype(jnp.bfloat16),
            dcontext,
            preferred_element_type=jnp.float32,
        )
        both_parts = jnp.concatenate([dscore_b, dscore_rest], axis=0)
        bucket_pair = jnp.einsum("gqk,qkr->gr", both_parts, hot, preferred_element_type=jnp.float32)
        dist_sum = dist_sum + bucket_pair[:heads] + bucket_pair[heads:]
        return ((dquery, dist_sum), (dkey, dvalue))

    start = (jnp.zeros(queries.shape, jnp.float32), jnp.zeros(dist_low.shape, jnp.float32))
    (dquery, dist_sum), (dkeys, dvalues) = lax.scan(
        step_back, start, (key_blocks, value_blocks, pos_blocks)
    )
    return (dquery, dist_sum, dkeys.reshape(key_heads.shape), dvalues.reshape(value_heads.shape))


def on_device(
    content_in,
    query_in,
    pred_order,
    cont_prompt,
    rel_bucket,
    w_query,
    b_query,
    w_key,
    w_value,
    b_value,
    w_out,
    b_out,
    ln1_gain,
    ln1_bias,
    w_up,
    b_up,
    w_down,
    b_down,
    ln2_gain,
    ln2_bias,
    bias_table,
    cot_content,
    cot_query,
):
    devices = lax.axis_size("fsdp")
    halfway = devices // 2
    own_rank = lax.axis_index("fsdp")
    plength = PD * halfway
    block = 2 * CH
    heads = bias_table.shape[1]
    head_dim = D // heads
    bucket_hot = (
        rel_bucket[:, None] == jnp.arange(bias_table.shape[0], dtype=jnp.int32)[None, :]
    ).astype(jnp.float32)
    dist_grid = jnp.dot(bucket_hot, bias_table.astype(jnp.float32), precision=PRECISE).T
    dist_low = dist_grid.astype(jnp.bfloat16)
    own_prompt = own_rank // halfway
    prompt_base = own_rank % halfway * PD
    cont_index = own_rank // 2
    cont_side = own_rank % 2
    prompt_pos = prompt_base + jnp.arange(PD, dtype=jnp.int32)
    cont_pos = plength + 2 * jnp.arange(CH, dtype=jnp.int32) + cont_side
    partner_pos = plength + 2 * jnp.arange(CH, dtype=jnp.int32) + 1 - cont_side
    key_pos_p = jnp.arange(plength, dtype=jnp.int32)
    key_pos_c = jnp.concatenate([key_pos_p, partner_pos, cont_pos])

    def split_heads(matrix):
        return matrix.reshape(matrix.shape[0], heads, head_dim)

    def key_sets(gathered, near_rows, own_cont, prompt_ref):
        own_slice = lax.dynamic_slice_in_dim(gathered, own_prompt * plength, plength, 0)
        map_slice = lax.dynamic_slice_in_dim(gathered, prompt_ref * plength, plength, 0)
        return (
            split_heads(own_slice),
            split_heads(jnp.concatenate([map_slice, near_rows, own_cont])),
        )

    outs_content = []
    outs_query = []
    grads_content = []
    grads_query = []
    summed = None
    for micro_step in range(MICRO):
        gathered_w = (
            lax.all_gather(w_query, "fsdp", axis=0, tiled=True),
            lax.all_gather(w_key, "fsdp", axis=0, tiled=True),
            lax.all_gather(w_value, "fsdp", axis=0, tiled=True),
            lax.all_gather(w_out, "fsdp", axis=0, tiled=True),
            lax.all_gather(w_up, "fsdp", axis=0, tiled=True),
            lax.all_gather(w_down, "fsdp", axis=0, tiled=True),
            lax.all_gather(b_query, "fsdp", axis=0, tiled=True),
            lax.all_gather(b_value, "fsdp", axis=0, tiled=True),
            lax.all_gather(b_out, "fsdp", axis=0, tiled=True),
            lax.all_gather(b_up, "fsdp", axis=0, tiled=True),
            lax.all_gather(b_down, "fsdp", axis=0, tiled=True),
            lax.all_gather(ln1_gain, "fsdp", axis=0, tiled=True),
            lax.all_gather(ln1_bias, "fsdp", axis=0, tiled=True),
            lax.all_gather(ln2_gain, "fsdp", axis=0, tiled=True),
            lax.all_gather(ln2_bias, "fsdp", axis=0, tiled=True),
        )
        query_weight, key_weight, value_weight, out_weight, up_weight, down_weight = gathered_w[:6]
        vectors = [entry.astype(jnp.float32) for entry in gathered_w[6:]]
        (
            query_bias,
            value_bias,
            out_bias,
            up_bias,
            down_bias,
            gain_one,
            shift_one,
            gain_two,
            shift_two,
        ) = vectors
        tokens_x = content_in[micro_step]
        extra_x = query_in[micro_step]
        order_ids = pred_order[micro_step, 0]
        prompt_map = cont_prompt[micro_step, 0]
        prompt_ref = jnp.sum(
            jnp.where(jnp.arange(prompt_map.shape[0], dtype=jnp.int32) == cont_index, prompt_map, 0)
        )
        queries = (
            jnp.dot(tokens_x, query_weight, preferred_element_type=jnp.float32) + query_bias
        ).astype(jnp.bfloat16)
        key_rows = jnp.dot(tokens_x, key_weight, preferred_element_type=jnp.float32).astype(
            jnp.bfloat16
        )
        value_rows = (
            jnp.dot(tokens_x, value_weight, preferred_element_type=jnp.float32) + value_bias
        ).astype(jnp.bfloat16)
        extra_q = (
            jnp.dot(extra_x, query_weight, preferred_element_type=jnp.float32) + query_bias
        ).astype(jnp.bfloat16)
        prompt_k, prompt_v = (
            lax.all_gather(key_rows[:PD], "fsdp", axis=0, tiled=True),
            lax.all_gather(value_rows[:PD], "fsdp", axis=0, tiled=True),
        )
        near_k, near_v = from_partner((key_rows[PD:], value_rows[PD:]), "fsdp", 0)
        own_kp, cont_kc = key_sets(prompt_k, near_k, key_rows[PD:], prompt_ref)
        own_vp, cont_vc = key_sets(prompt_v, near_v, value_rows[PD:], prompt_ref)
        in_prompt = order_ids < PD
        extra_pos_p = prompt_base + order_ids
        extra_pos_c = plength + 2 * (order_ids - PD) + cont_side
        pos_set_p = jnp.concatenate([prompt_pos, extra_pos_p])
        lim_set_p = jnp.concatenate(
            [prompt_pos + 1, jnp.where(in_prompt, jnp.maximum(extra_pos_p, 1), -1)]
        )
        pos_set_c = jnp.concatenate([cont_pos, extra_pos_c])
        lim_set_c = jnp.concatenate([cont_pos + 1, jnp.where(in_prompt, -1, extra_pos_c)])
        heads_p = split_heads(jnp.concatenate([queries[:PD], extra_q]))
        heads_c = split_heads(jnp.concatenate([queries[PD:], extra_q]))
        context_p, total_p = attend(
            heads_p, own_kp, own_vp, key_pos_p, pos_set_p, lim_set_p, dist_low, block
        )
        context_c, total_c = attend(
            heads_c, cont_kc, cont_vc, key_pos_c, pos_set_c, lim_set_c, dist_low, block
        )
        context = jnp.concatenate(
            [
                context_p[:PD],
                context_c[:CH],
                jnp.where(in_prompt[:, None, None], context_p[PD:], context_c[CH:]),
            ]
        ).reshape(-1, D)
        context_b = context.astype(jnp.bfloat16)
        residual = jnp.concatenate([tokens_x, extra_x]).astype(jnp.float32)
        first, normed_one, inverse_one = layer_norm(
            residual
            + jnp.dot(context_b, out_weight, preferred_element_type=jnp.float32)
            + out_bias,
            gain_one,
            shift_one,
        )
        first_b = first.astype(jnp.bfloat16)
        hidden = jnp.dot(first_b, up_weight, preferred_element_type=jnp.float32) + up_bias
        active = jax.nn.gelu(hidden, approximate=False).astype(jnp.bfloat16)
        final, normed_two, inverse_two = layer_norm(
            first + jnp.dot(active, down_weight, preferred_element_type=jnp.float32) + down_bias,
            gain_two,
            shift_two,
        )
        outs_content.append(final[:TD])
        outs_query.append(final[TD:])
        back_w = (
            lax.all_gather(w_query, "fsdp", axis=0, tiled=True),
            lax.all_gather(w_key, "fsdp", axis=0, tiled=True),
            lax.all_gather(w_value, "fsdp", axis=0, tiled=True),
            lax.all_gather(w_out, "fsdp", axis=0, tiled=True),
            lax.all_gather(w_up, "fsdp", axis=0, tiled=True),
            lax.all_gather(w_down, "fsdp", axis=0, tiled=True),
            lax.all_gather(b_query, "fsdp", axis=0, tiled=True),
            lax.all_gather(b_value, "fsdp", axis=0, tiled=True),
            lax.all_gather(b_out, "fsdp", axis=0, tiled=True),
            lax.all_gather(b_up, "fsdp", axis=0, tiled=True),
            lax.all_gather(b_down, "fsdp", axis=0, tiled=True),
            lax.all_gather(ln1_gain, "fsdp", axis=0, tiled=True),
            lax.all_gather(ln1_bias, "fsdp", axis=0, tiled=True),
            lax.all_gather(ln2_gain, "fsdp", axis=0, tiled=True),
            lax.all_gather(ln2_bias, "fsdp", axis=0, tiled=True),
        )
        again_k, again_v = (
            lax.all_gather(key_rows[:PD], "fsdp", axis=0, tiled=True),
            lax.all_gather(value_rows[:PD], "fsdp", axis=0, tiled=True),
        )
        back_kp, back_kc = key_sets(again_k, near_k, key_rows[PD:], prompt_ref)
        back_vp, back_vc = key_sets(again_v, near_v, value_rows[PD:], prompt_ref)
        upstream = jnp.concatenate([cot_content[micro_step], cot_query[micro_step]]).astype(
            jnp.float32
        )
        dres_two, dgain_two, dshift_two = norm_back(upstream, normed_two, inverse_two, gain_two)
        dbias_down = jnp.sum(dres_two, axis=0)
        dres_two_b = dres_two.astype(jnp.bfloat16)
        dweight_down = jnp.einsum(
            "rf,rd->fd", active, dres_two_b, preferred_element_type=jnp.float32
        )
        dactive = jnp.einsum(
            "rd,fd->rf", dres_two_b, back_w[5], preferred_element_type=jnp.float32
        ).astype(jnp.bfloat16)
        dhidden = (dactive.astype(jnp.float32) * gelu_slope(hidden)).astype(jnp.bfloat16)
        dbias_up = jnp.sum(dhidden.astype(jnp.float32), axis=0)
        dweight_up = jnp.einsum("rd,rf->df", first_b, dhidden, preferred_element_type=jnp.float32)
        dfirst = dres_two + jnp.einsum(
            "rf,df->rd", dhidden, back_w[4], preferred_element_type=jnp.float32
        )
        dres_one, dgain_one, dshift_one = norm_back(dfirst, normed_one, inverse_one, gain_one)
        dbias_out = jnp.sum(dres_one, axis=0)
        dres_one_b = dres_one.astype(jnp.bfloat16)
        dweight_out = jnp.einsum(
            "re,rd->ed", context_b, dres_one_b, preferred_element_type=jnp.float32
        )
        dcontext = split_heads(
            jnp.einsum(
                "rd,ed->re", dres_one_b, back_w[3], preferred_element_type=jnp.float32
            ).astype(jnp.bfloat16)
        )
        dcontext_q = dcontext[TD:]
        empty_q = jnp.zeros_like(dcontext_q)
        dcontext_p = jnp.concatenate(
            [dcontext[:PD], jnp.where(in_prompt[:, None, None], dcontext_q, empty_q)]
        )
        dcontext_c = jnp.concatenate(
            [dcontext[PD:TD], jnp.where(in_prompt[:, None, None], empty_q, dcontext_q)]
        )
        dquery_p, dist_p, dkey_p, dvalue_p = attend_back(
            heads_p,
            back_kp,
            back_vp,
            key_pos_p,
            pos_set_p,
            lim_set_p,
            dist_low,
            block,
            total_p,
            context_p,
            dcontext_p,
        )
        dquery_c, dist_c, dkey_c, dvalue_c = attend_back(
            heads_c,
            back_kc,
            back_vc,
            key_pos_c,
            pos_set_c,
            lim_set_c,
            dist_low,
            block,
            total_c,
            context_c,
            dcontext_c,
        )

        def prompt_term(from_own, from_cont):
            term = jnp.zeros((PD * devices, D), jnp.float32)
            term = lax.dynamic_update_slice_in_dim(
                term, from_own.reshape(plength, D), own_prompt * plength, 0
            )
            mapped = lax.dynamic_slice_in_dim(term, prompt_ref * plength, plength, 0) + from_cont[
                :plength
            ].reshape(plength, D)
            return lax.dynamic_update_slice_in_dim(term, mapped, prompt_ref * plength, 0)

        grad_pk, grad_pv = (
            lax.psum_scatter(
                prompt_term(dkey_p, dkey_c).astype(jnp.bfloat16),
                "fsdp",
                scatter_dimension=0,
                tiled=True,
            ).astype(jnp.float32),
            lax.psum_scatter(
                prompt_term(dvalue_p, dvalue_c).astype(jnp.bfloat16),
                "fsdp",
                scatter_dimension=0,
                tiled=True,
            ).astype(jnp.float32),
        )
        back_k, back_v = (
            from_partner(
                dkey_c[plength : plength + CH].reshape(CH, D).astype(jnp.bfloat16), "fsdp", 0
            ).astype(jnp.float32),
            from_partner(
                dvalue_c[plength : plength + CH].reshape(CH, D).astype(jnp.bfloat16), "fsdp", 0
            ).astype(jnp.float32),
        )
        dkey_rows = jnp.concatenate(
            [grad_pk, dkey_c[plength + CH :].reshape(CH, D) + back_k]
        ).astype(jnp.bfloat16)
        dvalue_rows = jnp.concatenate(
            [grad_pv, dvalue_c[plength + CH :].reshape(CH, D) + back_v]
        ).astype(jnp.bfloat16)
        dquery_rows = (
            jnp.concatenate([dquery_p[:PD], dquery_c[:CH]]).reshape(TD, D).astype(jnp.bfloat16)
        )
        dextra_rows = (dquery_p[PD:] + dquery_c[CH:]).reshape(-1, D).astype(jnp.bfloat16)
        dweight_query = jnp.einsum(
            "td,te->de", tokens_x, dquery_rows, preferred_element_type=jnp.float32
        ) + jnp.einsum("td,te->de", extra_x, dextra_rows, preferred_element_type=jnp.float32)
        dbias_query = jnp.sum(dquery_rows.astype(jnp.float32), axis=0) + jnp.sum(
            dextra_rows.astype(jnp.float32), axis=0
        )
        dweight_key = jnp.einsum(
            "td,te->de", tokens_x, dkey_rows, preferred_element_type=jnp.float32
        )
        dweight_value = jnp.einsum(
            "td,te->de", tokens_x, dvalue_rows, preferred_element_type=jnp.float32
        )
        dbias_value = jnp.sum(dvalue_rows.astype(jnp.float32), axis=0)
        dtokens = dres_one[:TD] + jnp.einsum(
            "te,de->td", dquery_rows, back_w[0], preferred_element_type=jnp.float32
        )
        dtokens = dtokens + jnp.einsum(
            "te,de->td", dkey_rows, back_w[1], preferred_element_type=jnp.float32
        )
        dtokens = dtokens + jnp.einsum(
            "te,de->td", dvalue_rows, back_w[2], preferred_element_type=jnp.float32
        )
        dextra = dres_one[TD:] + jnp.einsum(
            "te,de->td", dextra_rows, back_w[0], preferred_element_type=jnp.float32
        )
        grads_content.append(dtokens)
        grads_query.append(dextra)
        dtable = jnp.dot(bucket_hot.T, (dist_p + dist_c).T, precision=PRECISE)
        pieces = (
            dweight_query,
            dweight_key,
            dweight_value,
            dweight_out,
            dweight_up,
            dweight_down,
            dbias_query,
            dbias_value,
            dbias_out,
            dbias_up,
            dbias_down,
            dgain_one,
            dshift_one,
            dgain_two,
            dshift_two,
            dtable,
        )
        shares = (
            lax.psum_scatter(
                pieces[0].astype(jnp.bfloat16), "fsdp", scatter_dimension=0, tiled=True
            ).astype(jnp.float32),
            lax.psum_scatter(
                pieces[1].astype(jnp.bfloat16), "fsdp", scatter_dimension=0, tiled=True
            ).astype(jnp.float32),
            lax.psum_scatter(
                pieces[2].astype(jnp.bfloat16), "fsdp", scatter_dimension=0, tiled=True
            ).astype(jnp.float32),
            lax.psum_scatter(
                pieces[3].astype(jnp.bfloat16), "fsdp", scatter_dimension=0, tiled=True
            ).astype(jnp.float32),
            lax.psum_scatter(
                pieces[4].astype(jnp.bfloat16), "fsdp", scatter_dimension=0, tiled=True
            ).astype(jnp.float32),
            lax.psum_scatter(
                pieces[5].astype(jnp.bfloat16), "fsdp", scatter_dimension=0, tiled=True
            ).astype(jnp.float32),
            lax.psum_scatter(
                pieces[6].astype(jnp.bfloat16), "fsdp", scatter_dimension=0, tiled=True
            ).astype(jnp.float32),
            lax.psum_scatter(
                pieces[7].astype(jnp.bfloat16), "fsdp", scatter_dimension=0, tiled=True
            ).astype(jnp.float32),
            lax.psum_scatter(
                pieces[8].astype(jnp.bfloat16), "fsdp", scatter_dimension=0, tiled=True
            ).astype(jnp.float32),
            lax.psum_scatter(
                pieces[9].astype(jnp.bfloat16), "fsdp", scatter_dimension=0, tiled=True
            ).astype(jnp.float32),
            lax.psum_scatter(
                pieces[10].astype(jnp.bfloat16), "fsdp", scatter_dimension=0, tiled=True
            ).astype(jnp.float32),
            lax.psum_scatter(
                pieces[11].astype(jnp.bfloat16), "fsdp", scatter_dimension=0, tiled=True
            ).astype(jnp.float32),
            lax.psum_scatter(
                pieces[12].astype(jnp.bfloat16), "fsdp", scatter_dimension=0, tiled=True
            ).astype(jnp.float32),
            lax.psum_scatter(
                pieces[13].astype(jnp.bfloat16), "fsdp", scatter_dimension=0, tiled=True
            ).astype(jnp.float32),
            lax.psum_scatter(
                pieces[14].astype(jnp.bfloat16), "fsdp", scatter_dimension=0, tiled=True
            ).astype(jnp.float32),
            lax.psum_scatter(
                pieces[15].astype(jnp.bfloat16), "fsdp", scatter_dimension=0, tiled=True
            ).astype(jnp.float32),
        )
        summed = (
            shares
            if summed is None
            else tuple((left + right for left, right in zip(summed, shares)))
        )
    totals = (
        lax.psum(summed[0].astype(jnp.bfloat16), "grp").astype(jnp.float32),
        lax.psum(summed[1].astype(jnp.bfloat16), "grp").astype(jnp.float32),
        lax.psum(summed[2].astype(jnp.bfloat16), "grp").astype(jnp.float32),
        lax.psum(summed[3].astype(jnp.bfloat16), "grp").astype(jnp.float32),
        lax.psum(summed[4].astype(jnp.bfloat16), "grp").astype(jnp.float32),
        lax.psum(summed[5].astype(jnp.bfloat16), "grp").astype(jnp.float32),
        lax.psum(summed[6].astype(jnp.bfloat16), "grp").astype(jnp.float32),
        lax.psum(summed[7].astype(jnp.bfloat16), "grp").astype(jnp.float32),
        lax.psum(summed[8].astype(jnp.bfloat16), "grp").astype(jnp.float32),
        lax.psum(summed[9].astype(jnp.bfloat16), "grp").astype(jnp.float32),
        lax.psum(summed[10].astype(jnp.bfloat16), "grp").astype(jnp.float32),
        lax.psum(summed[11].astype(jnp.bfloat16), "grp").astype(jnp.float32),
        lax.psum(summed[12].astype(jnp.bfloat16), "grp").astype(jnp.float32),
        lax.psum(summed[13].astype(jnp.bfloat16), "grp").astype(jnp.float32),
        lax.psum(summed[14].astype(jnp.bfloat16), "grp").astype(jnp.float32),
        lax.psum(summed[15].astype(jnp.bfloat16), "grp").astype(jnp.float32),
    )
    return (
        jnp.stack(outs_content),
        jnp.stack(outs_query),
        jnp.stack(grads_content),
        jnp.stack(grads_query),
        totals[0],
        totals[6],
        totals[1],
        totals[2],
        totals[7],
        totals[3],
        totals[8],
        totals[11],
        totals[12],
        totals[4],
        totals[9],
        totals[5],
        totals[10],
        totals[13],
        totals[14],
        totals[15],
    )


def solution(mesh):
    in_specs = (
        P(None, ("grp", "fsdp"), None),
        P(None, ("grp", "fsdp"), None),
        P(None, ("grp", "fsdp"), None),
        P(None, "grp", None),
        P(),
        P("fsdp", None),
        P("fsdp"),
        P("fsdp", None),
        P("fsdp", None),
        P("fsdp"),
        P("fsdp", None),
        P("fsdp"),
        P("fsdp"),
        P("fsdp"),
        P("fsdp", None),
        P("fsdp"),
        P("fsdp", None),
        P("fsdp"),
        P("fsdp"),
        P("fsdp"),
        P(),
        P(None, ("grp", "fsdp"), None),
        P(None, ("grp", "fsdp"), None),
    )
    out_specs = (
        P(None, ("grp", "fsdp"), None),
        P(None, ("grp", "fsdp"), None),
        P(None, ("grp", "fsdp"), None),
        P(None, ("grp", "fsdp"), None),
        P("fsdp", None),
        P("fsdp"),
        P("fsdp", None),
        P("fsdp", None),
        P("fsdp"),
        P("fsdp", None),
        P("fsdp"),
        P("fsdp"),
        P("fsdp"),
        P("fsdp", None),
        P("fsdp"),
        P("fsdp", None),
        P("fsdp"),
        P("fsdp"),
        P("fsdp"),
        P("fsdp", None),
    )
    return jax.shard_map(
        on_device, mesh=mesh, in_specs=in_specs, out_specs=out_specs, check_vma=False
    )
```

profile of v0, /device:TPU:0, one launch (start us, length us, event | category | flops | bytes accessed | tf_op | source)
XLA Modules:
  0.0 2111.0 jit_solution(3143314449941014311)
XLA Ops:
  9.6 25.6 %all-gather.18.cloned.1.call-done = bf16[768,768]{1,0:T(8,128)(2,1)} async-done(((bf16[96,768]{1,0:T(8,128)(2,1)}), bf16[768,768]{1,0:T(8,128)(2,1)}) %all-gather.18.cloned.1.call-update) | async-done | bytes 1179664 | tf_op jit(solution)/shard_map/all_gather | solution.py:230
  41.0 27.9 %all-reduce.29 = (bf16[768]{0:T(1024)(128)(2,1)S(1)}, bf16[768]{0:T(1024)(128)(2,1)S(1)}, bf16[768]{0:T(1024)(128)(2,1)S(1)}, bf16[768]{0:T(1024)(128)(2,1)S(1)}...) all-reduce(bf16[768]{0:T(1024)(128)(2,1)S(1)} %dynamic-update-slice, ...), channel_id=1, replica_groups=mesh['grp'=4,'fsdp'=8] {'fsdp'}, use_global_device_ids=true, to_apply=%add.1 | all-reduce | flops 5376 | bytes 21504
  87.3 20.0 fusion.129
  107.3 20.2 fusion.127
  129.5 13.0 all-gather
  163.7 8.3 fusion.323
  184.3 147.9 %while.18 = (s32[]{:T(128)}, f32[12,312]{1,0:T(8,128)S(1)}, f32[12,312]{1,0:T(8,128)S(1)}, s32[2,512]{1,0:T(2,128)S(1)}, s32[312]{0:T(512)S(1)}, /*index=5*/bf16...) while((s32[]{:T(128)}, f32[12,312]{1,0:T(8,128)S(1)}, ...), condition=%wide.region_6.7_spmd.clone, body=%wide.region_3.6_spmd.clone.sunk | while | flops 768547072 | bytes 36409020 | solution.py:87
  184.5 61.5 %fusion.470 = f32[312,512,12]{1,2,0:T(8,128)S(1)} fusion(s32[312,512]{1,0:T(8,128)S(1)} %subtract_clamp_fusion.14, bf16[12,128]{1,0:T(8,128)(2,1)} %get-tuple-element.1933), kind=kOutput, calls=%fused_computation.1.clone.2 | convolution fusion | flops 511180800 | bytes 8309760 | tf_op jit(solution)/shard_map/while/body/eval_jaxpr/qkr,hr->hqk/dot_general | solution.py:61
  246.2 7.8 fusion.471
  258.5 61.5 %fusion.470 = f32[312,512,12]{1,2,0:T(8,128)S(1)} fusion(s32[312,512]{1,0:T(8,128)S(1)} %subtract_clamp_fusion.14, bf16[12,128]{1,0:T(8,128)(2,1)} %get-tuple-element.1933), kind=kOutput, calls=%fused_computation.1.clone.2 | convolution fusion | flops 511180800 | bytes 8309760 | tf_op jit(solution)/shard_map/while/body/eval_jaxpr/qkr,hr->hqk/dot_general | solution.py:61
  320.2 7.8 fusion.471
  347.3 112.5 %while.19 = (s32[]{:T(128)}, f32[312,12,64]{0,2,1:T(8,128)}, bf16[2,512,12,64]{1,3,2,0:T(8,128)(2,1)}, s32[2,512]{1,0:T(2,128)S(1)}, s32[312]{0:T(512)S(1)}, /*i...) while((s32[]{:T(128)}, f32[312,12,64]{0,2,1:T(8,128)}, ...), condition=%wide.region_8.9_spmd.clone, body=%wide.region_7.8_spmd.clone.sunk | while | flops 1012457472 | bytes 23829060 | solution.py:100
  347.7 42.6 %fusion.478 = f32[312,512,12]{1,2,0:T(8,128)} fusion(s32[312,512]{1,0:T(8,128)S(1)} %subtract_clamp_fusion.15, bf16[12,128]{1,0:T(8,128)(2,1)} %get-tuple-element.1968), kind=kOutput, calls=%fused_computation.17.clone.1 | convolution fusion | flops 511180800 | bytes 8309760 | tf_op jit(solution)/shard_map/while/body/eval_jaxpr/qkr,hr->hqk/dot_general | solution.py:61
  390.5 13.0 fusion.479
  403.7 42.6 %fusion.478 = f32[312,512,12]{1,2,0:T(8,128)} fusion(s32[312,512]{1,0:T(8,128)S(1)} %subtract_clamp_fusion.15, bf16[12,128]{1,0:T(8,128)(2,1)} %get-tuple-element.1968), kind=kOutput, calls=%fused_computation.17.clone.1 | convolution fusion | flops 511180800 | bytes 8309760 | tf_op jit(solution)/shard_map/while/body/eval_jaxpr/qkr,hr->hqk/dot_general | solution.py:61
  446.5 13.3 fusion.479
  477.8 149.5 %while.20 = (s32[]{:T(128)}, f32[12,312]{1,0:T(8,128)S(1)}, f32[12,312]{1,0:T(8,128)S(1)}, s32[2,512]{1,0:T(2,128)S(1)}, s32[312]{0:T(512)S(1)}, /*index=5*/bf16...) while((s32[]{:T(128)}, f32[12,312]{1,0:T(8,128)S(1)}, ...), condition=%wide.region_19.20_spmd.clone, body=%wide.region_16.19_spmd.clone.sunk | while | flops 768547072 | bytes 36409020 | solution.py:87
  478.9 61.5 %fusion.482 = f32[312,512,12]{1,2,0:T(8,128)S(1)} fusion(s32[312,512]{1,0:T(8,128)S(1)} %subtract_clamp_fusion.16, bf16[12,128]{1,0:T(8,128)(2,1)} %get-tuple-element.1864), kind=kOutput, calls=%fused_computation.41.clone.1 | convolution fusion | flops 511180800 | bytes 8309760 | tf_op jit(solution)/shard_map/while/body/eval_jaxpr/qkr,hr->hqk/dot_general | solution.py:61
  540.6 7.9 fusion.483
  553.5 61.5 %fusion.482 = f32[312,512,12]{1,2,0:T(8,128)S(1)} fusion(s32[312,512]{1,0:T(8,128)S(1)} %subtract_clamp_fusion.16, bf16[12,128]{1,0:T(8,128)(2,1)} %get-tuple-element.1864), kind=kOutput, calls=%fused_computation.41.clone.1 | convolution fusion | flops 511180800 | bytes 8309760 | tf_op jit(solution)/shard_map/while/body/eval_jaxpr/qkr,hr->hqk/dot_general | solution.py:61
  615.2 7.9 fusion.483
  646.0 114.3 %while.21 = (s32[]{:T(128)}, f32[312,12,64]{0,2,1:T(8,128)}, bf16[2,512,12,64]{1,3,2,0:T(8,128)(2,1)}, s32[2,512]{1,0:T(2,128)S(1)}, s32[312]{0:T(512)S(1)}, /*i...) while((s32[]{:T(128)}, f32[312,12,64]{0,2,1:T(8,128)}, ...), condition=%wide.region_21.22_spmd.clone, body=%wide.region_20.21_spmd.clone.sunk | while | flops 1012457472 | bytes 23829060 | solution.py:100
  647.2 42.6 %fusion.490 = f32[312,512,12]{1,2,0:T(8,128)} fusion(s32[312,512]{1,0:T(8,128)S(1)} %subtract_clamp_fusion.17, bf16[12,128]{1,0:T(8,128)(2,1)} %get-tuple-element.1899), kind=kOutput, calls=%fused_computation.57.clone.1 | convolution fusion | flops 511180800 | bytes 8309760 | tf_op jit(solution)/shard_map/while/body/eval_jaxpr/qkr,hr->hqk/dot_general | solution.py:61
  689.9 13.0 fusion.491
  703.8 42.6 %fusion.490 = f32[312,512,12]{1,2,0:T(8,128)} fusion(s32[312,512]{1,0:T(8,128)S(1)} %subtract_clamp_fusion.17, bf16[12,128]{1,0:T(8,128)(2,1)} %get-tuple-element.1899), kind=kOutput, calls=%fused_computation.57.clone.1 | convolution fusion | flops 511180800 | bytes 8309760 | tf_op jit(solution)/shard_map/while/body/eval_jaxpr/qkr,hr->hqk/dot_general | solution.py:61
  746.6 13.3 fusion.491
  764.4 6.4 fusion.325
  788.1 27.9 %fusion.136 = (bf16[440,3072]{1,0:T(8,128)(2,1)}, bf16[440,3072]{1,0:T(8,128)(2,1)}, f32[440,3072]{1,0:T(8,128)}) fusion(f32[3072]{0:T(1024)S(1)} %bitcast.680, f32[440,3072]{1,0:T(8,128)S(1)} %fusion.299, bf16[768,3072]{1,0:T(8,128)(2,1)S(1)} %copy-done.215, f32[440,768]{1,0:T(8,128)S(1)} %copy-done.106, f32[768]{0:T(1024)S(1)} %copy-done.199, ...), kind=kOutput, calls=%fused_computation.168 | convolution fusion | flops 2256291840 | bytes 22312384 | tf_op jit(solution)/shard_map/dot_general | solution.py:318
  863.9 272.3 %while.22 = (s32[]{:T(128)}, f32[312,12,64]{0,2,1:T(8,128)}, f32[12,128]{1,0:T(8,128)S(1)}, f32[2,512,12,64]{1,3,2,0:T(8,128)}, f32[2,512,12,64]{1,3,2,0:T(8,128...) while((s32[]{:T(128)}, f32[312,12,64]{0,2,1:T(8,128)}, ...), condition=%wide.region_31.32_spmd.clone, body=%wide.region_30.31_spmd.clone.sunk | while | flops 2766445056 | bytes 174099184 | solution.py:158
  864.3 61.5 %fusion.503 = f32[312,512,12]{1,2,0:T(8,128)S(1)} fusion(s32[312,512]{1,0:T(8,128)S(1)} %subtract_clamp_fusion.18, bf16[12,128]{1,0:T(8,128)(2,1)} %get-tuple-element.2067), kind=kOutput, calls=%fused_computation.82.clone.1 | convolution fusion | flops 511180800 | bytes 8309760 | tf_op jit(solution)/shard_map/while/body/eval_jaxpr/qkr,hr->hqk/dot_general | solution.py:61
  926.0 6.5 fusion.504
  937.8 7.1 pad_maximum_fusion.42
  944.9 45.3 %fusion.506 = f32[24,128]{1,0:T(8,128)S(1)} fusion(s32[312,512]{1,0:T(8,128)S(1)} %subtract_clamp_fusion.18, bf16[24,312,512]{2,1,0:T(8,128)(2,1)} %pad_maximum_fusion.42), kind=kOutput, calls=%fused_computation.100.clone.2 | convolution fusion | flops 1001914368 | bytes 8318976 | tf_op jit(solution)/shard_map/while/body/eval_jaxpr/gqk,qkr->gr/dot_general | solution.py:153
  999.3 61.5 %fusion.503 = f32[312,512,12]{1,2,0:T(8,128)S(1)} fusion(s32[312,512]{1,0:T(8,128)S(1)} %subtract_clamp_fusion.18, bf16[12,128]{1,0:T(8,128)(2,1)} %get-tuple-element.2067), kind=kOutput, calls=%fused_computation.82.clone.1 | convolution fusion | flops 511180800 | bytes 8309760 | tf_op jit(solution)/shard_map/while/body/eval_jaxpr/qkr,hr->hqk/dot_general | solution.py:61
  1061.0 6.5 fusion.504
  1072.9 7.1 pad_maximum_fusion.42
  1080.0 45.3 %fusion.506 = f32[24,128]{1,0:T(8,128)S(1)} fusion(s32[312,512]{1,0:T(8,128)S(1)} %subtract_clamp_fusion.18, bf16[24,312,512]{2,1,0:T(8,128)(2,1)} %pad_maximum_fusion.42), kind=kOutput, calls=%fused_computation.100.clone.2 | convolution fusion | flops 1001914368 | bytes 8318976 | tf_op jit(solution)/shard_map/while/body/eval_jaxpr/gqk,qkr->gr/dot_general | solution.py:153
  1149.8 273.9 %while.23 = (s32[]{:T(128)}, f32[312,12,64]{0,2,1:T(8,128)}, f32[12,128]{1,0:T(8,128)S(1)}, f32[2,512,12,64]{1,3,2,0:T(8,128)}, f32[2,512,12,64]{1,3,2,0:T(8,128...) while((s32[]{:T(128)}, f32[312,12,64]{0,2,1:T(8,128)}, ...), condition=%wide.region_39.40_spmd.clone, body=%wide.region_38.39_spmd.clone.sunk | while | flops 2766445056 | bytes 174099184 | solution.py:158
  1151.1 61.5 %fusion.518 = f32[312,512,12]{1,2,0:T(8,128)S(1)} fusion(s32[312,512]{1,0:T(8,128)S(1)} %subtract_clamp_fusion.19, bf16[12,128]{1,0:T(8,128)(2,1)} %get-tuple-element.2016), kind=kOutput, calls=%fused_computation.118.clone.1 | convolution fusion | flops 511180800 | bytes 8309760 | tf_op jit(solution)/shard_map/while/body/eval_jaxpr/qkr,hr->hqk/dot_general | solution.py:61
  1212.8 6.5 fusion.519
  1224.6 7.1 pad_maximum_fusion.43
  1231.7 45.3 %fusion.521 = f32[24,128]{1,0:T(8,128)S(1)} fusion(s32[312,512]{1,0:T(8,128)S(1)} %subtract_clamp_fusion.19, bf16[24,312,512]{2,1,0:T(8,128)(2,1)} %pad_maximum_fusion.43), kind=kOutput, calls=%fused_computation.136.clone.1 | convolution fusion | flops 1001914368 | bytes 8318976 | tf_op jit(solution)/shard_map/while/body/eval_jaxpr/gqk,qkr->gr/dot_general | solution.py:153
  1286.7 61.5 %fusion.518 = f32[312,512,12]{1,2,0:T(8,128)S(1)} fusion(s32[312,512]{1,0:T(8,128)S(1)} %subtract_clamp_fusion.19, bf16[12,128]{1,0:T(8,128)(2,1)} %get-tuple-element.2016), kind=kOutput, calls=%fused_computation.118.clone.1 | convolution fusion | flops 511180800 | bytes 8309760 | tf_op jit(solution)/shard_map/while/body/eval_jaxpr/qkr,hr->hqk/dot_general | solution.py:61
  1348.4 6.5 fusion.519
  1360.2 7.1 pad_maximum_fusion.43
  1367.3 45.3 %fusion.521 = f32[24,128]{1,0:T(8,128)S(1)} fusion(s32[312,512]{1,0:T(8,128)S(1)} %subtract_clamp_fusion.19, bf16[24,312,512]{2,1,0:T(8,128)(2,1)} %pad_maximum_fusion.43), kind=kOutput, calls=%fused_computation.136.clone.1 | convolution fusion | flops 1001914368 | bytes 8318976 | tf_op jit(solution)/shard_map/while/body/eval_jaxpr/gqk,qkr->gr/dot_general | solution.py:153
  1518.3 18.2 reduce-scatter.53.cloned.1.call-done
  1543.5 7.0 convolution_convert_fusion
  1551.0 7.1 convolution_convert_fusion.1
  1558.8 7.1 convolution_convert_fusion.3
  1566.6 7.2 convolution_convert_fusion.2
  1585.6 30.8 %fusion.212 = f32[24,128]{1,0:T(8,128)S(1)} fusion(s32[184,512]{1,0:T(8,128)S(1)} %copy-done.144, bf16[24,184,512]{2,1,0:T(8,128)(2,1)S(1)} %pad_maximum_fusion.2), kind=kOutput, calls=%fused_computation.358 | convolution fusion | flops 590872576 | bytes 4911104 | tf_op jit(solution)/shard_map/while/body/eval_jaxpr/gqk,qkr->gr/dot_general | solution.py:153
  1617.7 30.8 %fusion.215 = f32[24,128]{1,0:T(8,128)S(1)} fusion(s32[184,512]{1,0:T(8,128)S(1)} %copy-done.146, bf16[24,184,512]{2,1,0:T(8,128)(2,1)S(1)} %pad_maximum_fusion.3), kind=kOutput, calls=%fused_computation.359 | convolution fusion | flops 590872576 | bytes 4911104 | tf_op jit(solution)/shard_map/while/body/eval_jaxpr/gqk,qkr->gr/dot_general | solution.py:153
  1654.6 14.5 reduce-scatter.39.cloned.1.call-done
  1671.8 27.2 %all-reduce.28 = (bf16[768]{0:T(1024)(128)(2,1)S(1)}, bf16[768]{0:T(1024)(128)(2,1)}, bf16[768]{0:T(1024)(128)(2,1)}, bf16[768]{0:T(1024)(128)(2,1)S(1)}, bf16[7...) all-reduce(bf16[768]{0:T(1024)(128)(2,1)S(1)} %dynamic-update-slice, ...), channel_id=1, replica_groups=mesh['grp'=4,'fsdp'=8] {'fsdp'}, use_global_device_ids=true, to_apply=%add.7 | all-reduce | flops 19968 | bytes 79872
  1709.9 26.4 %reduce-scatter.67.cloned.1.call-done = bf16[96,768]{1,0:T(8,128)(2,1)} async-done(((bf16[768,768]{1,0:T(8,128)(2,1)}), bf16[96,768]{1,0:T(8,128)(2,1)}) %reduce-scatter.67.cloned.1.call-update) | async-done | bytes 147472
  1737.4 32.1 %reduce-scatter.61.cloned.1.call-done = bf16[96,768]{1,0:T(8,128)(2,1)} async-done(((bf16[768,768]{1,0:T(8,128)(2,1)}), bf16[96,768]{1,0:T(8,128)(2,1)}) %reduce-scatter.61.cloned.1.call-update) | async-done | bytes 147472
  1770.5 32.4 %reduce-scatter.63.cloned.1.call-done = bf16[96,768]{1,0:T(8,128)(2,1)} async-done(((bf16[768,768]{1,0:T(8,128)(2,1)}), bf16[96,768]{1,0:T(8,128)(2,1)}) %reduce-scatter.63.cloned.1.call-update) | async-done | bytes 147472
  1805.4 52.9 %reduce-scatter.47.cloned.1.call-done = bf16[384,768]{1,0:T(8,128)(2,1)} async-done(((bf16[3072,768]{1,0:T(8,128)(2,1)}), bf16[384,768]{1,0:T(8,128)(2,1)}) %reduce-scatter.47.cloned.1.call-update) | async-done | bytes 589840 | tf_op jit(solution)/shard_map/reduce_scatter | solution.py:518
  1858.4 55.5 %reduce-scatter.45.cloned.1.call-done = bf16[384,768]{1,0:T(8,128)(2,1)} async-done(((bf16[3072,768]{1,0:T(8,128)(2,1)}), bf16[384,768]{1,0:T(8,128)(2,1)}) %reduce-scatter.45.cloned.1.call-update) | async-done | bytes 589840 | tf_op jit(solution)/shard_map/reduce_scatter | solution.py:518
  1916.1 53.5 %reduce-scatter.41.cloned.1.call-done = bf16[96,3072]{1,0:T(8,128)(2,1)} async-done(((bf16[768,3072]{1,0:T(8,128)(2,1)}), bf16[96,3072]{1,0:T(8,128)(2,1)}) %reduce-scatter.41.cloned.1.call-update) | async-done | bytes 589840 | tf_op jit(solution)/shard_map/reduce_scatter | solution.py:515
  1969.6 55.5 %reduce-scatter.43.cloned.1.call-done = bf16[96,3072]{1,0:T(8,128)(2,1)} async-done(((bf16[768,3072]{1,0:T(8,128)(2,1)}), bf16[96,3072]{1,0:T(8,128)(2,1)}) %reduce-scatter.43.cloned.1.call-update) | async-done | bytes 589840 | tf_op jit(solution)/shard_map/reduce_scatter | solution.py:515
  2028.7 11.2 all-reduce.30
  2060.6 35.7 %all-reduce.34.cloned.1.call-done = (bf16[96,768]{0,1:T(8,128)(2,1)}, bf16[96,768]{0,1:T(8,128)(2,1)}, bf16[96,768]{0,1:T(8,128)(2,1)}, bf16[96,768]{1,0:T(8,128...) async-done(((bf16[96,768]{0,1:T(8,128)(2,1)}, bf16[96,768]{0,1:T(8,128)(2,1)}, bf16[96,768]{0,1:T(8,128)(2,1)}, bf16[96,768]{1,0:T(8,128)(2,1)}, ...) | async-done | bytes 1769488 | tf_op jit(solution)/shard_map/psum | solution.py:558
  (985 shorter events, 449.7 us)
Async XLA Ops:
  7.2 79.3 %copy-start = (bf16[32,12]{0,1:T(8,128)(2,1)S(1)}, bf16[32,12]{0,1:T(8,128)(2,1)}, u32[]{:S(2)}) copy-start(bf16[32,12]{0,1:T(8,128)(2,1)} %param.55) | copy-start | bytes 2308
  7.2 61.6 %copy-start.54 = (bf16[2,384,768]{2,1,0:T(8,128)(2,1)S(1)}, bf16[2,384,768]{2,1,0:T(8,128)(2,1)}, u32[]{:S(2)}) copy-start(bf16[2,384,768]{2,1,0:T(8,128)(2,1)} %param.35) | copy-start | bytes 3538948
  7.3 32.5 %copy-start.219 = (bf16[96]{0:T(256)(128)(2,1)S(1)}, bf16[96]{0:T(256)(128)(2,1)}, u32[]{:S(2)}) copy-start(bf16[96]{0:T(256)(128)(2,1)} %param.46) | copy-start | bytes 580
  7.3 32.8 %copy-start.220 = (bf16[96]{0:T(256)(128)(2,1)S(1)}, bf16[96]{0:T(256)(128)(2,1)}, u32[]{:S(2)}) copy-start(bf16[96]{0:T(256)(128)(2,1)} %param.47) | copy-start | bytes 580
  7.3 33.0 %copy-start.221 = (bf16[96]{0:T(256)(128)(2,1)S(1)}, bf16[96]{0:T(256)(128)(2,1)}, u32[]{:S(2)}) copy-start(bf16[96]{0:T(256)(128)(2,1)} %param.48) | copy-start | bytes 580
  7.3 33.2 %copy-start.222 = (bf16[96]{0:T(256)(128)(2,1)S(1)}, bf16[96]{0:T(256)(128)(2,1)}, u32[]{:S(2)}) copy-start(bf16[96]{0:T(256)(128)(2,1)} %param.52) | copy-start | bytes 580
  7.3 33.4 %copy-start.223 = (bf16[96]{0:T(256)(128)(2,1)S(1)}, bf16[96]{0:T(256)(128)(2,1)}, u32[]{:S(2)}) copy-start(bf16[96]{0:T(256)(128)(2,1)} %param.53) | copy-start | bytes 580
  7.3 27.9 %all-gather.18.cloned.1.call-start = ((), (), s32[]{:S(2)}) async-start(), calls=%async_computation.19 | async-start | bytes 1327104 | tf_op jit(solution)/shard_map/all_gather | solution.py:230
  8.0 60.8 %all-gather.12.cloned.1.call-start = ((), (), s32[]{:S(2)}) async-start(), calls=%async_computation.16 | async-start | bytes 1327104 | tf_op jit(solution)/shard_map/all_gather | solution.py:231
  8.8 140.0 %all-gather.16.cloned.1.call-start = ((), (), s32[]{:S(2)}) async-start(), calls=%async_computation.18 | async-start | bytes 1327104 | tf_op jit(solution)/shard_map/all_gather | solution.py:229
  9.5 151.5 %all-gather.20.cloned.1.call-start = ((), (), s32[]{:S(2)}) async-start(), calls=%async_computation.20 | async-start | bytes 1769472 | tf_op jit(solution)/shard_map/all_gather | solution.py:278
  37.3 35.1 %copy-start.60 = (bf16[768,768]{1,0:T(8,128)(2,1)S(1)}, bf16[768,768]{1,0:T(8,128)(2,1)}, u32[]{:S(2)}) copy-start(bf16[768,768]{1,0:T(8,128)(2,1)} %all-gather.18.cloned.1.call-done) | copy-start | bytes 3538948
  38.0 134.1 %all-gather.14.cloned.1.call-start = ((), (), s32[]{:S(2)}) async-start(), calls=%async_computation.17 | async-start | bytes 1769472 | tf_op jit(solution)/shard_map/all_gather | solution.py:279
  72.3 395.1 %all-gather.30.cloned.1.call-start = ((), (), s32[]{:S(2)}) async-start(), calls=%async_computation.25 | async-start | bytes 1769472 | tf_op jit(solution)/shard_map/all_gather | solution.py:278
  74.6 553.8 %all-gather.22.cloned.1.call-start = ((), (), s32[]{:S(2)}) async-start(), calls=%async_computation.21 | async-start | bytes 1327104 | tf_op jit(solution)/shard_map/all_gather | solution.py:232
  75.3 556.6 %all-gather.28.cloned.1.call-start = ((), (), s32[]{:S(2)}) async-start(), calls=%async_computation.24 | async-start | bytes 1769472 | tf_op jit(solution)/shard_map/all_gather | solution.py:279
  78.8 701.9 %all-gather.24.cloned.1.call-start = ((), (), s32[]{:S(2)}) async-start(), calls=%async_computation.22 | async-start | bytes 5308416 | tf_op jit(solution)/shard_map/all_gather | solution.py:233
  79.6 736.4 %all-gather.26.cloned.1.call-start = ((), (), s32[]{:S(2)}) async-start(), calls=%async_computation.23 | async-start | bytes 5308416 | tf_op jit(solution)/shard_map/all_gather | solution.py:234
  80.2 1402.1 %reduce-scatter.51.cloned.1.call-start = ((), (), s32[]{:S(2)}) async-start(), calls=%async_computation.33 | async-start | bytes 1769472
  107.3 36.9 %copy-start.111 = (bf16[2,384,768]{2,1,0:T(8,128)(2,1)S(1)}, bf16[2,384,768]{2,1,0:T(8,128)(2,1)}, u32[]{:S(2)}) copy-start(bf16[2,384,768]{2,1,0:T(8,128)(2,1)} %param.56) | copy-start | bytes 3538948
  155.1 19.7 collective-permute-start.1
  155.9 179.9 %collective-permute-start = (bf16[256,768]{1,0:T(8,128)(2,1)}, bf16[256,768]{1,0:T(8,128)(2,1)}, u32[]{:S(2)}, u32[]{:S(2)}) collective-permute-start(bf16[256,768]{1,0:T(8,128)(2,1)} %slice.356), channel_id=1, source_target_pairs={{0,1},{1,0},{2,3},{3,2},{4,5},{5,4},{6,7},{7,6},{8,9},{9,8},{10,11... | collective-permute-start | bytes 1179656 | tf_op jit(solution)/shard_map/ppermute | solution.py:24
  156.1 315.5 %collective-permute-start.3 = (bf16[256,768]{1,0:T(8,128)(2,1)S(1)}, bf16[256,768]{1,0:T(8,128)(2,1)}, u32[]{:S(2)}, u32[]{:S(2)}) collective-permute-start(bf16[256,768]{1,0:T(8,128)(2,1)S(1)} %slice.367), channel_id=1, source_target_pairs={{0,1},{1,0},{2,3},{3,2},{4,5},{5,4},{6,7},{7,6},{8,9},{9,8},{10,11... | collective-permute-start | bytes 1179656 | tf_op jit(solution)/shard_map/ppermute | solution.py:24
  158.9 475.4 %collective-permute-start.2 = (bf16[256,768]{1,0:T(8,128)(2,1)}, bf16[256,768]{1,0:T(8,128)(2,1)}, u32[]{:S(2)}, u32[]{:S(2)}) collective-permute-start(bf16[256,768]{1,0:T(8,128)(2,1)} %slice.366), channel_id=1, source_target_pairs={{0,1},{1,0},{2,3},{3,2},{4,5},{5,4},{6,7},{7,6},{8,9},{9,8},{10,11... | collective-permute-start | bytes 1179656 | tf_op jit(solution)/shard_map/ppermute | solution.py:24
  174.8 285.0 %copy-start.35 = (bf16[512,768]{0,1:T(8,128)(2,1)}, bf16[512,768]{0,1:T(8,128)(2,1)S(1)}, u32[]{:S(2)}) copy-start(bf16[512,768]{0,1:T(8,128)(2,1)S(1)} %copy.137) | copy-start | bytes 2359300
  335.7 124.1 %copy-start.149 = (f32[12,184]{1,0:T(8,128)}, f32[12,184]{1,0:T(8,128)S(1)}, u32[]{:S(2)}) copy-start(f32[12,184]{1,0:T(8,128)S(1)} %log_add_fusion.3) | copy-start | bytes 26500
  477.7 149.6 %copy-start.94 = (bf16[256,12,64]{0,2,1:T(8,128)(2,1)S(1)}, bf16[256,12,64]{0,2,1:T(8,128)(2,1)}, u32[]{:S(2)}) copy-start(bf16[256,12,64]{0,2,1:T(8,128)(2,1)} %slice.509) | copy-start | bytes 1179652
  477.7 149.6 %copy-start.121 = (bf16[128,12,64]{0,2,1:T(8,128)(2,1)S(1)}, bf16[128,12,64]{0,2,1:T(8,128)(2,1)}, u32[]{:S(2)}) copy-start(bf16[128,12,64]{0,2,1:T(8,128)(2,1)} %slice.511) | copy-start | bytes 589828
  477.8 149.6 %copy-start.126 = (bf16[56,12,64]{0,2,1:T(8,128)(2,1)S(1)}, bf16[56,12,64]{0,2,1:T(8,128)(2,1)}, u32[]{:S(2)}) copy-start(bf16[56,12,64]{0,2,1:T(8,128)(2,1)} %fusion.243) | copy-start | bytes 258052
  477.8 150.6 %copy-start.167 = (bf16[56,768]{1,0:T(8,128)(2,1)S(1)}, bf16[56,768]{1,0:T(8,128)(2,1)}, u32[]{:S(2)}) copy-start(bf16[56,768]{1,0:T(8,128)(2,1)} %get-tuple-element.1350) | copy-start | bytes 258052
  477.8 150.6 %copy-start.202 = (f32[768]{0:T(1024)S(1)}, f32[768]{0:T(1024)}, u32[]{:S(2)}) copy-start(f32[768]{0:T(1024)} %convert_element_type.637) | copy-start | bytes 9220
  634.3 207.7 %copy-start.189 = (f32[440]{0:T(512)}, f32[440]{0:T(512)S(1)}, u32[]{:S(2)}) copy-start(f32[440]{0:T(512)S(1)} %broadcast_multiply_fusion.11) | copy-start | bytes 5284
  779.6 72.3 %copy-start.41 = (f32[440,768]{1,0:T(8,128)}, f32[440,768]{1,0:T(8,128)S(1)}, u32[]{:S(2)}) copy-start(f32[440,768]{1,0:T(8,128)S(1)} %get-tuple-element.1388) | copy-start | bytes 4055044
  779.6 72.3 %copy-start.176 = (f32[440]{0:T(512)}, f32[440]{0:T(512)S(1)}, u32[]{:S(2)}) copy-start(f32[440]{0:T(512)S(1)} %broadcast_multiply_fusion.9) | copy-start | bytes 5284
  780.7 61.4 %copy-start.210 = (f32[440]{0:T(512)}, f32[440]{0:T(512)S(1)}, u32[]{:S(2)}) copy-start(f32[440]{0:T(512)S(1)} %add_rsqrt_fusion.3) | copy-start | bytes 5284
  780.7 71.2 %copy-start.191 = (f32[440]{0:T(512)}, f32[440]{0:T(512)S(1)}, u32[]{:S(2)}) copy-start(f32[440]{0:T(512)S(1)} %add_rsqrt_fusion.1) | copy-start | bytes 5284
  1145.0 349.2 %reduce-scatter.55.cloned.1.call-start = ((), (), s32[]{:S(2)}) async-start(), calls=%async_computation.35 | async-start | bytes 1769472
  1434.9 71.4 %reduce-scatter.49.cloned.1.call-start = ((), (), s32[]{:S(2)}) async-start(), calls=%async_computation.32 | async-start | bytes 1769472
  1446.4 90.1 %reduce-scatter.53.cloned.1.call-start = ((), (), s32[]{:S(2)}) async-start(), calls=%async_computation.34 | async-start | bytes 1769472
  1458.9 193.5 %reduce-scatter.57.cloned.1.call-start = ((), (), s32[]{:S(2)}) async-start(), calls=%async_computation.36 | async-start | bytes 1327104
  1464.2 189.3 %reduce-scatter.59.cloned.1.call-start = ((), (), s32[]{:S(2)}) async-start(), calls=%async_computation.37 | async-start | bytes 1327104
  1470.5 184.1 %reduce-scatter.37.cloned.1.call-start = ((), (), s32[]{:S(2)}) async-start(), calls=%async_computation.26 | async-start | bytes 1327104 | tf_op jit(solution)/shard_map/reduce_scatter | solution.py:512
  1474.0 195.1 %reduce-scatter.39.cloned.1.call-start = ((), (), s32[]{:S(2)}) async-start(), calls=%async_computation.27 | async-start | bytes 1327104 | tf_op jit(solution)/shard_map/reduce_scatter | solution.py:512
  1477.3 231.5 %reduce-scatter.65.cloned.1.call-start = ((), (), s32[]{:S(2)}) async-start(), calls=%async_computation.40 | async-start | bytes 1327104
  1479.6 1.8 collective-permute-start.5
  1489.2 247.0 %reduce-scatter.67.cloned.1.call-start = ((), (), s32[]{:S(2)}) async-start(), calls=%async_computation.41 | async-start | bytes 1327104
  1491.6 1.8 collective-permute-start.7
  1501.3 268.2 %reduce-scatter.61.cloned.1.call-start = ((), (), s32[]{:S(2)}) async-start(), calls=%async_computation.38 | async-start | bytes 1327104
  1503.6 1.8 collective-permute-start.4
  1513.3 289.6 %reduce-scatter.63.cloned.1.call-start = ((), (), s32[]{:S(2)}) async-start(), calls=%async_computation.39 | async-start | bytes 1327104
  1515.6 1.8 collective-permute-start.6
  1543.5 314.9 %reduce-scatter.47.cloned.1.call-start = ((), (), s32[]{:S(2)}) async-start(), calls=%async_computation.31 | async-start | bytes 5308416 | tf_op jit(solution)/shard_map/reduce_scatter | solution.py:518
  1550.5 363.4 %reduce-scatter.45.cloned.1.call-start = ((), (), s32[]{:S(2)}) async-start(), calls=%async_computation.30 | async-start | bytes 5308416 | tf_op jit(solution)/shard_map/reduce_scatter | solution.py:518
  1558.1 411.5 %reduce-scatter.41.cloned.1.call-start = ((), (), s32[]{:S(2)}) async-start(), calls=%async_computation.28 | async-start | bytes 5308416 | tf_op jit(solution)/shard_map/reduce_scatter | solution.py:515
  1565.9 459.1 %reduce-scatter.43.cloned.1.call-start = ((), (), s32[]{:S(2)}) async-start(), calls=%async_computation.29 | async-start | bytes 5308416 | tf_op jit(solution)/shard_map/reduce_scatter | solution.py:515
  1573.9 522.4 %all-reduce.34.cloned.1.call-start = ((), (), s32[]{:S(2)}) async-start(), calls=%async_computation.42 | async-start | bytes 3833856 | tf_op jit(solution)/shard_map/psum | solution.py:558
  1650.6 52.1 %copy-start.26 = (f32[440,768]{1,0:T(8,128)S(1)}, f32[440,768]{1,0:T(8,128)}, u32[]{:S(2)}) copy-start(f32[440,768]{1,0:T(8,128)} %copy-done.25) | copy-start | bytes 4055044
  1650.6 52.1 %copy-start.165 = (f32[768]{0:T(1024)S(1)}, f32[768]{0:T(1024)}, u32[]{:S(2)}) copy-start(f32[768]{0:T(1024)} %convert_element_type.644) | copy-start | bytes 9220
  1650.6 52.1 %copy-start.169 = (f32[440]{0:T(512)S(1)}, f32[440]{0:T(512)}, u32[]{:S(2)}) copy-start(f32[440]{0:T(512)} %copy-done.168) | copy-start | bytes 5284
  1650.6 52.1 %copy-start.171 = (f32[440]{0:T(512)S(1)}, f32[440]{0:T(512)}, u32[]{:S(2)}) copy-start(f32[440]{0:T(512)} %copy-done.170) | copy-start | bytes 5284
  1650.6 52.1 %copy-start.173 = (f32[440]{0:T(512)S(1)}, f32[440]{0:T(512)}, u32[]{:S(2)}) copy-start(f32[440]{0:T(512)} %copy-done.172) | copy-start | bytes 5284
  1650.7 52.1 %copy-start.175 = (f32[440]{0:T(512)S(1)}, f32[440]{0:T(512)}, u32[]{:S(2)}) copy-start(f32[440]{0:T(512)} %copy-done.174) | copy-start | bytes 5284
  1916.1 112.6 %copy-start.212 = (bf16[96]{0:T(256)(128)(2,1)S(1)}, bf16[96]{0:T(256)(128)(2,1)}, u32[]{:S(2)}) copy-start(bf16[96]{0:T(256)(128)(2,1)} %fusion.271) | copy-start | bytes 580
  1916.1 135.6 %copy-start.62 = (bf16[768,768]{1,0:T(8,128)(2,1)S(1)}, bf16[768,768]{1,0:T(8,128)(2,1)}, u32[]{:S(2)}) copy-start(bf16[768,768]{1,0:T(8,128)(2,1)} %all-gather.12.cloned.1.call-done) | copy-start | bytes 3538948
  (217 other events, 1401.7 us)
Sparse Core Ops, SparseCore 0:
  9.8 25.3 all-gather.17
  36.8 22.6 all-gather.11
  61.2 22.4 all-gather.15
  85.7 24.8 all-gather.19
  112.7 24.4 all-gather.13
  139.2 24.5 all-gather.29
  165.4 22.1 all-gather.21
  189.8 24.8 all-gather.27
  216.4 51.2 all-gather.23
  269.2 50.6 all-gather.25
  1145.2 32.7 reduce-scatter.50
  1435.0 32.2 reduce-scatter.54
  1469.6 32.4 reduce-scatter.48
  1504.2 32.2 reduce-scatter.52
  1538.6 30.6 reduce-scatter.56
  1571.5 31.1 reduce-scatter.58
  1604.8 30.9 reduce-scatter.36
  1637.9 31.1 reduce-scatter.38
  1671.4 31.4 reduce-scatter.64
  1705.1 31.1 reduce-scatter.66
  1738.6 30.8 reduce-scatter.60
  1771.7 31.1 reduce-scatter.62
  1805.2 53.1 reduce-scatter.46
  1860.5 53.3 reduce-scatter.44
  1916.2 53.3 reduce-scatter.40
  1971.7 53.3 reduce-scatter.42
  2029.9 66.3 all-reduce.33
where the time goes:
time: 2120 us; the launch traced here: 2110 us
  matrix products  1290 us (61%)
  waiting for transfers between devices  412 us (19%)
  local copies, waits for them, and re-layouts  152 us (7%)
  other arithmetic  146 us (7%)
  blocking collectives  79.3 us (4%)
  between operations  22 us (1%)
    dot_general x14, matrix products, block_scores(): jnp.einsum('qkr,hr->hqk', hot, dist_low, preferred_element_type=jnp.float32)  703 us
    dot_general x6, matrix products, step_back(): jnp.einsum('gqk,qkr->gr', both_parts, hot, preferred_element_type=jnp.flo...  243 us
    unnamed x37, waiting for transfers between devices  113 us
    reduce_scatter x2, waiting for transfers between devices, on_device(): lax.psum_scatter(pieces[4].astype(jnp.bfloat16), 'fsdp', scatter_dimensio...  109 us
    reduce_scatter x2, waiting for transfers between devices, on_device(): lax.psum_scatter(pieces[5].astype(jnp.bfloat16), 'fsdp', scatter_dimensio...  108 us
    dot_general x10, matrix products, block_scores(): jnp.einsum('qhd,khd->hqk', queries, key_block, preferred_element_type=jnp...  72.1 us
    unnamed x503, local copies, waits for them, and re-layouts  69.2 us
    dot_general x6, matrix products, mix(): jnp.einsum('hqk,khd->qhd', chance, value_block, preferred_element_type=jn...  59.9 us
  transfers between devices with their start and end apart: 35, of which 15 were waited for; matrix products, arithmetic and copies ran while one was open for 58% of the time, Pallas kernels for 0%

commit v1 on v0

v1 whole, which is shorter than its diff:
```python
import functools

import jax
import jax.numpy as jnp
from jax import lax
from jax.experimental import pallas as pl
from jax.experimental.pallas import tpu as pltpu
from jax.sharding import PartitionSpec as P

D = 768
PD = 128
CH = 256
MICRO = 2
TD = 384
QP = 64
HD = 64
LANES = 128
PAIRS = D // LANES

PRECISE = lax.Precision.HIGHEST
MASKED = -1e30
VMEM_LIMIT = 56 * 1024 * 1024


def dot_nt(left, right):
    return lax.dot_general(
        left, right, (((1,), (1,)), ((), ())), preferred_element_type=jnp.float32
    )


def dot_tn(left, right):
    return lax.dot_general(
        left, right, (((0,), (0,)), ((), ())), preferred_element_type=jnp.float32
    )


def dot_nn(left, right):
    return jnp.dot(left, right, preferred_element_type=jnp.float32)


def head_stack(block):
    lane = lax.broadcasted_iota(jnp.int32, block.shape, 1)
    zero = jnp.zeros_like(block)
    return jnp.concatenate(
        [jnp.where(lane < HD, block, zero), jnp.where(lane < HD, zero, block)], axis=0
    )


def head_merge(stacked):
    rows = stacked.shape[0] // 2
    lane = lax.broadcasted_iota(jnp.int32, (rows, LANES), 1)
    return jnp.where(lane < HD, stacked[:rows], stacked[rows:])


def lookup(table, index):
    return jnp.take_along_axis(table, index, axis=1, mode="promise_in_bounds")


def near_index(distance):
    return jnp.clip(distance, 0, LANES - 1)


def fill_keys(scratch, own_ref, map_ref, near_ref, cont_ref, plength):
    scratch[0:plength] = own_ref[...].reshape(plength, LANES)
    scratch[plength : 2 * plength] = map_ref[...].reshape(plength, LANES)
    near = near_ref[...].reshape(CH, LANES)
    at = 2 * plength
    scratch[at : at + 128] = near[0:128]
    scratch[at + 128 : at + 256] = cont_ref[PD : PD + 128]
    scratch[at + 256 : at + 384] = near[128:256]
    scratch[at + 384 : at + 512] = cont_ref[PD + 128 : PD + 256]


def attend_kernel(
    plength,
    meta,
    qc,
    qx,
    ko,
    vo,
    km,
    vm,
    kn,
    vn,
    kc,
    vc,
    table,
    xcol,
    ctx_c,
    ctx_x,
    full_c,
    full_x,
    lse_ref,
    keys,
    vals,
    scores,
    probs,
):
    base = meta[1]
    side = meta[2]
    blocks = plength // 128
    fill_keys(keys, ko, km, kn, kc, plength)
    fill_keys(vals, vo, vm, vn, vc, plength)
    row = lax.broadcasted_iota(jnp.int32, (128, 128), 0)
    col = lax.broadcasted_iota(jnp.int32, (128, 128), 1)
    tab_a = jnp.broadcast_to(table[0, 0:1, :], (128, 128))
    tab_b = jnp.broadcast_to(table[0, 1:2, :], (128, 128))
    tab_x = jnp.where(row < QP, tab_a, tab_b)
    lse_ref[...] = jnp.zeros_like(lse_ref)

    def solve(stack, first, plan, tables, lse_rows):
        count = len(plan)
        span = slice(first, first + 128 * count)
        halves = len(tables)
        width = 128 * count
        scores[0 : 128 * halves, 0:width] = dot_nt(stack, keys[span])
        for half in range(halves):
            rows = slice(128 * half, 128 * half + 128)
            peak = None
            for at, (index, visible) in enumerate(plan):
                cols = slice(128 * at, 128 * at + 128)
                s = scores[rows, cols]
                if index is not None:
                    s = s + lookup(tables[half], index)
                if visible is not None:
                    s = jnp.where(visible, s, MASKED)
                if index is not None or visible is not None:
                    scores[rows, cols] = s
                peak = s if peak is None else jnp.maximum(peak, s)
            top = jnp.max(peak, axis=1, keepdims=True)
            total = None
            for at in range(count):
                cols = slice(128 * at, 128 * at + 128)
                p = jnp.exp(scores[rows, cols] - top)
                total = p if total is None else total + p
                probs[rows, cols] = p.astype(jnp.bfloat16)
            total = jnp.sum(total, axis=1, keepdims=True)
            log_total = top + jnp.log(total)
            lse_ref[0, 0, lse_rows[half] : lse_rows[half] + 1, :] = jnp.transpose(
                jnp.broadcast_to(log_total, (128, 128))
            )[0:1, :]
            scores[rows, 0:128] = jnp.broadcast_to(1.0 / total, (128, 128))
        out = dot_nn(probs[0 : 128 * halves, 0:width], vals[span])
        return out * scores[0 : 128 * halves, 0:128]

    scale = jnp.asarray(0.125, jnp.bfloat16)
    q_p = head_stack(qc[0:PD] * scale)
    q_0 = head_stack(qc[PD : PD + 128] * scale)
    q_1 = head_stack(qc[PD + 128 : PD + 256] * scale)
    q_x = head_stack(qx[...] * scale)

    plan_p = []
    for b in range(blocks):
        d = base + row - (col + 128 * b)
        plan_p.append((near_index(d), d >= 0))
    out = head_merge(solve(q_p, 0, plan_p, (tab_a, tab_b), (0, 3)))
    ctx_c[0:PD] = out.astype(jnp.bfloat16)
    full_c[0:PD] = out

    far = (None, None)
    last = 128 + 2 * row + side - col
    near_d = 2 * (row - col) + 2 * side - 1
    own_d = 2 * (row - col)
    plan_0 = [far] * (blocks - 1) + [
        (near_index(last), None),
        (near_index(near_d), near_d >= 0),
        (near_index(own_d), own_d >= 0),
    ]
    out = head_merge(solve(q_0, plength, plan_0, (tab_a, tab_b), (1, 4)))
    ctx_c[PD : PD + 128] = out.astype(jnp.bfloat16)
    full_c[PD : PD + 128] = out
    plan_1 = [far] * blocks + [
        (near_index(near_d + 256), None),
        (near_index(own_d + 256), None),
        (near_index(near_d), near_d >= 0),
        (near_index(own_d), own_d >= 0),
    ]
    out = head_merge(solve(q_1, plength, plan_1, (tab_a, tab_b), (2, 5)))
    ctx_c[PD + 128 : PD + 256] = out.astype(jnp.bfloat16)
    full_c[PD + 128 : PD + 256] = out

    pos = jnp.broadcast_to(xcol[0, :, 0:1], (128, 128))
    lim_p = jnp.broadcast_to(xcol[0, :, 1:2], (128, 128))
    lim_c = jnp.broadcast_to(xcol[0, :, 2:3], (128, 128))
    plan_x = []
    for b in range(blocks):
        key = col + 128 * b
        plan_x.append((near_index(pos - key), key < lim_p))
    in_cont = lim_c > 0
    for b in range(blocks - 1):
        plan_x.append((None, in_cont))
    key = col + 128 * (blocks - 1)
    plan_x.append((near_index(pos - key), in_cont))
    for b in range(2):
        for offset in (1 - side, side):
            key = plength + 2 * (col + 128 * b) + offset
            plan_x.append((near_index(pos - key), key < lim_c))
    out = solve(q_x, 0, plan_x, (tab_x,), (6,))
    lane = lax.broadcasted_iota(jnp.int32, (QP, LANES), 1)
    out = jnp.where(lane < HD, out[0:QP], out[QP:])
    ctx_x[...] = out.astype(jnp.bfloat16)
    full_x[...] = out


def pair_column(shift):
    return lambda m, j, meta: (m, shift * PAIRS + j)


def prompt_specs(half):
    def at(kv, mapped):
        def index(m, j, meta):
            return (meta[3 + m] if mapped else meta[0], kv, m, 0, j)

        return pl.BlockSpec((half, 1, 1, PD, LANES), index)

    return [at(0, False), at(1, False), at(0, True), at(1, True)]


def near_spec(kv):
    return pl.BlockSpec((1, 1, CH, LANES), lambda m, j, meta: (kv, m, 0, j))


TABLE_SPEC = pl.BlockSpec((1, 8, LANES), lambda m, j, meta: (j, 0, 0))


def attend(meta, qkv, extra_q, prompt_kv, near_kv, table, xcol):
    half = prompt_kv.shape[0] // 2
    plength = half * PD
    n_keys = 2 * plength + 2 * CH
    content = pl.BlockSpec((TD, LANES), pair_column(0))
    extra = pl.BlockSpec((QP, LANES), pair_column(0))
    own_row = plength + 2 * CH
    pairs = MICRO * PAIRS * 2 * (128 * plength + 256 * own_row) + MICRO * PAIRS * 128 * n_keys
    return pl.pallas_call(
        functools.partial(attend_kernel, plength),
        name="attend",
        grid_spec=pltpu.PrefetchScalarGridSpec(
            num_scalar_prefetch=1,
            grid=(MICRO, PAIRS),
            in_specs=[content, extra]
            + prompt_specs(half)
            + [
                near_spec(0),
                near_spec(1),
                pl.BlockSpec((TD, LANES), pair_column(1)),
                pl.BlockSpec((TD, LANES), pair_column(2)),
                TABLE_SPEC,
                pl.BlockSpec((1, 128, 8), lambda m, j, meta: (m, 0, 0)),
            ],
            out_specs=[
                content,
                extra,
                content,
                extra,
                pl.BlockSpec((1, 1, 8, LANES), lambda m, j, meta: (m, j, 0, 0)),
            ],
            scratch_shapes=[
                pltpu.VMEM((n_keys, LANES), jnp.bfloat16),
                pltpu.VMEM((n_keys, LANES), jnp.bfloat16),
                pltpu.VMEM((256, n_keys), jnp.float32),
                pltpu.VMEM((256, n_keys), jnp.bfloat16),
            ],
        ),
        out_shape=[
            jax.ShapeDtypeStruct((MICRO * TD, D), jnp.bfloat16),
            jax.ShapeDtypeStruct((MICRO * QP, D), jnp.bfloat16),
            jax.ShapeDtypeStruct((MICRO * TD, D), jnp.float32),
            jax.ShapeDtypeStruct((MICRO * QP, D), jnp.float32),
            jax.ShapeDtypeStruct((MICRO, PAIRS, 8, LANES), jnp.float32),
        ],
        compiler_params=pltpu.CompilerParams(vmem_limit_bytes=VMEM_LIMIT),
        cost_estimate=pl.CostEstimate(
            flops=4 * pairs * LANES, bytes_accessed=16 * 1024 * 1024, transcendentals=pairs
        ),
    )(
        meta,
        qkv,
        extra_q,
        prompt_kv,
        prompt_kv,
        prompt_kv,
        prompt_kv,
        near_kv,
        near_kv,
        qkv,
        qkv,
        table,
        xcol,
    )


def attend_back_kernel(
    plength,
    meta,
    qc,
    qx,
    ko,
    vo,
    km,
    vm,
    kn,
    vn,
    kc,
    vc,
    table,
    xcol,
    xrow,
    lse_ref,
    dc,
    dx,
    full_c,
    full_x,
    dq_c,
    dq_x,
    dkv_prompt,
    dkv_near,
    dkv_own,
    hist,
    keys,
    vals,
    q_all,
    d_all,
    scores,
    dprobs,
    probs_t,
    dscores_t,
    ds_p,
    dk_acc,
    dv_acc,
    d_prompt,
):
    own_prompt = meta[0]
    base = meta[1]
    side = meta[2]
    mapped = meta[3 + pl.program_id(0)]
    blocks = plength // 128
    at_k1 = 2 * plength + 256
    n_keys = 2 * plength + 512
    fill_keys(keys, ko, km, kn, kc, plength)
    fill_keys(vals, vo, vm, vn, vc, plength)
    row = lax.broadcasted_iota(jnp.int32, (128, 128), 0)
    col = lax.broadcasted_iota(jnp.int32, (128, 128), 1)
    tab_a = jnp.broadcast_to(table[0, 0:1, :], (128, 128))
    tab_b = jnp.broadcast_to(table[0, 1:2, :], (128, 128))
    scale = jnp.asarray(0.125, jnp.bfloat16)

    p_at, x_at, c1_at, c0_at = 0, 256, 384, 640
    q_all[0:256] = head_stack(qc[0:PD] * scale)
    q_all[256:384] = head_stack(qx[...] * scale)
    q_all[384:640] = head_stack(qc[PD + 128 : PD + 256] * scale)
    q_all[640:896] = head_stack(qc[PD : PD + 128] * scale)
    d_all[0:256] = head_stack(dc[0:PD])
    d_all[256:384] = head_stack(dx[...])
    d_all[384:640] = head_stack(dc[PD + 128 : PD + 256])
    d_all[640:896] = head_stack(dc[PD : PD + 128])

    ones_lane = lax.broadcasted_iota(jnp.int32, (8, LANES), 1)
    ones_row = lax.broadcasted_iota(jnp.int32, (8, LANES), 0)
    pick = jnp.where((ones_lane < HD) == (ones_row == 0), 1.0, 0.0)
    pick = jnp.where(ones_row < 2, pick, 0.0)

    def deltas(upstream, context):
        product = upstream.astype(jnp.float32) * context
        return lax.dot_general(
            pick,
            product,
            (((1,), (1,)), ((), ())),
            precision=PRECISE,
            preferred_element_type=jnp.float32,
        )

    delta_p = deltas(dc[0:PD], full_c[0:PD])
    delta_0 = deltas(dc[PD : PD + 128], full_c[PD : PD + 128])
    delta_1 = deltas(dc[PD + 128 : PD + 256], full_c[PD + 128 : PD + 256])
    delta_x = deltas(dx[...], full_x[...])
    delta_x = jnp.concatenate([delta_x[0:1], delta_x[1:2]], axis=1)

    def block_back(first, plan, at_col, halves):
        count = len(plan)
        width = 128 * len(halves)
        span = slice(first, first + 128 * count)
        cols = slice(at_col, at_col + width)
        scores[0 : 128 * count, 0:width] = dot_nt(keys[span], q_all[cols])
        dprobs[0 : 128 * count, 0:width] = dot_nt(vals[span], d_all[cols])
        for half, (tables, lse_row, delta) in enumerate(halves):
            lane = slice(128 * half, 128 * half + 128)
            out_lane = slice(at_col + 128 * half, at_col + 128 * half + 128)
            lse = lse_ref[0, 0, lse_row : lse_row + 1, :]
            for at, (index, visible) in enumerate(plan):
                rows = slice(128 * at, 128 * at + 128)
                out_rows = slice(first + 128 * at, first + 128 * at + 128)
                s = scores[rows, lane]
                if index is not None:
                    bias = lookup(tables[0], index)
                    if len(tables) > 1:
                        bias = jnp.where(col < QP, bias, lookup(tables[1], index))
                    s = s + bias
                if visible is not None:
                    s = jnp.where(visible, s, MASKED)
                p = jnp.exp(s - lse)
                ds = p * (dprobs[rows, lane] - delta)
                probs_t[out_rows, out_lane] = p.astype(jnp.bfloat16)
                dscores_t[out_rows, out_lane] = ds.astype(jnp.bfloat16)
                yield half, at, ds

    extra_a = jnp.where(
        (xcol[0, :, 3:4] == lax.broadcasted_iota(jnp.int32, (128, TD), 1))
        & (lax.broadcasted_iota(jnp.int32, (128, TD), 0) < QP),
        1.0,
        0.0,
    ).astype(jnp.bfloat16)
    extra_b = jnp.where(
        (xcol[0, :, 3:4] == lax.broadcasted_iota(jnp.int32, (128, TD), 1))
        & (lax.broadcasted_iota(jnp.int32, (128, TD), 0) >= QP),
        1.0,
        0.0,
    ).astype(jnp.bfloat16)
    spread = (extra_a, extra_b)

    pos = xrow[0, 0:1, :]
    lim_p = xrow[0, 1:2, :]
    lim_c = xrow[0, 2:3, :]
    plan = []
    for b in range(blocks):
        key = row + 128 * b
        plan.append((near_index(pos - key), key < lim_p))
    in_cont = jnp.broadcast_to(lim_c > 0, (128, 128))
    for b in range(blocks - 1):
        plan.append((None, in_cont))
    plan.append((near_index(pos - (row + 128 * (blocks - 1))), in_cont))
    for b in range(2):
        for offset in (1 - side, side):
            key = plength + 2 * (row + 128 * b) + offset
            plan.append((near_index(pos - key), key < lim_c))
    for _ in block_back(0, plan, x_at, [((tab_a, tab_b), 6, delta_x)]):
        pass

    def spread_block(head, key_at, content_at):
        return dot_nn(
            dscores_t[pl.ds(key_at, 128), x_at : x_at + 128],
            spread[head][:, content_at : content_at + 128],
        )

    turn = (col + row) % 128
    turn_half = (col + row // 2) % 128

    def fold(block):
        return jnp.sum(block.reshape(16, 8, LANES), axis=0)

    plan = []
    for b in range(blocks):
        d = base + col - (row + 128 * b)
        plan.append((near_index(d), d >= 0))
    halves = [((tab_a,), 0, delta_p[0:1]), ((tab_b,), 3, delta_p[1:2])]
    for half, at, ds in block_back(0, plan, p_at, halves):
        ds_p[128 * at : 128 * at + 128, 128 * half : 128 * half + 128] = ds
    before = jnp.maximum(base - 128, 0)
    base_at = pl.multiple_of(base, 128)
    before_at = pl.multiple_of(before, 128)
    for head in range(2):
        lane = slice(128 * head, 128 * head + 128)
        here = ds_p[pl.ds(base_at, 128), lane] + spread_block(head, base_at, 0)
        prior = ds_p[pl.ds(before_at, 128), lane] + spread_block(head, before_at, 0)
        prior = jnp.where(base > 0, prior, 0.0)
        both = jnp.where(col >= row, here, prior)
        hist[0, 0, 32 * head : 32 * head + 8] = fold(lookup(both, turn))

    last = 128 + 2 * col + side - row
    near_d = 2 * (col - row) + 2 * side - 1
    own_d = 2 * (col - row)
    far = (None, None)
    plan_0 = [far] * (blocks - 1) + [
        (near_index(last), None),
        (near_index(near_d), near_d >= 0),
        (near_index(own_d), own_d >= 0),
    ]
    plan_1 = [far] * blocks + [
        (near_index(near_d + 256), None),
        (near_index(own_d + 256), None),
        (near_index(near_d), near_d >= 0),
        (near_index(own_d), own_d >= 0),
    ]
    halves = [((tab_a,), 1, delta_0[0:1]), ((tab_b,), 4, delta_0[1:2])]
    near_sum = {}
    own_sum = {}
    last_key = 2 * plength - 128
    for half, at, ds in block_back(plength, plan_0, c0_at, halves):
        if at == blocks - 1:
            ds = ds + spread_block(half, last_key, PD)
            ds = jnp.where(col < 64, ds, 0.0)
            hist[0, 0, 32 * half + 8 : 32 * half + 16] = fold(lookup(ds, turn_half))
        if at == blocks:
            ds = ds + spread_block(half, 2 * plength, PD)
            near_sum[half] = jnp.where(col >= row, ds, 0.0)
        if at == blocks + 1:
            ds = ds + spread_block(half, 2 * plength + 128, PD)
            own_sum[half] = jnp.where(col >= row, ds, 0.0)
    for half in range(2):
        lane = slice(128 * half, 128 * half + 128)
        ds_p[0:128, lane] = near_sum[half]
        ds_p[128:256, lane] = own_sum[half]
    halves = [((tab_a,), 2, delta_1[0:1]), ((tab_b,), 5, delta_1[1:2])]
    for half, at, ds in block_back(plength, plan_1, c1_at, halves):
        lane = slice(128 * half, 128 * half + 128)
        if at == blocks:
            ds = ds + spread_block(half, 2 * plength, PD + 128)
            ds_p[0:128, lane] = ds_p[0:128, lane] + jnp.where(col < row, ds, 0.0)
        if at == blocks + 1:
            ds = ds + spread_block(half, 2 * plength + 128, PD + 128)
            ds_p[128:256, lane] = ds_p[128:256, lane] + jnp.where(col < row, ds, 0.0)
        if at == blocks + 2:
            ds = ds + spread_block(half, at_k1, PD + 128)
            ds = ds_p[0:128, lane] + jnp.where(col >= row, ds, 0.0)
            hist[0, 0, 32 * half + 16 : 32 * half + 24] = fold(lookup(ds, turn))
        if at == blocks + 3:
            ds = ds + spread_block(half, at_k1 + 128, PD + 128)
            ds = ds_p[128:256, lane] + jnp.where(col >= row, ds, 0.0)
            hist[0, 0, 32 * half + 24 : 32 * half + 32] = fold(lookup(ds, turn))

    own = slice(0, plength)
    middle = slice(plength, at_k1)
    end = slice(at_k1, n_keys)
    for acc, left, right in ((dk_acc, dscores_t, q_all), (dv_acc, probs_t, d_all)):
        acc[own] = dot_nn(left[own, 0:384], right[0:384])
        acc[middle] = dot_nn(left[middle, 256:896], right[256:896])
        acc[end] = dot_nn(left[end, 256:640], right[256:640])

    dq_c[0:PD] = (
        head_merge(dot_tn(dscores_t[own, p_at : p_at + 256], keys[own])) * 0.125
    ).astype(jnp.bfloat16)
    dq_c[PD : PD + 128] = (
        head_merge(dot_tn(dscores_t[middle, c0_at : c0_at + 256], keys[middle])) * 0.125
    ).astype(jnp.bfloat16)
    cont = slice(plength, n_keys)
    dq_c[PD + 128 : PD + 256] = (
        head_merge(dot_tn(dscores_t[cont, c1_at : c1_at + 256], keys[cont])) * 0.125
    ).astype(jnp.bfloat16)
    out = dot_tn(dscores_t[:, x_at : x_at + 128], keys[...])
    lane = lax.broadcasted_iota(jnp.int32, (QP, LANES), 1)
    dq_x[...] = (jnp.where(lane < HD, out[0:QP], out[QP:]) * 0.125).astype(jnp.bfloat16)

    for kv, acc in ((0, dk_acc), (1, dv_acc)):
        near = jnp.concatenate([acc[at_k1 - 256 : at_k1 - 128], acc[at_k1 : at_k1 + 128]], axis=0)
        dkv_near[kv, 0] = near.astype(jnp.bfloat16)
        dkv_own[kv, 0, 0:128] = acc[at_k1 - 128 : at_k1]
        dkv_own[kv, 0, 128:256] = acc[at_k1 + 128 : at_k1 + 256]
        d_prompt[...] = jnp.zeros_like(d_prompt)
        own_at = pl.multiple_of(own_prompt * plength, 128)
        map_at = pl.multiple_of(mapped * plength, 128)
        d_prompt[pl.ds(own_at, plength), :] = acc[own]
        d_prompt[pl.ds(map_at, plength), :] = (
            d_prompt[pl.ds(map_at, plength), :] + acc[plength : 2 * plength]
        )
        dkv_prompt[:, kv, 0] = (
            d_prompt[...].astype(jnp.bfloat16).reshape(2 * blocks, PD, LANES)
        )


def attend_back(meta, qkv, extra_q, prompt_kv, near_kv, table, xcol, xrow, lse, dc, dx, fc, fx):
    devices = prompt_kv.shape[0]
    half = devices // 2
    plength = half * PD
    n_keys = 2 * plength + 2 * CH
    content = pl.BlockSpec((TD, LANES), pair_column(0))
    extra = pl.BlockSpec((QP, LANES), pair_column(0))
    own_row = plength + 2 * CH
    pairs = MICRO * PAIRS * 2 * (128 * plength + 256 * own_row) + MICRO * PAIRS * 128 * n_keys
    return pl.pallas_call(
        functools.partial(attend_back_kernel, plength),
        name="attend_back",
        grid_spec=pltpu.PrefetchScalarGridSpec(
            num_scalar_prefetch=1,
            grid=(MICRO, PAIRS),
            in_specs=[content, extra]
            + prompt_specs(half)
            + [
                near_spec(0),
                near_spec(1),
                pl.BlockSpec((TD, LANES), pair_column(1)),
                pl.BlockSpec((TD, LANES), pair_column(2)),
                TABLE_SPEC,
                pl.BlockSpec((1, 128, 8), lambda m, j, meta: (m, 0, 0)),
                pl.BlockSpec((1, 8, 128), lambda m, j, meta: (m, 0, 0)),
                pl.BlockSpec((1, 1, 8, LANES), lambda m, j, meta: (m, j, 0, 0)),
                content,
                extra,
                content,
                extra,
            ],
            out_specs=[
                content,
                extra,
                pl.BlockSpec((devices, 2, 1, PD, LANES), lambda m, j, meta: (0, 0, m, 0, j)),
                pl.BlockSpec((2, 1, CH, LANES), lambda m, j, meta: (0, m, 0, j)),
                pl.BlockSpec((2, 1, CH, LANES), lambda m, j, meta: (0, m, 0, j)),
                pl.BlockSpec((1, 1, 64, LANES), lambda m, j, meta: (m, j, 0, 0)),
            ],
            scratch_shapes=[
                pltpu.VMEM((n_keys, LANES), jnp.bfloat16),
                pltpu.VMEM((n_keys, LANES), jnp.bfloat16),
                pltpu.VMEM((896, LANES), jnp.bfloat16),
                pltpu.VMEM((896, LANES), jnp.bfloat16),
                pltpu.VMEM((n_keys, 256), jnp.float32),
                pltpu.VMEM((n_keys, 256), jnp.float32),
                pltpu.VMEM((n_keys, 896), jnp.bfloat16),
                pltpu.VMEM((n_keys, 896), jnp.bfloat16),
                pltpu.VMEM((plength, 256), jnp.float32),
                pltpu.VMEM((n_keys, LANES), jnp.float32),
                pltpu.VMEM((n_keys, LANES), jnp.float32),
                pltpu.VMEM((2 * plength, LANES), jnp.float32),
            ],
        ),
        out_shape=[
            jax.ShapeDtypeStruct((MICRO * TD, D), jnp.bfloat16),
            jax.ShapeDtypeStruct((MICRO * QP, D), jnp.bfloat16),
            jax.ShapeDtypeStruct((devices, 2, MICRO, PD, D), jnp.bfloat16),
            jax.ShapeDtypeStruct((2, MICRO, CH, D), jnp.bfloat16),
            jax.ShapeDtypeStruct((2, MICRO, CH, D), jnp.float32),
            jax.ShapeDtypeStruct((MICRO, PAIRS, 64, LANES), jnp.float32),
        ],
        compiler_params=pltpu.CompilerParams(vmem_limit_bytes=VMEM_LIMIT),
        cost_estimate=pl.CostEstimate(
            flops=10 * pairs * LANES, bytes_accessed=32 * 1024 * 1024, transcendentals=pairs
        ),
    )(
        meta,
        qkv,
        extra_q,
        prompt_kv,
        prompt_kv,
        prompt_kv,
        prompt_kv,
        near_kv,
        near_kv,
        qkv,
        qkv,
        table,
        xcol,
        xrow,
        lse,
        dc,
        dx,
        fc,
        fx,
    )


def from_partner(block, axis):
    count = lax.axis_size(axis)
    return lax.ppermute(block, axis, [(i, i ^ 1) for i in range(count)])


def layer_norm(value, gain, shift):
    centred = value - jnp.mean(value, axis=-1, keepdims=True)
    inverse = lax.rsqrt(jnp.mean(centred * centred, axis=-1, keepdims=True) + 1e-05)
    normed = centred * inverse
    return (normed * gain + shift, normed, inverse)


def norm_back(upstream, normed, inverse, gain):
    scaled = upstream * gain
    inner = (
        scaled
        - jnp.mean(scaled, axis=-1, keepdims=True)
        - normed * jnp.mean(scaled * normed, axis=-1, keepdims=True)
    )
    return (inverse * inner, jnp.sum(upstream * normed, axis=0), jnp.sum(upstream, axis=0))


def gelu_slope(hidden):
    return (
        0.5 * (1.0 + lax.erf(hidden * 0.7071067811865476))
        + hidden * jnp.exp(-0.5 * hidden * hidden) * 0.3989422804014327
    )


def pad_rows(block):
    return jnp.pad(block, ((0, 0), (0, QP - block.shape[1]), (0, 0))).reshape(MICRO * QP, D)


def table_gradient(hist, rel_bucket, buckets, side, heads):
    summed = jnp.sum(hist, axis=0).reshape(PAIRS, 2, 4, 8, LANES)
    prompt = jnp.sum(summed[:, :, 0], axis=2)
    even = jnp.sum(summed[:, :, 1, 0::2], axis=2)
    odd = jnp.sum(summed[:, :, 1, 1::2], axis=2)
    near = jnp.sum(summed[:, :, 2], axis=2)
    own = jnp.sum(summed[:, :, 3], axis=2)
    lanes = jnp.arange(LANES, dtype=jnp.int32)
    signed = jnp.where(lanes < 64, lanes, lanes - 128)
    distance = jnp.stack(
        [
            lanes,
            128 + side + 2 * signed,
            127 + side + 2 * signed,
            2 * lanes + 2 * side - 1,
            2 * lanes,
        ]
    ).reshape(-1)
    hot = (distance[:, None] == lanes[None, :]) & (lanes[None, :] < LANES - 1)
    parts = jnp.stack([prompt, even, odd, near, own], axis=2).reshape(heads, 5 * LANES)
    close = jnp.dot(parts, hot.astype(jnp.float32), precision=PRECISE)
    close = jnp.where(
        lanes[None, :] == LANES - 1, -jnp.sum(close, axis=1, keepdims=True), close
    )
    bucket_hot = (rel_bucket[:, None] == jnp.arange(buckets, dtype=jnp.int32)[None, :]).astype(
        jnp.float32
    )
    return jnp.dot(bucket_hot.T, close.T, precision=PRECISE)


def on_device(
    content_in,
    query_in,
    pred_order,
    cont_prompt,
    rel_bucket,
    w_query,
    b_query,
    w_key,
    w_value,
    b_value,
    w_out,
    b_out,
    ln1_gain,
    ln1_bias,
    w_up,
    b_up,
    w_down,
    b_down,
    ln2_gain,
    ln2_bias,
    bias_table,
    cot_content,
    cot_query,
):
    devices = lax.axis_size("fsdp")
    halfway = devices // 2
    own_rank = lax.axis_index("fsdp")
    plength = PD * halfway
    heads = bias_table.shape[1]
    extra_rows = query_in.shape[1]
    own_prompt = own_rank // halfway
    prompt_base = own_rank % halfway * PD
    cont_index = own_rank // 2
    side = own_rank % 2

    def gather(entry):
        return lax.all_gather(entry, "fsdp", axis=0, tiled=True)

    vectors = jnp.concatenate(
        [b_query, b_value, b_out, b_down, ln1_gain, ln1_bias, ln2_gain, ln2_bias, b_up]
    )
    query_weight, key_weight, value_weight = gather(w_query), gather(w_key), gather(w_value)
    all_vectors = gather(vectors[None])
    shard = b_query.shape[0]
    singles = [
        all_vectors[:, shard * i : shard * i + shard].reshape(-1).astype(jnp.float32)
        for i in range(8)
    ]
    (
        query_bias,
        value_bias,
        out_bias,
        down_bias,
        gain_one,
        shift_one,
        gain_two,
        shift_two,
    ) = singles
    up_bias = all_vectors[:, 8 * shard :].reshape(-1).astype(jnp.float32)
    out_weight, up_weight, down_weight = gather(w_out), gather(w_up), gather(w_down)

    prompt_map = cont_prompt[:, 0, :]
    prompt_ref = jnp.sum(
        jnp.where(
            jnp.arange(prompt_map.shape[1], dtype=jnp.int32)[None, :] == cont_index, prompt_map, 0
        ),
        axis=1,
    )
    meta = jnp.concatenate([jnp.stack([own_prompt, prompt_base, side]), prompt_ref]).astype(
        jnp.int32
    )
    order = jnp.pad(pred_order[:, 0, :], ((0, 0), (0, QP - extra_rows)), constant_values=-1)
    real = order >= 0
    in_prompt = order < PD
    position = jnp.where(
        in_prompt, prompt_base + order, plength + 2 * (order - PD) + side
    )
    limit_p = jnp.where(real & in_prompt, jnp.maximum(position, 1), -1)
    limit_c = jnp.where(real & ~in_prompt, position, -1)
    info = jnp.stack([position, limit_p, limit_c, order], axis=1)
    info = jnp.concatenate([info, info], axis=2)
    xrow = jnp.pad(info, ((0, 0), (0, 4), (0, 0))).astype(jnp.int32)
    xcol = jnp.swapaxes(xrow, 1, 2)
    dist = bias_table.astype(jnp.float32)[rel_bucket].T
    dist = dist - dist[:, LANES - 1 :]
    table = jnp.pad(dist.reshape(PAIRS, 2, LANES), ((0, 0), (0, 6), (0, 0)))

    tokens_x = content_in.reshape(MICRO * TD, D)
    extra_x = pad_rows(query_in)
    x_all = jnp.concatenate([tokens_x, extra_x])
    qkv_weight = jnp.concatenate([query_weight, key_weight, value_weight], axis=1)
    qkv_bias = jnp.concatenate([query_bias, jnp.zeros((D,), jnp.float32), value_bias])
    qkv = (
        jnp.dot(tokens_x, qkv_weight, preferred_element_type=jnp.float32) + qkv_bias
    ).astype(jnp.bfloat16)
    extra_q = (
        jnp.dot(extra_x, query_weight, preferred_element_type=jnp.float32) + query_bias
    ).astype(jnp.bfloat16)
    kv = qkv[:, D:].reshape(MICRO, TD, 2, D)
    kv = jnp.transpose(kv, (2, 0, 1, 3))
    prompt_kv = lax.all_gather(kv[:, :, :PD], "fsdp", axis=0)
    near_kv = from_partner(kv[:, :, PD:], "fsdp")

    ctx_c, ctx_x, full_c, full_x, lse = attend(
        meta, qkv, extra_q, prompt_kv, near_kv, table, xcol
    )
    context = jnp.concatenate([ctx_c, ctx_x])
    first, normed_one, inverse_one = layer_norm(
        x_all.astype(jnp.float32)
        + jnp.dot(context, out_weight, preferred_element_type=jnp.float32)
        + out_bias,
        gain_one,
        shift_one,
    )
    first_b = first.astype(jnp.bfloat16)
    hidden = jnp.dot(first_b, up_weight, preferred_element_type=jnp.float32) + up_bias
    active = jax.nn.gelu(hidden, approximate=False).astype(jnp.bfloat16)
    final, normed_two, inverse_two = layer_norm(
        first + jnp.dot(active, down_weight, preferred_element_type=jnp.float32) + down_bias,
        gain_two,
        shift_two,
    )
    rows_c = MICRO * TD
    out_content = final[:rows_c].reshape(MICRO, TD, D)
    out_query = final[rows_c:].reshape(MICRO, QP, D)[:, :extra_rows]

    upstream = jnp.concatenate(
        [cot_content.reshape(rows_c, D), pad_rows(cot_query)]
    ).astype(jnp.float32)
    dres_two, dgain_two, dshift_two = norm_back(upstream, normed_two, inverse_two, gain_two)
    dbias_down = jnp.sum(dres_two, axis=0)
    dres_two_b = dres_two.astype(jnp.bfloat16)
    dweight_down = dot_tn(active, dres_two_b)
    dactive = dot_nt(dres_two_b, down_weight).astype(jnp.bfloat16)
    dhidden = (dactive.astype(jnp.float32) * gelu_slope(hidden)).astype(jnp.bfloat16)
    dbias_up = jnp.sum(dhidden.astype(jnp.float32), axis=0)
    dweight_up = dot_tn(first_b, dhidden)
    dfirst = dres_two + dot_nt(dhidden, up_weight)
    dres_one, dgain_one, dshift_one = norm_back(dfirst, normed_one, inverse_one, gain_one)
    dbias_out = jnp.sum(dres_one, axis=0)
    dres_one_b = dres_one.astype(jnp.bfloat16)
    dweight_out = dot_tn(context, dres_one_b)
    dcontext = dot_nt(dres_one_b, out_weight).astype(jnp.bfloat16)

    dq_c, dq_x, dkv_prompt, dkv_near, dkv_own, hist = attend_back(
        meta,
        qkv,
        extra_q,
        prompt_kv,
        near_kv,
        table,
        xcol,
        xrow,
        lse,
        dcontext[:rows_c],
        dcontext[rows_c:],
        full_c,
        full_x,
    )
    own_prompt_grad = lax.psum_scatter(dkv_prompt, "fsdp", scatter_dimension=0)
    from_near = from_partner(dkv_near, "fsdp").astype(jnp.float32)
    dkv = jnp.concatenate(
        [own_prompt_grad, (dkv_own + from_near).astype(jnp.bfloat16)], axis=2
    ).reshape(2, rows_c, D)
    dqkv = jnp.concatenate([dq_c, dkv[0], dkv[1]], axis=1)
    dq_all = jnp.concatenate([dq_c, dq_x])
    dweight_query = dot_tn(x_all, dq_all)
    dbias_query = jnp.sum(dq_all.astype(jnp.float32), axis=0)
    dweight_kv = dot_tn(tokens_x, dqkv[:, D:])
    dbias_value = jnp.sum(dkv[1].astype(jnp.float32), axis=0)
    dtokens = dres_one[:rows_c] + dot_nt(dqkv, qkv_weight)
    dextra = dres_one[rows_c:] + dot_nt(dq_x, query_weight)
    grad_content = dtokens.reshape(MICRO, TD, D)
    grad_query = dextra.reshape(MICRO, QP, D)[:, :extra_rows]
    dtable = table_gradient(hist, rel_bucket, bias_table.shape[0], side, heads)

    def scatter(piece):
        return lax.psum_scatter(
            piece.astype(jnp.bfloat16), "fsdp", scatter_dimension=0, tiled=True
        )

    small = jnp.concatenate(
        [
            entry.reshape(devices, -1)
            for entry in (
                dbias_query,
                dbias_value,
                dbias_out,
                dbias_down,
                dgain_one,
                dshift_one,
                dgain_two,
                dshift_two,
                dbias_up,
                dtable,
            )
        ],
        axis=1,
    )
    shares = (
        scatter(dweight_down),
        scatter(dweight_up),
        scatter(dweight_out),
        scatter(dweight_query),
        scatter(dweight_kv),
        scatter(small),
    )
    totals = [lax.psum(entry, "grp").astype(jnp.float32) for entry in shares]
    t_down, t_up, t_out, t_query, t_kv, t_small = totals
    t_small = t_small.reshape(-1)
    pieces = [t_small[shard * i : shard * i + shard] for i in range(8)]
    up_at = 8 * shard
    up_size = b_up.shape[0]
    t_table = t_small[up_at + up_size :].reshape(-1, heads)
    return (
        out_content,
        out_query,
        grad_content,
        grad_query,
        t_query,
        pieces[0],
        t_kv[:, :D],
        t_kv[:, D:],
        pieces[1],
        t_out,
        pieces[2],
        pieces[4],
        pieces[5],
        t_up,
        t_small[up_at : up_at + up_size],
        t_down,
        pieces[3],
        pieces[6],
        pieces[7],
        t_table,
    )


def solution(mesh):
    rows = P(None, ("grp", "fsdp"), None)
    matrix = P("fsdp", None)
    vector = P("fsdp")
    in_specs = (
        rows,
        rows,
        rows,
        P(None, "grp", None),
        P(),
        matrix,
        vector,
        matrix,
        matrix,
        vector,
        matrix,
        vector,
        vector,
        vector,
        matrix,
        vector,
        matrix,
        vector,
        vector,
        vector,
        P(),
        rows,
        rows,
    )
    out_specs = (
        rows,
        rows,
        rows,
        rows,
        matrix,
        vector,
        matrix,
        matrix,
        vector,
        matrix,
        vector,
        vector,
        vector,
        matrix,
        vector,
        matrix,
        vector,
        vector,
        vector,
        matrix,
    )
    return jax.shard_map(
        on_device, mesh=mesh, in_specs=in_specs, out_specs=out_specs, check_vma=False
    )
```

time: 2120 us -> 771 us (0.36)
  matrix products: 1290 us -> 113 us
  other arithmetic: 146 us -> 28.5 us
  Pallas kernels: 0 us -> 96.8 us
  local copies, waits for them, and re-layouts: 152 us -> 71.1 us
  blocking collectives: 79.3 us -> 51.8 us
  waiting for transfers between devices: 412 us -> 386 us
    dot_general x99 -> x14, matrix products: 1250 us -> 71.4 us  [the longest x5 32.2 us: dot_tn(): lax.dot_general(left, right, (((0,), (0,)), ((), ())), preferred_element_...]
    all_gather x10 -> x7, waiting for transfers between devices: 25.6 us -> 138 us  [the longest x6 91.5 us: gather(): return lax.all_gather(entry, 'fsdp', axis=0, tiled=True)]
    unnamed x37 -> x15, waiting for transfers between devices: 113 us -> 3.94 us
    pallas_call x0 -> x2, Pallas kernels: none -> 96.8 us  [the longest x1 52.6 us: attend_back(): pl.pallas_call(functools.partial(attend_back_kernel, plength), name='atte...]
    unnamed x503 -> x89, local copies, waits for them, and re-layouts: 69.2 us -> 21.8 us
    concatenate x21 -> x3, other arithmetic: 41.3 us -> 0.68 us  [the longest x1 0.59 us: on_device(): jnp.concatenate([jnp.stack([own_prompt, prompt_base, side]), prompt_ref])]
    unnamed x2 -> x1, blocking collectives: 55.1 us -> 25.9 us
    convert_element_type x44 -> x8, other arithmetic: 38.3 us -> 11.3 us  [the longest x5 5.9 us: on_device(): totals = [lax.psum(entry, 'grp').astype(jnp.float32) for entry in shares]]
  transfers between devices with their start and end apart: 35 -> 16, of which waited for: 15 -> 13; matrix products, arithmetic and copies ran while one was open for 58% -> 18% of each run, Pallas kernels for 0% -> 6%
where the time goes in v1:
time: 771 us; the launch traced here: 764 us
  waiting for transfers between devices  386 us (50%)
  matrix products  113 us (15%)
  Pallas kernels  96.8 us (13%)
  local copies, waits for them, and re-layouts  71.1 us (9%)
  blocking collectives  51.8 us (7%)
  other arithmetic  28.5 us (4%)
  between operations  14.9 us (2%)
    reduce_scatter x4, waiting for transfers between devices, scatter(): lax.psum_scatter(piece.astype(jnp.bfloat16), 'fsdp', scatter_dimension=0,...  161 us
    all_gather x6, waiting for transfers between devices, gather(): return lax.all_gather(entry, 'fsdp', axis=0, tiled=True)  91.5 us
    reduce_scatter x1, waiting for transfers between devices, on_device(): own_prompt_grad = lax.psum_scatter(dkv_prompt, 'fsdp', scatter_dimension=0)  61 us
    pallas_call x1, Pallas kernels, attend_back(): pl.pallas_call(functools.partial(attend_back_kernel, plength), name='atte...  52.6 us
    all_gather x1, waiting for transfers between devices, on_device(): prompt_kv = lax.all_gather(kv[:, :, :PD], 'fsdp', axis=0)  46.5 us
    pallas_call x1, Pallas kernels, attend(): pl.pallas_call(functools.partial(attend_kernel, plength), name='attend',...  44.3 us
    dot_general x5, matrix products, dot_tn(): lax.dot_general(left, right, (((0,), (0,)), ((), ())), preferred_element_...  32.2 us
    dot_general x1, matrix products, on_device(): jnp.dot(first_b, up_weight, preferred_element_type=jnp.float32) + up_bias  31.7 us
  transfers between devices with their start and end apart: 16, of which 13 were waited for; matrix products, arithmetic and copies ran while one was open for 18% of the time, Pallas kernels for 6%

profile of v1, /device:TPU:0, one launch (start us, length us, event | category | flops | bytes accessed | tf_op | source)
XLA Modules:
  0.0 764.0 jit_solution(13813520436698382141)
XLA Ops:
  9.5 6.1 concatenate.43
  15.6 15.9 %all-gather.2 = bf16[8,1,1152]{2,1,0:T(2,128)(2,1)S(1)} all-gather(bf16[1,1,1152]{2,1,0:T(2,128)(2,1)S(1)} %reshape.351), channel_id=2, replica_groups=mesh['grp'=4,'fsdp'=8] {'fsdp'}, dimensions={0}, use_global_device_ids=true | all-gather | bytes 20736 | tf_op jit(solution)/shard_map/all_gather | solution.py:748
  33.4 1.9 all-gather.11.cloned.1.call-done
  35.3 1.3 constant_dynamic-update-slice_fusion.2
  36.6 22.8 %all-gather.13.cloned.1.call-done = bf16[768,768]{1,0:T(8,128)(2,1)} async-done(((bf16[96,768]{1,0:T(8,128)(2,1)}), bf16[768,768]{1,0:T(8,128)(2,1)}) %all-gather.13.cloned.1.call-update) | async-done | bytes 1179664 | tf_op jit(solution)/shard_map/all_gather | solution.py:748
  59.4 1.3 constant_dynamic-update-slice_fusion.1
  60.7 22.8 %all-gather.15.cloned.1.call-done = bf16[768,768]{1,0:T(8,128)(2,1)} async-done(((bf16[96,768]{1,0:T(8,128)(2,1)}), bf16[768,768]{1,0:T(8,128)(2,1)}) %all-gather.15.cloned.1.call-update) | async-done | bytes 1179664 | tf_op jit(solution)/shard_map/all_gather | solution.py:748
  83.5 1.3 constant_dynamic-update-slice_fusion
  84.9 1.8 copy-done.18
  86.6 5.3 fusion.16.qc.kc.vc
  91.9 1.8 slice.206
  93.7 6.2 reshape.310
  99.8 2.0 copy.130
  101.8 1.4 copy-done.6
  108.5 1.2 slice.208
  116.8 0.9 pad.19
  119.2 1.5 pad_reduce_fusion
  120.8 1.7 fusion.41.qx
  122.4 46.5 %all-gather.23.cloned.1.call-done = bf16[16,2,128,768]{3,2,1,0:T(8,128)(2,1)} async-done(((bf16[2,2,128,768]{3,2,1,0:T(8,128)(2,1)}), bf16[16,2,128,768]{3,2,1,0:T(8,128)(2,1)}) %all-gather.23.cloned.1.call-update) | async-done | bytes 6291472 | tf_op jit(solution)/shard_map/all_gather | solution.py:812
  168.9 44.3 %attend.1 = (bf16[768,768]{1,0:T(8,128)(2,1)}, bf16[128,768]{1,0:T(8,128)(2,1)}, f32[768,768]{1,0:T(8,128)}, f32[128,768]{1,0:T(8,128)}, f32[2,6,8,128]{3,2,1,0:T(8,128)}) custom-call(s32[5]{0:T(128)} %pad_add_fusion.meta, bf16[768,2304]{1,0:T(8,128)(2,1)} %copy-done, bf16[128,768]{1,0:T(8,128)(2,1)} %fusion.41.qx, bf16[8,2,2,128,768]{4,3,2,1,0:T(8,128)(2,1)} %bitcast.98, ...), custom_call_target="tpu_custom_call" | custom-call | flops 5234491392 | bytes 16777216 | tf_op jit(solution)/shard_map/attend/pallas_call | solution.py:234
  213.2 2.4 constant_dynamic-update-slice_fusion.4
  215.6 1.6 constant_dynamic-update-slice_fusion.3
  217.2 3.4 fusion.69
  221.1 23.6 %all-gather.19.cloned.1.call-done = bf16[768,3072]{1,0:T(8,128)(2,1)} async-done(((bf16[96,3072]{1,0:T(8,128)(2,1)}), bf16[768,3072]{1,0:T(8,128)(2,1)}) %all-gather.19.cloned.1.call-update) | async-done | bytes 4718608 | tf_op jit(solution)/shard_map/all_gather | solution.py:748
  244.7 31.7 %fusion.2 = (bf16[896,3072]{1,0:T(8,128)(2,1)}, f32[896,3072]{1,0:T(8,128)}) fusion(f32[3072]{0:T(1024)S(1)} %reshape.336, bf16[768,3072]{1,0:T(8,128)(2,1)} %all-gather.19.cloned.1.call-done, f32[896,768]{1,0:T(8,128)S(1)} %get-tuple-element.212, f32[768]{0:T(1024)S(1)} %reshape.335, f32[768]{0:T(1024)S(1)} %reshape.334, f32[896]{0:T(1024)S(1)} %add_rsqrt_fusion.1, ...), kind=kOutput, calls=%fused_computation.5 | convolution fusion | flops 4412964864 | bytes 24011776 | tf_op jit(solution)/shard_map/dot_general | solution.py:827
  276.4 20.5 %all-gather.21.cloned.1.call-done = bf16[3072,768]{1,0:T(8,128)(2,1)} async-done(((bf16[384,768]{1,0:T(8,128)(2,1)}), bf16[3072,768]{1,0:T(8,128)(2,1)}) %all-gather.21.cloned.1.call-update) | async-done | bytes 4718608 | tf_op jit(solution)/shard_map/all_gather | solution.py:748
  296.9 8.7 %fusion.70 = (f32[896]{0:T(1024)S(1)}, f32[896,768]{1,0:T(8,128)S(1)}) fusion(f32[768]{0:T(1024)S(1)} %reshape.337, bf16[896,3072]{1,0:T(8,128)(2,1)} %get-tuple-element.213, bf16[3072,768]{1,0:T(8,128)(2,1)} %all-gather.21.cloned.1.call-done, f32[768]{0:T(1024)S(1)} %reshape.335, f32[768]{0:T(1024)S(1)} %reshape.334, f32[896]{0:T(1024)S(1)} %add_rsqrt_fusion.1, ...), kind=kOutput, calls=%fused_computation.174 | convolution fusion | flops 4232674304 | bytes 15748608 | tf_op jit(solution)/shard_map/dot_general | solution.py:830
  306.9 1.3 fusion.30
  308.2 1.6 fusion.63
  310.5 12.1 %fusion.71 = (bf16[3072]{0:T(1024)(128)(2,1)}, bf16[896,3072]{1,0:T(8,128)(2,1)S(1)}) fusion(f32[896,3072]{1,0:T(8,128)} %get-tuple-element.214, f32[3072]{0:T(1024)S(1)} %reshape.336, bf16[3072,768]{1,0:T(8,128)(2,1)S(1)} %copy-done.28, f32[896,768]{1,0:T(8,128)S(1)} %get-tuple-element.178), kind=kOutput, calls=%fused_computation.175 | convolution fusion | flops 4267078656 | bytes 24004608 | tf_op jit(solution)/shard_map/dot_general | solution.py:26
  322.6 5.6 multiply_reduce_fusion
  328.2 1.7 fusion.65
  330.0 1.3 convolution_convert_fusion.3
  331.6 1.1 slice.221.dc
  333.4 52.6 %attend_back.1 = (bf16[768,768]{1,0:T(8,128)(2,1)}, bf16[128,768]{1,0:T(8,128)(2,1)}, bf16[8,2,2,128,768]{4,3,2,1,0:T(8,128)(2,1)}, bf16[2,2,256,768]{3,2,1,0:T(...) custom-call(s32[5]{0:T(128)} %pad_add_fusion.meta, bf16[768,2304]{1,0:T(8,128)(2,1)} %copy-done, ...), custom_call_target="tpu_custom_call" | custom-call | flops 13086228480 | bytes 33554432 | tf_op jit(solution)/shard_map/attend_back/pallas_call | solution.py:568
  386.3 3.4 collective-permute-done.1
  389.7 4.0 add_convert_fusion.1
  393.7 61.0 %reduce-scatter.9.cloned.1.call-done = bf16[1,2,2,128,768]{4,3,2,1,0:T(8,128)(2,1)} async-done(((bf16[8,2,2,128,768]{4,3,2,1,0:T(8,128)(2,1)}), bf16[1,2,2,128,768]{4,3,2,1,0:T(8,128)(2,1)}) %reduce-scatter.9.cloned.1.call-update) | async-done | bytes 786448 | tf_op jit(solution)/shard_map/reduce_scatter | solution.py:871
  454.7 2.5 fusion.66
  457.3 1.0 copy-done.13
  458.6 3.5 fusion.26
  462.1 4.3 copy.124
  466.5 4.8 convolution_convert_fusion.4
  471.3 4.1 convolution_convert_fusion.5
  475.5 9.7 %convolution_convert_fusion = bf16[3072,768]{1,0:T(8,128)(2,1)} fusion(bf16[896,3072]{1,0:T(8,128)(2,1)} %get-tuple-element.213, f32[896,768]{1,0:T(8,128)} %copy-done.10), kind=kOutput, calls=%fused_computation.28 | convolution fusion | flops 4230905856 | bytes 12976128 | tf_op jit(solution)/shard_map/dot_general | solution.py:32
  485.3 10.2 %convolution_convert_fusion.1 = bf16[768,3072]{1,0:T(8,128)(2,1)} fusion(bf16[896,3072]{1,0:T(8,128)(2,1)} %copy-done.33, f32[896,768]{1,0:T(8,128)} %copy-done.1, f32[768]{0:T(1024)S(1)} %reshape.335, f32[768]{0:T(1024)S(1)} %reshape.334, f32[896]{0:T(1024)S(1)} %add_rsqrt_fusion.1, f32[896]{0:T(1024)S(1)} %broadcast_multiply_fusion.5), kind=kOutput, calls=%fused_computation.29 | convolution fusion | flops 4233658368 | bytes 12989440 | tf_op jit(solution)/shard_map/dot_general | solution.py:32
  495.5 1.6 reduce.12
  500.1 3.6 slice.177
  503.6 3.5 slice.178
  507.2 1.5 reduce.10
  508.7 1.6 slice.217
  512.1 1.1 fusion.72
  517.5 1.9 copy.125
  519.4 16.0 %reduce-scatter.13.cloned.1.call-done = bf16[96,768]{1,0:T(8,128)(2,1)} async-done(((bf16[768,768]{1,0:T(8,128)(2,1)}), bf16[96,768]{1,0:T(8,128)(2,1)}) %reduce-scatter.13.cloned.1.call-update) | async-done | bytes 147472 | tf_op jit(solution)/shard_map/reduce_scatter | solution.py:889
  535.5 33.9 %reduce-scatter.11.cloned.1.call-done = bf16[96,768]{1,0:T(8,128)(2,1)} async-done(((bf16[768,768]{1,0:T(8,128)(2,1)}), bf16[96,768]{1,0:T(8,128)(2,1)}) %reduce-scatter.11.cloned.1.call-update) | async-done | bytes 147472 | tf_op jit(solution)/shard_map/reduce_scatter | solution.py:889
  569.3 55.2 %reduce-scatter.17.cloned.1.call-done = bf16[384,768]{1,0:T(8,128)(2,1)} async-done(((bf16[3072,768]{1,0:T(8,128)(2,1)}), bf16[384,768]{1,0:T(8,128)(2,1)}) %reduce-scatter.17.cloned.1.call-update) | async-done | bytes 589840 | tf_op jit(solution)/shard_map/reduce_scatter | solution.py:889
  624.5 55.7 %reduce-scatter.15.cloned.1.call-done = bf16[96,3072]{1,0:T(8,128)(2,1)} async-done(((bf16[768,3072]{1,0:T(8,128)(2,1)}), bf16[96,3072]{1,0:T(8,128)(2,1)}) %reduce-scatter.15.cloned.1.call-update) | async-done | bytes 589840 | tf_op jit(solution)/shard_map/reduce_scatter | solution.py:889
  680.2 1.6 convolution_add_fusion.1
  683.5 25.9 %all-reduce.5 = bf16[8,1200]{1,0:T(8,128)(2,1)S(1)} all-reduce(bf16[8,1200]{1,0:T(8,128)(2,1)S(1)} %concatenate.51), channel_id=6, replica_groups=mesh['grp'=4,'fsdp'=8] {'fsdp'}, use_global_device_ids=true, to_apply=%region_28.29.clone | all-reduce | flops 9600 | bytes 38400
  710.2 10.0 %psum.43 = bf16[1,1200]{1,0:T(2,128)(2,1)S(1)} all-reduce(bf16[1,1200]{1,0:T(2,128)(2,1)S(1)} %constant_dynamic-slice_fusion), channel_id=1, replica_groups=mesh['grp'=4,'fsdp'=8] {'grp'}, use_global_device_ids=true, to_apply=%region_29.30 | all-reduce | flops 1200 | bytes 4800 | tf_op jit(solution)/shard_map/psum | solution.py:919
  722.1 8.0 %slice_add_fusion = f32[768,768]{1,0:T(8,128)} fusion(f32[896,768]{1,0:T(8,128)} %copy-done.9, bf16[768,2304]{1,0:T(8,128)(2,1)} %copy-done.18, bf16[768,768]{1,0:T(8,128)(2,1)} %bitcast.116, bf16[768,768]{1,0:T(8,128)(2,1)} %bitcast.118, bf16[768,768]{1,0:T(8,128)(2,1)S(1)} %copy-done.12), kind=kOutput, calls=%fused_computation.62 | convolution fusion | flops 2729115648 | bytes 11796480 | tf_op jit(solution)/shard_map/dot_general | solution.py:26
  730.0 19.3 %all-reduce.9.cloned.1.call-done = (bf16[96,1536]{0,1:T(8,128)(2,1)}, bf16[96,768]{1,0:T(8,128)(2,1)}, bf16[96,768]{1,0:T(8,128)(2,1)}, bf16[96,3072]{1,0:T(8,128)(2,1)}, bf16[384,768]{1,0:T(8,128)(2,1)}) async-done(((bf16[96,1536]{0,1:T(8,128)(2,1)}, bf16[96,768]{1,0:T(8,128)(2,1)}, bf16[96,768]{1,0:T(8,128)(2,1)}, bf16[96,3072]{1,0:T(8,128)(2,1)}, bf16[384,768]{1,0:T(8,128)(2,1)}), ...) | async-done | bytes 1769488 | tf_op jit(solution)/shard_map/psum | solution.py:919
  749.4 2.2 convert_element_type.233
  751.6 2.2 convert_element_type.235
  (196 shorter events, 39.0 us)
Async XLA Ops:
  7.2 28.1 %all-gather.11.cloned.1.call-start = ((), (), s32[]{:S(2)}) async-start(), calls=%async_computation.6 | async-start | bytes 1327104 | tf_op jit(solution)/shard_map/all_gather | solution.py:748
  7.9 51.5 %all-gather.13.cloned.1.call-start = ((), (), s32[]{:S(2)}) async-start(), calls=%async_computation.7 | async-start | bytes 1327104 | tf_op jit(solution)/shard_map/all_gather | solution.py:748
  8.7 74.8 %all-gather.15.cloned.1.call-start = ((), (), s32[]{:S(2)}) async-start(), calls=%async_computation.8 | async-start | bytes 1327104 | tf_op jit(solution)/shard_map/all_gather | solution.py:748
  9.4 159.5 %all-gather.23.cloned.1.call-start = ((), (), s32[]{:S(2)}) async-start(), calls=%async_computation.17 | async-start | bytes 7077888 | tf_op jit(solution)/shard_map/all_gather | solution.py:812
  31.4 0.6 copy-start.22
  32.8 0.6 copy-start.23
  84.8 1.8 copy-start.18
  91.9 8.0 %copy-start = (bf16[768,2304]{1,0:T(8,128)(2,1)}, bf16[768,2304]{1,0:T(8,128)(2,1)S(1)}, u32[]{:S(2)}) copy-start(bf16[768,2304]{1,0:T(8,128)(2,1)S(1)} %fusion.16.qc.kc.vc) | copy-start | bytes 10616836
  101.8 1.4 copy-start.6
  101.8 4.4 copy-start.27
  104.2 4.3 copy-start.7
  104.2 113.0 %all-gather.17.cloned.1.call-start = ((), (), s32[]{:S(2)}) async-start(), calls=%async_computation.9 | async-start | bytes 1327104 | tf_op jit(solution)/shard_map/all_gather | solution.py:748
  104.8 139.9 %all-gather.19.cloned.1.call-start = ((), (), s32[]{:S(2)}) async-start(), calls=%async_computation.10 | async-start | bytes 5308416 | tf_op jit(solution)/shard_map/all_gather | solution.py:748
  105.3 15.4 %copy-start.4 = (bf16[768,768]{1,0:T(8,128)(2,1)S(1)}, bf16[768,768]{1,0:T(8,128)(2,1)}, u32[]{:S(2)}) copy-start(bf16[768,768]{1,0:T(8,128)(2,1)} %all-gather.11.cloned.1.call-done) | copy-start | bytes 3538948
  105.4 191.5 %all-gather.21.cloned.1.call-start = ((), (), s32[]{:S(2)}) async-start(), calls=%async_computation.11 | async-start | bytes 5308416 | tf_op jit(solution)/shard_map/all_gather | solution.py:748
  106.1 348.6 %reduce-scatter.9.cloned.1.call-start = ((), (), s32[]{:S(2)}) async-start(), calls=%async_computation.12 | async-start | bytes 7077888 | tf_op jit(solution)/shard_map/reduce_scatter | solution.py:871
  108.5 1.5 copy-start.31
  109.7 12.7 %collective-permute-start = (bf16[2,2,256,768]{3,2,1,0:T(8,128)(2,1)}, bf16[2,2,256,768]{3,2,1,0:T(8,128)(2,1)S(1)}, u32[]{:S(2)}, u32[]{:S(2)}) collective-permute-start(bf16[2,2,256,768]{3,2,1,0:T(8,128)(2,1)} %slice.208), channel_id=1, source_target_pairs={{0,1},{1,0},{2,3},{3,2},{4,5},{5,4},{6,7},{7,6},{8,9},{9,8},{10,11... | collective-permute-start | bytes 4718600 | tf_op jit(solution)/shard_map/ppermute | solution.py:650
  117.8 99.5 %copy-start.16 = (bf16[2,64,768]{2,1,0:T(8,128)(2,1)}, bf16[2,64,768]{2,1,0:T(8,128)(2,1)S(1)}, u32[]{:S(2)}) copy-start(bf16[2,64,768]{2,1,0:T(8,128)(2,1)S(1)} %pad.19) | copy-start | bytes 589828
  122.4 46.5 %copy-start.8 = (bf16[2,2,256,768]{3,2,1,0:T(8,128)(2,1)}, bf16[2,2,256,768]{3,2,1,0:T(8,128)(2,1)S(1)}, u32[]{:S(2)}) copy-start(bf16[2,2,256,768]{3,2,1,0:T(8,128)(2,1)S(1)} %collective-permute-done.kn.vn) | copy-start | bytes 4718596
  220.6 76.3 %copy-start.1 = (f32[896,768]{1,0:T(8,128)}, f32[896,768]{1,0:T(8,128)S(1)}, u32[]{:S(2)}) copy-start(f32[896,768]{1,0:T(8,128)S(1)} %get-tuple-element.212) | copy-start | bytes 8257540
  305.6 1.3 copy-start.3
  308.2 2.3 copy-start.28
  308.2 14.4 %slice-start = ((s8[4718592]{0:T(1024)(128)(4,1)}), s8[4194304]{0:T(1024)(128)(4,1)S(1)}, s32[]{:S(2)}) async-start(s8[4718592]{0:T(1024)(128)(4,1)} %bitcast.140), calls=%async_computation.20 | async-start | bytes 8388608
  309.8 12.8 %copy-start.10 = (f32[896,768]{1,0:T(8,128)}, f32[896,768]{1,0:T(8,128)S(1)}, u32[]{:S(2)}) copy-start(f32[896,768]{1,0:T(8,128)S(1)} %get-tuple-element.178) | copy-start | bytes 8257540
  310.5 12.1 %copy-start.2 = (f32[896,768]{1,0:T(8,128)S(1)}, f32[896,768]{1,0:T(8,128)}, u32[]{:S(2)}) copy-start(f32[896,768]{1,0:T(8,128)} %copy-done.1) | copy-start | bytes 8257540
  310.5 12.1 %slice-start.1 = ((s8[4718592]{0:T(1024)(128)(4,1)}), s8[524288]{0:T(1024)(128)(4,1)S(1)}, s32[]{:S(2)}) async-start(s8[4718592]{0:T(1024)(128)(4,1)} %bitcast.140), calls=%async_computation.21 | async-start | bytes 1048576
  322.6 5.6 copy-start.33
  328.2 1.7 copy-start.30
  330.0 1.6 copy-start.9
  385.9 131.6 %reduce-scatter.19.cloned.1.call-start = ((), (), s32[]{:S(2)}) async-start(), calls=%async_computation.18 | async-start | bytes 2654208
  386.0 3.7 collective-permute-start.1
  454.7 3.9 copy-start.29
  457.3 1.0 copy-start.13
  457.3 1.4 copy-start.14
  466.4 4.9 copy-start.15
  466.4 4.9 copy-start.17
  466.4 69.0 %reduce-scatter.13.cloned.1.call-start = ((), (), s32[]{:S(2)}) async-start(), calls=%async_computation.14 | async-start | bytes 1327104 | tf_op jit(solution)/shard_map/reduce_scatter | solution.py:889
  471.3 98.0 %reduce-scatter.11.cloned.1.call-start = ((), (), s32[]{:S(2)}) async-start(), calls=%async_computation.13 | async-start | bytes 1327104 | tf_op jit(solution)/shard_map/reduce_scatter | solution.py:889
  475.5 149.1 %reduce-scatter.17.cloned.1.call-start = ((), (), s32[]{:S(2)}) async-start(), calls=%async_computation.16 | async-start | bytes 5308416 | tf_op jit(solution)/shard_map/reduce_scatter | solution.py:889
  485.2 195.0 %reduce-scatter.15.cloned.1.call-start = ((), (), s32[]{:S(2)}) async-start(), calls=%async_computation.15 | async-start | bytes 5308416 | tf_op jit(solution)/shard_map/reduce_scatter | solution.py:889
  495.4 1.7 copy-start.24
  495.4 2.3 copy-start.32
  495.4 4.6 copy-start.19
  495.5 253.9 %all-reduce.9.cloned.1.call-start = ((), (), s32[]{:S(2)}) async-start(), calls=%async_computation.19 | async-start | bytes 3735552 | tf_op jit(solution)/shard_map/psum | solution.py:919
  510.3 169.9 %copy-start.5 = (bf16[768,768]{1,0:T(8,128)(2,1)S(1)}, bf16[768,768]{1,0:T(8,128)(2,1)}, u32[]{:S(2)}) copy-start(bf16[768,768]{1,0:T(8,128)(2,1)} %all-gather.11.cloned.1.call-done) | copy-start | bytes 3538948
  519.4 163.9 %copy-start.25 = (bf16[768]{0:T(1024)(128)(2,1)S(1)}, bf16[768]{0:T(1024)(128)(2,1)}, u32[]{:S(2)}) copy-start(bf16[768]{0:T(1024)(128)(2,1)} %get-tuple-element.181) | copy-start | bytes 4612
  519.4 164.0 %copy-start.26 = (bf16[8,96]{1,0:T(8,128)(2,1)S(1)}, bf16[8,96]{1,0:T(8,128)(2,1)}, u32[]{:S(2)}) copy-start(bf16[8,96]{1,0:T(8,128)(2,1)} %reshape.325) | copy-start | bytes 4612
  680.2 41.9 %copy-start.12 = (bf16[768,768]{1,0:T(8,128)(2,1)S(1)}, bf16[768,768]{1,0:T(8,128)(2,1)}, u32[]{:S(2)}) copy-start(bf16[768,768]{1,0:T(8,128)(2,1)} %get-tuple-element.36) | copy-start | bytes 3538948
  749.4 4.4 copy-start.11
  751.6 4.0 copy-start.21
  751.6 4.7 copy-start.20
Sparse Core Ops, SparseCore 0:
  9.7 25.5 all-gather.10
  36.9 22.4 all-gather.12
  61.0 22.4 all-gather.14
  104.3 64.5 all-gather.22
  170.4 21.2 all-gather.16
  193.2 51.4 all-gather.18
  246.3 50.5 all-gather.20
  386.1 68.6 reduce-scatter.8
  466.5 34.6 reduce-scatter.18
  503.4 32.0 reduce-scatter.12
  538.3 30.9 reduce-scatter.10
  571.5 53.0 reduce-scatter.16
  626.8 53.3 reduce-scatter.14
  683.7 65.5 all-reduce.8

commit v2 on v1

--- a/solution.py
+++ b/solution.py
@@ -60,15 +60,19 @@
     return jnp.clip(distance, 0, LANES - 1)
 
 
-def fill_keys(scratch, own_ref, map_ref, near_ref, cont_ref, plength):
-    scratch[0:plength] = own_ref[...].reshape(plength, LANES)
-    scratch[plength : 2 * plength] = map_ref[...].reshape(plength, LANES)
-    near = near_ref[...].reshape(CH, LANES)
-    at = 2 * plength
-    scratch[at : at + 128] = near[0:128]
-    scratch[at + 128 : at + 256] = cont_ref[PD : PD + 128]
-    scratch[at + 256 : at + 384] = near[128:256]
-    scratch[at + 384 : at + 512] = cont_ref[PD + 128 : PD + 256]
+def fill_keys(scratch, rows_ref, own_prompt, mapped, plength):
+    own_at = pl.multiple_of(own_prompt * plength, 128)
+    scratch[0:plength] = rows_ref[pl.ds(own_at, plength), :]
+    scratch[plength : 2 * plength] = jnp.where(
+        mapped == 0, rows_ref[0:plength], rows_ref[plength : 2 * plength]
+    )
+    scratch[2 * plength :] = rows_ref[2 * plength :]
+
+
+def place(plength):
+    rank = lax.axis_index("fsdp")
+    halfway = plength // PD
+    return rank // halfway, rank % halfway * PD, rank % 2
 
 
 def attend_kernel(
@@ -76,31 +80,66 @@
     meta,
     qc,
     qx,
-    ko,
-    vo,
-    km,
-    vm,
-    kn,
-    vn,
-    kc,
-    vc,
+    k_rows,
+    v_rows,
     table,
     xcol,
+    w_ref,
     ctx_c,
     ctx_x,
     full_c,
     full_x,
     lse_ref,
+    w_all,
     keys,
     vals,
     scores,
     probs,
+    send_sem,
+    recv_sem,
+    local_sem,
 ):
-    base = meta[1]
-    side = meta[2]
+    step = pl.program_id(0) * PAIRS + pl.program_id(1)
+    grp = lax.axis_index("grp")
+    rank = lax.axis_index("fsdp")
+    core_mate = (grp, rank ^ 1)
+    x_mate = (grp ^ 1, rank)
+    local = pltpu.make_async_copy(w_ref, w_all.at[0], local_sem)
+    swap = pltpu.make_async_remote_copy(
+        w_ref, w_all.at[1], send_sem.at[0], recv_sem.at[0], device_id=core_mate,
+        device_id_type=pl.DeviceIdType.MESH,
+    )
+    cross = pltpu.make_async_remote_copy(
+        w_all.at[0:2], w_all.at[2:4], send_sem.at[1], recv_sem.at[1], device_id=x_mate,
+        device_id_type=pl.DeviceIdType.MESH,
+    )
+
+    @pl.when(step == 0)
+    def _():
+        barrier = pltpu.get_barrier_semaphore()
+        for mate in (core_mate, x_mate):
+            pl.semaphore_signal(
+                barrier, inc=1, device_id=mate, device_id_type=pl.DeviceIdType.MESH
+            )
+        pl.semaphore_wait(barrier, 2)
+        local.start()
+        swap.start()
+
+    @pl.when(step == 5)
+    def _():
+        local.wait()
+        swap.wait()
+        cross.start()
+
+    @pl.when(step == 11)
+    def _():
+        cross.wait()
+
+    own_prompt, base, side = place(plength)
+    mapped = meta[pl.program_id(0)]
     blocks = plength // 128
-    fill_keys(keys, ko, km, kn, kc, plength)
-    fill_keys(vals, vo, vm, vn, vc, plength)
+    fill_keys(keys, k_rows, own_prompt, mapped, plength)
+    fill_keys(vals, v_rows, own_prompt, mapped, plength)
     row = lax.broadcasted_iota(jnp.int32, (128, 128), 0)
     col = lax.broadcasted_iota(jnp.int32, (128, 128), 1)
     tab_a = jnp.broadcast_to(table[0, 0:1, :], (128, 128))
@@ -206,27 +245,16 @@
     return lambda m, j, meta: (m, shift * PAIRS + j)
 
 
-def prompt_specs(half):
-    def at(kv, mapped):
-        def index(m, j, meta):
-            return (meta[3 + m] if mapped else meta[0], kv, m, 0, j)
-
-        return pl.BlockSpec((half, 1, 1, PD, LANES), index)
-
-    return [at(0, False), at(1, False), at(0, True), at(1, True)]
-
-
-def near_spec(kv):
-    return pl.BlockSpec((1, 1, CH, LANES), lambda m, j, meta: (kv, m, 0, j))
+def key_spec(n_keys, shift):
+    return pl.BlockSpec((n_keys, LANES), lambda m, j, meta: (m, shift * PAIRS + j))
 
 
 TABLE_SPEC = pl.BlockSpec((1, 8, LANES), lambda m, j, meta: (j, 0, 0))
 
 
-def attend(meta, qkv, extra_q, prompt_kv, near_kv, table, xcol):
-    half = prompt_kv.shape[0] // 2
-    plength = half * PD
-    n_keys = 2 * plength + 2 * CH
+def attend(meta, queries, extra_q, key_rows, table, xcol, weight):
+    n_keys = key_rows.shape[0] // MICRO
+    plength = (n_keys - 2 * CH) // 2
     content = pl.BlockSpec((TD, LANES), pair_column(0))
     extra = pl.BlockSpec((QP, LANES), pair_column(0))
     own_row = plength + 2 * CH
@@ -238,14 +266,12 @@
             num_scalar_prefetch=1,
             grid=(MICRO, PAIRS),
             in_specs=[content, extra]
-            + prompt_specs(half)
             + [
-                near_spec(0),
-                near_spec(1),
-                pl.BlockSpec((TD, LANES), pair_column(1)),
-                pl.BlockSpec((TD, LANES), pair_column(2)),
+                key_spec(n_keys, 0),
+                key_spec(n_keys, 1),
                 TABLE_SPEC,
                 pl.BlockSpec((1, 128, 8), lambda m, j, meta: (m, 0, 0)),
+                pl.BlockSpec(memory_space=pl.ANY),
             ],
             out_specs=[
                 content,
@@ -253,12 +279,16 @@
                 content,
                 extra,
                 pl.BlockSpec((1, 1, 8, LANES), lambda m, j, meta: (m, j, 0, 0)),
+                pl.BlockSpec(memory_space=pl.ANY),
             ],
             scratch_shapes=[
                 pltpu.VMEM((n_keys, LANES), jnp.bfloat16),
                 pltpu.VMEM((n_keys, LANES), jnp.bfloat16),
                 pltpu.VMEM((256, n_keys), jnp.float32),
                 pltpu.VMEM((256, n_keys), jnp.bfloat16),
+                pltpu.SemaphoreType.DMA((2,)),
+                pltpu.SemaphoreType.DMA((2,)),
+                pltpu.SemaphoreType.DMA,
             ],
         ),
         out_shape=[
@@ -267,25 +297,23 @@
             jax.ShapeDtypeStruct((MICRO * TD, D), jnp.float32),
             jax.ShapeDtypeStruct((MICRO * QP, D), jnp.float32),
             jax.ShapeDtypeStruct((MICRO, PAIRS, 8, LANES), jnp.float32),
+            jax.ShapeDtypeStruct((4,) + weight.shape, weight.dtype),
         ],
-        compiler_params=pltpu.CompilerParams(vmem_limit_bytes=VMEM_LIMIT),
+        compiler_params=pltpu.CompilerParams(
+            vmem_limit_bytes=VMEM_LIMIT, collective_id=1, has_side_effects=True
+        ),
         cost_estimate=pl.CostEstimate(
             flops=4 * pairs * LANES, bytes_accessed=16 * 1024 * 1024, transcendentals=pairs
         ),
     )(
         meta,
-        qkv,
+        queries,
         extra_q,
-        prompt_kv,
-        prompt_kv,
-        prompt_kv,
-        prompt_kv,
-        near_kv,
-        near_kv,
-        qkv,
-        qkv,
+        key_rows,
+        key_rows,
         table,
         xcol,
+        weight,
     )
 
 
@@ -294,14 +322,8 @@
     meta,
     qc,
     qx,
-    ko,
-    vo,
-    km,
-    vm,
-    kn,
-    vn,
-    kc,
-    vc,
+    k_rows,
+    v_rows,
     table,
     xcol,
     xrow,
@@ -312,9 +334,8 @@
     full_x,
     dq_c,
     dq_x,
-    dkv_prompt,
-    dkv_near,
-    dkv_own,
+    dk_rows,
+    dv_rows,
     hist,
     keys,
     vals,
@@ -327,17 +348,14 @@
     ds_p,
     dk_acc,
     dv_acc,
-    d_prompt,
 ):
-    own_prompt = meta[0]
-    base = meta[1]
-    side = meta[2]
-    mapped = meta[3 + pl.program_id(0)]
+    own_prompt, base, side = place(plength)
+    mapped = meta[pl.program_id(0)]
     blocks = plength // 128
     at_k1 = 2 * plength + 256
     n_keys = 2 * plength + 512
-    fill_keys(keys, ko, km, kn, kc, plength)
-    fill_keys(vals, vo, vm, vn, vc, plength)
+    fill_keys(keys, k_rows, own_prompt, mapped, plength)
+    fill_keys(vals, v_rows, own_prompt, mapped, plength)
     row = lax.broadcasted_iota(jnp.int32, (128, 128), 0)
     col = lax.broadcasted_iota(jnp.int32, (128, 128), 1)
     tab_a = jnp.broadcast_to(table[0, 0:1, :], (128, 128))
@@ -539,28 +557,17 @@
     lane = lax.broadcasted_iota(jnp.int32, (QP, LANES), 1)
     dq_x[...] = (jnp.where(lane < HD, out[0:QP], out[QP:]) * 0.125).astype(jnp.bfloat16)
 
-    for kv, acc in ((0, dk_acc), (1, dv_acc)):
-        near = jnp.concatenate([acc[at_k1 - 256 : at_k1 - 128], acc[at_k1 : at_k1 + 128]], axis=0)
-        dkv_near[kv, 0] = near.astype(jnp.bfloat16)
-        dkv_own[kv, 0, 0:128] = acc[at_k1 - 128 : at_k1]
-        dkv_own[kv, 0, 128:256] = acc[at_k1 + 128 : at_k1 + 256]
-        d_prompt[...] = jnp.zeros_like(d_prompt)
-        own_at = pl.multiple_of(own_prompt * plength, 128)
-        map_at = pl.multiple_of(mapped * plength, 128)
-        d_prompt[pl.ds(own_at, plength), :] = acc[own]
-        d_prompt[pl.ds(map_at, plength), :] = (
-            d_prompt[pl.ds(map_at, plength), :] + acc[plength : 2 * plength]
-        )
-        dkv_prompt[:, kv, 0] = (
-            d_prompt[...].astype(jnp.bfloat16).reshape(2 * blocks, PD, LANES)
-        )
-
-
-def attend_back(meta, qkv, extra_q, prompt_kv, near_kv, table, xcol, xrow, lse, dc, dx, fc, fx):
-    devices = prompt_kv.shape[0]
-    half = devices // 2
-    plength = half * PD
-    n_keys = 2 * plength + 2 * CH
+    for out_ref, acc in ((dk_rows, dk_acc), (dv_rows, dv_acc)):
+        for p in range(2):
+            mine = jnp.where(own_prompt == p, acc[own], 0.0)
+            other = jnp.where(mapped == p, acc[plength : 2 * plength], 0.0)
+            out_ref[p * plength : (p + 1) * plength] = (mine + other).astype(jnp.bfloat16)
+        out_ref[2 * plength :] = acc[2 * plength :].astype(jnp.bfloat16)
+
+
+def attend_back(meta, queries, extra_q, key_rows, table, xcol, xrow, lse, dc, dx, fc, fx):
+    n_keys = key_rows.shape[0] // MICRO
+    plength = (n_keys - 2 * CH) // 2
     content = pl.BlockSpec((TD, LANES), pair_column(0))
     extra = pl.BlockSpec((QP, LANES), pair_column(0))
     own_row = plength + 2 * CH
@@ -572,12 +579,9 @@
             num_scalar_prefetch=1,
             grid=(MICRO, PAIRS),
             in_specs=[content, extra]
-            + prompt_specs(half)
             + [
-                near_spec(0),
-                near_spec(1),
-                pl.BlockSpec((TD, LANES), pair_column(1)),
-                pl.BlockSpec((TD, LANES), pair_column(2)),
+                key_spec(n_keys, 0),
+                key_spec(n_keys, 1),
                 TABLE_SPEC,
                 pl.BlockSpec((1, 128, 8), lambda m, j, meta: (m, 0, 0)),
                 pl.BlockSpec((1, 8, 128), lambda m, j, meta: (m, 0, 0)),
@@ -590,9 +594,8 @@
             out_specs=[
                 content,
                 extra,
-                pl.BlockSpec((devices, 2, 1, PD, LANES), lambda m, j, meta: (0, 0, m, 0, j)),
-                pl.BlockSpec((2, 1, CH, LANES), lambda m, j, meta: (0, m, 0, j)),
-                pl.BlockSpec((2, 1, CH, LANES), lambda m, j, meta: (0, m, 0, j)),
+                key_spec(n_keys, 0),
+                key_spec(n_keys, 0),
                 pl.BlockSpec((1, 1, 64, LANES), lambda m, j, meta: (m, j, 0, 0)),
             ],
             scratch_shapes=[
@@ -607,15 +610,13 @@
                 pltpu.VMEM((plength, 256), jnp.float32),
                 pltpu.VMEM((n_keys, LANES), jnp.float32),
                 pltpu.VMEM((n_keys, LANES), jnp.float32),
-                pltpu.VMEM((2 * plength, LANES), jnp.float32),
             ],
         ),
         out_shape=[
             jax.ShapeDtypeStruct((MICRO * TD, D), jnp.bfloat16),
             jax.ShapeDtypeStruct((MICRO * QP, D), jnp.bfloat16),
-            jax.ShapeDtypeStruct((devices, 2, MICRO, PD, D), jnp.bfloat16),
-            jax.ShapeDtypeStruct((2, MICRO, CH, D), jnp.bfloat16),
-            jax.ShapeDtypeStruct((2, MICRO, CH, D), jnp.float32),
+            jax.ShapeDtypeStruct((MICRO * n_keys, D), jnp.bfloat16),
+            jax.ShapeDtypeStruct((MICRO * n_keys, D), jnp.bfloat16),
             jax.ShapeDtypeStruct((MICRO, PAIRS, 64, LANES), jnp.float32),
         ],
         compiler_params=pltpu.CompilerParams(vmem_limit_bytes=VMEM_LIMIT),
@@ -624,16 +625,10 @@
         ),
     )(
         meta,
-        qkv,
+        queries,
         extra_q,
-        prompt_kv,
-        prompt_kv,
-        prompt_kv,
-        prompt_kv,
-        near_kv,
-        near_kv,
-        qkv,
-        qkv,
+        key_rows,
+        key_rows,
         table,
         xcol,
         xrow,
@@ -739,7 +734,6 @@
     plength = PD * halfway
     heads = bias_table.shape[1]
     extra_rows = query_in.shape[1]
-    own_prompt = own_rank // halfway
     prompt_base = own_rank % halfway * PD
     cont_index = own_rank // 2
     side = own_rank % 2
@@ -777,9 +771,7 @@
         ),
         axis=1,
     )
-    meta = jnp.concatenate([jnp.stack([own_prompt, prompt_base, side]), prompt_ref]).astype(
-        jnp.int32
-    )
+    meta = prompt_ref.astype(jnp.int32)
     order = jnp.pad(pred_order[:, 0, :], ((0, 0), (0, QP - extra_rows)), constant_values=-1)
     real = order >= 0
     in_prompt = order < PD
@@ -799,21 +791,25 @@
     tokens_x = content_in.reshape(MICRO * TD, D)
     extra_x = pad_rows(query_in)
     x_all = jnp.concatenate([tokens_x, extra_x])
-    qkv_weight = jnp.concatenate([query_weight, key_weight, value_weight], axis=1)
-    qkv_bias = jnp.concatenate([query_bias, jnp.zeros((D,), jnp.float32), value_bias])
-    qkv = (
-        jnp.dot(tokens_x, qkv_weight, preferred_element_type=jnp.float32) + qkv_bias
+    n_keys = 2 * plength + 2 * CH
+    prompt_x = lax.all_gather(content_in[:, :PD], "fsdp", axis=1, tiled=True)
+    near_x = from_partner(content_in[:, PD:], "fsdp").reshape(MICRO, 2, 1, 128, D)
+    own_x = content_in[:, PD:].reshape(MICRO, 2, 1, 128, D)
+    cont_x = jnp.concatenate([near_x, own_x], axis=2).reshape(MICRO, 2 * CH, D)
+    keys_x = jnp.concatenate([prompt_x, cont_x], axis=1).reshape(MICRO * n_keys, D)
+    kv_weight = jnp.concatenate([key_weight, value_weight], axis=1)
+    kv_bias = jnp.concatenate([jnp.zeros((D,), jnp.float32), value_bias])
+    key_rows = (
+        jnp.dot(keys_x, kv_weight, preferred_element_type=jnp.float32) + kv_bias
     ).astype(jnp.bfloat16)
-    extra_q = (
-        jnp.dot(extra_x, query_weight, preferred_element_type=jnp.float32) + query_bias
+    q_all = (
+        jnp.dot(x_all, query_weight, preferred_element_type=jnp.float32) + query_bias
     ).astype(jnp.bfloat16)
-    kv = qkv[:, D:].reshape(MICRO, TD, 2, D)
-    kv = jnp.transpose(kv, (2, 0, 1, 3))
-    prompt_kv = lax.all_gather(kv[:, :, :PD], "fsdp", axis=0)
-    near_kv = from_partner(kv[:, :, PD:], "fsdp")
-
-    ctx_c, ctx_x, full_c, full_x, lse = attend(
-        meta, qkv, extra_q, prompt_kv, near_kv, table, xcol
+    queries = q_all[: MICRO * TD]
+    extra_q = q_all[MICRO * TD :]
+
+    ctx_c, ctx_x, full_c, full_x, lse, _ = attend(
+        meta, queries, extra_q, key_rows, table, xcol, w_out
     )
     context = jnp.concatenate([ctx_c, ctx_x])
     first, normed_one, inverse_one = layer_norm(
@@ -853,12 +849,11 @@
     dweight_out = dot_tn(context, dres_one_b)
     dcontext = dot_nt(dres_one_b, out_weight).astype(jnp.bfloat16)
 
-    dq_c, dq_x, dkv_prompt, dkv_near, dkv_own, hist = attend_back(
+    dq_c, dq_x, dk_rows, dv_rows, hist = attend_back(
         meta,
-        qkv,
+        queries,
         extra_q,
-        prompt_kv,
-        near_kv,
+        key_rows,
         table,
         xcol,
         xrow,
@@ -868,20 +863,25 @@
         full_c,
         full_x,
     )
-    own_prompt_grad = lax.psum_scatter(dkv_prompt, "fsdp", scatter_dimension=0)
-    from_near = from_partner(dkv_near, "fsdp").astype(jnp.float32)
-    dkv = jnp.concatenate(
-        [own_prompt_grad, (dkv_own + from_near).astype(jnp.bfloat16)], axis=2
-    ).reshape(2, rows_c, D)
-    dqkv = jnp.concatenate([dq_c, dkv[0], dkv[1]], axis=1)
+    dkv_rows = jnp.concatenate([dk_rows, dv_rows], axis=1)
     dq_all = jnp.concatenate([dq_c, dq_x])
     dweight_query = dot_tn(x_all, dq_all)
     dbias_query = jnp.sum(dq_all.astype(jnp.float32), axis=0)
-    dweight_kv = dot_tn(tokens_x, dqkv[:, D:])
-    dbias_value = jnp.sum(dkv[1].astype(jnp.float32), axis=0)
-    dtokens = dres_one[:rows_c] + dot_nt(dqkv, qkv_weight)
-    dextra = dres_one[rows_c:] + dot_nt(dq_x, query_weight)
-    grad_content = dtokens.reshape(MICRO, TD, D)
+    dweight_kv = dot_tn(keys_x, dkv_rows)
+    dbias_value = jnp.sum(dv_rows.astype(jnp.float32), axis=0)
+    dkeys_x = dot_nt(dkv_rows, kv_weight).reshape(MICRO, n_keys, D)
+    from_prompts = lax.psum_scatter(
+        dkeys_x[:, : 2 * plength].astype(jnp.bfloat16), "fsdp", scatter_dimension=1, tiled=True
+    ).astype(jnp.float32)
+    dcont = dkeys_x[:, 2 * plength :].reshape(MICRO, 2, 2, 128, D)
+    from_near = from_partner(dcont[:, :, 0].astype(jnp.bfloat16), "fsdp").astype(jnp.float32)
+    dcont = (dcont[:, :, 1] + from_near).reshape(MICRO, CH, D)
+    dx_all = dres_one + dot_nt(dq_all, query_weight)
+    dtokens = dx_all[:rows_c].reshape(MICRO, TD, D) + jnp.concatenate(
+        [from_prompts, dcont], axis=1
+    )
+    dextra = dx_all[rows_c:]
+    grad_content = dtokens
     grad_query = dextra.reshape(MICRO, QP, D)[:, :extra_rows]
     dtable = table_gradient(hist, rel_bucket, bias_table.shape[0], side, heads)
 

time: 771 us -> 694 us (0.900)
  waiting for transfers between devices: 386 us -> 298 us
  matrix products: 113 us -> 129 us
  local copies, waits for them, and re-layouts: 71.1 us -> 59 us
  other arithmetic: 28.5 us -> 36.4 us
    reduce_scatter x1, waiting for transfers between devices: 61 us -> 0.01 us  [on_device(): lax.psum_scatter(dkeys_x[:, :2 * plength].astype(jnp.bfloat16), 'fsdp', s...]
    psum x1, waiting for transfers between devices: 19.3 us -> 56.6 us  [on_device(): totals = [lax.psum(entry, 'grp').astype(jnp.float32) for entry in shares]]
    reduce_scatter x4 -> x5, waiting for transfers between devices: 161 us -> 129 us  [scatter(): lax.psum_scatter(piece.astype(jnp.bfloat16), 'fsdp', scatter_dimension=0,...]
    all_gather x6, waiting for transfers between devices: 91.5 us -> 70.7 us  [gather(): return lax.all_gather(entry, 'fsdp', axis=0, tiled=True)]
    all_gather x1, waiting for transfers between devices: 46.5 us -> 37.8 us  [on_device(): prompt_x = lax.all_gather(content_in[:, :PD], 'fsdp', axis=1, tiled=True)]
    reshape x2 -> x0, local copies, waits for them, and re-layouts: 8.12 us -> none  [on_device(): kv = qkv[:, D:].reshape(MICRO, TD, 2, D)]
    unnamed x89 -> x123, local copies, waits for them, and re-layouts: 21.8 us -> 22.2 us
  transfers between devices with their start and end apart: 16 -> 16, of which waited for: 13 -> 9; matrix products, arithmetic and copies ran while one was open for 18% -> 24% of each run, Pallas kernels for 6% -> 6%
where the time goes in v2:
time: 694 us; the launch traced here: 686 us
  waiting for transfers between devices  298 us (43%)
  matrix products  129 us (19%)
  Pallas kernels  94.3 us (14%)
  local copies, waits for them, and re-layouts  59 us (9%)
  blocking collectives  52.5 us (8%)
  other arithmetic  36.4 us (5%)
  between operations  15.2 us (2%)
    reduce_scatter x5, waiting for transfers between devices, scatter(): lax.psum_scatter(piece.astype(jnp.bfloat16), 'fsdp', scatter_dimension=0,...  129 us
    all_gather x6, waiting for transfers between devices, gather(): return lax.all_gather(entry, 'fsdp', axis=0, tiled=True)  70.7 us
    psum x1, waiting for transfers between devices, on_device(): totals = [lax.psum(entry, 'grp').astype(jnp.float32) for entry in shares]  56.6 us
    pallas_call x1, Pallas kernels, attend_back(): pl.pallas_call(functools.partial(attend_back_kernel, plength), name='atte...  49.9 us
    pallas_call x1, Pallas kernels, attend(): pl.pallas_call(functools.partial(attend_kernel, plength), name='attend',...  44.4 us
    all_gather x1, waiting for transfers between devices, on_device(): prompt_x = lax.all_gather(content_in[:, :PD], 'fsdp', axis=1, tiled=True)  37.8 us
    dot_general x5, matrix products, dot_nt(): lax.dot_general(left, right, (((1,), (1,)), ((), ())), preferred_element_...  35.8 us
    dot_general x5, matrix products, dot_tn(): lax.dot_general(left, right, (((0,), (0,)), ((), ())), preferred_element_...  35.8 us
  transfers between devices with their start and end apart: 16, of which 9 were waited for; matrix products, arithmetic and copies ran while one was open for 24% of the time, Pallas kernels for 6%

profile of v2, /device:TPU:0, one launch (start us, length us, event | category | flops | bytes accessed | tf_op | source)
XLA Modules:
  0.0 685.5 jit_solution(10907516272909986108)
XLA Ops:
  9.6 1.8 slice.163
  13.6 15.7 %all-gather.1 = bf16[8,1,1152]{2,1,0:T(2,128)(2,1)S(1)} all-gather(bf16[1,1,1152]{2,1,0:T(2,128)(2,1)S(1)} %reshape.369), channel_id=2, replica_groups=mesh['grp'=4,'fsdp'=8] {'fsdp'}, dimensions={0}, use_global_device_ids=true | all-gather | bytes 20736 | tf_op jit(solution)/shard_map/all_gather | solution.py:742
  34.5 1.3 pad_maximum_fusion.1
  36.0 2.5 add_convert_fusion.1
  38.5 1.1 slice.215.qc
  40.3 19.0 %all-gather.14.cloned.1.call-done = bf16[768,768]{1,0:T(8,128)(2,1)} async-done(((bf16[96,768]{1,0:T(8,128)(2,1)}), bf16[768,768]{1,0:T(8,128)(2,1)}) %all-gather.14.cloned.1.call-update) | async-done | bytes 1179664 | tf_op jit(solution)/shard_map/all_gather | solution.py:742
  59.3 2.4 constant_dynamic-update-slice_fusion.1
  61.7 21.7 %all-gather.16.cloned.1.call-done = bf16[768,768]{1,0:T(8,128)(2,1)} async-done(((bf16[96,768]{1,0:T(8,128)(2,1)}), bf16[768,768]{1,0:T(8,128)(2,1)}) %all-gather.16.cloned.1.call-update) | async-done | bytes 1179664 | tf_op jit(solution)/shard_map/all_gather | solution.py:742
  83.4 2.4 constant_dynamic-update-slice_fusion
  85.8 37.8 %all-gather.12.cloned.1.call-done = bf16[2,1024,768]{2,1,0:T(8,128)(2,1)} async-done(((bf16[2,128,768]{2,1,0:T(8,128)(2,1)}), bf16[2,1024,768]{2,1,0:T(8,128)(2,1)}) %all-gather.12.cloned.1.call-update) | async-done | bytes 3145744 | tf_op jit(solution)/shard_map/all_gather | solution.py:795
  123.5 2.3 pad_maximum_fusion
  125.9 2.1 copy-done.5
  128.0 9.4 %add_convert_fusion.k_rows.v_rows = bf16[3072,1536]{1,0:T(8,128)(2,1)} fusion(bf16[3072,768]{1,0:T(8,128)(2,1)S(1)} %bitcast.108, bf16[768,1536]{1,0:T(8,128)(2,1)S(1)} %copy-done.13, f32[1536]{0:T(1024)S(1)} %pad_convert_fusion), kind=kOutput, calls=%fused_computation.1 | convolution fusion | flops 7257194496 | bytes 16521216 | tf_op jit(solution)/shard_map/dot_general | solution.py:803
  137.5 44.4 %attend.1 = (bf16[768,768]{1,0:T(8,128)(2,1)}, bf16[128,768]{1,0:T(8,128)(2,1)}, f32[768,768]{1,0:T(8,128)}, f32[128,768]{1,0:T(8,128)}, f32[2,6,8,128]{3,2,1,0:T(8,128)}, /*index=5*/bf16[4,96,768]{2,1,0:T(8,128)(2,1)}) custom-call(s32[2]{0:T(128)} %select_reduce_fusion.meta, bf16[768,768]{1,0:T(8,128)(2,1)} %slice.215.qc, bf16[128,768]{1,0:T(8,128)(2,1)} %slice.216.qx, ...), custom_call_target="tpu_custom_call" | custom-call | flops 5234491392 | bytes 16777216 | tf_op jit(solution)/shard_map/attend/pallas_call | solution.py:262
  181.9 2.4 constant_dynamic-update-slice_fusion.3
  184.2 1.6 constant_dynamic-update-slice_fusion.2
  185.9 3.5 fusion.54
  189.8 9.8 %all-gather.20.cloned.1.call-done = bf16[768,3072]{1,0:T(8,128)(2,1)} async-done(((bf16[96,3072]{1,0:T(8,128)(2,1)}), bf16[768,3072]{1,0:T(8,128)(2,1)}) %all-gather.20.cloned.1.call-update) | async-done | bytes 4718608 | tf_op jit(solution)/shard_map/all_gather | solution.py:742
  199.6 32.1 %fusion.2 = (bf16[896,3072]{1,0:T(8,128)(2,1)}, f32[896,3072]{1,0:T(8,128)}) fusion(f32[3072]{0:T(1024)S(1)} %reshape.355, bf16[768,3072]{1,0:T(8,128)(2,1)} %all-gather.20.cloned.1.call-done, f32[896,768]{1,0:T(8,128)S(1)} %get-tuple-element.93, f32[768]{0:T(1024)S(1)} %reshape.354, f32[768]{0:T(1024)S(1)} %reshape.353, f32[896]{0:T(1024)S(1)} %add_rsqrt_fusion.1, ...), kind=kOutput, calls=%fused_computation.6 | convolution fusion | flops 4412964864 | bytes 24011776 | tf_op jit(solution)/shard_map/dot_general | solution.py:823
  231.7 20.1 %all-gather.22.cloned.1.call-done = bf16[3072,768]{1,0:T(8,128)(2,1)} async-done(((bf16[384,768]{1,0:T(8,128)(2,1)}), bf16[3072,768]{1,0:T(8,128)(2,1)}) %all-gather.22.cloned.1.call-update) | async-done | bytes 4718608 | tf_op jit(solution)/shard_map/all_gather | solution.py:742
  251.8 8.7 %fusion.55 = (f32[896]{0:T(1024)S(1)}, f32[896,768]{1,0:T(8,128)S(1)}) fusion(f32[768]{0:T(1024)S(1)} %reshape.356, bf16[896,3072]{1,0:T(8,128)(2,1)} %get-tuple-element.94, bf16[3072,768]{1,0:T(8,128)(2,1)} %all-gather.22.cloned.1.call-done, f32[768]{0:T(1024)S(1)} %reshape.354, f32[768]{0:T(1024)S(1)} %reshape.353, f32[896]{0:T(1024)S(1)} %add_rsqrt_fusion.1, ...), kind=kOutput, calls=%fused_computation.162 | convolution fusion | flops 4232674304 | bytes 15748608 | tf_op jit(solution)/shard_map/dot_general | solution.py:826
  261.8 1.8 fusion.22
  263.6 2.2 fusion.46
  265.9 12.1 %fusion.56 = (bf16[3072]{0:T(1024)(128)(2,1)}, bf16[896,3072]{1,0:T(8,128)(2,1)S(1)}) fusion(f32[896,3072]{1,0:T(8,128)} %get-tuple-element.95, f32[3072]{0:T(1024)S(1)} %reshape.355, bf16[3072,768]{1,0:T(8,128)(2,1)S(1)} %copy-done.41, f32[896,768]{1,0:T(8,128)S(1)} %get-tuple-element.56), kind=kOutput, calls=%fused_computation.163 | convolution fusion | flops 4267078656 | bytes 24004608 | tf_op jit(solution)/shard_map/dot_general | solution.py:26
  278.0 5.6 multiply_reduce_fusion
  283.6 1.7 fusion.48
  285.3 1.3 convolution_convert_fusion.3
  286.8 1.1 slice.229.dc
  288.6 49.9 %attend_back.1 = (bf16[768,768]{1,0:T(8,128)(2,1)}, bf16[128,768]{1,0:T(8,128)(2,1)}, bf16[3072,768]{1,0:T(8,128)(2,1)}, bf16[3072,768]{1,0:T(8,128)(2,1)}, f32[2,6,64,128]{3,2,1,0:T(8,128)}) custom-call(s32[2]{0:T(128)} %select_reduce_fusion.meta, bf16[768,768]{1,0:T(8,128)(2,1)} %slice.215.qc, bf16[128,768]{1,0:T(8,128)(2,1)} %slice.216.qx, ...), custom_call_target="tpu_custom_call" | custom-call | flops 13086228480 | bytes 33554432 | tf_op jit(solution)/shard_map/attend_back/pallas_call | solution.py:575
  338.5 2.2 fusion.50
  340.7 1.6 fusion.52
  342.3 1.1 copy-done.4
  343.4 2.5 convolution_convert_fusion.5
  345.9 4.7 convolution_convert_fusion.4
  350.7 2.9 constant_dynamic-update-slice_fusion.7
  354.4 1.8 fusion.49
  356.2 3.7 copy-done.8
  359.8 9.2 %convolution_convert_fusion.2 = bf16[768,1536]{1,0:T(8,128)(2,1)} fusion(bf16[3072,768]{1,0:T(8,128)(2,1)S(1)} %bitcast.111, bf16[3072,1536]{1,0:T(8,128)(2,1)S(1)} %get-tuple-element.62), kind=kOutput, calls=%fused_computation.37 | convolution fusion | flops 7248936960 | bytes 16515072 | tf_op jit(solution)/shard_map/dot_general | solution.py:32
  369.1 10.1 %convolution_convert_fusion.1 = bf16[768,3072]{1,0:T(8,128)(2,1)} fusion(bf16[896,3072]{1,0:T(8,128)(2,1)} %copy-done.48, f32[896,768]{1,0:T(8,128)} %copy-done.1, f32[768]{0:T(1024)S(1)} %reshape.354, f32[768]{0:T(1024)S(1)} %reshape.353, f32[896]{0:T(1024)S(1)} %add_rsqrt_fusion.1, f32[896]{0:T(1024)S(1)} %broadcast_multiply_fusion.5), kind=kOutput, calls=%fused_computation.30 | convolution fusion | flops 4233658368 | bytes 12989440 | tf_op jit(solution)/shard_map/dot_general | solution.py:32
  379.2 9.4 %convolution_convert_fusion = bf16[3072,768]{1,0:T(8,128)(2,1)} fusion(bf16[896,3072]{1,0:T(8,128)(2,1)} %get-tuple-element.94, f32[896,768]{1,0:T(8,128)} %copy-done.7), kind=kOutput, calls=%fused_computation.29 | convolution fusion | flops 4230905856 | bytes 12976128 | tf_op jit(solution)/shard_map/dot_general | solution.py:32
  388.7 11.4 %fusion.58 = f32[3072,768]{1,0:T(8,128)S(1)} fusion(bf16[3072,1536]{1,0:T(8,128)(2,1)} %copy-done.8, bf16[768,1536]{1,0:T(8,128)(2,1)} %constant_dynamic-update-slice_fusion), kind=kOutput, calls=%fused_computation.165 | convolution fusion | flops 7247757312 | bytes 21233664 | tf_op jit(solution)/shard_map/dot_general | solution.py:26
  400.1 3.6 copy-done.6
  403.8 2.0 slice.276
  405.8 1.5 reduce.11
  410.3 3.8 slice.233
  414.2 3.6 slice.187
  417.7 3.5 slice.188
  421.3 1.5 fusion.25
  426.2 5.5 convolution_add_fusion
  431.7 17.0 %reduce-scatter.11.cloned.1.call-done = bf16[96,1536]{1,0:T(8,128)(2,1)} async-done(((bf16[768,1536]{1,0:T(8,128)(2,1)}), bf16[96,1536]{1,0:T(8,128)(2,1)}) %reduce-scatter.11.cloned.1.call-update) | async-done | bytes 294928 | tf_op jit(solution)/shard_map/reduce_scatter | solution.py:889
  448.7 56.6 %reduce-scatter.15.cloned.1.call-done = bf16[96,3072]{1,0:T(8,128)(2,1)} async-done(((bf16[768,3072]{1,0:T(8,128)(2,1)}), bf16[96,3072]{1,0:T(8,128)(2,1)}) %reduce-scatter.15.cloned.1.call-update) | async-done | bytes 589840 | tf_op jit(solution)/shard_map/reduce_scatter | solution.py:889
  505.3 55.5 %reduce-scatter.17.cloned.1.call-done = bf16[384,768]{1,0:T(8,128)(2,1)} async-done(((bf16[3072,768]{1,0:T(8,128)(2,1)}), bf16[384,768]{1,0:T(8,128)(2,1)}) %reduce-scatter.17.cloned.1.call-update) | async-done | bytes 589840 | tf_op jit(solution)/shard_map/reduce_scatter | solution.py:889
  560.9 1.2 fusion.57
  562.3 1.6 slice.226
  566.7 26.8 %all-reduce.6 = bf16[8,1200]{1,0:T(8,128)(2,1)S(1)} all-reduce(bf16[8,1200]{1,0:T(8,128)(2,1)S(1)} %concatenate.55), channel_id=5, replica_groups=mesh['grp'=4,'fsdp'=8] {'fsdp'}, use_global_device_ids=true, to_apply=%region_28.29.clone | all-reduce | flops 9600 | bytes 38400
  594.1 10.0 %psum.43 = bf16[1,1200]{1,0:T(2,128)(2,1)S(1)} all-reduce(bf16[1,1200]{1,0:T(2,128)(2,1)S(1)} %constant_dynamic-slice_fusion), channel_id=1, replica_groups=mesh['grp'=4,'fsdp'=8] {'grp'}, use_global_device_ids=true, to_apply=%region_29.30 | all-reduce | flops 1200 | bytes 4800 | tf_op jit(solution)/shard_map/psum | solution.py:919
  606.0 2.9 fusion.24
  610.0 3.5 maximum_add_fusion
  613.5 56.6 %all-reduce.10.cloned.1.call-done = (bf16[96,768]{1,0:T(8,128)(2,1)}, bf16[96,1536]{1,0:T(8,128)(2,1)}, bf16[96,768]{1,0:T(8,128)(2,1)}, bf16[96,3072]{1,0:T(8,128)(2,1)}, bf16[384,768]{1,0:T(8,128)(2,1)}) async-done(((bf16[96,768]{1,0:T(8,128)(2,1)}, bf16[96,1536]{1,0:T(8,128)(2,1)}, bf16[96,768]{1,0:T(8,128)(2,1)}, bf16[96,3072]{1,0:T(8,128)(2,1)}, bf16[384,768]{1,0:T(8,128)(2,1)}), ...) | async-done | bytes 1769488 | tf_op jit(solution)/shard_map/psum | solution.py:919
  670.1 1.7 convert_element_type.218
  671.8 1.8 fusion.51
  673.7 1.6 convert_element_type.226
  675.3 2.2 convert_element_type.228
  677.5 1.1 convert_element_type.230
  (241 shorter events, 27.1 us)
Async XLA Ops:
  7.2 5.5 copy-start.9
  7.2 6.2 copy-start.33
  7.2 6.2 copy-start.34
  7.2 6.2 copy-start.35
  7.2 6.2 copy-start.36
  7.2 6.2 copy-start.37
  7.3 6.2 copy-start.38
  7.3 6.2 copy-start.39
  7.3 6.2 copy-start.40
  7.3 6.2 copy-start.31
  7.3 22.1 %copy-start.26 = (bf16[32,12]{0,1:T(8,128)(2,1)S(1)}, bf16[32,12]{0,1:T(8,128)(2,1)}, u32[]{:S(2)}) copy-start(bf16[32,12]{0,1:T(8,128)(2,1)} %param.43) | copy-start | bytes 2308
  7.3 22.2 %copy-start.43 = (s32[128]{0:T(128)S(1)}, s32[128]{0:T(128)}, u32[]{:S(2)}) copy-start(s32[128]{0:T(128)} %param.27) | copy-start | bytes 1540
  7.3 23.2 %copy-start.28 = (s32[2,1,56]{2,1,0:T(1,128)S(1)}, s32[2,1,56]{2,1,0:T(1,128)}, u32[]{:S(2)}) copy-start(s32[2,1,56]{2,1,0:T(1,128)} %param.25) | copy-start | bytes 1348
  7.3 28.6 %all-gather.10.cloned.1.call-start = ((), (), s32[]{:S(2)}) async-start(), calls=%async_computation.6 | async-start | bytes 1327104 | tf_op jit(solution)/shard_map/all_gather | solution.py:742
  8.1 51.2 %all-gather.14.cloned.1.call-start = ((), (), s32[]{:S(2)}) async-start(), calls=%async_computation.8 | async-start | bytes 1327104 | tf_op jit(solution)/shard_map/all_gather | solution.py:742
  8.8 23.8 %copy-start.15 = (bf16[2,56,768]{2,1,0:T(8,128)(2,1)S(1)}, bf16[2,56,768]{2,1,0:T(8,128)(2,1)}, u32[]{:S(2)}) copy-start(bf16[2,56,768]{2,1,0:T(8,128)(2,1)} %param.24) | copy-start | bytes 516100
  8.8 74.6 %all-gather.16.cloned.1.call-start = ((), (), s32[]{:S(2)}) async-start(), calls=%async_computation.9 | async-start | bytes 1327104 | tf_op jit(solution)/shard_map/all_gather | solution.py:742
  9.6 23.7 %copy-start.32 = (s32[2,1,4]{2,1,0:T(1,128)S(1)}, s32[2,1,4]{2,1,0:T(1,128)}, u32[]{:S(2)}) copy-start(s32[2,1,4]{2,1,0:T(1,128)} %param.26) | copy-start | bytes 100
  9.6 24.3 %copy-start.16 = (bf16[2,56,768]{2,1,0:T(8,128)(2,1)S(1)}, bf16[2,56,768]{2,1,0:T(8,128)(2,1)}, u32[]{:S(2)}) copy-start(bf16[2,56,768]{2,1,0:T(8,128)(2,1)} %param.45) | copy-start | bytes 516100
  9.6 114.0 %all-gather.12.cloned.1.call-start = ((), (), s32[]{:S(2)}) async-start(), calls=%async_computation.7 | async-start | bytes 3538944 | tf_op jit(solution)/shard_map/all_gather | solution.py:795
  11.5 174.4 %all-gather.18.cloned.1.call-start = ((), (), s32[]{:S(2)}) async-start(), calls=%async_computation.10 | async-start | bytes 1327104 | tf_op jit(solution)/shard_map/all_gather | solution.py:742
  12.0 187.5 %all-gather.20.cloned.1.call-start = ((), (), s32[]{:S(2)}) async-start(), calls=%async_computation.11 | async-start | bytes 5308416 | tf_op jit(solution)/shard_map/all_gather | solution.py:742
  12.6 239.2 %all-gather.22.cloned.1.call-start = ((), (), s32[]{:S(2)}) async-start(), calls=%async_computation.12 | async-start | bytes 5308416 | tf_op jit(solution)/shard_map/all_gather | solution.py:742
  12.7 21.8 %collective-permute-start = (bf16[2,256,768]{2,1,0:T(8,128)(2,1)S(1)}, bf16[2,256,768]{2,1,0:T(8,128)(2,1)}, u32[]{:S(2)}, u32[]{:S(2)}) collective-permute-start(bf16[2,256,768]{2,1,0:T(8,128)(2,1)S(1)} %slice.164), channel_id=1, source_target_pairs={{0,1},{1,0},{2,3},{3,2},{4,5},{5,4},{6,7},{7,6},{8,9},{9,8},{10,11... | collective-permute-start | bytes 2359304 | tf_op jit(solution)/shard_map/ppermute | solution.py:645
  13.4 418.3 %reduce-scatter.9.cloned.1.call-start = ((), (), s32[]{:S(2)}) async-start(), calls=%async_computation.14 | async-start | bytes 1327104 | tf_op jit(solution)/shard_map/reduce_scatter | solution.py:889
  123.5 4.5 copy-start.13
  125.9 2.2 copy-start.5
  189.3 62.5 %copy-start.1 = (f32[896,768]{1,0:T(8,128)}, f32[896,768]{1,0:T(8,128)S(1)}, u32[]{:S(2)}) copy-start(f32[896,768]{1,0:T(8,128)S(1)} %get-tuple-element.93) | copy-start | bytes 8257540
  263.6 2.3 copy-start.41
  263.6 14.4 %slice-start.6 = ((s8[4718592]{0:T(1024)(128)(4,1)}), s8[4194304]{0:T(1024)(128)(4,1)S(1)}, s32[]{:S(2)}) async-start(s8[4718592]{0:T(1024)(128)(4,1)} %bitcast.142), calls=%async_computation.26 | async-start | bytes 8388608
  265.7 12.2 %copy-start.7 = (f32[896,768]{1,0:T(8,128)}, f32[896,768]{1,0:T(8,128)S(1)}, u32[]{:S(2)}) copy-start(f32[896,768]{1,0:T(8,128)S(1)} %get-tuple-element.56) | copy-start | bytes 8257540
  265.9 12.1 %copy-start.2 = (f32[896,768]{1,0:T(8,128)S(1)}, f32[896,768]{1,0:T(8,128)}, u32[]{:S(2)}) copy-start(f32[896,768]{1,0:T(8,128)} %copy-done.1) | copy-start | bytes 8257540
  265.9 12.1 %slice-start.7 = ((s8[4718592]{0:T(1024)(128)(4,1)}), s8[524288]{0:T(1024)(128)(4,1)S(1)}, s32[]{:S(2)}) async-start(s8[4718592]{0:T(1024)(128)(4,1)} %bitcast.142), calls=%async_computation.27 | async-start | bytes 1048576
  278.0 5.6 copy-start.48
  338.5 4.9 copy-start.10
  345.9 85.8 %reduce-scatter.13.cloned.1.call-start = ((), (), s32[]{:S(2)}) async-start(), calls=%async_computation.16 | async-start | bytes 1327104 | tf_op jit(solution)/shard_map/reduce_scatter | solution.py:889
  350.6 98.1 %reduce-scatter.11.cloned.1.call-start = ((), (), s32[]{:S(2)}) async-start(), calls=%async_computation.15 | async-start | bytes 2654208 | tf_op jit(solution)/shard_map/reduce_scatter | solution.py:889
  350.7 3.6 slice-start.2
  350.7 3.7 slice-start.3
  350.7 9.2 %slice-start.4 = ((s8[4718592]{0:T(1024)(128)(4,1)}), s8[4194304]{0:T(1024)(128)(4,1)S(1)}, s32[]{:S(2)}) async-start(s8[4718592]{0:T(1024)(128)(4,1)} %bitcast.109), calls=%async_computation.24 | async-start | bytes 8388608
  354.4 5.4 slice-start.5
  356.2 3.7 copy-start.8
  369.0 136.3 %reduce-scatter.15.cloned.1.call-start = ((), (), s32[]{:S(2)}) async-start(), calls=%async_computation.17 | async-start | bytes 5308416 | tf_op jit(solution)/shard_map/reduce_scatter | solution.py:889
  379.2 181.7 %reduce-scatter.17.cloned.1.call-start = ((), (), s32[]{:S(2)}) async-start(), calls=%async_computation.18 | async-start | bytes 5308416 | tf_op jit(solution)/shard_map/reduce_scatter | solution.py:889
  388.7 220.3 %reduce-scatter.7.cloned.1.call-start = ((), (), s32[]{:S(2)}) async-start(), calls=%async_computation.13 | async-start | bytes 3538944 | tf_op jit(solution)/shard_map/reduce_scatter | solution.py:873
  400.1 3.7 copy-start.6
  405.8 2.3 copy-start.45
  405.8 264.3 %all-reduce.10.cloned.1.call-start = ((), (), s32[]{:S(2)}) async-start(), calls=%async_computation.19 | async-start | bytes 3538944 | tf_op jit(solution)/shard_map/psum | solution.py:919
  410.3 3.9 copy-start.14
  414.2 7.1 %copy-start.11 = (f32[6,64,128]{2,1,0:T(8,128)}, f32[6,64,128]{2,1,0:T(8,128)S(1)}, u32[]{:S(2)}) copy-start(f32[6,64,128]{2,1,0:T(8,128)S(1)} %reduce_sum.243) | copy-start | bytes 589828
  422.8 183.3 %collective-permute-start.1 = (bf16[2,2,128,768]{3,2,1,0:T(8,128)(2,1)S(1)}, bf16[2,2,128,768]{3,2,1,0:T(8,128)(2,1)}, u32[]{:S(2)}, u32[]{:S(2)}) collective-permute-start(bf16[2,2,128,768]{3,2,1,0:T(8,128)(2,1)S(1)} %fusion.25), channel_id=1, source_target_pairs={{0,1},{1,0},{2,3},{3,2},{4,5},{5,4},{6,7},{7,6},{8,9},{9,8},{10,11... | collective-permute-start | bytes 2359304 | tf_op jit(solution)/shard_map/ppermute | solution.py:645
  426.2 134.7 %copy-start.27 = (s32[5,128]{1,0:T(8,128)S(1)}, s32[5,128]{1,0:T(8,128)}, u32[]{:S(2)}) copy-start(s32[5,128]{1,0:T(8,128)} %stack.52) | copy-start | bytes 7684
  426.2 134.7 %copy-start.47 = (pred[128]{0:T(512)(128)(4,1)S(1)}, pred[128]{0:T(512)(128)(4,1)}, u32[]{:S(2)}) copy-start(pred[128]{0:T(512)(128)(4,1)} %iota_compare_fusion.3) | copy-start | bytes 388
  426.2 135.9 %copy-start.44 = (s32[128]{0:T(128)S(1)}, s32[128]{0:T(128)}, u32[]{:S(2)}) copy-start(s32[128]{0:T(128)} %param.27) | copy-start | bytes 1540
  426.2 136.0 %copy-start.46 = (pred[128]{0:T(512)(128)(4,1)S(1)}, pred[128]{0:T(512)(128)(4,1)}, u32[]{:S(2)}) copy-start(pred[128]{0:T(512)(128)(4,1)} %iota_compare_fusion.4) | copy-start | bytes 388
  564.0 1.9 copy-start.24
  564.0 2.0 copy-start.20
  564.0 2.1 copy-start.30
  564.0 2.1 copy-start.29
  564.0 2.2 copy-start.19
  564.0 2.3 copy-start.25
  564.1 2.5 copy-start.22
  565.7 44.3 %slice-start = ((f32[896,768]{1,0:T(8,128)}), f32[768,768]{1,0:T(8,128)S(1)}, s32[]{:S(2)}) async-start(f32[896,768]{1,0:T(8,128)} %convolution_add_fusion), calls=%async_computation.20 | async-start | bytes 4718592 | tf_op jit(solution)/shard_map/slice | solution.py:880
  670.1 7.4 %copy-start.12 = (bf16[384,768]{1,0:T(8,128)(2,1)S(1)}, bf16[384,768]{1,0:T(8,128)(2,1)}, u32[]{:S(2)}) copy-start(bf16[384,768]{1,0:T(8,128)(2,1)} %get-tuple-element.54) | copy-start | bytes 1769476
  (9 other events, 13.5 us)
Sparse Core Ops, SparseCore 0:
  9.8 25.5 all-gather.9
  37.0 22.2 all-gather.13
  60.9 22.4 all-gather.15
  85.4 38.0 all-gather.11
  125.0 21.5 all-gather.17
  148.1 51.4 all-gather.19
  201.2 50.5 all-gather.21
  346.0 31.4 reduce-scatter.8
  380.4 31.1 reduce-scatter.12
  414.3 34.3 reduce-scatter.10
  451.0 54.2 reduce-scatter.14
  507.5 53.3 reduce-scatter.16
  563.2 39.2 reduce-scatter.6
  606.0 64.0 all-reduce.9

commit v3 on v2

--- a/solution.py
+++ b/solution.py
@@ -69,72 +69,458 @@
     scratch[2 * plength :] = rows_ref[2 * plength :]
 
 
+MESH = pl.DeviceIdType.MESH
+ANY_SPEC = pl.BlockSpec(memory_space=pl.ANY)
+
+
+class Net:
+    def __init__(self):
+        self.g = lax.axis_index("grp")
+        self.f = lax.axis_index("fsdp")
+        self.x = self.g % 2
+        self.y = self.g // 2
+        self.z = self.f // 2
+        self.c = self.f % 2
+        self.gx = self.g + 1 - 2 * self.x
+        self.gy = self.g + 2 - 4 * self.y
+        self.mate = self.f + 1 - 2 * self.c
+        self.z_of = [
+            self.z + 1 - 2 * (self.z % 2),
+            (self.z + 2) % 4,
+            3 - self.z,
+        ]
+        self.f_of = [2 * other + self.c for other in self.z_of]
+        self.to_x = (self.gx, self.f)
+        self.to_y = (self.gy, self.f)
+        self.to_mate = (self.g, self.mate)
+        self.to_z = [(self.g, other) for other in self.f_of]
+
+    def greet(self):
+        barrier = pltpu.get_barrier_semaphore()
+        everyone = [self.to_x, self.to_y, self.to_mate] + self.to_z
+        for device in everyone:
+            pl.semaphore_signal(barrier, inc=1, device_id=device, device_id_type=MESH)
+        pl.semaphore_wait(barrier, len(everyone))
+
+
+class Copies:
+    def __init__(self, sends, recvs):
+        self.sends = sends
+        self.recvs = recvs
+        self.used = 0
+        self.all = []
+
+    def to(self, device, src, dst):
+        copy = pltpu.make_async_remote_copy(
+            src_ref=src,
+            dst_ref=dst,
+            send_sem=self.sends.at[self.used],
+            recv_sem=self.recvs.at[self.used],
+            device_id=device,
+            device_id_type=MESH,
+        )
+        self.used += 1
+        self.all.append(copy)
+        return copy
+
+    def finish(self):
+        for copy in self.all:
+            copy.wait_send()
+
+
+def start(copies):
+    for copy in copies:
+        copy.start()
+
+
+def arrive(copies):
+    for copy in copies:
+        copy.wait_recv()
+
+
+GATHER_COPIES = 19
+
+
+def gather_stages(net, copies, local_sem, shard, full):
+    part, width = shard.shape[1:]
+    half = width // 2
+
+    def rows(owner, quarter):
+        return 4 * owner + quarter
+
+    def whole(owner):
+        return pl.ds(4 * owner, 4)
+
+    local = pltpu.make_async_copy(shard, full.at[whole(net.f)], local_sem)
+    mine = shard.at[net.g]
+    along_z = [copies.to(device, mine, full.at[rows(net.f, net.g)]) for device in net.to_z]
+    to_mate = [copies.to(net.to_mate, shard, full.at[whole(net.f)])]
+    to_x, to_y, on_x, on_y, later = [], [], [], [], []
+    for owner in net.f_of:
+        got = full.at[rows(owner, net.g)]
+        to_x.append(copies.to(net.to_x, got, got))
+        to_y.append(copies.to(net.to_y, got, got))
+        left = full.at[rows(owner, net.gx), :, pl.ds(0, half)]
+        on_y.append(copies.to(net.to_y, left, left))
+        right = full.at[rows(owner, net.gy), :, pl.ds(half, half)]
+        on_x.append(copies.to(net.to_x, right, right))
+        shared = full.at[whole(owner)]
+        later.append(copies.to(net.to_mate, shared, shared))
+
+    def begin():
+        local.start()
+        start(along_z)
+        start(to_mate)
+
+    def plane():
+        arrive(along_z)
+        start(to_x + to_y)
+
+    def corners():
+        arrive(to_x + to_y)
+        start(on_y + on_x)
+
+    def mates():
+        arrive(on_y + on_x)
+        start(later)
+
+    def end():
+        arrive(to_mate + later)
+        local.wait()
+        for copy in along_z + to_mate + to_x + to_y + on_x + on_y + later:
+            copy.wait_send()
+
+    return [begin, plane, corners, mates, end]
+
+
+REDUCE_COPIES = 19
+
+
+def reduce_buffers(size, width):
+    part, half = size // 4, width // 2
+    return [
+        pltpu.VMEM((4, 4, part, width), jnp.bfloat16),
+        pltpu.VMEM((4, 4, part, width), jnp.bfloat16),
+        pltpu.VMEM((4, 2, part, half), jnp.bfloat16),
+        pltpu.VMEM((4, 2, part, half), jnp.bfloat16),
+        pltpu.VMEM((2, 4, part, half), jnp.bfloat16),
+        pltpu.VMEM((2, 3, part, half), jnp.bfloat16),
+        pltpu.VMEM((2, 4, part, half), jnp.bfloat16),
+        pltpu.SemaphoreType.DMA((2,)),
+        pltpu.SemaphoreType.DMA((REDUCE_COPIES,)),
+        pltpu.SemaphoreType.DMA((REDUCE_COPIES,)),
+    ]
+
+
+def reduce_stages(net, grad, share, buffers):
+    own, other, side_a, side_b, line, along, done, local_sem, sends, recvs = buffers
+    copies = Copies(sends, recvs)
+    half = grad.shape[4] // 2
+    left, right = pl.ds(0, half), pl.ds(half, half)
+    load = pltpu.make_async_copy(grad.at[:, net.c], own, local_sem.at[0])
+    to_mate = [copies.to(net.to_mate, grad.at[:, 1 - net.c], other)]
+    first = []
+    for i in range(2):
+        first.append(
+            copies.to(net.to_x, own.at[:, 2 * i + 1 - net.x, :, left], side_a.at[:, i])
+        )
+        first.append(
+            copies.to(net.to_y, own.at[:, 2 - 2 * net.y + i, :, right], side_b.at[:, i])
+        )
+    second = [
+        copies.to(net.to_y, side_a.at[:, 1 - net.y], line.at[0]),
+        copies.to(net.to_x, side_b.at[:, 1 - net.x], line.at[1]),
+    ]
+    third = []
+    for k in range(3):
+        for h in range(2):
+            third.append(
+                copies.to(net.to_z[k], line.at[h, net.z_of[k]], along.at[h, k])
+            )
+    fourth = []
+    fifth = []
+    for h in range(2):
+        fourth.append(copies.to(net.to_x, done.at[h, net.g], done.at[h, net.g]))
+        fourth.append(copies.to(net.to_y, done.at[h, net.g], done.at[h, net.g]))
+    fifth.append(copies.to(net.to_y, done.at[0, net.gx], done.at[0, net.gx]))
+    fifth.append(copies.to(net.to_x, done.at[1, net.gy], done.at[1, net.gy]))
+    store = [
+        pltpu.make_async_copy(done.at[0], share.at[:, :, left], local_sem.at[0]),
+        pltpu.make_async_copy(done.at[1], share.at[:, :, right], local_sem.at[1]),
+    ]
+
+    def begin():
+        load.start()
+        start(to_mate)
+
+    def plane():
+        load.wait()
+        arrive(to_mate)
+
+        @pl.loop(0, 16)
+        def _(i):
+            zi, qi = i // 4, i % 4
+            own[zi, qi] = own[zi, qi] + other[zi, qi]
+
+        start(first)
+
+    def cross():
+        arrive(first)
+
+        @pl.loop(0, 8)
+        def _(i):
+            zi, qi = i // 2, i % 2
+            side_a[zi, qi] = side_a[zi, qi] + own[zi, 2 * qi + net.x, :, 0:half]
+            side_b[zi, qi] = side_b[zi, qi] + own[zi, 2 * net.y + qi, :, half : 2 * half]
+
+        start(second)
+
+    def column():
+        arrive(second)
+
+        @pl.loop(0, 4)
+        def _(zi):
+            line[0, zi] = line[0, zi] + side_a[zi, net.y]
+            line[1, zi] = line[1, zi] + side_b[zi, net.x]
+
+        start(third)
+
+    def spread():
+        arrive(third)
+
+        @pl.loop(0, 2)
+        def _(h):
+            total = line[h, net.z].astype(jnp.float32)
+            for k in range(3):
+                total = total + along[h, k].astype(jnp.float32)
+            done[h, net.g] = total.astype(jnp.bfloat16)
+
+        start(fourth)
+
+    def corners():
+        arrive(fourth)
+        start(fifth)
+
+    def end():
+        arrive(fifth)
+        start(store)
+        for copy in store:
+            copy.wait()
+        copies.finish()
+
+    return [begin, plane, cross, column, spread, corners, end]
+
+
+def gather_first_kernel(
+    w_ref, v_ref, x_ref, w_full, v_full, keys_x, w_s, w_r, v_s, v_r, x_s, x_r, local_sem
+):
+    net = Net()
+    net.greet()
+    weights = gather_stages(net, Copies(w_s, w_r), local_sem.at[0], w_ref, w_full)
+    vectors = gather_stages(net, Copies(v_s, v_r), local_sem.at[1], v_ref, v_full)
+    plength = PD * 4
+    at = 2 * plength
+
+    def block(owner):
+        return pl.ds(pl.multiple_of(owner * PD, 128), PD)
+
+    prompt = x_ref.at[:, pl.ds(0, PD)]
+    cont = [x_ref.at[:, pl.ds(PD + 128 * i, 128)] for i in range(2)]
+    near = [keys_x.at[:, pl.ds(at + 256 * i, 128)] for i in range(2)]
+    here = [keys_x.at[:, pl.ds(at + 256 * i + 128, 128)] for i in range(2)]
+    copies = Copies(x_s, x_r)
+    local = [pltpu.make_async_copy(prompt, keys_x.at[:, block(net.f)], local_sem.at[2])]
+    local += [
+        pltpu.make_async_copy(cont[i], here[i], local_sem.at[3 + i]) for i in range(2)
+    ]
+    to_mate = [copies.to(net.to_mate, prompt, keys_x.at[:, block(net.f)])]
+    to_mate += [copies.to(net.to_mate, cont[i], near[i]) for i in range(2)]
+    along_z = [copies.to(device, prompt, keys_x.at[:, block(net.f)]) for device in net.to_z]
+    later = [
+        copies.to(net.to_mate, keys_x.at[:, block(owner)], keys_x.at[:, block(owner)])
+        for owner in net.f_of
+    ]
+    weights[0]()
+    vectors[0]()
+    start(local)
+    start(to_mate)
+    weights[1]()
+    start(along_z)
+    vectors[1]()
+    weights[2]()
+    vectors[2]()
+    weights[3]()
+    vectors[3]()
+    arrive(along_z)
+    start(later)
+    weights[4]()
+    vectors[4]()
+    arrive(to_mate + later)
+    for copy in local:
+        copy.wait()
+    copies.finish()
+
+
+def gather_first(w_shard, v_shard, content_in):
+    def sems(count):
+        return [pltpu.SemaphoreType.DMA((count,))] * 2
+
+    return pl.pallas_call(
+        gather_first_kernel,
+        name="gather_first",
+        in_specs=[ANY_SPEC] * 3,
+        out_specs=[ANY_SPEC] * 3,
+        out_shape=[
+            jax.ShapeDtypeStruct((8 * 4,) + w_shard.shape[1:], jnp.bfloat16),
+            jax.ShapeDtypeStruct((8 * 4,) + v_shard.shape[1:], jnp.bfloat16),
+            jax.ShapeDtypeStruct((MICRO, 8 * PD + 2 * CH, D), jnp.bfloat16),
+        ],
+        scratch_shapes=sems(GATHER_COPIES)
+        + sems(GATHER_COPIES)
+        + sems(9)
+        + [pltpu.SemaphoreType.DMA((5,))],
+        compiler_params=pltpu.CompilerParams(collective_id=1, has_side_effects=True),
+    )(w_shard, v_shard, content_in)
+
+
+def reduce_last_kernel(w_ref, v_ref, p_ref, n_ref, w_out, v_out, p_out, n_out, *scratch):
+    w_buf, v_buf = scratch[:10], scratch[10:20]
+    mine, theirs, along, total, n_buf, x_s, x_r, x_local = scratch[20:]
+    net = Net()
+    net.greet()
+    weights = reduce_stages(net, w_ref, w_out, w_buf)
+    vectors = reduce_stages(net, v_ref, v_out, v_buf)
+    copies = Copies(x_s, x_r)
+    load = pltpu.make_async_copy(p_ref.at[:, :, net.c], mine, x_local)
+    to_mate = [
+        copies.to(net.to_mate, p_ref.at[:, :, 1 - net.c], theirs),
+        copies.to(net.to_mate, n_ref, n_buf),
+    ]
+    third = [
+        copies.to(net.to_z[k], mine.at[:, net.z_of[k]], along.at[k]) for k in range(3)
+    ]
+    weights[0]()
+    vectors[0]()
+    load.start()
+    start(to_mate)
+    weights[1]()
+    vectors[1]()
+    load.wait()
+    arrive(to_mate)
+
+    @pl.loop(0, 8)
+    def _(i):
+        m, zi = i // 4, i % 4
+        mine[m, zi] = mine[m, zi] + theirs[m, zi]
+
+    start(third)
+    for i in range(2, 4):
+        weights[i]()
+        vectors[i]()
+    arrive(third)
+    weights[4]()
+    vectors[4]()
+
+    @pl.loop(0, 2)
+    def _(m):
+        s = mine[m, net.z].astype(jnp.float32)
+        for k in range(3):
+            s = s + along[k, m].astype(jnp.float32)
+        total[m] = s
+
+    out = pltpu.make_async_copy(total, p_out, x_local)
+    out.start()
+    out.wait()
+    out = pltpu.make_async_copy(n_buf, n_out, x_local)
+    out.start()
+    out.wait()
+    for i in range(5, 7):
+        weights[i]()
+        vectors[i]()
+    copies.finish()
+
+
+def reduce_last(w_grad, v_grad, p_grad, n_grad):
+    def buffers(grad):
+        return reduce_buffers(4 * grad.shape[3], grad.shape[4])
+
+    return pl.pallas_call(
+        reduce_last_kernel,
+        name="reduce_last",
+        in_specs=[ANY_SPEC] * 4,
+        out_specs=[ANY_SPEC] * 4,
+        out_shape=[
+            jax.ShapeDtypeStruct(w_grad.shape[2:], jnp.bfloat16),
+            jax.ShapeDtypeStruct(v_grad.shape[2:], jnp.bfloat16),
+            jax.ShapeDtypeStruct((MICRO, PD, D), jnp.float32),
+            jax.ShapeDtypeStruct(n_grad.shape, jnp.bfloat16),
+        ],
+        scratch_shapes=buffers(w_grad)
+        + buffers(v_grad)
+        + [
+            pltpu.VMEM((MICRO, 4, PD, D), jnp.bfloat16),
+            pltpu.VMEM((MICRO, 4, PD, D), jnp.bfloat16),
+            pltpu.VMEM((3, MICRO, PD, D), jnp.bfloat16),
+            pltpu.VMEM((MICRO, PD, D), jnp.float32),
+            pltpu.VMEM(n_grad.shape, jnp.bfloat16),
+            pltpu.SemaphoreType.DMA((5,)),
+            pltpu.SemaphoreType.DMA((5,)),
+            pltpu.SemaphoreType.DMA,
+        ],
+        compiler_params=pltpu.CompilerParams(
+            collective_id=4, has_side_effects=True, vmem_limit_bytes=VMEM_LIMIT
+        ),
+    )(w_grad, v_grad, p_grad, n_grad)
+
+
+def hosted(plan, step):
+    for at, stage in plan:
+
+        @pl.when(step == at)
+        def _():
+            stage()
+
+
 def place(plength):
     rank = lax.axis_index("fsdp")
     halfway = plength // PD
     return rank // halfway, rank % halfway * PD, rank % 2
 
 
-def attend_kernel(
-    plength,
-    meta,
-    qc,
-    qx,
-    k_rows,
-    v_rows,
-    table,
-    xcol,
-    w_ref,
-    ctx_c,
-    ctx_x,
-    full_c,
-    full_x,
-    lse_ref,
-    w_all,
-    keys,
-    vals,
-    scores,
-    probs,
-    send_sem,
-    recv_sem,
-    local_sem,
-):
+def attend_kernel(plength, carried, *refs):
+    (meta, qc, qx, k_rows, v_rows, table, xcol), refs = refs[:7], refs[7:]
+    shards, refs = refs[:carried], refs[carried:]
+    (ctx_c, ctx_x, full_c, full_x, lse_ref), refs = refs[:5], refs[5:]
+    fulls, refs = refs[:carried], refs[carried:]
+    keys, vals, scores, probs = refs[:4]
     step = pl.program_id(0) * PAIRS + pl.program_id(1)
-    grp = lax.axis_index("grp")
-    rank = lax.axis_index("fsdp")
-    core_mate = (grp, rank ^ 1)
-    x_mate = (grp ^ 1, rank)
-    local = pltpu.make_async_copy(w_ref, w_all.at[0], local_sem)
-    swap = pltpu.make_async_remote_copy(
-        w_ref, w_all.at[1], send_sem.at[0], recv_sem.at[0], device_id=core_mate,
-        device_id_type=pl.DeviceIdType.MESH,
-    )
-    cross = pltpu.make_async_remote_copy(
-        w_all.at[0:2], w_all.at[2:4], send_sem.at[1], recv_sem.at[1], device_id=x_mate,
-        device_id_type=pl.DeviceIdType.MESH,
-    )
-
-    @pl.when(step == 0)
-    def _():
-        barrier = pltpu.get_barrier_semaphore()
-        for mate in (core_mate, x_mate):
-            pl.semaphore_signal(
-                barrier, inc=1, device_id=mate, device_id_type=pl.DeviceIdType.MESH
+    stages = []
+    if carried:
+        net = Net()
+        for i in range(carried):
+            sends, recvs = refs[4 + 2 * i : 6 + 2 * i]
+            stages.append(
+                gather_stages(
+                    net, Copies(sends, recvs), refs[-1].at[i], shards[i], fulls[i]
+                )
             )
-        pl.semaphore_wait(barrier, 2)
-        local.start()
-        swap.start()
-
-    @pl.when(step == 5)
-    def _():
-        local.wait()
-        swap.wait()
-        cross.start()
-
-    @pl.when(step == 11)
-    def _():
-        cross.wait()
-
+        up, down, proj = stages
+        hosted([(0, net.greet)], step)
+        hosted(
+            [
+                (0, up[0]),
+                (3, up[1]),
+                (3, down[0]),
+                (6, up[2]),
+                (7, down[1]),
+                (7, proj[0]),
+                (8, up[3]),
+                (8, proj[1]),
+                (10, down[2]),
+                (10, proj[2]),
+            ],
+            step,
+        )
     own_prompt, base, side = place(plength)
     mapped = meta[pl.program_id(0)]
     blocks = plength // 128
@@ -239,6 +625,8 @@
     out = jnp.where(lane < HD, out[0:QP], out[QP:])
     ctx_x[...] = out.astype(jnp.bfloat16)
     full_x[...] = out
+    if carried:
+        hosted([(11, s) for s in (down[3], proj[3], up[4], down[4], proj[4])], step)
 
 
 def pair_column(shift):
@@ -252,7 +640,16 @@
 TABLE_SPEC = pl.BlockSpec((1, 8, LANES), lambda m, j, meta: (j, 0, 0))
 
 
-def attend(meta, queries, extra_q, key_rows, table, xcol, weight):
+def host_params(collective_id, carried):
+    if carried:
+        return pltpu.CompilerParams(
+            vmem_limit_bytes=VMEM_LIMIT, collective_id=collective_id, has_side_effects=True
+        )
+    return pltpu.CompilerParams(vmem_limit_bytes=VMEM_LIMIT)
+
+
+def attend(meta, queries, extra_q, key_rows, table, xcol, shards):
+    carried = len(shards)
     n_keys = key_rows.shape[0] // MICRO
     plength = (n_keys - 2 * CH) // 2
     content = pl.BlockSpec((TD, LANES), pair_column(0))
@@ -260,7 +657,7 @@
     own_row = plength + 2 * CH
     pairs = MICRO * PAIRS * 2 * (128 * plength + 256 * own_row) + MICRO * PAIRS * 128 * n_keys
     return pl.pallas_call(
-        functools.partial(attend_kernel, plength),
+        functools.partial(attend_kernel, plength, carried),
         name="attend",
         grid_spec=pltpu.PrefetchScalarGridSpec(
             num_scalar_prefetch=1,
@@ -271,25 +668,24 @@
                 key_spec(n_keys, 1),
                 TABLE_SPEC,
                 pl.BlockSpec((1, 128, 8), lambda m, j, meta: (m, 0, 0)),
-                pl.BlockSpec(memory_space=pl.ANY),
-            ],
+            ]
+            + [ANY_SPEC] * carried,
             out_specs=[
                 content,
                 extra,
                 content,
                 extra,
                 pl.BlockSpec((1, 1, 8, LANES), lambda m, j, meta: (m, j, 0, 0)),
-                pl.BlockSpec(memory_space=pl.ANY),
-            ],
+            ]
+            + [ANY_SPEC] * carried,
             scratch_shapes=[
                 pltpu.VMEM((n_keys, LANES), jnp.bfloat16),
                 pltpu.VMEM((n_keys, LANES), jnp.bfloat16),
                 pltpu.VMEM((256, n_keys), jnp.float32),
                 pltpu.VMEM((256, n_keys), jnp.bfloat16),
-                pltpu.SemaphoreType.DMA((2,)),
-                pltpu.SemaphoreType.DMA((2,)),
-                pltpu.SemaphoreType.DMA,
-            ],
+            ]
+            + [pltpu.SemaphoreType.DMA((GATHER_COPIES,))] * (2 * carried)
+            + [pltpu.SemaphoreType.DMA((4,))],
         ),
         out_shape=[
             jax.ShapeDtypeStruct((MICRO * TD, D), jnp.bfloat16),
@@ -297,11 +693,12 @@
             jax.ShapeDtypeStruct((MICRO * TD, D), jnp.float32),
             jax.ShapeDtypeStruct((MICRO * QP, D), jnp.float32),
             jax.ShapeDtypeStruct((MICRO, PAIRS, 8, LANES), jnp.float32),
-            jax.ShapeDtypeStruct((4,) + weight.shape, weight.dtype),
+        ]
+        + [
+            jax.ShapeDtypeStruct((8 * 4,) + shard.shape[1:], shard.dtype)
+            for shard in shards
         ],
-        compiler_params=pltpu.CompilerParams(
-            vmem_limit_bytes=VMEM_LIMIT, collective_id=1, has_side_effects=True
-        ),
+        compiler_params=host_params(2, carried),
         cost_estimate=pl.CostEstimate(
             flops=4 * pairs * LANES, bytes_accessed=16 * 1024 * 1024, transcendentals=pairs
         ),
@@ -313,42 +710,47 @@
         key_rows,
         table,
         xcol,
-        weight,
-    )
-
-
-def attend_back_kernel(
-    plength,
-    meta,
-    qc,
-    qx,
-    k_rows,
-    v_rows,
-    table,
-    xcol,
-    xrow,
-    lse_ref,
-    dc,
-    dx,
-    full_c,
-    full_x,
-    dq_c,
-    dq_x,
-    dk_rows,
-    dv_rows,
-    hist,
-    keys,
-    vals,
-    q_all,
-    d_all,
-    scores,
-    dprobs,
-    probs_t,
-    dscores_t,
-    ds_p,
-    dk_acc,
-    dv_acc,
-):
+        *shards,
+    )
+
+
+def attend_back_kernel(plength, carried, *refs):
+    (meta, qc, qx, k_rows, v_rows, table, xcol, xrow, lse_ref, dc, dx, full_c, full_x), refs = (
+        refs[:13],
+        refs[13:],
+    )
+    grads, refs = refs[:carried], refs[carried:]
+    (dq_c, dq_x, dk_rows, dv_rows, hist), refs = refs[:5], refs[5:]
+    shares, refs = refs[:carried], refs[carried:]
+    keys, vals, q_all, d_all, scores, dprobs, probs_t, dscores_t, ds_p, dk_acc, dv_acc = refs[:11]
+    refs = refs[11:]
+    step = pl.program_id(0) * PAIRS + pl.program_id(1)
+    if carried:
+        net = Net()
+        up, down, proj = (
+            reduce_stages(net, grads[i], shares[i], refs[10 * i : 10 * i + 10])
+            for i in range(carried)
+        )
+        hosted([(0, net.greet)], step)
+        hosted(
+            [
+                (0, up[0]),
+                (0, down[0]),
+                (0, proj[0]),
+                (1, up[1]),
+                (4, up[2]),
+                (4, down[1]),
+                (6, up[3]),
+                (7, down[2]),
+                (7, proj[1]),
+                (9, down[3]),
+                (9, proj[2]),
+                (9, up[4]),
+                (10, proj[3]),
+                (10, up[5]),
+            ],
+            step,
+        )
     own_prompt, base, side = place(plength)
     mapped = meta[pl.program_id(0)]
     blocks = plength // 128
@@ -563,9 +965,13 @@
             other = jnp.where(mapped == p, acc[plength : 2 * plength], 0.0)
             out_ref[p * plength : (p + 1) * plength] = (mine + other).astype(jnp.bfloat16)
         out_ref[2 * plength :] = acc[2 * plength :].astype(jnp.bfloat16)
-
-
-def attend_back(meta, queries, extra_q, key_rows, table, xcol, xrow, lse, dc, dx, fc, fx):
+    if carried:
+        rest = (down[4], proj[4], up[6], down[5], proj[5], down[6], proj[6])
+        hosted([(11, s) for s in rest], step)
+
+
+def attend_back(meta, queries, extra_q, key_rows, table, xcol, xrow, lse, dc, dx, fc, fx, grads):
+    carried = len(grads)
     n_keys = key_rows.shape[0] // MICRO
     plength = (n_keys - 2 * CH) // 2
     content = pl.BlockSpec((TD, LANES), pair_column(0))
@@ -573,7 +979,7 @@
     own_row = plength + 2 * CH
     pairs = MICRO * PAIRS * 2 * (128 * plength + 256 * own_row) + MICRO * PAIRS * 128 * n_keys
     return pl.pallas_call(
-        functools.partial(attend_back_kernel, plength),
+        functools.partial(attend_back_kernel, plength, carried),
         name="attend_back",
         grid_spec=pltpu.PrefetchScalarGridSpec(
             num_scalar_prefetch=1,
@@ -590,14 +996,16 @@
                 extra,
                 content,
                 extra,
-            ],
+            ]
+            + [ANY_SPEC] * carried,
             out_specs=[
                 content,
                 extra,
                 key_spec(n_keys, 0),
                 key_spec(n_keys, 0),
                 pl.BlockSpec((1, 1, 64, LANES), lambda m, j, meta: (m, j, 0, 0)),
-            ],
+            ]
+            + [ANY_SPEC] * carried,
             scratch_shapes=[
                 pltpu.VMEM((n_keys, LANES), jnp.bfloat16),
                 pltpu.VMEM((n_keys, LANES), jnp.bfloat16),
@@ -610,6 +1018,11 @@
                 pltpu.VMEM((plength, 256), jnp.float32),
                 pltpu.VMEM((n_keys, LANES), jnp.float32),
                 pltpu.VMEM((n_keys, LANES), jnp.float32),
+            ]
+            + [
+                buffer
+                for grad in grads
+                for buffer in reduce_buffers(4 * grad.shape[3], grad.shape[4])
             ],
         ),
         out_shape=[
@@ -618,8 +1031,9 @@
             jax.ShapeDtypeStruct((MICRO * n_keys, D), jnp.bfloat16),
             jax.ShapeDtypeStruct((MICRO * n_keys, D), jnp.bfloat16),
             jax.ShapeDtypeStruct((MICRO, PAIRS, 64, LANES), jnp.float32),
-        ],
-        compiler_params=pltpu.CompilerParams(vmem_limit_bytes=VMEM_LIMIT),
+        ]
+        + [jax.ShapeDtypeStruct(grad.shape[2:], grad.dtype) for grad in grads],
+        compiler_params=host_params(3, carried),
         cost_estimate=pl.CostEstimate(
             flops=10 * pairs * LANES, bytes_accessed=32 * 1024 * 1024, transcendentals=pairs
         ),
@@ -637,6 +1051,7 @@
         dx,
         fc,
         fx,
+        *grads,
     )
 
 
@@ -738,15 +1153,40 @@
     cont_index = own_rank // 2
     side = own_rank % 2
 
+    own_links = lax.axis_size("grp") == 4 and devices == 8
+
     def gather(entry):
         return lax.all_gather(entry, "fsdp", axis=0, tiled=True)
 
+    def quarters(entry):
+        return entry.reshape(4, -1, entry.shape[1])
+
+    n_keys = 2 * plength + 2 * CH
+    shard = b_query.shape[0]
+    up_size = b_up.shape[0]
     vectors = jnp.concatenate(
         [b_query, b_value, b_out, b_down, ln1_gain, ln1_bias, ln2_gain, ln2_bias, b_up]
     )
-    query_weight, key_weight, value_weight = gather(w_query), gather(w_key), gather(w_value)
-    all_vectors = gather(vectors[None])
-    shard = b_query.shape[0]
+    qkv_shard = jnp.concatenate([w_query, w_key, w_value], axis=1)
+    if own_links:
+        vector_shard = jnp.pad(vectors, (0, 32 * 256 - vectors.shape[0])).reshape(4, 8, 256)
+        qkv_weight, all_vectors, keys_x = gather_first(
+            quarters(qkv_shard), vector_shard, content_in
+        )
+        qkv_weight = qkv_weight.reshape(-1, qkv_shard.shape[1])
+        all_vectors = all_vectors.reshape(devices, -1)
+        carried = tuple(quarters(shard) for shard in (w_up, w_down, w_out))
+    else:
+        qkv_weight, all_vectors = gather(qkv_shard), gather(vectors[None])
+        up_weight, down_weight, out_weight = gather(w_up), gather(w_down), gather(w_out)
+        carried = ()
+        prompt_x = lax.all_gather(content_in[:, :PD], "fsdp", axis=1, tiled=True)
+        near_x = from_partner(content_in[:, PD:], "fsdp").reshape(MICRO, 2, 1, 128, D)
+        own_x = content_in[:, PD:].reshape(MICRO, 2, 1, 128, D)
+        cont_x = jnp.concatenate([near_x, own_x], axis=2).reshape(MICRO, 2 * CH, D)
+        keys_x = jnp.concatenate([prompt_x, cont_x], axis=1)
+    keys_x = keys_x.reshape(MICRO * n_keys, D)
+    query_weight, kv_weight = qkv_weight[:, :D], qkv_weight[:, D:]
     singles = [
         all_vectors[:, shard * i : shard * i + shard].reshape(-1).astype(jnp.float32)
         for i in range(8)
@@ -761,8 +1201,7 @@
         gain_two,
         shift_two,
     ) = singles
-    up_bias = all_vectors[:, 8 * shard :].reshape(-1).astype(jnp.float32)
-    out_weight, up_weight, down_weight = gather(w_out), gather(w_up), gather(w_down)
+    up_bias = all_vectors[:, 8 * shard : 8 * shard + up_size].reshape(-1).astype(jnp.float32)
 
     prompt_map = cont_prompt[:, 0, :]
     prompt_ref = jnp.sum(
@@ -791,13 +1230,6 @@
     tokens_x = content_in.reshape(MICRO * TD, D)
     extra_x = pad_rows(query_in)
     x_all = jnp.concatenate([tokens_x, extra_x])
-    n_keys = 2 * plength + 2 * CH
-    prompt_x = lax.all_gather(content_in[:, :PD], "fsdp", axis=1, tiled=True)
-    near_x = from_partner(content_in[:, PD:], "fsdp").reshape(MICRO, 2, 1, 128, D)
-    own_x = content_in[:, PD:].reshape(MICRO, 2, 1, 128, D)
-    cont_x = jnp.concatenate([near_x, own_x], axis=2).reshape(MICRO, 2 * CH, D)
-    keys_x = jnp.concatenate([prompt_x, cont_x], axis=1).reshape(MICRO * n_keys, D)
-    kv_weight = jnp.concatenate([key_weight, value_weight], axis=1)
     kv_bias = jnp.concatenate([jnp.zeros((D,), jnp.float32), value_bias])
     key_rows = (
         jnp.dot(keys_x, kv_weight, preferred_element_type=jnp.float32) + kv_bias
@@ -808,9 +1240,13 @@
     queries = q_all[: MICRO * TD]
     extra_q = q_all[MICRO * TD :]
 
-    ctx_c, ctx_x, full_c, full_x, lse, _ = attend(
-        meta, queries, extra_q, key_rows, table, xcol, w_out
-    )
+    ctx_c, ctx_x, full_c, full_x, lse, *gathered = attend(
+        meta, queries, extra_q, key_rows, table, xcol, carried
+    )
+    if own_links:
+        up_weight, down_weight, out_weight = (
+            entry.reshape(-1, entry.shape[2]) for entry in gathered
+        )
     context = jnp.concatenate([ctx_c, ctx_x])
     first, normed_one, inverse_one = layer_norm(
         x_all.astype(jnp.float32)
@@ -849,7 +1285,14 @@
     dweight_out = dot_tn(context, dres_one_b)
     dcontext = dot_nt(dres_one_b, out_weight).astype(jnp.bfloat16)
 
-    dq_c, dq_x, dk_rows, dv_rows, hist = attend_back(
+    def by_quarter(grad):
+        grad = grad.astype(jnp.bfloat16)
+        return grad.reshape(4, 2, 4, grad.shape[0] // 32, grad.shape[1])
+
+    to_reduce = ()
+    if own_links:
+        to_reduce = tuple(by_quarter(g) for g in (dweight_up, dweight_down, dweight_out))
+    dq_c, dq_x, dk_rows, dv_rows, hist, *reduced = attend_back(
         meta,
         queries,
         extra_q,
@@ -862,6 +1305,7 @@
         dcontext[rows_c:],
         full_c,
         full_x,
+        to_reduce,
     )
     dkv_rows = jnp.concatenate([dk_rows, dv_rows], axis=1)
     dq_all = jnp.concatenate([dq_c, dq_x])
@@ -870,26 +1314,7 @@
     dweight_kv = dot_tn(keys_x, dkv_rows)
     dbias_value = jnp.sum(dv_rows.astype(jnp.float32), axis=0)
     dkeys_x = dot_nt(dkv_rows, kv_weight).reshape(MICRO, n_keys, D)
-    from_prompts = lax.psum_scatter(
-        dkeys_x[:, : 2 * plength].astype(jnp.bfloat16), "fsdp", scatter_dimension=1, tiled=True
-    ).astype(jnp.float32)
-    dcont = dkeys_x[:, 2 * plength :].reshape(MICRO, 2, 2, 128, D)
-    from_near = from_partner(dcont[:, :, 0].astype(jnp.bfloat16), "fsdp").astype(jnp.float32)
-    dcont = (dcont[:, :, 1] + from_near).reshape(MICRO, CH, D)
-    dx_all = dres_one + dot_nt(dq_all, query_weight)
-    dtokens = dx_all[:rows_c].reshape(MICRO, TD, D) + jnp.concatenate(
-        [from_prompts, dcont], axis=1
-    )
-    dextra = dx_all[rows_c:]
-    grad_content = dtokens
-    grad_query = dextra.reshape(MICRO, QP, D)[:, :extra_rows]
     dtable = table_gradient(hist, rel_bucket, bias_table.shape[0], side, heads)
-
-    def scatter(piece):
-        return lax.psum_scatter(
-            piece.astype(jnp.bfloat16), "fsdp", scatter_dimension=0, tiled=True
-        )
-
     small = jnp.concatenate(
         [
             entry.reshape(devices, -1)
@@ -907,31 +1332,61 @@
             )
         ],
         axis=1,
-    )
-    shares = (
-        scatter(dweight_down),
-        scatter(dweight_up),
-        scatter(dweight_out),
-        scatter(dweight_query),
-        scatter(dweight_kv),
-        scatter(small),
-    )
-    totals = [lax.psum(entry, "grp").astype(jnp.float32) for entry in shares]
-    t_down, t_up, t_out, t_query, t_kv, t_small = totals
-    t_small = t_small.reshape(-1)
+    ).astype(jnp.bfloat16)
+    dprompts = dkeys_x[:, : 2 * plength].astype(jnp.bfloat16)
+    dcont = dkeys_x[:, 2 * plength :].reshape(MICRO, 2, 2, 128, D)
+    dnear = dcont[:, :, 0].astype(jnp.bfloat16)
+    dweight_qkv = jnp.concatenate(
+        [dweight_query.astype(jnp.bfloat16), dweight_kv.astype(jnp.bfloat16)], axis=1
+    )
+    small_size = small.shape[1]
+    if own_links:
+        small = jnp.pad(small, ((0, 0), (0, 32 * 256 - small_size)))
+        t_qkv, t_small, from_prompts, from_near = reduce_last(
+            by_quarter(dweight_qkv),
+            small.reshape(4, 2, 4, 8, 256),
+            dprompts.reshape(MICRO, 4, 2, PD, D),
+            dnear,
+        )
+        t_up, t_down, t_out = reduced
+        shares = (t_down, t_up, t_out, t_qkv, t_small)
+        totals = [
+            entry.reshape(-1, entry.shape[-1]).astype(jnp.float32) for entry in shares
+        ]
+    else:
+
+        def scatter(piece, dimension=0):
+            return lax.psum_scatter(
+                piece.astype(jnp.bfloat16), "fsdp", scatter_dimension=dimension, tiled=True
+            )
+
+        from_prompts = scatter(dprompts, 1).astype(jnp.float32)
+        from_near = from_partner(dnear, "fsdp")
+        shares = [
+            scatter(piece)
+            for piece in (dweight_down, dweight_up, dweight_out, dweight_qkv, small)
+        ]
+        totals = [lax.psum(entry, "grp").astype(jnp.float32) for entry in shares]
+    dcont = (dcont[:, :, 1] + from_near.astype(jnp.float32)).reshape(MICRO, CH, D)
+    dx_all = dres_one + dot_nt(dq_all, query_weight)
+    grad_content = dx_all[:rows_c].reshape(MICRO, TD, D) + jnp.concatenate(
+        [from_prompts, dcont], axis=1
+    )
+    grad_query = dx_all[rows_c:].reshape(MICRO, QP, D)[:, :extra_rows]
+    t_down, t_up, t_out, t_qkv, t_small = totals
+    t_small = t_small.reshape(-1)[:small_size]
     pieces = [t_small[shard * i : shard * i + shard] for i in range(8)]
     up_at = 8 * shard
-    up_size = b_up.shape[0]
     t_table = t_small[up_at + up_size :].reshape(-1, heads)
     return (
         out_content,
         out_query,
         grad_content,
         grad_query,
-        t_query,
+        t_qkv[:, :D],
         pieces[0],
-        t_kv[:, :D],
-        t_kv[:, D:],
+        t_qkv[:, D : 2 * D],
+        t_qkv[:, 2 * D :],
         pieces[1],
         t_out,
         pieces[2],

time: 694 us -> 451 us (0.65)
  waiting for transfers between devices: 298 us -> 0 us
  Pallas kernels: 94.3 us -> 259 us
  blocking collectives: 52.5 us -> 0 us
  local copies, waits for them, and re-layouts: 59 us -> 34.1 us
  between operations: 15.2 us -> 1.89 us
  other arithmetic: 36.4 us -> 24.3 us
    pallas_call x2 -> x4, Pallas kernels: 94.3 us -> 259 us  [the longest x1 81.2 us: attend_back(): pl.pallas_call(functools.partial(attend_back_kernel, plength, carried), n...]
    reduce_scatter x6 -> x0, waiting for transfers between devices: 129 us -> none  [the longest x5 129 us: scatter(): lax.psum_scatter(piece.astype(jnp.bfloat16), 'fsdp', scatter_dimension=0,...]
    all_gather x7 -> x0, waiting for transfers between devices: 108 us -> none  [the longest x6 70.7 us: gather(): return lax.all_gather(entry, 'fsdp', axis=0, tiled=True)]
    psum x1 -> x0, waiting for transfers between devices: 56.6 us -> none  [on_device(): totals = [lax.psum(entry, 'grp').astype(jnp.float32) for entry in shares]]
    unnamed x1 -> x0, blocking collectives: 26.8 us -> none
    unnamed x123 -> x90, local copies, waits for them, and re-layouts: 22.2 us -> 6.48 us
    all_gather x1 -> x0, blocking collectives: 15.7 us -> none  [gather(): return lax.all_gather(entry, 'fsdp', axis=0, tiled=True)]
    psum x1 -> x0, blocking collectives: 10 us -> none  [on_device(): totals = [lax.psum(entry, 'grp').astype(jnp.float32) for entry in shares]]
  transfers between devices with their start and end apart: 16 -> 0, of which waited for: 9 -> 0; matrix products, arithmetic and copies ran while one was open for 24% -> 0% of each run, Pallas kernels for 6% -> 0%
where the time goes in v3:
time: 451 us; the launch traced here: 443 us
  Pallas kernels  259 us (57%)
  matrix products  123 us (27%)
  local copies, waits for them, and re-layouts  34.1 us (8%)
  other arithmetic  24.3 us (5%)
    pallas_call x1, Pallas kernels, attend_back(): pl.pallas_call(functools.partial(attend_back_kernel, plength, carried), n...  81.2 us
    pallas_call x1, Pallas kernels, reduce_last(): pl.pallas_call(reduce_last_kernel, name='reduce_last', in_specs=[ANY_SPEC...  63.2 us
    pallas_call x1, Pallas kernels, attend(): pl.pallas_call(functools.partial(attend_kernel, plength, carried), name='...  57.9 us
    pallas_call x1, Pallas kernels, gather_first(): pl.pallas_call(gather_first_kernel, name='gather_first', in_specs=[ANY_SP...  56.7 us
    dot_general x1, matrix products, on_device(): jnp.dot(first_b, up_weight, preferred_element_type=jnp.float32) + up_bias  33.4 us
    dot_general x5, matrix products, dot_tn(): lax.dot_general(left, right, (((0,), (0,)), ((), ())), preferred_element_...  31.3 us
    dot_general x5, matrix products, dot_nt(): lax.dot_general(left, right, (((1,), (1,)), ((), ())), preferred_element_...  31 us
    dot_general x1, matrix products, on_device(): jnp.dot(keys_x, kv_weight, preferred_element_type=jnp.float32) + kv_bias  12.8 us

profile of v3, /device:TPU:0, one launch (start us, length us, event | category | flops | bytes accessed | tf_op | source)
XLA Modules:
  0.0 442.6 jit_solution(3689353827778226870)
XLA Ops:
  0.7 1.9 pad_maximum_fusion.3
  2.6 6.1 %concatenate.41 = bf16[1152]{0:T(1024)(128)(2,1)S(1)} concatenate(bf16[96]{0:T(256)(128)(2,1)} %param.29, bf16[96]{0:T(256)(128)(2,1)} %param.32, bf16[96]{0:T(256)(128)(2,1)} %param.34, bf16[96]{0:T(256)(128)(2,1)} %param.40, bf16[96]{0:T(256)(128)(2,1)} %param.35, bf16[96]{0:T(256)(128)(2,1)} %param.36, bf16[96]{0:T(256)(128)(2,1)} %param.41, bf16[96]{0:T(256)(128)(2,1)} %param.42, ...), dimensions={0} | concatenate | bytes 4608 | tf_op jit(solution)/shard_map/concatenate | solution.py:1167
  8.7 0.6 reshape.369.v_ref
  9.4 56.7 %gather_first.1 = (bf16[32,24,2304]{2,1,0:T(8,128)(2,1)}, bf16[32,8,256]{2,1,0:T(8,128)(2,1)}, bf16[2,1536,768]{2,1,0:T(8,128)(2,1)}) custom-call(bf16[4,24,2304]{2,1,0:T(8,128)(2,1)} %bitcast.120, bf16[4,8,256]{2,1,0:T(8,128)(2,1)} %reshape.369.v_ref, bf16[2,384,768]{2,1,0:T(8,128)(2,1)} %x_ref.1), custom_call_target="tpu_custom_call" | custom-call | tf_op jit(solution)/shard_map/gather_first/pallas_call | solution.py:368
  66.1 1.0 reshape.371
  67.2 0.6 select_reduce_fusion.refs_0_
  68.0 2.6 add_convert_fusion.1
  70.5 1.1 slice.193.refs_1_
  71.6 0.7 slice.194.refs_2_
  72.4 12.8 %add_convert_fusion.refs_3_.refs_4_ = bf16[3072,1536]{1,0:T(8,128)(2,1)} fusion(bf16[3072,768]{1,0:T(8,128)(2,1)} %bitcast.155, f32[1536]{0:T(1024)S(1)} %pad_convert_fusion, bf16[768,2304]{1,0:T(8,128)(2,1)} %bitcast.133), kind=kOutput, calls=%fused_computation.1 | convolution fusion | flops 7257194496 | bytes 16521216 | tf_op jit(solution)/shard_map/dot_general | solution.py:1235
  85.4 0.6 gather_fusion
  86.4 0.6 pad.31.refs_5_
  87.1 0.6 fusion.59
  87.7 0.8 copy.96.refs_6_
  88.5 57.9 %attend.1 = (bf16[768,768]{1,0:T(8,128)(2,1)}, bf16[128,768]{1,0:T(8,128)(2,1)}, f32[768,768]{1,0:T(8,128)}, f32[128,768]{1,0:T(8,128)}, f32[2,6,8,128]{3,2,1,0:...) custom-call(s32[2]{0:T(128)} %select_reduce_fusion.refs_0_, ...), custom_call_target="tpu_custom_call" | custom-call | flops 5234491392 | bytes 16777216 | tf_op jit(solution)/shard_map/attend/pallas_call | solution.py:659
  146.5 1.4 constant_dynamic-update-slice_fusion.1
  147.9 0.9 constant_dynamic-update-slice_fusion
  148.9 3.1 fusion.60
  152.2 0.4 multiply_reduce_fusion.3
  152.7 33.4 %fusion.2 = (bf16[896,3072]{1,0:T(8,128)(2,1)S(1)}, f32[896,3072]{1,0:T(8,128)}) fusion(f32[3072]{0:T(1024)S(1)} %reshape.412, bf16[768,3072]{1,0:T(8,128)(2,1)} %bitcast.157, f32[896,768]{1,0:T(8,128)S(1)} %get-tuple-element.115, f32[768]{0:T(1024)S(1)} %reshape.411, f32[768]{0:T(1024)S(1)} %reshape.410, f32[896]{0:T(1024)S(1)} %add_rsqrt_fusion.1, ...), kind=kOutput, calls=%fused_computation.6 | convolution fusion | flops 4412964864 | bytes 24011776 | tf_op jit(solution)/shard_map/dot_general | solution.py:1259
  186.1 8.5 %fusion.61 = (f32[896]{0:T(1024)S(1)}, f32[896,768]{1,0:T(8,128)S(1)}) fusion(f32[768]{0:T(1024)S(1)} %reshape.413, bf16[896,3072]{1,0:T(8,128)(2,1)S(1)} %get-tuple-element.116, bf16[3072,768]{1,0:T(8,128)(2,1)S(1)} %bitcast.162, f32[768]{0:T(1024)S(1)} %reshape.411, f32[768]{0:T(1024)S(1)} %reshape.410, f32[896]{0:T(1024)S(1)} %add_rsqrt_fusion.1, ...), kind=kOutput, calls=%fused_computation.159 | convolution fusion | flops 4232674304 | bytes 15748608 | tf_op jit(solution)/shard_map/dot_general | solution.py:1262
  194.7 0.4 multiply_reduce_fusion.2
  195.1 0.5 copy-done.17
  195.7 2.5 fusion.22
  198.3 2.7 fusion.51
  201.0 1.6 slice.205
  202.6 0.8 slice.207
  203.3 10.9 %fusion.62 = (bf16[3072]{0:T(1024)(128)(2,1)S(1)}, bf16[896,3072]{1,0:T(8,128)(2,1)S(1)}) fusion(f32[896,3072]{1,0:T(8,128)} %get-tuple-element.117, f32[3072]{0:T(1024)S(1)} %reshape.412, bf16[3072,768]{1,0:T(8,128)(2,1)} %bitcast.161, f32[896,768]{1,0:T(8,128)S(1)} %get-tuple-element.77), kind=kOutput, calls=%fused_computation.160 | convolution fusion | flops 4267078656 | bytes 24004608 | tf_op jit(solution)/shard_map/dot_general | solution.py:26
  214.3 5.1 %multiply_reduce_fusion = (bf16[768]{0:T(1024)(128)(2,1)S(1)}, f32[896]{0:T(1024)S(1)}, f32[896]{0:T(1024)S(1)}, bf16[768]{0:T(1024)(128)(2,1)S(1)}, f32[896,768]{1,0:T(8,128)S(1)}) fusion(f32[896,768]{1,0:T(8,128)S(1)} %copy-done.2, f32[896]{0:T(1024)S(1)} %add_rsqrt_fusion.1, f32[896]{0:T(1024)S(1)} %broadcast_multiply_fusion.5, f32[768]{0:T(1024)S(1)} %reshape.410, ...), kind=kOutput, calls=%fused_computation.42 | convolution fusion | flops 4234736384 | bytes 18501632 | tf_op jit(solution)/shard_map/dot_general | solution.py:26
  219.4 1.0 fusion.53
  220.7 1.3 convolution_convert_fusion.3
  222.0 1.1 slice.208.refs_9_
  223.1 0.7 slice.209.refs_10_
  223.8 7.7 %convolution_convert_fusion.1 = bf16[768,3072]{1,0:T(8,128)(2,1)} fusion(bf16[896,3072]{1,0:T(8,128)(2,1)S(1)} %bitcast.169, f32[896,768]{1,0:T(8,128)S(1)} %copy-done.2, f32[768]{0:T(1024)S(1)} %reshape.411, f32[768]{0:T(1024)S(1)} %reshape.410, f32[896]{0:T(1024)S(1)} %add_rsqrt_fusion.1, f32[896]{0:T(1024)S(1)} %broadcast_multiply_fusion.5), kind=kOutput, calls=%fused_computation.30 | convolution fusion | flops 4233658368 | bytes 12989440 | tf_op jit(solution)/shard_map/dot_general | solution.py:32
  231.5 7.0 %convolution_convert_fusion = bf16[3072,768]{1,0:T(8,128)(2,1)} fusion(bf16[896,3072]{1,0:T(8,128)(2,1)S(1)} %bitcast.171, f32[896,768]{1,0:T(8,128)S(1)} %get-tuple-element.77), kind=kOutput, calls=%fused_computation.29 | convolution fusion | flops 4230905856 | bytes 12976128 | tf_op jit(solution)/shard_map/dot_general | solution.py:32
  238.5 2.5 convolution_convert_fusion.5
  241.0 81.2 %attend_back.1 = (bf16[768,768]{1,0:T(8,128)(2,1)}, bf16[128,768]{1,0:T(8,128)(2,1)}, bf16[3072,768]{1,0:T(8,128)(2,1)}, bf16[3072,768]{1,0:T(8,128)(2,1)}, f32[...) custom-call(s32[2]{0:T(128)} %select_reduce_fusion.refs_0_, ...), custom_call_target="tpu_custom_call" | custom-call | flops 13086228480 | bytes 33554432 | tf_op jit(solution)/shard_map/attend_back/pallas_call | solution.py:981
  322.2 1.6 fusion.55
  323.8 1.0 fusion.57
  324.8 2.7 convolution_add_fusion
  327.9 1.1 copy-done
  329.0 1.7 slice-done.2
  330.8 1.2 fusion.54
  332.0 12.6 %convolution_convert_fusion.2 = bf16[768,1536]{1,0:T(8,128)(2,1)} fusion(bf16[3072,768]{1,0:T(8,128)(2,1)} %bitcast.156, bf16[3072,1536]{1,0:T(8,128)(2,1)S(1)} %get-tuple-element.83), kind=kOutput, calls=%fused_computation.37 | convolution fusion | flops 7248936960 | bytes 16515072 | tf_op jit(solution)/shard_map/dot_general | solution.py:32
  344.7 1.5 convolution_convert_fusion.4
  346.2 0.6 copy.98
  346.8 3.8 pad_maximum_fusion
  352.6 0.4 fusion.63
  353.6 0.7 copy.106
  354.2 11.1 %fusion.24 = f32[3072,768]{1,0:T(8,128)S(1)} fusion(bf16[3072,1536]{1,0:T(8,128)(2,1)} %copy-done.4, bf16[768,2304]{1,0:T(8,128)(2,1)} %bitcast.135), kind=kOutput, calls=%fused_computation.57 | convolution fusion | flops 7247757312 | bytes 21233664 | tf_op jit(solution)/shard_map/dot_general | solution.py:26
  365.3 2.0 slice.254
  367.5 1.0 fusion.30.n_ref
  368.5 63.2 %reduce_last.1 = (bf16[4,24,2304]{2,1,0:T(8,128)(2,1)}, bf16[4,8,256]{2,1,0:T(8,128)(2,1)}, f32[2,128,768]{2,1,0:T(8,128)}, bf16[2,2,128,768]{3,2,1,0:T(8,128)(2,1)}) custom-call(bf16[4,2,4,24,2304]{4,3,2,1,0:T(8,128)(2,1)} %bitcast.102, bf16[4,2,4,8,256]{4,3,2,1,0:T(8,128)(2,1)} %bitcast.131, bf16[2,4,2,128,768]{4,3,2,1,0:T(8,128)(2,1)} %bitcast.103, ...), custom_call_target="tpu_custom_call" | custom-call | tf_op jit(solution)/shard_map/reduce_last/pallas_call | solution.py:447
  431.7 1.4 fusion.27
  433.1 0.4 slice-done
  433.8 1.7 maximum_add_fusion
  435.5 0.8 slice.219
  436.3 0.9 fusion.56
  437.3 0.6 fusion.58
  437.9 0.7 bitcast_convert_fusion.3
  438.6 1.2 bitcast_convert_fusion.1
  439.8 0.6 slice.228
  440.4 1.1 bitcast_convert_fusion
  441.5 0.7 reshape.407
  (163 shorter events, 5.1 us)
Async XLA Ops:
  0.7 67.3 %copy-start.5 = (bf16[2,384,768]{2,1,0:T(8,128)(2,1)S(1)}, bf16[2,384,768]{2,1,0:T(8,128)(2,1)}, u32[]{:S(2)}) copy-start(bf16[2,384,768]{2,1,0:T(8,128)(2,1)} %x_ref.1) | copy-start | bytes 3538948
  0.7 66.5 %copy-start.22 = (s32[2,1,4]{2,1,0:T(1,128)S(1)}, s32[2,1,4]{2,1,0:T(1,128)}, u32[]{:S(2)}) copy-start(s32[2,1,4]{2,1,0:T(1,128)} %param.26) | copy-start | bytes 100
  0.7 67.2 %copy-start.16 = (bf16[2,56,768]{2,1,0:T(8,128)(2,1)S(1)}, bf16[2,56,768]{2,1,0:T(8,128)(2,1)}, u32[]{:S(2)}) copy-start(bf16[2,56,768]{2,1,0:T(8,128)(2,1)} %param.24) | copy-start | bytes 516100
  67.9 81.0 %copy-start.14 = (bf16[2,64,768]{2,1,0:T(8,128)(2,1)}, bf16[2,64,768]{2,1,0:T(8,128)(2,1)S(1)}, u32[]{:S(2)}) copy-start(bf16[2,64,768]{2,1,0:T(8,128)(2,1)S(1)} %pad.29) | copy-start | bytes 589828
  72.4 12.8 %copy-start.20 = (bf16[32,12]{0,1:T(8,128)(2,1)S(1)}, bf16[32,12]{0,1:T(8,128)(2,1)}, u32[]{:S(2)}) copy-start(bf16[32,12]{0,1:T(8,128)(2,1)} %param.43) | copy-start | bytes 2308
  72.4 12.9 %copy-start.26 = (s32[128]{0:T(128)S(1)}, s32[128]{0:T(128)}, u32[]{:S(2)}) copy-start(s32[128]{0:T(128)} %param.27) | copy-start | bytes 1540
  72.4 14.6 %copy-start.21 = (s32[2,1,56]{2,1,0:T(1,128)S(1)}, s32[2,1,56]{2,1,0:T(1,128)}, u32[]{:S(2)}) copy-start(s32[2,1,56]{2,1,0:T(1,128)} %param.25) | copy-start | bytes 1348
  146.5 2.4 copy-start.24
  148.9 3.2 copy-start.7
  152.1 34.1 %copy-start.1 = (f32[896,768]{1,0:T(8,128)}, f32[896,768]{1,0:T(8,128)S(1)}, u32[]{:S(2)}) copy-start(f32[896,768]{1,0:T(8,128)S(1)} %get-tuple-element.115) | copy-start | bytes 8257540
  152.7 33.5 %copy-start.23 = (bf16[32,96,768]{2,1,0:T(8,128)(2,1)S(1)}, bf16[32,96,768]{2,1,0:T(8,128)(2,1)}, u32[]{:S(2)}) copy-start(bf16[32,96,768]{2,1,0:T(8,128)(2,1)} %get-tuple-element.50) | copy-start | bytes 14155780
  186.1 8.5 %copy-start.29 = (bf16[896,3072]{1,0:T(8,128)(2,1)}, bf16[896,3072]{1,0:T(8,128)(2,1)S(1)}, u32[]{:S(2)}) copy-start(bf16[896,3072]{1,0:T(8,128)(2,1)S(1)} %get-tuple-element.116) | copy-start | bytes 16515076
  194.6 0.9 copy-start.17
  201.0 13.3 %slice-start.6 = ((s8[4718592]{0:T(1024)(128)(4,1)}), s8[4194304]{0:T(1024)(128)(4,1)S(1)}, s32[]{:S(2)}) async-start(s8[4718592]{0:T(1024)(128)(4,1)} %bitcast.158), calls=%async_computation.6 | async-start | bytes 8388608
  203.3 11.0 %copy-start.2 = (f32[896,768]{1,0:T(8,128)S(1)}, f32[896,768]{1,0:T(8,128)}, u32[]{:S(2)}) copy-start(f32[896,768]{1,0:T(8,128)} %copy-done.1) | copy-start | bytes 8257540
  203.3 11.0 %slice-start.7 = ((s8[4718592]{0:T(1024)(128)(4,1)}), s8[524288]{0:T(1024)(128)(4,1)S(1)}, s32[]{:S(2)}) async-start(s8[4718592]{0:T(1024)(128)(4,1)} %bitcast.158), calls=%async_computation.7 | async-start | bytes 1048576
  214.3 5.1 %copy-start.28 = (bf16[896,3072]{1,0:T(8,128)(2,1)}, bf16[896,3072]{1,0:T(8,128)(2,1)S(1)}, u32[]{:S(2)}) copy-start(bf16[896,3072]{1,0:T(8,128)(2,1)S(1)} %get-tuple-element.122) | copy-start | bytes 16515076
  219.4 1.3 copy-start.25
  219.4 4.3 slice-start.8
  220.7 3.1 slice-start.9
  222.0 9.5 %slice-start.10 = ((s8[5505024]{0:T(1024)(128)(4,1)}), s8[4194304]{0:T(1024)(128)(4,1)S(1)}, s32[]{:S(2)}) async-start(s8[5505024]{0:T(1024)(128)(4,1)} %bitcast.170), calls=%async_computation.10 | async-start | bytes 8388608
  223.8 7.7 %slice-start.11 = ((s8[5505024]{0:T(1024)(128)(4,1)}), s8[1310720]{0:T(1024)(128)(4,1)S(1)}, s32[]{:S(2)}) async-start(s8[5505024]{0:T(1024)(128)(4,1)} %bitcast.170), calls=%async_computation.11 | async-start | bytes 2621440
  231.5 7.1 %copy-start.8 = (bf16[896,768]{1,0:T(8,128)(2,1)S(1)}, bf16[896,768]{1,0:T(8,128)(2,1)}, u32[]{:S(2)}) copy-start(bf16[896,768]{1,0:T(8,128)(2,1)} %copy-done.7) | copy-start | bytes 4128772
  324.7 2.7 slice-start.4
  324.8 2.7 slice-start.5
  327.5 1.5 copy-start
  327.5 3.2 slice-start.2
  327.5 3.3 slice-start.3
  332.0 12.7 %copy-start.4 = (bf16[3072,1536]{1,0:T(8,128)(2,1)}, bf16[3072,1536]{1,0:T(8,128)(2,1)S(1)}, u32[]{:S(2)}) copy-start(bf16[3072,1536]{1,0:T(8,128)(2,1)S(1)} %get-tuple-element.83) | copy-start | bytes 28311556
  332.0 12.7 %copy-start.6 = (bf16[2,384,768]{2,1,0:T(8,128)(2,1)S(1)}, bf16[2,384,768]{2,1,0:T(8,128)(2,1)}, u32[]{:S(2)}) copy-start(bf16[2,384,768]{2,1,0:T(8,128)(2,1)} %x_ref.1) | copy-start | bytes 3538948
  332.0 12.7 %copy-start.15 = (bf16[2,64,768]{2,1,0:T(8,128)(2,1)S(1)}, bf16[2,64,768]{2,1,0:T(8,128)(2,1)}, u32[]{:S(2)}) copy-start(bf16[2,64,768]{2,1,0:T(8,128)(2,1)} %copy-done.14) | copy-start | bytes 589828
  346.8 4.4 copy-start.3
  346.8 4.8 %copy-start.13 = (f32[2,6,64,128]{3,2,1,0:T(8,128)S(1)}, f32[2,6,64,128]{3,2,1,0:T(8,128)}, u32[]{:S(2)}) copy-start(f32[2,6,64,128]{3,2,1,0:T(8,128)} %get-tuple-element.58) | copy-start | bytes 1179652
  350.6 2.4 copy-start.27
  431.7 1.9 slice-start
  431.7 2.1 copy-start.9
  433.8 1.7 slice-start.1
  433.8 2.5 copy-start.12
  435.5 1.8 copy-start.19
  435.5 2.4 copy-start.18
  435.5 3.2 copy-start.11
  436.2 4.2 copy-start.10

commit v4 on v3

--- a/solution.py
+++ b/solution.py
@@ -381,96 +381,6 @@
         + [pltpu.SemaphoreType.DMA((5,))],
         compiler_params=pltpu.CompilerParams(collective_id=1, has_side_effects=True),
     )(w_shard, v_shard, content_in)
-
-
-def reduce_last_kernel(w_ref, v_ref, p_ref, n_ref, w_out, v_out, p_out, n_out, *scratch):
-    w_buf, v_buf = scratch[:10], scratch[10:20]
-    mine, theirs, along, total, n_buf, x_s, x_r, x_local = scratch[20:]
-    net = Net()
-    net.greet()
-    weights = reduce_stages(net, w_ref, w_out, w_buf)
-    vectors = reduce_stages(net, v_ref, v_out, v_buf)
-    copies = Copies(x_s, x_r)
-    load = pltpu.make_async_copy(p_ref.at[:, :, net.c], mine, x_local)
-    to_mate = [
-        copies.to(net.to_mate, p_ref.at[:, :, 1 - net.c], theirs),
-        copies.to(net.to_mate, n_ref, n_buf),
-    ]
-    third = [
-        copies.to(net.to_z[k], mine.at[:, net.z_of[k]], along.at[k]) for k in range(3)
-    ]
-    weights[0]()
-    vectors[0]()
-    load.start()
-    start(to_mate)
-    weights[1]()
-    vectors[1]()
-    load.wait()
-    arrive(to_mate)
-
-    @pl.loop(0, 8)
-    def _(i):
-        m, zi = i // 4, i % 4
-        mine[m, zi] = mine[m, zi] + theirs[m, zi]
-
-    start(third)
-    for i in range(2, 4):
-        weights[i]()
-        vectors[i]()
-    arrive(third)
-    weights[4]()
-    vectors[4]()
-
-    @pl.loop(0, 2)
-    def _(m):
-        s = mine[m, net.z].astype(jnp.float32)
-        for k in range(3):
-            s = s + along[k, m].astype(jnp.float32)
-        total[m] = s
-
-    out = pltpu.make_async_copy(total, p_out, x_local)
-    out.start()
-    out.wait()
-    out = pltpu.make_async_copy(n_buf, n_out, x_local)
-    out.start()
-    out.wait()
-    for i in range(5, 7):
-        weights[i]()
-        vectors[i]()
-    copies.finish()
-
-
-def reduce_last(w_grad, v_grad, p_grad, n_grad):
-    def buffers(grad):
-        return reduce_buffers(4 * grad.shape[3], grad.shape[4])
-
-    return pl.pallas_call(
-        reduce_last_kernel,
-        name="reduce_last",
-        in_specs=[ANY_SPEC] * 4,
-        out_specs=[ANY_SPEC] * 4,
-        out_shape=[
-            jax.ShapeDtypeStruct(w_grad.shape[2:], jnp.bfloat16),
-            jax.ShapeDtypeStruct(v_grad.shape[2:], jnp.bfloat16),
-            jax.ShapeDtypeStruct((MICRO, PD, D), jnp.float32),
-            jax.ShapeDtypeStruct(n_grad.shape, jnp.bfloat16),
-        ],
-        scratch_shapes=buffers(w_grad)
-        + buffers(v_grad)
-        + [
-            pltpu.VMEM((MICRO, 4, PD, D), jnp.bfloat16),
-            pltpu.VMEM((MICRO, 4, PD, D), jnp.bfloat16),
-            pltpu.VMEM((3, MICRO, PD, D), jnp.bfloat16),
-            pltpu.VMEM((MICRO, PD, D), jnp.float32),
-            pltpu.VMEM(n_grad.shape, jnp.bfloat16),
-            pltpu.SemaphoreType.DMA((5,)),
-            pltpu.SemaphoreType.DMA((5,)),
-            pltpu.SemaphoreType.DMA,
-        ],
-        compiler_params=pltpu.CompilerParams(
-            collective_id=4, has_side_effects=True, vmem_limit_bytes=VMEM_LIMIT
-        ),
-    )(w_grad, v_grad, p_grad, n_grad)
 
 
 def hosted(plan, step):
@@ -1060,28 +970,527 @@
     return lax.ppermute(block, axis, [(i, i ^ 1) for i in range(count)])
 
 
-def layer_norm(value, gain, shift):
-    centred = value - jnp.mean(value, axis=-1, keepdims=True)
-    inverse = lax.rsqrt(jnp.mean(centred * centred, axis=-1, keepdims=True) + 1e-05)
-    normed = centred * inverse
-    return (normed * gain + shift, normed, inverse)
-
-
-def norm_back(upstream, normed, inverse, gain):
-    scaled = upstream * gain
-    inner = (
-        scaled
-        - jnp.mean(scaled, axis=-1, keepdims=True)
-        - normed * jnp.mean(scaled * normed, axis=-1, keepdims=True)
-    )
-    return (inverse * inner, jnp.sum(upstream * normed, axis=0), jnp.sum(upstream, axis=0))
-
-
-def gelu_slope(hidden):
-    return (
-        0.5 * (1.0 + lax.erf(hidden * 0.7071067811865476))
-        + hidden * jnp.exp(-0.5 * hidden * hidden) * 0.3989422804014327
-    )
+TAIL_RATE = 0.24
+TAIL = (
+    0.08952757299725976,
+    0.1555125511021828,
+    -0.15404562880205064,
+    0.6255850035411683,
+    -0.6460658211054147,
+    0.554571568104313,
+    -0.12508524614530675,
+)
+
+
+def gelu_parts(hidden):
+    bell = jnp.exp(-0.5 * hidden * hidden)
+    t = 1.0 / (1.0 + TAIL_RATE * jnp.abs(hidden))
+    poly = TAIL[-1]
+    for term in TAIL[-2::-1]:
+        poly = poly * t + term
+    tail = poly * t * bell
+    cdf = jnp.where(hidden < 0.0, tail, 1.0 - tail)
+    return hidden * cdf, cdf + hidden * bell * 0.3989422804014327
+
+
+TILE = 448
+GRAD_STEPS = 9
+
+
+def fold_rows(term):
+    return jnp.sum(term.reshape(-1, 8, term.shape[1]), axis=0)
+
+
+def middle_kernel(
+    x,
+    ctx,
+    cot,
+    w_out,
+    w_up_ref,
+    w_down_ref,
+    vec,
+    up_bias,
+    out_c,
+    out_x,
+    dres,
+    dctx_c,
+    dctx_x,
+    g_down,
+    g_up,
+    g_out,
+    sums_out,
+    act,
+    dhid,
+    slope,
+    first_b,
+    dres_two_b,
+    dres_one_b,
+    norm_one,
+    inverse_one,
+    work,
+    outs,
+    dctx,
+    sums,
+    sems,
+    w_up,
+    w_down,
+    load_sems,
+):
+    step = pl.program_id(0)
+    load_up = pltpu.make_async_copy(w_up_ref, w_up, load_sems.at[0])
+    load_down = pltpu.make_async_copy(w_down_ref, w_down, load_sems.at[1])
+    width = w_up.shape[1]
+    rows_c = out_c.shape[0]
+    tiles = x.shape[0] // TILE
+    out_bias, gain_one, shift_one = vec[0:1], vec[1:2], vec[2:3]
+    down_bias, gain_two, shift_two = vec[3:4], vec[4:5], vec[5:6]
+    split = rows_c - TILE
+    moves = [
+        [
+            (outs.at[pl.ds(0, TILE)], out_c.at[pl.ds(0, TILE)]),
+            (dctx.at[pl.ds(0, TILE)], dctx_c.at[pl.ds(0, TILE)]),
+        ],
+        [
+            (outs.at[pl.ds(TILE, split)], out_c.at[pl.ds(TILE, split)]),
+            (dctx.at[pl.ds(TILE, split)], dctx_c.at[pl.ds(TILE, split)]),
+            (outs.at[pl.ds(rows_c, 2 * QP)], out_x),
+            (dctx.at[pl.ds(rows_c, 2 * QP)], dctx_x),
+        ],
+    ]
+    count = 0
+    for group in moves:
+        for i, (src, dst) in enumerate(group):
+            group[i] = pltpu.make_async_copy(src, dst, sems.at[count])
+            count += 1
+
+    def mean(value):
+        return jnp.mean(value, axis=-1, keepdims=True)
+
+    @pl.when(step == 0)
+    def _():
+        load_up.start()
+        load_down.start()
+        sums[...] = jnp.zeros_like(sums)
+
+    @pl.when(step < tiles)
+    def _():
+        base = pl.multiple_of(step * TILE, 64)
+        rows = pl.ds(base, TILE)
+        work[...] = dot_nn(ctx[rows], w_out[...])
+
+        value = x[rows].astype(jnp.float32) + work[...] + out_bias
+        centred = value - mean(value)
+        inverse = lax.rsqrt(mean(centred * centred) + 1e-05)
+        normed = centred * inverse
+        norm_one[...] = normed
+        inverse_one[...] = jnp.broadcast_to(inverse, (TILE, LANES))
+        first_b[rows] = (normed * gain_one + shift_one).astype(jnp.bfloat16)
+
+        @pl.when(step == 0)
+        def _():
+            load_up.wait()
+
+        parts = 12
+        block = width // parts
+
+        def lift(c):
+            cols = slice(block * c, block * c + block)
+            slope[:, cols] = dot_nn(first_b[rows], w_up[:, cols])
+
+        lift(0)
+        for c in range(parts):
+            cols = slice(block * c, block * c + block)
+            if c + 1 < parts:
+                lift(c + 1)
+            active, gradient = gelu_parts(slope[:, cols] + up_bias[0:1, cols])
+            act[rows, cols] = active.astype(jnp.bfloat16)
+            slope[:, cols] = gradient
+
+        @pl.when(step == 0)
+        def _():
+            load_down.wait()
+
+        work[...] = dot_nn(act[rows], w_down[...])
+
+        value = norm_one[...] * gain_one + shift_one + work[...] + down_bias
+        centred = value - mean(value)
+        inverse = lax.rsqrt(mean(centred * centred) + 1e-05)
+        normed = centred * inverse
+        outs[rows] = normed * gain_two + shift_two
+        upstream = cot[rows].astype(jnp.float32)
+        scaled = upstream * gain_two
+        grad = inverse * (scaled - mean(scaled) - normed * mean(scaled * normed))
+        work[...] = grad
+        dres_two_b[rows] = grad.astype(jnp.bfloat16)
+        for k, term in enumerate((upstream * normed, upstream, grad)):
+            sums[8 * k : 8 * k + 8, 0:D] += fold_rows(term)
+
+        block = width // 12
+        for c in range(12):
+            cols = slice(block * c, block * c + block)
+            dact = dot_nt(dres_two_b[rows], w_down[cols]).astype(jnp.bfloat16)
+            grad = dact.astype(jnp.float32) * slope[:, cols]
+            grad_b = grad.astype(jnp.bfloat16)
+            dhid[rows, cols] = grad_b
+            sums[48:56, cols] += jnp.sum(
+                grad_b.astype(jnp.float32).reshape(TILE // 8, 8, block), axis=0
+            )
+        work[...] += dot_nt(dhid[rows], w_up[...])
+
+        normed = norm_one[...]
+        inverse = inverse_one[:, 0:1]
+        upstream = work[...]
+        scaled = upstream * gain_one
+        grad = inverse * (scaled - mean(scaled) - normed * mean(scaled * normed))
+        dres[...] = grad
+        dres_one_b[rows] = grad.astype(jnp.bfloat16)
+        for k, term in enumerate((upstream * normed, upstream, grad)):
+            sums[24 + 8 * k : 32 + 8 * k, 0:D] += fold_rows(term)
+
+        dctx[rows] = dot_nt(dres_one_b[rows], w_out[...]).astype(jnp.bfloat16)
+
+    for tile in range(2):
+
+        @pl.when(step == tile)
+        def _():
+            for copy in moves[tile]:
+                copy.start()
+
+    quarter = width // 4
+    for c in range(4):
+        cols = slice(quarter * c, quarter * c + quarter)
+
+        @pl.when(step == tiles + c)
+        def _():
+            g_down[...] = dot_tn(act[:, cols], dres_two_b[...]).astype(jnp.bfloat16)
+
+        @pl.when(step == tiles + 4 + c)
+        def _():
+            g_up[...] = dot_tn(first_b[...], dhid[:, cols]).astype(jnp.bfloat16)
+
+    @pl.when(step == tiles + 8)
+    def _():
+        g_out[...] = dot_tn(ctx[...], dres_one_b[...]).astype(jnp.bfloat16)
+        for k in range(7):
+            sums_out[k : k + 1] = jnp.sum(sums[8 * k : 8 * k + 8], axis=0, keepdims=True)
+        sums_out[7:8] = jnp.zeros_like(sums_out[7:8])
+        for group in moves:
+            for copy in group:
+                copy.wait()
+
+
+def middle(x, ctx, cot, w_out, w_up, w_down, vec, up_bias):
+    rows = x.shape[0]
+    rows_c = MICRO * TD
+    width = w_up.shape[1]
+    tiles = rows // TILE
+    quarter = width // 4
+    def once(array):
+        return pl.BlockSpec(array.shape, lambda s: (0, 0), pipeline_mode=pl.Buffered(1))
+
+    bf, f32 = jnp.bfloat16, jnp.float32
+    return pl.pallas_call(
+        middle_kernel,
+        name="middle",
+        grid=(tiles + GRAD_STEPS,),
+        in_specs=[
+            once(x),
+            once(ctx),
+            once(cot),
+            once(w_out),
+            ANY_SPEC,
+            ANY_SPEC,
+            once(vec),
+            once(up_bias),
+        ],
+        out_specs=[
+            ANY_SPEC,
+            ANY_SPEC,
+            pl.BlockSpec((TILE, D), lambda s: (jnp.minimum(s, tiles - 1), 0)),
+            ANY_SPEC,
+            ANY_SPEC,
+            pl.BlockSpec((quarter, D), lambda s: (jnp.clip(s - tiles, 0, 3), 0)),
+            pl.BlockSpec((D, quarter), lambda s: (0, jnp.clip(s - tiles - 4, 0, 3))),
+            pl.BlockSpec((D, D), lambda s: (0, 0)),
+            pl.BlockSpec((8, width), lambda s: (0, 0)),
+        ],
+        out_shape=[
+            jax.ShapeDtypeStruct((rows_c, D), f32),
+            jax.ShapeDtypeStruct((rows - rows_c, D), f32),
+            jax.ShapeDtypeStruct((rows, D), f32),
+            jax.ShapeDtypeStruct((rows_c, D), bf),
+            jax.ShapeDtypeStruct((rows - rows_c, D), bf),
+            jax.ShapeDtypeStruct((width, D), bf),
+            jax.ShapeDtypeStruct((D, width), bf),
+            jax.ShapeDtypeStruct((D, D), bf),
+            jax.ShapeDtypeStruct((8, width), f32),
+        ],
+        scratch_shapes=[
+            pltpu.VMEM((rows, width), bf),
+            pltpu.VMEM((rows, width), bf),
+            pltpu.VMEM((TILE, width), f32),
+            pltpu.VMEM((rows, D), bf),
+            pltpu.VMEM((rows, D), bf),
+            pltpu.VMEM((rows, D), bf),
+            pltpu.VMEM((TILE, D), f32),
+            pltpu.VMEM((TILE, LANES), f32),
+            pltpu.VMEM((TILE, D), f32),
+            pltpu.VMEM((rows, D), f32),
+            pltpu.VMEM((rows, D), bf),
+            pltpu.VMEM((56, width), f32),
+            pltpu.SemaphoreType.DMA((6,)),
+            pltpu.VMEM(w_up.shape, bf),
+            pltpu.VMEM(w_down.shape, bf),
+            pltpu.SemaphoreType.DMA((2,)),
+        ],
+        compiler_params=pltpu.CompilerParams(vmem_limit_bytes=60 * 1024 * 1024),
+        cost_estimate=pl.CostEstimate(
+            flops=2 * rows * D * (6 * width + 3 * D),
+            bytes_accessed=40 * 1024 * 1024,
+            transcendentals=2 * rows * width,
+        ),
+    )(x, ctx, cot, w_out, w_up, w_down, vec, up_bias)
+
+
+SMALL_ROWS = 32
+
+
+def table_rows(hist, buckets_of, side):
+    lane = lax.broadcasted_iota(jnp.int32, (LANES, LANES), 0)
+    target = lax.broadcasted_iota(jnp.int32, (LANES, LANES), 1)
+    signed = jnp.where(lane < 64, lane, lane - 128)
+    distances = (
+        lane,
+        128 + side + 2 * signed,
+        127 + side + 2 * signed,
+        2 * lane + 2 * side - 1,
+        2 * lane,
+    )
+    kinds = [[] for _ in distances]
+    row = lax.broadcasted_iota(jnp.int32, (8, LANES), 0)
+    for pair in range(PAIRS):
+        for head in range(2):
+            block = [
+                sum(hist[m, pair, 32 * head + 8 * k : 32 * head + 8 * k + 8] for m in range(MICRO))
+                for k in range(4)
+            ]
+            picks = (
+                block[0],
+                jnp.where(row % 2 == 0, block[1], 0.0),
+                jnp.where(row % 2 == 0, 0.0, block[1]),
+                block[2],
+                block[3],
+            )
+            for kind, pick in zip(kinds, picks):
+                kind.append(jnp.sum(pick, axis=0, keepdims=True))
+    pad = [jnp.zeros((16 - 2 * PAIRS, LANES), jnp.float32)]
+    close = jnp.zeros((16, LANES), jnp.float32)
+    for kind, distance in zip(kinds, distances):
+        hot = jnp.where((distance == target) & (target < LANES - 1), 1.0, 0.0)
+        close = close + jnp.dot(
+            jnp.concatenate(kind + pad, axis=0),
+            hot,
+            precision=PRECISE,
+            preferred_element_type=jnp.float32,
+        )
+    last = lax.broadcasted_iota(jnp.int32, (16, LANES), 1) == LANES - 1
+    close = jnp.where(last, -jnp.sum(close, axis=1, keepdims=True), close)
+    bucket_hot = jnp.where(lane == buckets_of[0:1], 1.0, 0.0)
+    return lax.dot_general(
+        close,
+        bucket_hot,
+        (((1,), (1,)), ((), ())),
+        precision=PRECISE,
+        preferred_element_type=jnp.float32,
+    )
+
+
+def finish_kernel(
+    dq_c,
+    dq_x,
+    dk,
+    dv,
+    keys_x,
+    x_c,
+    x_q,
+    w_qkv,
+    dres,
+    hist,
+    buckets_of,
+    sums,
+    w_share,
+    small_out,
+    grad_c,
+    grad_q,
+    *scratch,
+):
+    w_buf = scratch[:10]
+    (
+        grads,
+        prompts,
+        theirs,
+        along,
+        nears,
+        near_got,
+        owns,
+        out_c,
+        small,
+        x_s,
+        x_r,
+        sm_s,
+        sm_r,
+        sem,
+    ) = scratch[10:]
+    net = Net()
+    net.greet()
+    weights = reduce_stages(net, grads, w_share, w_buf)
+    copies = Copies(x_s, x_r)
+    to_mate = [
+        copies.to(net.to_mate, prompts.at[:, :, 1 - net.c], theirs),
+        copies.to(net.to_mate, nears, near_got),
+    ]
+    third = [
+        copies.to(net.to_z[k], prompts.at[:, net.z_of[k], net.c], along.at[k]) for k in range(3)
+    ]
+    hops = Copies(sm_s, sm_r)
+    partners = [net.to_mate, net.to_x, net.to_y, net.to_z[0], net.to_z[1]]
+    butterfly = [
+        hops.to(partner, small.at[i], small.at[i + 1]) for i, partner in enumerate(partners)
+    ]
+
+    def hop(i):
+        butterfly[i].wait_recv()
+        small[i + 1] = small[i + 1] + small[i]
+        if i + 1 < len(butterfly):
+            butterfly[i + 1].start()
+
+    n_keys = dk.shape[0] // MICRO
+    n_prompt = n_keys - 2 * CH
+
+    for m in range(MICRO):
+        for part in range(n_prompt // 512):
+            rows = slice(m * n_keys + 512 * part, m * n_keys + 512 * part + 512)
+            value = dot_nt(dk[rows], w_qkv[:, D : 2 * D]) + dot_nt(dv[rows], w_qkv[:, 2 * D :])
+            for i in range(4):
+                owner = 4 * part + i
+                prompts[m, owner // 2, owner % 2] = value[128 * i : 128 * i + 128].astype(
+                    jnp.bfloat16
+                )
+        rows = slice(m * n_keys + n_prompt, (m + 1) * n_keys)
+        value = dot_nt(dk[rows], w_qkv[:, D : 2 * D]) + dot_nt(dv[rows], w_qkv[:, 2 * D :])
+        for i in range(2):
+            nears[m, i] = value[256 * i : 256 * i + 128].astype(jnp.bfloat16)
+            owns[m, i] = value[256 * i + 128 : 256 * i + 256]
+    start(to_mate)
+
+    def put(value, shift):
+        part = D // 32
+        for owner in range(8):
+            for q in range(4):
+                at = (4 * owner + q) * part
+                grads[owner // 2, owner % 2, q, :, shift : shift + D] = value[
+                    at : at + part
+                ].astype(jnp.bfloat16)
+
+    put(dot_tn(keys_x[...], dk[...]), D)
+    put(dot_tn(keys_x[...], dv[...]), 2 * D)
+    put(dot_tn(x_c[...], dq_c[...]) + dot_tn(x_q[...], dq_x[...]), 0)
+    weights[0]()
+
+    small[0] = jnp.zeros_like(small[0])
+    sum_q = jnp.sum(dq_c[...].astype(jnp.float32), axis=0, keepdims=True)
+    sum_q = sum_q + jnp.sum(dq_x[...].astype(jnp.float32), axis=0, keepdims=True)
+    small[0, 0:1] = sum_q
+    small[0, 1:2] = jnp.sum(dv[...].astype(jnp.float32), axis=0, keepdims=True)
+    for i in range(6):
+        small[0, 2 + i : 3 + i] = sums[i : i + 1, 0:D]
+    for i in range(4):
+        small[0, 8 + i : 9 + i] = sums[6:7, D * i : D * i + D]
+    small[0, 16:32, 0:LANES] = table_rows(hist, buckets_of, net.c)
+    butterfly[0].start()
+
+    arrive(to_mate)
+
+    @pl.loop(0, 8)
+    def _(i):
+        m, zi = i // 4, i % 4
+        prompts[m, zi, net.c] = prompts[m, zi, net.c] + theirs[m, zi]
+
+    start(third)
+    weights[1]()
+    hop(0)
+    rows_c = x_c.shape[0]
+    out_c[0:rows_c] = dres[0:rows_c] + dot_nt(dq_c[...], w_qkv[:, 0:D])
+    out_c[rows_c:] = dres[rows_c:] + dot_nt(dq_x[...], w_qkv[:, 0:D])
+    for m in range(MICRO):
+        for i in range(2):
+            rows = slice(m * TD + PD + 128 * i, m * TD + PD + 128 * i + 128)
+            out_c[rows] = out_c[rows] + owns[m, i] + near_got[m, i].astype(jnp.float32)
+    hop(1)
+    weights[2]()
+    hop(2)
+    weights[3]()
+    hop(3)
+    arrive(third)
+    for m in range(MICRO):
+        total = prompts[m, net.z, net.c].astype(jnp.float32)
+        for k in range(3):
+            total = total + along[k, m].astype(jnp.float32)
+        rows = slice(m * TD, m * TD + PD)
+        out_c[rows] = out_c[rows] + total
+    stores = [
+        pltpu.make_async_copy(out_c.at[pl.ds(0, rows_c)], grad_c, sem.at[0]),
+        pltpu.make_async_copy(out_c.at[pl.ds(rows_c, 2 * QP)], grad_q, sem.at[1]),
+    ]
+    start(stores)
+    hop(4)
+    keep = pltpu.make_async_copy(small.at[5], small_out, sem.at[2])
+    keep.start()
+    for i in range(4, 7):
+        weights[i]()
+    for copy in stores + [keep]:
+        copy.wait()
+    copies.finish()
+    hops.finish()
+
+
+def finish(dq_c, dq_x, dk, dv, keys_x, x_c, x_q, w_qkv, dres, hist, buckets_of, sums):
+    whole = pl.BlockSpec(memory_space=pltpu.VMEM)
+    bf, f32 = jnp.bfloat16, jnp.float32
+    rows_c, rows_x = x_c.shape[0], x_q.shape[0]
+    part, width = D // 32, w_qkv.shape[1]
+    return pl.pallas_call(
+        finish_kernel,
+        name="finish",
+        in_specs=[whole] * 12,
+        out_specs=[ANY_SPEC] * 4,
+        out_shape=[
+            jax.ShapeDtypeStruct((4, part, width), bf),
+            jax.ShapeDtypeStruct((SMALL_ROWS, D), f32),
+            jax.ShapeDtypeStruct((rows_c, D), f32),
+            jax.ShapeDtypeStruct((rows_x, D), f32),
+        ],
+        scratch_shapes=reduce_buffers(4 * part, width)
+        + [
+            pltpu.VMEM((4, 2, 4, part, width), bf),
+            pltpu.VMEM((MICRO, 4, 2, PD, D), bf),
+            pltpu.VMEM((MICRO, 4, PD, D), bf),
+            pltpu.VMEM((3, MICRO, PD, D), bf),
+            pltpu.VMEM((MICRO, 2, 128, D), bf),
+            pltpu.VMEM((MICRO, 2, 128, D), bf),
+            pltpu.VMEM((MICRO, 2, 128, D), f32),
+            pltpu.VMEM((rows_c + rows_x, D), f32),
+            pltpu.VMEM((6, SMALL_ROWS, D), f32),
+            pltpu.SemaphoreType.DMA((5,)),
+            pltpu.SemaphoreType.DMA((5,)),
+            pltpu.SemaphoreType.DMA((5,)),
+            pltpu.SemaphoreType.DMA((5,)),
+            pltpu.SemaphoreType.DMA((3,)),
+        ],
+        compiler_params=pltpu.CompilerParams(
+            collective_id=4, has_side_effects=True, vmem_limit_bytes=60 * 1024 * 1024
+        ),
+    )(dq_c, dq_x, dk, dv, keys_x, x_c, x_q, w_qkv, dres, hist, buckets_of, sums)
 
 
 def pad_rows(block):
@@ -1247,43 +1656,25 @@
         up_weight, down_weight, out_weight = (
             entry.reshape(-1, entry.shape[2]) for entry in gathered
         )
+    rows_c = MICRO * TD
     context = jnp.concatenate([ctx_c, ctx_x])
-    first, normed_one, inverse_one = layer_norm(
-        x_all.astype(jnp.float32)
-        + jnp.dot(context, out_weight, preferred_element_type=jnp.float32)
-        + out_bias,
-        gain_one,
-        shift_one,
-    )
-    first_b = first.astype(jnp.bfloat16)
-    hidden = jnp.dot(first_b, up_weight, preferred_element_type=jnp.float32) + up_bias
-    active = jax.nn.gelu(hidden, approximate=False).astype(jnp.bfloat16)
-    final, normed_two, inverse_two = layer_norm(
-        first + jnp.dot(active, down_weight, preferred_element_type=jnp.float32) + down_bias,
-        gain_two,
-        shift_two,
-    )
-    rows_c = MICRO * TD
-    out_content = final[:rows_c].reshape(MICRO, TD, D)
-    out_query = final[rows_c:].reshape(MICRO, QP, D)[:, :extra_rows]
-
-    upstream = jnp.concatenate(
-        [cot_content.reshape(rows_c, D), pad_rows(cot_query)]
-    ).astype(jnp.float32)
-    dres_two, dgain_two, dshift_two = norm_back(upstream, normed_two, inverse_two, gain_two)
-    dbias_down = jnp.sum(dres_two, axis=0)
-    dres_two_b = dres_two.astype(jnp.bfloat16)
-    dweight_down = dot_tn(active, dres_two_b)
-    dactive = dot_nt(dres_two_b, down_weight).astype(jnp.bfloat16)
-    dhidden = (dactive.astype(jnp.float32) * gelu_slope(hidden)).astype(jnp.bfloat16)
-    dbias_up = jnp.sum(dhidden.astype(jnp.float32), axis=0)
-    dweight_up = dot_tn(first_b, dhidden)
-    dfirst = dres_two + dot_nt(dhidden, up_weight)
-    dres_one, dgain_one, dshift_one = norm_back(dfirst, normed_one, inverse_one, gain_one)
-    dbias_out = jnp.sum(dres_one, axis=0)
-    dres_one_b = dres_one.astype(jnp.bfloat16)
-    dweight_out = dot_tn(context, dres_one_b)
-    dcontext = dot_nt(dres_one_b, out_weight).astype(jnp.bfloat16)
+    upstream = jnp.concatenate([cot_content.reshape(rows_c, D), pad_rows(cot_query)])
+    vec = jnp.stack([out_bias, gain_one, shift_one, down_bias, gain_two, shift_two])
+    (
+        out_content,
+        out_query,
+        dres_one,
+        dctx_c,
+        dctx_x,
+        dweight_down,
+        dweight_up,
+        dweight_out,
+        sums,
+    ) = middle(
+        x_all, context, upstream, out_weight, up_weight, down_weight, vec, up_bias[None]
+    )
+    out_content = out_content.reshape(MICRO, TD, D)
+    out_query = out_query.reshape(MICRO, QP, D)[:, :extra_rows]
 
     def by_quarter(grad):
         grad = grad.astype(jnp.bfloat16)
@@ -1301,59 +1692,77 @@
         xcol,
         xrow,
         lse,
-        dcontext[:rows_c],
-        dcontext[rows_c:],
+        dctx_c,
+        dctx_x,
         full_c,
         full_x,
         to_reduce,
     )
-    dkv_rows = jnp.concatenate([dk_rows, dv_rows], axis=1)
-    dq_all = jnp.concatenate([dq_c, dq_x])
-    dweight_query = dot_tn(x_all, dq_all)
-    dbias_query = jnp.sum(dq_all.astype(jnp.float32), axis=0)
-    dweight_kv = dot_tn(keys_x, dkv_rows)
-    dbias_value = jnp.sum(dv_rows.astype(jnp.float32), axis=0)
-    dkeys_x = dot_nt(dkv_rows, kv_weight).reshape(MICRO, n_keys, D)
-    dtable = table_gradient(hist, rel_bucket, bias_table.shape[0], side, heads)
-    small = jnp.concatenate(
-        [
-            entry.reshape(devices, -1)
-            for entry in (
-                dbias_query,
-                dbias_value,
-                dbias_out,
-                dbias_down,
-                dgain_one,
-                dshift_one,
-                dgain_two,
-                dshift_two,
-                dbias_up,
-                dtable,
-            )
-        ],
-        axis=1,
-    ).astype(jnp.bfloat16)
-    dprompts = dkeys_x[:, : 2 * plength].astype(jnp.bfloat16)
-    dcont = dkeys_x[:, 2 * plength :].reshape(MICRO, 2, 2, 128, D)
-    dnear = dcont[:, :, 0].astype(jnp.bfloat16)
-    dweight_qkv = jnp.concatenate(
-        [dweight_query.astype(jnp.bfloat16), dweight_kv.astype(jnp.bfloat16)], axis=1
-    )
-    small_size = small.shape[1]
     if own_links:
-        small = jnp.pad(small, ((0, 0), (0, 32 * 256 - small_size)))
-        t_qkv, t_small, from_prompts, from_near = reduce_last(
-            by_quarter(dweight_qkv),
-            small.reshape(4, 2, 4, 8, 256),
-            dprompts.reshape(MICRO, 4, 2, PD, D),
-            dnear,
+        t_qkv, small, grad_content, grad_query = finish(
+            dq_c,
+            dq_x,
+            dk_rows,
+            dv_rows,
+            keys_x,
+            tokens_x,
+            extra_x,
+            qkv_weight,
+            dres_one,
+            hist,
+            jnp.broadcast_to(rel_bucket[None], (8, LANES)),
+            sums,
         )
+        grad_content = grad_content.reshape(MICRO, TD, D)
+        grad_query = grad_query.reshape(MICRO, QP, D)[:, :extra_rows]
         t_up, t_down, t_out = reduced
-        shares = (t_down, t_up, t_out, t_qkv, t_small)
-        totals = [
+        shares = (t_down, t_up, t_out, t_qkv)
+        t_down, t_up, t_out, t_qkv = [
             entry.reshape(-1, entry.shape[-1]).astype(jnp.float32) for entry in shares
         ]
+        pieces = lax.dynamic_slice_in_dim(small[:8], own_rank * shard, shard, 1)
+        t_bup = lax.dynamic_index_in_dim(
+            small[8:12].reshape(devices, up_size), own_rank, 0, keepdims=False
+        )
+        t_table = lax.dynamic_slice_in_dim(
+            small[16 : 16 + heads, : bias_table.shape[0]],
+            own_rank * (bias_table.shape[0] // devices),
+            bias_table.shape[0] // devices,
+            1,
+        ).T
     else:
+        dgain_two, dshift_two, dbias_down, dgain_one, dshift_one, dbias_out = sums[:6, :D]
+        dbias_up = sums[6]
+        dkv_rows = jnp.concatenate([dk_rows, dv_rows], axis=1)
+        dq_all = jnp.concatenate([dq_c, dq_x])
+        dbias_query = jnp.sum(dq_all.astype(jnp.float32), axis=0)
+        dbias_value = jnp.sum(dv_rows.astype(jnp.float32), axis=0)
+        dkeys_x = dot_nt(dkv_rows, kv_weight).reshape(MICRO, n_keys, D)
+        dtable = table_gradient(hist, rel_bucket, bias_table.shape[0], side, heads)
+        small = jnp.concatenate(
+            [
+                entry.reshape(devices, -1)
+                for entry in (
+                    dbias_query,
+                    dbias_value,
+                    dgain_two,
+                    dshift_two,
+                    dbias_down,
+                    dgain_one,
+                    dshift_one,
+                    dbias_out,
+                    dbias_up,
+                    dtable,
+                )
+            ],
+            axis=1,
+        ).astype(jnp.bfloat16)
+        dprompts = dkeys_x[:, : 2 * plength].astype(jnp.bfloat16)
+        dcont = dkeys_x[:, 2 * plength :].reshape(MICRO, 2, 2, 128, D)
+        dnear = dcont[:, :, 0].astype(jnp.bfloat16)
+        dweight_qkv = jnp.concatenate(
+            [dot_tn(x_all, dq_all), dot_tn(keys_x, dkv_rows)], axis=1
+        )
 
         def scatter(piece, dimension=0):
             return lax.psum_scatter(
@@ -1366,18 +1775,20 @@
             scatter(piece)
             for piece in (dweight_down, dweight_up, dweight_out, dweight_qkv, small)
         ]
-        totals = [lax.psum(entry, "grp").astype(jnp.float32) for entry in shares]
-    dcont = (dcont[:, :, 1] + from_near.astype(jnp.float32)).reshape(MICRO, CH, D)
-    dx_all = dres_one + dot_nt(dq_all, query_weight)
-    grad_content = dx_all[:rows_c].reshape(MICRO, TD, D) + jnp.concatenate(
-        [from_prompts, dcont], axis=1
-    )
-    grad_query = dx_all[rows_c:].reshape(MICRO, QP, D)[:, :extra_rows]
-    t_down, t_up, t_out, t_qkv, t_small = totals
-    t_small = t_small.reshape(-1)[:small_size]
-    pieces = [t_small[shard * i : shard * i + shard] for i in range(8)]
-    up_at = 8 * shard
-    t_table = t_small[up_at + up_size :].reshape(-1, heads)
+        t_down, t_up, t_out, t_qkv, t_small = [
+            lax.psum(entry, "grp").astype(jnp.float32) for entry in shares
+        ]
+        dcont = (dcont[:, :, 1] + from_near.astype(jnp.float32)).reshape(MICRO, CH, D)
+        dx_all = dres_one + dot_nt(dq_all, query_weight)
+        grad_content = dx_all[:rows_c].reshape(MICRO, TD, D) + jnp.concatenate(
+            [from_prompts, dcont], axis=1
+        )
+        grad_query = dx_all[rows_c:].reshape(MICRO, QP, D)[:, :extra_rows]
+        t_small = t_small.reshape(-1)
+        pieces = [t_small[shard * i : shard * i + shard] for i in range(8)]
+        up_at = 8 * shard
+        t_bup = t_small[up_at : up_at + up_size]
+        t_table = t_small[up_at + up_size :].reshape(-1, heads)
     return (
         out_content,
         out_query,
@@ -1389,15 +1800,15 @@
         t_qkv[:, 2 * D :],
         pieces[1],
         t_out,
+        pieces[7],
+        pieces[5],
+        pieces[6],
+        t_up,
+        t_bup,
+        t_down,
+        pieces[4],
         pieces[2],
-        pieces[4],
-        pieces[5],
-        t_up,
-        t_small[up_at : up_at + up_size],
-        t_down,
         pieces[3],
-        pieces[6],
-        pieces[7],
         t_table,
     )
 

time: 451 us -> 418 us (0.927)
  matrix products: 123 us -> 15.4 us
  Pallas kernels: 259 us -> 357 us
  local copies, waits for them, and re-layouts: 34.1 us -> 22.5 us
  other arithmetic: 24.3 us -> 14.1 us
    dot_general x15 -> x0, matrix products: 108 us -> none  [the longest x1 33.4 us: on_device(): jnp.dot(first_b, up_weight, preferred_element_type=jnp.float32) + up_bias]
    pallas_call x1 -> x2, Pallas kernels: 63.2 us -> 161 us  [the longest x1 88 us: finish(): pl.pallas_call(finish_kernel, name='finish', in_specs=[whole] * 12, out_s...]
    reduce_sum x16 -> x0, other arithmetic: 11.3 us -> none  [the longest x1 2.68 us: on_device(): dbias_down = jnp.sum(dres_two, axis=0)]
    slice x17 -> x5, local copies, waits for them, and re-layouts: 9.31 us -> 3.68 us  [the longest x1 0.75 us: on_device(): grad_query = grad_query.reshape(MICRO, QP, D)[:, :extra_rows]]
where the time goes in v4:
time: 418 us; the launch traced here: 410 us
  Pallas kernels  357 us (85%)
  local copies, waits for them, and re-layouts  22.5 us (5%)
  matrix products  15.4 us (4%)
  other arithmetic  14.1 us (3%)
    pallas_call x1, Pallas kernels, finish(): pl.pallas_call(finish_kernel, name='finish', in_specs=[whole] * 12, out_s...  88 us
    pallas_call x1, Pallas kernels, attend_back(): pl.pallas_call(functools.partial(attend_back_kernel, plength, carried), n...  81.3 us
    pallas_call x1, Pallas kernels, middle(): pl.pallas_call(middle_kernel, name='middle', grid=(tiles + GRAD_STEPS,),...  73.2 us
    pallas_call x1, Pallas kernels, attend(): pl.pallas_call(functools.partial(attend_kernel, plength, carried), name='...  57.9 us
    pallas_call x1, Pallas kernels, gather_first(): pl.pallas_call(gather_first_kernel, name='gather_first', in_specs=[ANY_SP...  56.7 us
    dot_general x1, matrix products, on_device(): jnp.dot(keys_x, kv_weight, preferred_element_type=jnp.float32) + kv_bias  12.8 us

profile of v4, /device:TPU:0, one launch (start us, length us, event | category | flops | bytes accessed | tf_op | source)
XLA Modules:
  0.0 410.3 jit_solution(1869411967279762668)
XLA Ops:
  0.7 0.0 copy-start
  0.7 0.8 and_select_fusion.1
  1.5 0.7 and_select_fusion
  2.2 0.1 add_add_fusion
  2.3 0.6 fusion.4
  2.9 0.8 copy.67.refs_6_
  3.7 1.3 select_reduce_fusion.refs_0_
  5.0 1.8 pad_maximum_fusion.3
  6.8 6.1 %concatenate.25 = bf16[1152]{0:T(1024)(128)(2,1)S(1)} concatenate(bf16[96]{0:T(256)(128)(2,1)} %param.29, bf16[96]{0:T(256)(128)(2,1)} %param.32, bf16[96]{0:T(256)(128)(2,1)} %param.34, bf16[96]{0:T(256)(128)(2,1)} %param.40, bf16[96]{0:T(256)(128)(2,1)} %param.35, bf16[96]{0:T(256)(128)(2,1)} %param.36, bf16[96]{0:T(256)(128)(2,1)} %param.41, bf16[96]{0:T(256)(128)(2,1)} %param.42, ...), dimensions={0} | concatenate | bytes 4608 | tf_op jit(solution)/shard_map/concatenate | solution.py:1576
  13.0 0.6 reshape.236.v_ref
  13.6 56.7 %gather_first.1 = (bf16[32,24,2304]{2,1,0:T(8,128)(2,1)}, bf16[32,8,256]{2,1,0:T(8,128)(2,1)}, bf16[2,1536,768]{2,1,0:T(8,128)(2,1)}) custom-call(bf16[4,24,2304]{2,1,0:T(8,128)(2,1)} %bitcast.85, bf16[4,8,256]{2,1,0:T(8,128)(2,1)} %reshape.236.v_ref, bf16[2,384,768]{2,1,0:T(8,128)(2,1)} %x_ref.1), custom_call_target="tpu_custom_call" | custom-call | tf_op jit(solution)/shard_map/gather_first/pallas_call | solution.py:368
  70.3 1.0 reshape.238
  71.2 0.1 fusion.3
  71.3 0.1 reshape.257
  71.4 0.0 copy-start.2
  71.4 2.6 add_convert_fusion.1
  74.0 1.1 slice.124.refs_1_
  75.1 0.7 slice.125.refs_2_
  75.8 0.1 convert_element_type.136
  75.9 0.0 copy-start.12
  75.9 12.8 %add_convert_fusion.refs_3_.refs_4_ = bf16[3072,1536]{1,0:T(8,128)(2,1)} fusion(bf16[3072,768]{1,0:T(8,128)(2,1)} %bitcast.76, f32[1536]{0:T(1024)S(1)} %pad_convert_fusion, bf16[768,2304]{1,0:T(8,128)(2,1)} %bitcast.79), kind=kOutput, calls=%fused_computation.1 | convolution fusion | flops 7257194496 | bytes 16521216 | tf_op jit(solution)/shard_map/dot_general | solution.py:1644
  88.7 0.1 copy.61
  88.9 0.6 gather_fusion
  89.5 0.1 copy.62
  89.6 0.2 slice_reduce_fusion
  89.8 0.1 broadcast_subtract_fusion
  89.8 0.6 pad.27.refs_5_
  90.5 57.9 %attend.1 = (bf16[768,768]{1,0:T(8,128)(2,1)}, bf16[128,768]{1,0:T(8,128)(2,1)}, f32[768,768]{1,0:T(8,128)}, f32[128,768]{1,0:T(8,128)}, f32[2,6,8,128]{3,2,1,0:...) custom-call(s32[2]{0:T(128)} %select_reduce_fusion.refs_0_, ...), custom_call_target="tpu_custom_call" | custom-call | flops 5234491392 | bytes 16777216 | tf_op jit(solution)/shard_map/attend/pallas_call | solution.py:569
  148.4 0.0 copy-start.9
  148.4 0.0 copy-start.3
  148.5 3.2 pad_maximum_fusion
  151.7 0.1 convert_element_type.139
  151.7 0.1 convert_element_type.140
  151.8 0.1 convert_element_type.141
  151.9 0.1 convert_element_type.142
  152.0 0.1 convert_element_type.143
  152.1 0.1 convert_element_type.144
  152.2 0.1 stack.31
  152.2 0.6 stack.32.vec
  152.8 0.6 copy.70
  153.4 0.0 copy-done.9
  153.5 0.0 copy-done.3
  153.5 1.2 pad_maximum_fusion.2.cot
  154.7 73.2 %middle.1 = (f32[768,768]{1,0:T(8,128)}, f32[128,768]{1,0:T(8,128)}, f32[896,768]{1,0:T(8,128)}, bf16[768,768]{1,0:T(8,128)(2,1)}, bf16[128,768]{1,0:T(8,128)(2,...) custom-call(bf16[896,768]{1,0:T(8,128)(2,1)} %get-tuple-element.169.x,, ...), custom_call_target="tpu_custom_call" | custom-call | flops 28538044416 | bytes 41943040 | tf_op jit(solution)/shard_map/middle/pallas_call | solution.py:1192
  227.9 81.3 %attend_back.1 = (bf16[768,768]{1,0:T(8,128)(2,1)}, bf16[128,768]{1,0:T(8,128)(2,1)}, bf16[3072,768]{1,0:T(8,128)(2,1)}, bf16[3072,768]{1,0:T(8,128)(2,1)}, f32[...) custom-call(s32[2]{0:T(128)} %select_reduce_fusion.refs_0_, ...), custom_call_target="tpu_custom_call" | custom-call | flops 13086228480 | bytes 33554432 | tf_op jit(solution)/shard_map/attend_back/pallas_call | solution.py:891
  309.1 0.6 broadcast_in_dim.35.buckets_of
  309.7 88.0 %finish.1 = (bf16[4,24,2304]{2,1,0:T(8,128)(2,1)}, f32[32,768]{1,0:T(8,128)}, f32[768,768]{1,0:T(8,128)}, f32[128,768]{1,0:T(8,128)}) custom-call(bf16[768,768]{1,0:T(8,128)(2,1)} %get-tuple-element.70.dq_c, bf16[128,768]{1,0:T(8,128)(2,1)} %get-tuple-element.71.dq_x, bf16[3072,768]{1,0:T(8,128)(2,1)} %get-tuple-element.72.dk, ...), custom_call_target="tpu_custom_call" | custom-call | tf_op jit(solution)/shard_map/finish/pallas_call | solution.py:1462
  397.8 0.0 copy-start.7
  397.8 1.2 bitcast_convert_fusion.2
  398.9 0.9 fusion.2
  399.9 0.8 slice.137
  400.6 0.7 slice.107
  401.4 0.1 constant_dynamic-slice_fusion
  401.4 0.5 slice_bitcast_fusion
  402.0 0.7 slice.115
  402.7 0.6 dynamic-slice_reduce_fusion
  403.3 0.7 slice.119
  404.0 0.1 dynamic-slice_bitcast_fusion
  404.1 0.7 copy.69
  404.8 1.1 bitcast_convert_fusion
  405.9 1.2 bitcast_convert_fusion.1
  407.1 0.7 bitcast_convert_fusion.3
  407.8 0.8 slice.136
  408.6 1.4 copy.72
  (28 shorter events, 0.1 us)
Async XLA Ops:
  0.7 70.8 %copy-start = (bf16[2,384,768]{2,1,0:T(8,128)(2,1)S(1)}, bf16[2,384,768]{2,1,0:T(8,128)(2,1)}, u32[]{:S(2)}) copy-start(bf16[2,384,768]{2,1,0:T(8,128)(2,1)} %x_ref.1) | copy-start | bytes 3538948
  0.7 70.7 %copy-start.8 = (bf16[2,56,768]{2,1,0:T(8,128)(2,1)S(1)}, bf16[2,56,768]{2,1,0:T(8,128)(2,1)}, u32[]{:S(2)}) copy-start(bf16[2,56,768]{2,1,0:T(8,128)(2,1)} %param.24) | copy-start | bytes 516100
  71.4 77.0 %copy-start.2 = (bf16[2,64,768]{2,1,0:T(8,128)(2,1)}, bf16[2,64,768]{2,1,0:T(8,128)(2,1)S(1)}, u32[]{:S(2)}) copy-start(bf16[2,64,768]{2,1,0:T(8,128)(2,1)S(1)} %pad.25) | copy-start | bytes 589828
  75.9 12.8 %copy-start.11 = (bf16[32,12]{0,1:T(8,128)(2,1)S(1)}, bf16[32,12]{0,1:T(8,128)(2,1)}, u32[]{:S(2)}) copy-start(bf16[32,12]{0,1:T(8,128)(2,1)} %param.43) | copy-start | bytes 2308
  75.9 12.9 %copy-start.12 = (s32[128]{0:T(128)S(1)}, s32[128]{0:T(128)}, u32[]{:S(2)}) copy-start(s32[128]{0:T(128)} %param.27) | copy-start | bytes 1540
  148.4 5.0 %copy-start.9 = (bf16[2,56,768]{2,1,0:T(8,128)(2,1)S(1)}, bf16[2,56,768]{2,1,0:T(8,128)(2,1)}, u32[]{:S(2)}) copy-start(bf16[2,56,768]{2,1,0:T(8,128)(2,1)} %param.45) | copy-start | bytes 516100
  148.4 5.0 %copy-start.3 = (bf16[2,384,768]{2,1,0:T(8,128)(2,1)S(1)}, bf16[2,384,768]{2,1,0:T(8,128)(2,1)}, u32[]{:S(2)}) copy-start(bf16[2,384,768]{2,1,0:T(8,128)(2,1)} %param.44) | copy-start | bytes 3538948
  397.8 2.1 copy-start.7
  397.8 7.0 %copy-start.5 = (bf16[4,96,768]{2,1,0:T(8,128)(2,1)S(1)}, bf16[4,96,768]{2,1,0:T(8,128)(2,1)}, u32[]{:S(2)}) copy-start(bf16[4,96,768]{2,1,0:T(8,128)(2,1)} %get-tuple-element.83) | copy-start | bytes 1769476
  398.9 7.0 %copy-start.4 = (bf16[4,24,3072]{2,1,0:T(8,128)(2,1)S(1)}, bf16[4,24,3072]{2,1,0:T(8,128)(2,1)}, u32[]{:S(2)}) copy-start(bf16[4,24,3072]{2,1,0:T(8,128)(2,1)} %get-tuple-element.82) | copy-start | bytes 1769476
  404.0 4.5 %copy-start.1 = (f32[768,768]{1,0:T(8,128)S(1)}, f32[768,768]{1,0:T(8,128)}, u32[]{:S(2)}) copy-start(f32[768,768]{1,0:T(8,128)} %get-tuple-element.77) | copy-start | bytes 7077892
  404.8 2.3 copy-start.10
  404.8 3.0 copy-start.6

commit v5 on v4

--- a/solution.py
+++ b/solution.py
@@ -153,7 +153,9 @@
 
     local = pltpu.make_async_copy(shard, full.at[whole(net.f)], local_sem)
     mine = shard.at[net.g]
-    along_z = [copies.to(device, mine, full.at[rows(net.f, net.g)]) for device in net.to_z]
+    along_z = [copies.to(device, mine, full.at[rows(net.f, net.g)]) for device in net.to_z[:2]]
+    passed = full.at[rows(net.f_of[1], net.g)]
+    relay = copies.to(net.to_z[0], passed, passed)
     to_mate = [copies.to(net.to_mate, shard, full.at[whole(net.f)])]
     to_x, to_y, on_x, on_y, later = [], [], [], [], []
     for owner in net.f_of:
@@ -172,8 +174,12 @@
         start(along_z)
         start(to_mate)
 
+    def onward():
+        along_z[1].wait_recv()
+        relay.start()
+
     def plane():
-        arrive(along_z)
+        arrive([along_z[0], relay])
         start(to_x + to_y)
 
     def corners():
@@ -187,10 +193,9 @@
     def end():
         arrive(to_mate + later)
         local.wait()
-        for copy in along_z + to_mate + to_x + to_y + on_x + on_y + later:
-            copy.wait_send()
-
-    return [begin, plane, corners, mates, end]
+        copies.finish()
+
+    return [begin, onward, plane, corners, mates, end]
 
 
 REDUCE_COPIES = 19
@@ -232,11 +237,10 @@
         copies.to(net.to_x, side_b.at[:, 1 - net.x], line.at[1]),
     ]
     third = []
-    for k in range(3):
-        for h in range(2):
-            third.append(
-                copies.to(net.to_z[k], line.at[h, net.z_of[k]], along.at[h, k])
-            )
+    for h in range(2):
+        third.append(copies.to(net.to_z[0], line.at[h, net.z_of[2]], along.at[h, 0]))
+        third.append(copies.to(net.to_z[0], line.at[h, net.z_of[0]], along.at[h, 1]))
+    relay = [copies.to(net.to_z[1], line.at[h, net.z_of[1]], along.at[h, 2]) for h in range(2)]
     fourth = []
     fifth = []
     for h in range(2):
@@ -285,13 +289,22 @@
 
         start(third)
 
+    def onward():
+        arrive(third[0::2])
+
+        @pl.loop(0, 2)
+        def _(h):
+            line[h, net.z_of[1]] = line[h, net.z_of[1]] + along[h, 0]
+
+        start(relay)
+
     def spread():
-        arrive(third)
+        arrive(third[1::2] + relay)
 
         @pl.loop(0, 2)
         def _(h):
             total = line[h, net.z].astype(jnp.float32)
-            for k in range(3):
+            for k in range(1, 3):
                 total = total + along[h, k].astype(jnp.float32)
             done[h, net.g] = total.astype(jnp.bfloat16)
 
@@ -308,79 +321,109 @@
             copy.wait()
         copies.finish()
 
-    return [begin, plane, cross, column, spread, corners, end]
-
-
-def gather_first_kernel(
-    w_ref, v_ref, x_ref, w_full, v_full, keys_x, w_s, w_r, v_s, v_r, x_s, x_r, local_sem
-):
+    return [begin, plane, cross, column, onward, spread, corners, end]
+
+
+ROW_COPIES = 9
+
+
+def rows_stages(net, copies, local_sems, x_ref, keys_x):
+    at = 8 * PD
+
+    def block(owner):
+        return keys_x.at[pl.ds(pl.multiple_of(owner * PD, 128), PD)]
+
+    prompt = x_ref.at[pl.ds(0, PD)]
+    cont = [x_ref.at[pl.ds(PD + 128 * i, 128)] for i in range(2)]
+    local = [pltpu.make_async_copy(prompt, block(net.f), local_sems.at[0])]
+    to_mate = [copies.to(net.to_mate, prompt, block(net.f))]
+    for i in range(2):
+        near = keys_x.at[pl.ds(at + 256 * i, 128)]
+        here = keys_x.at[pl.ds(at + 256 * i + 128, 128)]
+        local.append(pltpu.make_async_copy(cont[i], here, local_sems.at[1 + i]))
+        to_mate.append(copies.to(net.to_mate, cont[i], near))
+    along_z = [copies.to(device, prompt, block(net.f)) for device in net.to_z[:2]]
+    relay = copies.to(net.to_z[0], block(net.f_of[1]), block(net.f_of[1]))
+    later = [copies.to(net.to_mate, block(owner), block(owner)) for owner in net.f_of]
+
+    def begin():
+        start(local)
+        start(to_mate)
+
+    def column():
+        start(along_z)
+
+    def onward():
+        along_z[1].wait_recv()
+        relay.start()
+
+    def mates():
+        arrive([along_z[0], relay])
+        start(later)
+
+    def end():
+        arrive(to_mate + later)
+        for copy in local:
+            copy.wait()
+        copies.finish()
+
+    return [begin, column, onward, mates, end]
+
+
+def gather_first_kernel(*refs):
+    shards, x_ref, fulls, keys_x = refs[:4], refs[4], refs[5:9], refs[9]
+    sems, local_sem, row_sems = refs[10:20], refs[20], refs[21]
     net = Net()
     net.greet()
-    weights = gather_stages(net, Copies(w_s, w_r), local_sem.at[0], w_ref, w_full)
-    vectors = gather_stages(net, Copies(v_s, v_r), local_sem.at[1], v_ref, v_full)
-    plength = PD * 4
-    at = 2 * plength
-
-    def block(owner):
-        return pl.ds(pl.multiple_of(owner * PD, 128), PD)
-
-    prompt = x_ref.at[:, pl.ds(0, PD)]
-    cont = [x_ref.at[:, pl.ds(PD + 128 * i, 128)] for i in range(2)]
-    near = [keys_x.at[:, pl.ds(at + 256 * i, 128)] for i in range(2)]
-    here = [keys_x.at[:, pl.ds(at + 256 * i + 128, 128)] for i in range(2)]
-    copies = Copies(x_s, x_r)
-    local = [pltpu.make_async_copy(prompt, keys_x.at[:, block(net.f)], local_sem.at[2])]
-    local += [
-        pltpu.make_async_copy(cont[i], here[i], local_sem.at[3 + i]) for i in range(2)
+    parts = [
+        gather_stages(
+            net, Copies(sems[2 * i], sems[2 * i + 1]), local_sem.at[i], shards[i], fulls[i]
+        )
+        for i in range(4)
     ]
-    to_mate = [copies.to(net.to_mate, prompt, keys_x.at[:, block(net.f)])]
-    to_mate += [copies.to(net.to_mate, cont[i], near[i]) for i in range(2)]
-    along_z = [copies.to(device, prompt, keys_x.at[:, block(net.f)]) for device in net.to_z]
-    later = [
-        copies.to(net.to_mate, keys_x.at[:, block(owner)], keys_x.at[:, block(owner)])
-        for owner in net.f_of
-    ]
-    weights[0]()
-    vectors[0]()
-    start(local)
-    start(to_mate)
-    weights[1]()
-    start(along_z)
-    vectors[1]()
-    weights[2]()
-    vectors[2]()
-    weights[3]()
-    vectors[3]()
-    arrive(along_z)
-    start(later)
-    weights[4]()
-    vectors[4]()
-    arrive(to_mate + later)
-    for copy in local:
-        copy.wait()
-    copies.finish()
-
-
-def gather_first(w_shard, v_shard, content_in):
-    def sems(count):
-        return [pltpu.SemaphoreType.DMA((count,))] * 2
-
+    rows = rows_stages(net, Copies(sems[8], sems[9]), row_sems, x_ref.at[0], keys_x)
+    for part in parts:
+        part[0]()
+    rows[0]()
+    for part in parts:
+        part[1]()
+    rows[1]()
+    for part in parts:
+        part[2]()
+    for part in parts:
+        part[3]()
+    rows[2]()
+    for part in parts:
+        part[4]()
+    rows[3]()
+    for part in parts:
+        part[5]()
+    rows[4]()
+
+
+def gather_first(shards, content_in):
     return pl.pallas_call(
         gather_first_kernel,
         name="gather_first",
-        in_specs=[ANY_SPEC] * 3,
-        out_specs=[ANY_SPEC] * 3,
-        out_shape=[
-            jax.ShapeDtypeStruct((8 * 4,) + w_shard.shape[1:], jnp.bfloat16),
-            jax.ShapeDtypeStruct((8 * 4,) + v_shard.shape[1:], jnp.bfloat16),
-            jax.ShapeDtypeStruct((MICRO, 8 * PD + 2 * CH, D), jnp.bfloat16),
-        ],
-        scratch_shapes=sems(GATHER_COPIES)
-        + sems(GATHER_COPIES)
-        + sems(9)
-        + [pltpu.SemaphoreType.DMA((5,))],
+        in_specs=[ANY_SPEC] * 5,
+        out_specs=[ANY_SPEC] * 5,
+        out_shape=[jax.ShapeDtypeStruct((8 * 4,) + s.shape[1:], jnp.bfloat16) for s in shards]
+        + [jax.ShapeDtypeStruct((8 * PD + 2 * CH, D), jnp.bfloat16)],
+        scratch_shapes=[pltpu.SemaphoreType.DMA((GATHER_COPIES,))] * 8
+        + [pltpu.SemaphoreType.DMA((ROW_COPIES,))] * 2
+        + [pltpu.SemaphoreType.DMA((4,)), pltpu.SemaphoreType.DMA((3,))],
         compiler_params=pltpu.CompilerParams(collective_id=1, has_side_effects=True),
-    )(w_shard, v_shard, content_in)
+    )(*shards, content_in)
+
+
+def halves_of(ref):
+    rows, columns = ref.shape[-2:]
+    rest = (slice(None),) * (len(ref.shape) - 2)
+    if columns > rows * 16:
+        cut = columns // 2
+        return [ref.at[rest + (slice(None), pl.ds(cut * i, cut))] for i in range(2)]
+    cut = rows // 2
+    return [ref.at[rest + (pl.ds(cut * i, cut),)] for i in range(2)]
 
 
 def hosted(plan, step):
@@ -398,39 +441,82 @@
 
 
 def attend_kernel(plength, carried, *refs):
-    (meta, qc, qx, k_rows, v_rows, table, xcol), refs = refs[:7], refs[7:]
+    (meta, x_c, x_q, w_q, w_k, w_v, bias, table, xcol, first_rows, other), refs = (
+        refs[:11],
+        refs[11:],
+    )
     shards, refs = refs[:carried], refs[carried:]
-    (ctx_c, ctx_x, full_c, full_x, lse_ref), refs = refs[:5], refs[5:]
+    (ctx_c, ctx_x, full_c, full_x, lse_ref, qc, qx, k_rows, v_rows), refs = refs[:9], refs[9:]
+    second_rows = other
+    if carried:
+        second_rows, refs = refs[0], refs[1:]
     fulls, refs = refs[:carried], refs[carried:]
-    keys, vals, scores, probs = refs[:4]
+    keys, vals, scores, probs, x_keys, load_sem = refs[:6]
+    refs = refs[6:]
     step = pl.program_id(0) * PAIRS + pl.program_id(1)
-    stages = []
     if carried:
         net = Net()
-        for i in range(carried):
-            sends, recvs = refs[4 + 2 * i : 6 + 2 * i]
-            stages.append(
-                gather_stages(
-                    net, Copies(sends, recvs), refs[-1].at[i], shards[i], fulls[i]
-                )
+        pieces = []
+        for i in range(2):
+            pieces += list(zip(halves_of(shards[i]), halves_of(fulls[i])))
+        pieces.append((shards[2], fulls[2]))
+        one, two, three, four, proj = (
+            gather_stages(
+                net, Copies(refs[2 * i], refs[2 * i + 1]), refs[12].at[i], src, dst
             )
-        up, down, proj = stages
+            for i, (src, dst) in enumerate(pieces)
+        )
+        rows = rows_stages(
+            net, Copies(refs[10], refs[11]), refs[13], other.at[1], second_rows
+        )
         hosted([(0, net.greet)], step)
         hosted(
             [
-                (0, up[0]),
-                (3, up[1]),
-                (3, down[0]),
-                (6, up[2]),
-                (7, down[1]),
-                (7, proj[0]),
-                (8, up[3]),
-                (8, proj[1]),
-                (10, down[2]),
-                (10, proj[2]),
+                (0, rows[0]),
+                (0, rows[1]),
+                (2, one[0]),
+                (2, proj[0]),
+                (3, rows[2]),
+                (3, two[0]),
+                (4, one[1]),
+                (4, proj[1]),
+                (5, rows[3]),
+                (6, rows[4]),
+                (6, one[2]),
+                (6, proj[2]),
+                (6, two[1]),
+                (6, three[0]),
+                (7, two[2]),
+                (7, four[0]),
+                (8, one[3]),
+                (8, proj[3]),
+                (8, three[1]),
+                (9, three[2]),
+                (9, four[1]),
+                (10, one[4]),
+                (10, proj[4]),
+                (10, two[3]),
+                (10, four[2]),
+                (11, three[3]),
             ],
             step,
         )
+    for m, source in enumerate((first_rows, second_rows)):
+
+        @pl.when(step == m * PAIRS)
+        def _():
+            load = pltpu.make_async_copy(source, x_keys, load_sem)
+            load.start()
+            load.wait()
+
+    w_kv = jnp.concatenate([w_k[...], w_v[...]], axis=1)
+    for at in range(0, x_keys.shape[0], 512):
+        part = slice(at, at + 512)
+        value = dot_nn(x_keys[part], w_kv)
+        k_rows[part] = value[:, :LANES].astype(jnp.bfloat16)
+        v_rows[part] = (value[:, LANES:] + bias[1:2]).astype(jnp.bfloat16)
+    qc[...] = (dot_nn(x_c[...], w_q[...]) + bias[0:1]).astype(jnp.bfloat16)
+    qx[...] = (dot_nn(x_q[...], w_q[...]) + bias[0:1]).astype(jnp.bfloat16)
     own_prompt, base, side = place(plength)
     mapped = meta[pl.program_id(0)]
     blocks = plength // 128
@@ -536,15 +622,16 @@
     ctx_x[...] = out.astype(jnp.bfloat16)
     full_x[...] = out
     if carried:
-        hosted([(11, s) for s in (down[3], proj[3], up[4], down[4], proj[4])], step)
-
-
-def pair_column(shift):
-    return lambda m, j, meta: (m, shift * PAIRS + j)
-
-
-def key_spec(n_keys, shift):
-    return pl.BlockSpec((n_keys, LANES), lambda m, j, meta: (m, shift * PAIRS + j))
+        rest = (four[3], two[4], three[4], four[4], one[5], proj[5], two[5], three[5], four[5])
+        hosted([(11, stage) for stage in rest], step)
+
+
+def pair_column():
+    return lambda m, j, meta: (m, j)
+
+
+def key_spec(n_keys):
+    return pl.BlockSpec((n_keys, LANES), lambda m, j, meta: (m, j))
 
 
 TABLE_SPEC = pl.BlockSpec((1, 8, LANES), lambda m, j, meta: (j, 0, 0))
@@ -558,12 +645,12 @@
     return pltpu.CompilerParams(vmem_limit_bytes=VMEM_LIMIT)
 
 
-def attend(meta, queries, extra_q, key_rows, table, xcol, shards):
+def attend(meta, x_c, x_q, weights, bias, table, xcol, first_rows, other, shards):
     carried = len(shards)
-    n_keys = key_rows.shape[0] // MICRO
+    n_keys = first_rows.shape[0]
     plength = (n_keys - 2 * CH) // 2
-    content = pl.BlockSpec((TD, LANES), pair_column(0))
-    extra = pl.BlockSpec((QP, LANES), pair_column(0))
+    content = pl.BlockSpec((TD, LANES), pair_column())
+    extra = pl.BlockSpec((QP, LANES), pair_column())
     own_row = plength + 2 * CH
     pairs = MICRO * PAIRS * 2 * (128 * plength + 256 * own_row) + MICRO * PAIRS * 128 * n_keys
     return pl.pallas_call(
@@ -572,12 +659,17 @@
         grid_spec=pltpu.PrefetchScalarGridSpec(
             num_scalar_prefetch=1,
             grid=(MICRO, PAIRS),
-            in_specs=[content, extra]
+            in_specs=[
+                pl.BlockSpec((TD, D), lambda m, j, meta: (m, 0)),
+                pl.BlockSpec((QP, D), lambda m, j, meta: (m, 0)),
+            ]
+            + [pl.BlockSpec((D, LANES), lambda m, j, meta: (0, j))] * 3
             + [
-                key_spec(n_keys, 0),
-                key_spec(n_keys, 1),
+                pl.BlockSpec((8, LANES), lambda m, j, meta: (0, j)),
                 TABLE_SPEC,
                 pl.BlockSpec((1, 128, 8), lambda m, j, meta: (m, 0, 0)),
+                ANY_SPEC,
+                ANY_SPEC,
             ]
             + [ANY_SPEC] * carried,
             out_specs=[
@@ -586,16 +678,26 @@
                 content,
                 extra,
                 pl.BlockSpec((1, 1, 8, LANES), lambda m, j, meta: (m, j, 0, 0)),
+                content,
+                extra,
+                key_spec(n_keys),
+                key_spec(n_keys),
             ]
-            + [ANY_SPEC] * carried,
+            + [ANY_SPEC] * (carried + 1 if carried else 0),
             scratch_shapes=[
                 pltpu.VMEM((n_keys, LANES), jnp.bfloat16),
                 pltpu.VMEM((n_keys, LANES), jnp.bfloat16),
                 pltpu.VMEM((256, n_keys), jnp.float32),
                 pltpu.VMEM((256, n_keys), jnp.bfloat16),
             ]
-            + [pltpu.SemaphoreType.DMA((GATHER_COPIES,))] * (2 * carried)
-            + [pltpu.SemaphoreType.DMA((4,))],
+            + [pltpu.VMEM((n_keys, D), jnp.bfloat16), pltpu.SemaphoreType.DMA]
+            + (
+                [pltpu.SemaphoreType.DMA((GATHER_COPIES,))] * 10
+                + [pltpu.SemaphoreType.DMA((ROW_COPIES,))] * 2
+                + [pltpu.SemaphoreType.DMA((5,)), pltpu.SemaphoreType.DMA((3,))]
+                if carried
+                else []
+            ),
         ),
         out_shape=[
             jax.ShapeDtypeStruct((MICRO * TD, D), jnp.bfloat16),
@@ -603,7 +705,12 @@
             jax.ShapeDtypeStruct((MICRO * TD, D), jnp.float32),
             jax.ShapeDtypeStruct((MICRO * QP, D), jnp.float32),
             jax.ShapeDtypeStruct((MICRO, PAIRS, 8, LANES), jnp.float32),
+            jax.ShapeDtypeStruct((MICRO * TD, D), jnp.bfloat16),
+            jax.ShapeDtypeStruct((MICRO * QP, D), jnp.bfloat16),
+            jax.ShapeDtypeStruct((MICRO * n_keys, D), jnp.bfloat16),
+            jax.ShapeDtypeStruct((MICRO * n_keys, D), jnp.bfloat16),
         ]
+        + ([jax.ShapeDtypeStruct((n_keys, D), jnp.bfloat16)] if carried else [])
         + [
             jax.ShapeDtypeStruct((8 * 4,) + shard.shape[1:], shard.dtype)
             for shard in shards
@@ -614,12 +721,14 @@
         ),
     )(
         meta,
-        queries,
-        extra_q,
-        key_rows,
-        key_rows,
+        x_c,
+        x_q,
+        *weights,
+        bias,
         table,
         xcol,
+        first_rows,
+        other,
         *shards,
     )
 
@@ -637,27 +746,34 @@
     step = pl.program_id(0) * PAIRS + pl.program_id(1)
     if carried:
         net = Net()
-        up, down, proj = (
-            reduce_stages(net, grads[i], shares[i], refs[10 * i : 10 * i + 10])
-            for i in range(carried)
+        pieces = list(zip(halves_of(grads[0]), halves_of(shares[0])))
+        pieces.append((grads[1], shares[1]))
+        one, two, proj = (
+            reduce_stages(net, src, dst, refs[10 * i : 10 * i + 10])
+            for i, (src, dst) in enumerate(pieces)
         )
         hosted([(0, net.greet)], step)
         hosted(
             [
-                (0, up[0]),
-                (0, down[0]),
+                (0, one[0]),
+                (0, two[0]),
                 (0, proj[0]),
-                (1, up[1]),
-                (4, up[2]),
-                (4, down[1]),
-                (6, up[3]),
-                (7, down[2]),
-                (7, proj[1]),
-                (9, down[3]),
-                (9, proj[2]),
-                (9, up[4]),
-                (10, proj[3]),
-                (10, up[5]),
+                (1, one[1]),
+                (2, two[1]),
+                (3, proj[1]),
+                (4, one[2]),
+                (5, two[2]),
+                (6, proj[2]),
+                (6, one[3]),
+                (7, two[3]),
+                (8, proj[3]),
+                (8, one[4]),
+                (9, two[4]),
+                (10, proj[4]),
+                (10, one[5]),
+                (11, two[5]),
+                (11, proj[5]),
+                (11, one[6]),
             ],
             step,
         )
@@ -876,16 +992,24 @@
             out_ref[p * plength : (p + 1) * plength] = (mine + other).astype(jnp.bfloat16)
         out_ref[2 * plength :] = acc[2 * plength :].astype(jnp.bfloat16)
     if carried:
-        rest = (down[4], proj[4], up[6], down[5], proj[5], down[6], proj[6])
-        hosted([(11, s) for s in rest], step)
-
-
-def attend_back(meta, queries, extra_q, key_rows, table, xcol, xrow, lse, dc, dx, fc, fx, grads):
+        rest = (two[6], proj[6], one[7], two[7], proj[7])
+        hosted([(11, stage) for stage in rest], step)
+
+
+def attend_back(
+    meta, queries, extra_q, k_rows, v_rows, table, xcol, xrow, lse, dc, dx, fc, fx, grads
+):
     carried = len(grads)
-    n_keys = key_rows.shape[0] // MICRO
+    sizes, kept = [], []
+    if carried:
+        part, width = grads[0].shape[3:]
+        tall, narrow = grads[1].shape[3:]
+        sizes = [(4 * part, width // 2)] * 2 + [(4 * tall, narrow)]
+        kept = [jax.ShapeDtypeStruct((4,) + grad.shape[3:], jnp.bfloat16) for grad in grads]
+    n_keys = k_rows.shape[0] // MICRO
     plength = (n_keys - 2 * CH) // 2
-    content = pl.BlockSpec((TD, LANES), pair_column(0))
-    extra = pl.BlockSpec((QP, LANES), pair_column(0))
+    content = pl.BlockSpec((TD, LANES), pair_column())
+    extra = pl.BlockSpec((QP, LANES), pair_column())
     own_row = plength + 2 * CH
     pairs = MICRO * PAIRS * 2 * (128 * plength + 256 * own_row) + MICRO * PAIRS * 128 * n_keys
     return pl.pallas_call(
@@ -896,8 +1020,8 @@
             grid=(MICRO, PAIRS),
             in_specs=[content, extra]
             + [
-                key_spec(n_keys, 0),
-                key_spec(n_keys, 1),
+                key_spec(n_keys),
+                key_spec(n_keys),
                 TABLE_SPEC,
                 pl.BlockSpec((1, 128, 8), lambda m, j, meta: (m, 0, 0)),
                 pl.BlockSpec((1, 8, 128), lambda m, j, meta: (m, 0, 0)),
@@ -911,8 +1035,8 @@
             out_specs=[
                 content,
                 extra,
-                key_spec(n_keys, 0),
-                key_spec(n_keys, 0),
+                key_spec(n_keys),
+                key_spec(n_keys),
                 pl.BlockSpec((1, 1, 64, LANES), lambda m, j, meta: (m, j, 0, 0)),
             ]
             + [ANY_SPEC] * carried,
@@ -929,11 +1053,7 @@
                 pltpu.VMEM((n_keys, LANES), jnp.float32),
                 pltpu.VMEM((n_keys, LANES), jnp.float32),
             ]
-            + [
-                buffer
-                for grad in grads
-                for buffer in reduce_buffers(4 * grad.shape[3], grad.shape[4])
-            ],
+            + [buffer for size in sizes for buffer in reduce_buffers(*size)],
         ),
         out_shape=[
             jax.ShapeDtypeStruct((MICRO * TD, D), jnp.bfloat16),
@@ -942,7 +1062,7 @@
             jax.ShapeDtypeStruct((MICRO * n_keys, D), jnp.bfloat16),
             jax.ShapeDtypeStruct((MICRO, PAIRS, 64, LANES), jnp.float32),
         ]
-        + [jax.ShapeDtypeStruct(grad.shape[2:], grad.dtype) for grad in grads],
+        + kept,
         compiler_params=host_params(3, carried),
         cost_estimate=pl.CostEstimate(
             flops=10 * pairs * LANES, bytes_accessed=32 * 1024 * 1024, transcendentals=pairs
@@ -951,8 +1071,8 @@
         meta,
         queries,
         extra_q,
-        key_rows,
-        key_rows,
+        k_rows,
+        v_rows,
         table,
         xcol,
         xrow,
@@ -1310,21 +1430,29 @@
     dq_x,
     dk,
     dv,
-    keys_x,
+    keys_0,
+    keys_1,
     x_c,
     x_q,
-    w_qkv,
+    w_q,
+    w_k,
+    w_v,
     dres,
     hist,
     buckets_of,
     sums,
-    w_share,
+    d_ref,
+    q_share,
+    k_share,
+    v_share,
+    d_share,
     small_out,
     grad_c,
     grad_q,
     *scratch,
 ):
-    w_buf = scratch[:10]
+    shares = (q_share, k_share, v_share, d_share)
+    buffers = [scratch[10 * i : 10 * i + 10] for i in range(4)]
     (
         grads,
         prompts,
@@ -1340,18 +1468,29 @@
         sm_s,
         sm_r,
         sem,
-    ) = scratch[10:]
+    ) = scratch[40:]
     net = Net()
     net.greet()
-    weights = reduce_stages(net, grads, w_share, w_buf)
+    sources = [grads.at[i] for i in range(3)] + [d_ref]
+    one, two, three, down = (
+        reduce_stages(net, sources[i], shares[i], buffers[i]) for i in range(4)
+    )
+    down[0]()
     copies = Copies(x_s, x_r)
     to_mate = [
-        copies.to(net.to_mate, prompts.at[:, :, 1 - net.c], theirs),
-        copies.to(net.to_mate, nears, near_got),
+        copies.to(net.to_mate, prompts.at[m, :, 1 - net.c], theirs.at[m]) for m in range(MICRO)
     ]
-    third = [
-        copies.to(net.to_z[k], prompts.at[:, net.z_of[k], net.c], along.at[k]) for k in range(3)
-    ]
+    swap = copies.to(net.to_mate, nears, near_got)
+    third, relay = [], []
+    for m in range(MICRO):
+        third.append(
+            [
+                copies.to(net.to_z[0], prompts.at[m, net.z_of[2], net.c], along.at[0, m]),
+                copies.to(net.to_z[0], prompts.at[m, net.z_of[0], net.c], along.at[1, m]),
+            ]
+        )
+        passed = prompts.at[m, net.z_of[1], net.c]
+        relay.append(copies.to(net.to_z[1], passed, along.at[2, m]))
     hops = Copies(sm_s, sm_r)
     partners = [net.to_mate, net.to_x, net.to_y, net.to_z[0], net.to_z[1]]
     butterfly = [
@@ -1367,35 +1506,55 @@
     n_keys = dk.shape[0] // MICRO
     n_prompt = n_keys - 2 * CH
 
+    def put(value, which):
+        part = D // 32
+        for owner in range(8):
+            for q in range(4):
+                at = (4 * owner + q) * part
+                grads[which, owner // 2, owner % 2, q] = value[at : at + part].astype(
+                    jnp.bfloat16
+                )
+
+    def back(rows):
+        return dot_nt(dk[rows], w_k[...]) + dot_nt(dv[rows], w_v[...])
+
+    def onward(m):
+        to_mate[m].wait_recv()
+
+        @pl.loop(0, 4)
+        def _(zi):
+            prompts[m, zi, net.c] = prompts[m, zi, net.c] + theirs[m, zi]
+
+        start(third[m])
+
+    def onto(m):
+        third[m][0].wait_recv()
+        prompts[m, net.z_of[1], net.c] = prompts[m, net.z_of[1], net.c] + along[0, m]
+        relay[m].start()
+
     for m in range(MICRO):
         for part in range(n_prompt // 512):
-            rows = slice(m * n_keys + 512 * part, m * n_keys + 512 * part + 512)
-            value = dot_nt(dk[rows], w_qkv[:, D : 2 * D]) + dot_nt(dv[rows], w_qkv[:, 2 * D :])
+            value = back(slice(m * n_keys + 512 * part, m * n_keys + 512 * part + 512))
             for i in range(4):
                 owner = 4 * part + i
                 prompts[m, owner // 2, owner % 2] = value[128 * i : 128 * i + 128].astype(
                     jnp.bfloat16
                 )
-        rows = slice(m * n_keys + n_prompt, (m + 1) * n_keys)
-        value = dot_nt(dk[rows], w_qkv[:, D : 2 * D]) + dot_nt(dv[rows], w_qkv[:, 2 * D :])
-        for i in range(2):
-            nears[m, i] = value[256 * i : 256 * i + 128].astype(jnp.bfloat16)
-            owns[m, i] = value[256 * i + 128 : 256 * i + 256]
-    start(to_mate)
-
-    def put(value, shift):
-        part = D // 32
-        for owner in range(8):
-            for q in range(4):
-                at = (4 * owner + q) * part
-                grads[owner // 2, owner % 2, q, :, shift : shift + D] = value[
-                    at : at + part
-                ].astype(jnp.bfloat16)
-
-    put(dot_tn(keys_x[...], dk[...]), D)
-    put(dot_tn(keys_x[...], dv[...]), 2 * D)
+        to_mate[m].start()
+        if m == 0:
+            down[1]()
     put(dot_tn(x_c[...], dq_c[...]) + dot_tn(x_q[...], dq_x[...]), 0)
-    weights[0]()
+    one[0]()
+    onward(0)
+    put(dot_tn(keys_0[...], dk[:n_keys]) + dot_tn(keys_1[...], dk[n_keys:]), 1)
+    two[0]()
+    onward(1)
+    one[1]()
+    put(dot_tn(keys_0[...], dv[:n_keys]) + dot_tn(keys_1[...], dv[n_keys:]), 2)
+    three[0]()
+    two[1]()
+    onto(0)
+    down[2]()
 
     small[0] = jnp.zeros_like(small[0])
     sum_q = jnp.sum(dq_c[...].astype(jnp.float32), axis=0, keepdims=True)
@@ -1408,33 +1567,43 @@
         small[0, 8 + i : 9 + i] = sums[6:7, D * i : D * i + D]
     small[0, 16:32, 0:LANES] = table_rows(hist, buckets_of, net.c)
     butterfly[0].start()
-
-    arrive(to_mate)
-
-    @pl.loop(0, 8)
-    def _(i):
-        m, zi = i // 4, i % 4
-        prompts[m, zi, net.c] = prompts[m, zi, net.c] + theirs[m, zi]
-
-    start(third)
-    weights[1]()
+    three[1]()
+    one[2]()
+    for m in range(MICRO):
+        value = back(slice(m * n_keys + n_prompt, (m + 1) * n_keys))
+        for i in range(2):
+            nears[m, i] = value[256 * i : 256 * i + 128].astype(jnp.bfloat16)
+            owns[m, i] = value[256 * i + 128 : 256 * i + 256]
+    swap.start()
+    onto(1)
+    two[2]()
     hop(0)
     rows_c = x_c.shape[0]
-    out_c[0:rows_c] = dres[0:rows_c] + dot_nt(dq_c[...], w_qkv[:, 0:D])
-    out_c[rows_c:] = dres[rows_c:] + dot_nt(dq_x[...], w_qkv[:, 0:D])
+    out_c[0:rows_c] = dres[0:rows_c] + dot_nt(dq_c[...], w_q[...])
+    out_c[rows_c:] = dres[rows_c:] + dot_nt(dq_x[...], w_q[...])
+    down[3]()
+    one[3]()
+    three[2]()
+    hop(1)
+    two[3]()
+    one[4]()
+    swap.wait_recv()
     for m in range(MICRO):
         for i in range(2):
             rows = slice(m * TD + PD + 128 * i, m * TD + PD + 128 * i + 128)
             out_c[rows] = out_c[rows] + owns[m, i] + near_got[m, i].astype(jnp.float32)
-    hop(1)
-    weights[2]()
+    three[3]()
     hop(2)
-    weights[3]()
+    two[4]()
+    down[4]()
+    one[5]()
     hop(3)
-    arrive(third)
+    three[4]()
+    two[5]()
     for m in range(MICRO):
+        arrive([third[m][1], relay[m]])
         total = prompts[m, net.z, net.c].astype(jnp.float32)
-        for k in range(3):
+        for k in range(1, 3):
             total = total + along[k, m].astype(jnp.float32)
         rows = slice(m * TD, m * TD + PD)
         out_c[rows] = out_c[rows] + total
@@ -1443,36 +1612,62 @@
         pltpu.make_async_copy(out_c.at[pl.ds(rows_c, 2 * QP)], grad_q, sem.at[1]),
     ]
     start(stores)
+    one[6]()
+    down[5]()
+    three[5]()
     hop(4)
     keep = pltpu.make_async_copy(small.at[5], small_out, sem.at[2])
     keep.start()
-    for i in range(4, 7):
-        weights[i]()
+    two[6]()
+    one[7]()
+    down[6]()
+    three[6]()
+    two[7]()
+    down[7]()
+    three[7]()
     for copy in stores + [keep]:
         copy.wait()
     copies.finish()
     hops.finish()
 
 
-def finish(dq_c, dq_x, dk, dv, keys_x, x_c, x_q, w_qkv, dres, hist, buckets_of, sums):
+def finish(
+    dq_c,
+    dq_x,
+    dk,
+    dv,
+    keys_x,
+    x_c,
+    x_q,
+    weights,
+    dres,
+    hist,
+    buckets_of,
+    sums,
+    down_grad,
+):
     whole = pl.BlockSpec(memory_space=pltpu.VMEM)
     bf, f32 = jnp.bfloat16, jnp.float32
     rows_c, rows_x = x_c.shape[0], x_q.shape[0]
-    part, width = D // 32, w_qkv.shape[1]
+    part, tall = D // 32, down_grad.shape[3]
     return pl.pallas_call(
         finish_kernel,
         name="finish",
-        in_specs=[whole] * 12,
-        out_specs=[ANY_SPEC] * 4,
+        in_specs=[whole] * 15 + [ANY_SPEC],
+        out_specs=[ANY_SPEC] * 7,
         out_shape=[
-            jax.ShapeDtypeStruct((4, part, width), bf),
+            jax.ShapeDtypeStruct((4, part, D), bf),
+            jax.ShapeDtypeStruct((4, part, D), bf),
+            jax.ShapeDtypeStruct((4, part, D), bf),
+            jax.ShapeDtypeStruct((4, tall, D), bf),
             jax.ShapeDtypeStruct((SMALL_ROWS, D), f32),
             jax.ShapeDtypeStruct((rows_c, D), f32),
             jax.ShapeDtypeStruct((rows_x, D), f32),
         ],
-        scratch_shapes=reduce_buffers(4 * part, width)
+        scratch_shapes=reduce_buffers(4 * part, D) * 3
+        + reduce_buffers(4 * tall, D)
         + [
-            pltpu.VMEM((4, 2, 4, part, width), bf),
+            pltpu.VMEM((3, 4, 2, 4, part, D), bf),
             pltpu.VMEM((MICRO, 4, 2, PD, D), bf),
             pltpu.VMEM((MICRO, 4, PD, D), bf),
             pltpu.VMEM((3, MICRO, PD, D), bf),
@@ -1481,8 +1676,8 @@
             pltpu.VMEM((MICRO, 2, 128, D), f32),
             pltpu.VMEM((rows_c + rows_x, D), f32),
             pltpu.VMEM((6, SMALL_ROWS, D), f32),
-            pltpu.SemaphoreType.DMA((5,)),
-            pltpu.SemaphoreType.DMA((5,)),
+            pltpu.SemaphoreType.DMA((9,)),
+            pltpu.SemaphoreType.DMA((9,)),
             pltpu.SemaphoreType.DMA((5,)),
             pltpu.SemaphoreType.DMA((5,)),
             pltpu.SemaphoreType.DMA((3,)),
@@ -1490,7 +1685,7 @@
         compiler_params=pltpu.CompilerParams(
             collective_id=4, has_side_effects=True, vmem_limit_bytes=60 * 1024 * 1024
         ),
-    )(dq_c, dq_x, dk, dv, keys_x, x_c, x_q, w_qkv, dres, hist, buckets_of, sums)
+    )(dq_c, dq_x, dk, dv, *keys_x, x_c, x_q, *weights, dres, hist, buckets_of, sums, down_grad)
 
 
 def pad_rows(block):
@@ -1573,31 +1768,34 @@
     n_keys = 2 * plength + 2 * CH
     shard = b_query.shape[0]
     up_size = b_up.shape[0]
-    vectors = jnp.concatenate(
-        [b_query, b_value, b_out, b_down, ln1_gain, ln1_bias, ln2_gain, ln2_bias, b_up]
-    )
-    qkv_shard = jnp.concatenate([w_query, w_key, w_value], axis=1)
+    vectors = jnp.stack(
+        [b_query, b_value, b_out, b_down, ln1_gain, ln1_bias, ln2_gain, ln2_bias]
+        + [b_up[shard * i : shard * i + shard] for i in range(up_size // shard)]
+    )
+    tokens_x = content_in.reshape(MICRO * TD, D)
+    extra_x = pad_rows(query_in)
     if own_links:
-        vector_shard = jnp.pad(vectors, (0, 32 * 256 - vectors.shape[0])).reshape(4, 8, 256)
-        qkv_weight, all_vectors, keys_x = gather_first(
-            quarters(qkv_shard), vector_shard, content_in
+        lines = vectors.shape[0]
+        vector_shard = jnp.pad(vectors, ((0, 32 - lines), (0, 256 - shard))).reshape(4, 8, 256)
+        *qkv_weights, all_vectors, first_rows = gather_first(
+            [quarters(w_query), quarters(w_key), quarters(w_value), vector_shard], content_in
         )
-        qkv_weight = qkv_weight.reshape(-1, qkv_shard.shape[1])
-        all_vectors = all_vectors.reshape(devices, -1)
+        qkv_weights = [entry.reshape(-1, D) for entry in qkv_weights]
+        all_vectors = all_vectors.reshape(devices, 32, 256)[:, :lines, :shard]
+        other = content_in
         carried = tuple(quarters(shard) for shard in (w_up, w_down, w_out))
     else:
-        qkv_weight, all_vectors = gather(qkv_shard), gather(vectors[None])
+        qkv_weights = [gather(w_query), gather(w_key), gather(w_value)]
+        all_vectors = gather(vectors[None])
         up_weight, down_weight, out_weight = gather(w_up), gather(w_down), gather(w_out)
         carried = ()
         prompt_x = lax.all_gather(content_in[:, :PD], "fsdp", axis=1, tiled=True)
         near_x = from_partner(content_in[:, PD:], "fsdp").reshape(MICRO, 2, 1, 128, D)
         own_x = content_in[:, PD:].reshape(MICRO, 2, 1, 128, D)
         cont_x = jnp.concatenate([near_x, own_x], axis=2).reshape(MICRO, 2 * CH, D)
-        keys_x = jnp.concatenate([prompt_x, cont_x], axis=1)
-    keys_x = keys_x.reshape(MICRO * n_keys, D)
-    query_weight, kv_weight = qkv_weight[:, :D], qkv_weight[:, D:]
+        first_rows, other = jnp.concatenate([prompt_x, cont_x], axis=1)
     singles = [
-        all_vectors[:, shard * i : shard * i + shard].reshape(-1).astype(jnp.float32)
+        all_vectors[:, i].reshape(-1).astype(jnp.float32)
         for i in range(8)
     ]
     (
@@ -1610,7 +1808,7 @@
         gain_two,
         shift_two,
     ) = singles
-    up_bias = all_vectors[:, 8 * shard : 8 * shard + up_size].reshape(-1).astype(jnp.float32)
+    up_bias = all_vectors[:, 8:].reshape(-1).astype(jnp.float32)
 
     prompt_map = cont_prompt[:, 0, :]
     prompt_ref = jnp.sum(
@@ -1636,25 +1834,16 @@
     dist = dist - dist[:, LANES - 1 :]
     table = jnp.pad(dist.reshape(PAIRS, 2, LANES), ((0, 0), (0, 6), (0, 0)))
 
-    tokens_x = content_in.reshape(MICRO * TD, D)
-    extra_x = pad_rows(query_in)
     x_all = jnp.concatenate([tokens_x, extra_x])
-    kv_bias = jnp.concatenate([jnp.zeros((D,), jnp.float32), value_bias])
-    key_rows = (
-        jnp.dot(keys_x, kv_weight, preferred_element_type=jnp.float32) + kv_bias
-    ).astype(jnp.bfloat16)
-    q_all = (
-        jnp.dot(x_all, query_weight, preferred_element_type=jnp.float32) + query_bias
-    ).astype(jnp.bfloat16)
-    queries = q_all[: MICRO * TD]
-    extra_q = q_all[MICRO * TD :]
-
-    ctx_c, ctx_x, full_c, full_x, lse, *gathered = attend(
-        meta, queries, extra_q, key_rows, table, xcol, carried
-    )
+    bias = jnp.pad(jnp.stack([query_bias, value_bias]), ((0, 6), (0, 0)))
+    ctx_c, ctx_x, full_c, full_x, lse, queries, extra_q, k_rows, v_rows, *gathered = attend(
+        meta, tokens_x, extra_x, qkv_weights, bias, table, xcol, first_rows, other, carried
+    )
+    keys_x = (first_rows, other)
     if own_links:
+        keys_x = (first_rows, gathered[0])
         up_weight, down_weight, out_weight = (
-            entry.reshape(-1, entry.shape[2]) for entry in gathered
+            entry.reshape(-1, entry.shape[2]) for entry in gathered[1:]
         )
     rows_c = MICRO * TD
     context = jnp.concatenate([ctx_c, ctx_x])
@@ -1682,12 +1871,13 @@
 
     to_reduce = ()
     if own_links:
-        to_reduce = tuple(by_quarter(g) for g in (dweight_up, dweight_down, dweight_out))
+        to_reduce = (by_quarter(dweight_up), by_quarter(dweight_out))
     dq_c, dq_x, dk_rows, dv_rows, hist, *reduced = attend_back(
         meta,
         queries,
         extra_q,
-        key_rows,
+        k_rows,
+        v_rows,
         table,
         xcol,
         xrow,
@@ -1699,7 +1889,7 @@
         to_reduce,
     )
     if own_links:
-        t_qkv, small, grad_content, grad_query = finish(
+        *t_qkv, t_down, small, grad_content, grad_query = finish(
             dq_c,
             dq_x,
             dk_rows,
@@ -1707,17 +1897,18 @@
             keys_x,
             tokens_x,
             extra_x,
-            qkv_weight,
+            qkv_weights,
             dres_one,
             hist,
             jnp.broadcast_to(rel_bucket[None], (8, LANES)),
             sums,
+            by_quarter(dweight_down),
         )
         grad_content = grad_content.reshape(MICRO, TD, D)
         grad_query = grad_query.reshape(MICRO, QP, D)[:, :extra_rows]
-        t_up, t_down, t_out = reduced
-        shares = (t_down, t_up, t_out, t_qkv)
-        t_down, t_up, t_out, t_qkv = [
+        t_up, t_out = reduced
+        shares = (t_down, t_up, t_out, *t_qkv)
+        t_down, t_up, t_out, *t_qkv = [
             entry.reshape(-1, entry.shape[-1]).astype(jnp.float32) for entry in shares
         ]
         pieces = lax.dynamic_slice_in_dim(small[:8], own_rank * shard, shard, 1)
@@ -1737,6 +1928,9 @@
         dq_all = jnp.concatenate([dq_c, dq_x])
         dbias_query = jnp.sum(dq_all.astype(jnp.float32), axis=0)
         dbias_value = jnp.sum(dv_rows.astype(jnp.float32), axis=0)
+        query_weight, key_weight, value_weight = qkv_weights
+        kv_weight = jnp.concatenate([key_weight, value_weight], axis=1)
+        keys_x = jnp.concatenate(keys_x)
         dkeys_x = dot_nt(dkv_rows, kv_weight).reshape(MICRO, n_keys, D)
         dtable = table_gradient(hist, rel_bucket, bias_table.shape[0], side, heads)
         small = jnp.concatenate(
@@ -1778,6 +1972,7 @@
         t_down, t_up, t_out, t_qkv, t_small = [
             lax.psum(entry, "grp").astype(jnp.float32) for entry in shares
         ]
+        t_qkv = [t_qkv[:, D * i : D * i + D] for i in range(3)]
         dcont = (dcont[:, :, 1] + from_near.astype(jnp.float32)).reshape(MICRO, CH, D)
         dx_all = dres_one + dot_nt(dq_all, query_weight)
         grad_content = dx_all[:rows_c].reshape(MICRO, TD, D) + jnp.concatenate(
@@ -1794,10 +1989,10 @@
         out_query,
         grad_content,
         grad_query,
-        t_qkv[:, :D],
+        t_qkv[0],
         pieces[0],
-        t_qkv[:, D : 2 * D],
-        t_qkv[:, 2 * D :],
+        t_qkv[1],
+        t_qkv[2],
         pieces[1],
         t_out,
         pieces[7],

time: 418 us -> 363 us (0.87)
  Pallas kernels: 357 us -> 323 us
  matrix products: 15.4 us -> 0 us
  local copies, waits for them, and re-layouts: 22.5 us -> 16.4 us
    pallas_call x1, Pallas kernels: 81.3 us -> 62.3 us  [attend_back(): pl.pallas_call(functools.partial(attend_back_kernel, plength, carried), n...]
    pallas_call x1, Pallas kernels: 56.7 us -> 39.5 us  [gather_first(): pl.pallas_call(gather_first_kernel, name='gather_first', in_specs=[ANY_SP...]
    dot_general x2 -> x0, matrix products: 15.4 us -> none  [the longest x1 12.8 us: on_device(): jnp.dot(keys_x, kv_weight, preferred_element_type=jnp.float32) + kv_bias]
    pallas_call x1, Pallas kernels: 57.9 us -> 69 us  [attend(): pl.pallas_call(functools.partial(attend_kernel, plength, carried), name='...]
    pallas_call x1, Pallas kernels: 88 us -> 79.3 us  [finish(): pl.pallas_call(finish_kernel, name='finish', in_specs=[whole] * 15 + [ANY...]
    concatenate x1 -> x0, local copies, waits for them, and re-layouts: 6.11 us -> none  [on_device(): jnp.concatenate([b_query, b_value, b_out, b_down, ln1_gain, ln1_bias, ln2...]
where the time goes in v5:
time: 363 us; the launch traced here: 357 us
  Pallas kernels  323 us (89%)
  local copies, waits for them, and re-layouts  16.4 us (5%)
  other arithmetic  15.5 us (4%)
    pallas_call x1, Pallas kernels, finish(): pl.pallas_call(finish_kernel, name='finish', in_specs=[whole] * 15 + [ANY...  79.3 us
    pallas_call x1, Pallas kernels, middle(): pl.pallas_call(middle_kernel, name='middle', grid=(tiles + GRAD_STEPS,),...  73.2 us
    pallas_call x1, Pallas kernels, attend(): pl.pallas_call(functools.partial(attend_kernel, plength, carried), name='...  69 us
    pallas_call x1, Pallas kernels, attend_back(): pl.pallas_call(functools.partial(attend_back_kernel, plength, carried), n...  62.3 us
    pallas_call x1, Pallas kernels, gather_first(): pl.pallas_call(gather_first_kernel, name='gather_first', in_specs=[ANY_SP...  39.5 us

profile of v5, /device:TPU:0, one launch (start us, length us, event | category | flops | bytes accessed | tf_op | source)
XLA Modules:
  0.0 356.5 jit_solution(15968401221073627306)
XLA Ops:
  0.7 0.0 copy-start.13
  0.7 0.7 and_select_fusion.1
  1.4 0.7 and_select_fusion
  2.1 0.1 add_add_fusion
  2.2 0.6 fusion.5
  2.8 0.8 copy.94.refs_8_.refs_6_
  3.6 1.3 select_reduce_fusion.refs_0_
  4.9 0.9 slice_bitcast_fusion.8
  5.8 0.8 stack.83
  6.6 0.6 pad_bitcast_fusion.refs_3_
  7.2 39.5 %gather_first.1 = (bf16[32,24,768]{2,1,0:T(8,128)(2,1)}, bf16[32,24,768]{2,1,0:T(8,128)(2,1)}, bf16[32,24,768]{2,1,0:T(8,128)(2,1)}, bf16[32,8,256]{2,1,0:T(8,128)(2,1)}, bf16[1536,768]{1,0:T(8,128)(2,1)}) custom-call(bf16[4,24,768]{2,1,0:T(8,128)(2,1)} %bitcast.130, bf16[4,24,768]{2,1,0:T(8,128)(2,1)} %bitcast.131, bf16[4,24,768]{2,1,0:T(8,128)(2,1)} %bitcast.132, ...), custom_call_target="tpu_custom_call" | custom-call | tf_op jit(solution)/shard_map/gather_first/pallas_call | solution.py:405
  46.7 1.2 fusion.4
  48.0 0.1 convert_element_type.149
  48.0 0.1 convert_element_type.150
  48.1 0.6 fusion.3.refs_6_
  48.8 0.0 copy-done.13
  48.8 0.1 copy.88
  48.9 0.6 gather_fusion
  49.5 0.1 copy.89
  49.6 0.2 slice_reduce_fusion
  49.8 0.1 broadcast_subtract_fusion
  49.9 0.6 pad.33.refs_7_.refs_5_
  50.5 0.0 copy-done.7
  50.5 0.7 pad.29
  51.2 69.0 %attend.1 = (bf16[768,768]{1,0:T(8,128)(2,1)}, bf16[128,768]{1,0:T(8,128)(2,1)}, f32[768,768]{1,0:T(8,128)}, f32[128,768]{1,0:T(8,128)}, f32[2,6,8,128]{3,2,1,0:...) custom-call(s32[2]{0:T(128)} %select_reduce_fusion.refs_0_, ...), custom_call_target="tpu_custom_call" | custom-call | flops 5234491392 | bytes 16777216 | tf_op jit(solution)/shard_map/attend/pallas_call | solution.py:656
  120.2 0.0 copy-start.8
  120.3 0.0 copy-start.3
  120.3 3.2 pad_maximum_fusion
  123.5 0.1 convert_element_type.152
  123.6 0.1 convert_element_type.153
  123.7 0.1 convert_element_type.154
  123.7 0.1 convert_element_type.155
  123.8 0.1 convert_element_type.156
  123.9 0.1 convert_element_type.157
  124.1 0.6 stack.91.vec
  124.7 0.7 slice_convert_fusion
  125.4 0.7 reshape.281.up_bias
  126.1 1.2 pad_maximum_fusion.2.cot
  127.3 73.2 %middle.1 = (f32[768,768]{1,0:T(8,128)}, f32[128,768]{1,0:T(8,128)}, f32[896,768]{1,0:T(8,128)}, bf16[768,768]{1,0:T(8,128)(2,1)}, bf16[128,768]{1,0:T(8,128)(2,...) custom-call(bf16[896,768]{1,0:T(8,128)(2,1)} %get-tuple-element.208.x,, ...), custom_call_target="tpu_custom_call" | custom-call | flops 28538044416 | bytes 41943040 | tf_op jit(solution)/shard_map/middle/pallas_call | solution.py:1312
  200.6 62.3 %attend_back.1 = (bf16[768,768]{1,0:T(8,128)(2,1)}, bf16[128,768]{1,0:T(8,128)(2,1)}, bf16[3072,768]{1,0:T(8,128)(2,1)}, bf16[3072,768]{1,0:T(8,128)(2,1)}, f32[...) custom-call(s32[2]{0:T(128)} %select_reduce_fusion.refs_0_, ...), custom_call_target="tpu_custom_call" | custom-call | flops 13086228480 | bytes 33554432 | tf_op jit(solution)/shard_map/attend_back/pallas_call | solution.py:1015
  262.9 0.6 broadcast_in_dim.32.buckets_of
  263.5 79.3 %finish.1 = (bf16[4,24,768]{2,1,0:T(8,128)(2,1)}, bf16[4,24,768]{2,1,0:T(8,128)(2,1)}, bf16[4,24,768]{2,1,0:T(8,128)(2,1)}, bf16[4,96,768]{2,1,0:T(8,128)(2,1)},...) custom-call(bf16[768,768]{1,0:T(8,128)(2,1)} %get-tuple-element.84.dq_c, ...), custom_call_target="tpu_custom_call" | custom-call | tf_op jit(solution)/shard_map/finish/pallas_call | solution.py:1653
  342.8 0.0 copy-start.6
  342.8 0.0 copy-start.12
  342.8 0.0 copy-start.11
  342.8 0.0 copy-start.10
  342.8 2.2 bitcast_convert_fusion
  345.1 0.8 slice.131
  345.8 0.7 bitcast_convert_fusion.3
  346.6 0.7 bitcast_convert_fusion.4
  347.3 0.7 bitcast_convert_fusion.5
  348.1 0.7 slice.107
  348.8 0.1 constant_dynamic-slice_fusion
  348.9 0.5 slice_bitcast_fusion
  349.4 0.7 slice.113
  350.2 0.6 dynamic-slice_reduce_fusion
  350.8 0.7 slice.117
  351.5 0.1 dynamic-slice_bitcast_fusion
  351.5 0.7 copy.102
  352.2 1.2 bitcast_convert_fusion.1
  353.4 0.0 copy-done.9
  353.4 0.7 bitcast_convert_fusion.2
  354.1 0.8 slice.130
  354.9 1.4 copy.112
  (35 shorter events, 0.2 us)
Async XLA Ops:
  0.7 48.1 %copy-start.13 = (bf16[32,12]{0,1:T(8,128)(2,1)S(1)}, bf16[32,12]{0,1:T(8,128)(2,1)}, u32[]{:S(2)}) copy-start(bf16[32,12]{0,1:T(8,128)(2,1)} %param.43) | copy-start | bytes 2308
  0.7 48.2 %copy-start.14 = (s32[128]{0:T(128)S(1)}, s32[128]{0:T(128)}, u32[]{:S(2)}) copy-start(s32[128]{0:T(128)} %param.27) | copy-start | bytes 1540
  2.8 47.7 %copy-start.7 = (bf16[2,56,768]{2,1,0:T(8,128)(2,1)S(1)}, bf16[2,56,768]{2,1,0:T(8,128)(2,1)}, u32[]{:S(2)}) copy-start(bf16[2,56,768]{2,1,0:T(8,128)(2,1)} %param.24) | copy-start | bytes 516100
  51.2 69.0 %copy-start = (bf16[2,384,768]{2,1,0:T(8,128)(2,1)S(1)}, bf16[2,384,768]{2,1,0:T(8,128)(2,1)}, u32[]{:S(2)}) copy-start(bf16[2,384,768]{2,1,0:T(8,128)(2,1)} %refs_10_.1) | copy-start | bytes 3538948
  51.2 69.0 %copy-start.2 = (bf16[2,64,768]{2,1,0:T(8,128)(2,1)S(1)}, bf16[2,64,768]{2,1,0:T(8,128)(2,1)}, u32[]{:S(2)}) copy-start(bf16[2,64,768]{2,1,0:T(8,128)(2,1)} %pad.29) | copy-start | bytes 589828
  120.2 5.9 %copy-start.8 = (bf16[2,56,768]{2,1,0:T(8,128)(2,1)S(1)}, bf16[2,56,768]{2,1,0:T(8,128)(2,1)}, u32[]{:S(2)}) copy-start(bf16[2,56,768]{2,1,0:T(8,128)(2,1)} %param.45) | copy-start | bytes 516100
  120.3 5.9 %copy-start.3 = (bf16[2,384,768]{2,1,0:T(8,128)(2,1)S(1)}, bf16[2,384,768]{2,1,0:T(8,128)(2,1)}, u32[]{:S(2)}) copy-start(bf16[2,384,768]{2,1,0:T(8,128)(2,1)} %param.44) | copy-start | bytes 3538948
  342.8 2.3 copy-start.6
  342.8 3.0 copy-start.12
  342.8 3.8 %copy-start.11 = (bf16[4,24,768]{2,1,0:T(8,128)(2,1)S(1)}, bf16[4,24,768]{2,1,0:T(8,128)(2,1)}, u32[]{:S(2)}) copy-start(bf16[4,24,768]{2,1,0:T(8,128)(2,1)} %get-tuple-element.97) | copy-start | bytes 442372
  342.8 4.5 %copy-start.10 = (bf16[4,24,768]{2,1,0:T(8,128)(2,1)S(1)}, bf16[4,24,768]{2,1,0:T(8,128)(2,1)}, u32[]{:S(2)}) copy-start(bf16[4,24,768]{2,1,0:T(8,128)(2,1)} %get-tuple-element.95) | copy-start | bytes 442372
  345.1 7.2 %copy-start.4 = (bf16[4,24,3072]{2,1,0:T(8,128)(2,1)S(1)}, bf16[4,24,3072]{2,1,0:T(8,128)(2,1)}, u32[]{:S(2)}) copy-start(bf16[4,24,3072]{2,1,0:T(8,128)(2,1)} %get-tuple-element.100) | copy-start | bytes 1769476
  346.6 6.8 %copy-start.9 = (bf16[4,24,768]{2,1,0:T(8,128)(2,1)S(1)}, bf16[4,24,768]{2,1,0:T(8,128)(2,1)}, u32[]{:S(2)}) copy-start(bf16[4,24,768]{2,1,0:T(8,128)(2,1)} %get-tuple-element.99) | copy-start | bytes 442372
  347.3 6.8 %copy-start.5 = (f32[128,768]{1,0:T(8,128)S(1)}, f32[128,768]{1,0:T(8,128)}, u32[]{:S(2)}) copy-start(f32[128,768]{1,0:T(8,128)} %get-tuple-element.72) | copy-start | bytes 1179652
  352.2 2.7 copy-start.1

commit v6 on v5

--- a/solution.py
+++ b/solution.py
@@ -211,6 +211,7 @@
         pltpu.VMEM((2, 4, part, half), jnp.bfloat16),
         pltpu.VMEM((2, 3, part, half), jnp.bfloat16),
         pltpu.VMEM((2, 4, part, half), jnp.bfloat16),
+        pltpu.VMEM((4, part, width), jnp.float32),
         pltpu.SemaphoreType.DMA((2,)),
         pltpu.SemaphoreType.DMA((REDUCE_COPIES,)),
         pltpu.SemaphoreType.DMA((REDUCE_COPIES,)),
@@ -218,7 +219,7 @@
 
 
 def reduce_stages(net, grad, share, buffers):
-    own, other, side_a, side_b, line, along, done, local_sem, sends, recvs = buffers
+    own, other, side_a, side_b, line, along, done, wide, local_sem, sends, recvs = buffers
     copies = Copies(sends, recvs)
     half = grad.shape[4] // 2
     left, right = pl.ds(0, half), pl.ds(half, half)
@@ -248,10 +249,7 @@
         fourth.append(copies.to(net.to_y, done.at[h, net.g], done.at[h, net.g]))
     fifth.append(copies.to(net.to_y, done.at[0, net.gx], done.at[0, net.gx]))
     fifth.append(copies.to(net.to_x, done.at[1, net.gy], done.at[1, net.gy]))
-    store = [
-        pltpu.make_async_copy(done.at[0], share.at[:, :, left], local_sem.at[0]),
-        pltpu.make_async_copy(done.at[1], share.at[:, :, right], local_sem.at[1]),
-    ]
+    store = pltpu.make_async_copy(wide, share, local_sem.at[1])
 
     def begin():
         load.start()
@@ -316,9 +314,14 @@
 
     def end():
         arrive(fifth)
-        start(store)
-        for copy in store:
-            copy.wait()
+
+        @pl.loop(0, 4)
+        def _(qi):
+            for h in range(2):
+                wide[qi, :, h * half : h * half + half] = done[h, qi].astype(jnp.float32)
+
+        store.start()
+        store.wait()
         copies.finish()
 
     return [begin, plane, cross, column, onward, spread, corners, end]
@@ -451,8 +454,9 @@
     if carried:
         second_rows, refs = refs[0], refs[1:]
     fulls, refs = refs[:carried], refs[carried:]
-    keys, vals, scores, probs, x_keys, load_sem = refs[:6]
-    refs = refs[6:]
+    keys, vals, x_keys, load_sem = refs[:4]
+    all_scores, all_probs = refs[4:8], refs[8:12]
+    refs = refs[12:]
     step = pl.program_id(0) * PAIRS + pl.program_id(1)
     if carried:
         net = Net()
@@ -529,7 +533,8 @@
     tab_x = jnp.where(row < QP, tab_a, tab_b)
     lse_ref[...] = jnp.zeros_like(lse_ref)
 
-    def solve(stack, first, plan, tables, lse_rows):
+    def solve(which, stack, first, plan, tables, lse_rows):
+        scores, probs = all_scores[which], all_probs[which]
         count = len(plan)
         span = slice(first, first + 128 * count)
         halves = len(tables)
@@ -574,7 +579,7 @@
     for b in range(blocks):
         d = base + row - (col + 128 * b)
         plan_p.append((near_index(d), d >= 0))
-    out = head_merge(solve(q_p, 0, plan_p, (tab_a, tab_b), (0, 3)))
+    out = head_merge(solve(0, q_p, 0, plan_p, (tab_a, tab_b), (0, 3)))
     ctx_c[0:PD] = out.astype(jnp.bfloat16)
     full_c[0:PD] = out
 
@@ -587,7 +592,7 @@
         (near_index(near_d), near_d >= 0),
         (near_index(own_d), own_d >= 0),
     ]
-    out = head_merge(solve(q_0, plength, plan_0, (tab_a, tab_b), (1, 4)))
+    out = head_merge(solve(1, q_0, plength, plan_0, (tab_a, tab_b), (1, 4)))
     ctx_c[PD : PD + 128] = out.astype(jnp.bfloat16)
     full_c[PD : PD + 128] = out
     plan_1 = [far] * blocks + [
@@ -596,7 +601,7 @@
         (near_index(near_d), near_d >= 0),
         (near_index(own_d), own_d >= 0),
     ]
-    out = head_merge(solve(q_1, plength, plan_1, (tab_a, tab_b), (2, 5)))
+    out = head_merge(solve(2, q_1, plength, plan_1, (tab_a, tab_b), (2, 5)))
     ctx_c[PD + 128 : PD + 256] = out.astype(jnp.bfloat16)
     full_c[PD + 128 : PD + 256] = out
 
@@ -616,7 +621,7 @@
         for offset in (1 - side, side):
             key = plength + 2 * (col + 128 * b) + offset
             plan_x.append((near_index(pos - key), key < lim_c))
-    out = solve(q_x, 0, plan_x, (tab_x,), (6,))
+    out = solve(3, q_x, 0, plan_x, (tab_x,), (6,))
     lane = lax.broadcasted_iota(jnp.int32, (QP, LANES), 1)
     out = jnp.where(lane < HD, out[0:QP], out[QP:])
     ctx_x[...] = out.astype(jnp.bfloat16)
@@ -649,6 +654,7 @@
     carried = len(shards)
     n_keys = first_rows.shape[0]
     plength = (n_keys - 2 * CH) // 2
+    groups = [(256, plength), (256, plength + 256), (256, plength + 512), (128, n_keys)]
     content = pl.BlockSpec((TD, LANES), pair_column())
     extra = pl.BlockSpec((QP, LANES), pair_column())
     own_row = plength + 2 * CH
@@ -687,10 +693,11 @@
             scratch_shapes=[
                 pltpu.VMEM((n_keys, LANES), jnp.bfloat16),
                 pltpu.VMEM((n_keys, LANES), jnp.bfloat16),
-                pltpu.VMEM((256, n_keys), jnp.float32),
-                pltpu.VMEM((256, n_keys), jnp.bfloat16),
+                pltpu.VMEM((n_keys, D), jnp.bfloat16),
+                pltpu.SemaphoreType.DMA,
             ]
-            + [pltpu.VMEM((n_keys, D), jnp.bfloat16), pltpu.SemaphoreType.DMA]
+            + [pltpu.VMEM(group, jnp.float32) for group in groups]
+            + [pltpu.VMEM(group, jnp.bfloat16) for group in groups]
             + (
                 [pltpu.SemaphoreType.DMA((GATHER_COPIES,))] * 10
                 + [pltpu.SemaphoreType.DMA((ROW_COPIES,))] * 2
@@ -741,15 +748,16 @@
     grads, refs = refs[:carried], refs[carried:]
     (dq_c, dq_x, dk_rows, dv_rows, hist), refs = refs[:5], refs[5:]
     shares, refs = refs[:carried], refs[carried:]
-    keys, vals, q_all, d_all, scores, dprobs, probs_t, dscores_t, ds_p, dk_acc, dv_acc = refs[:11]
-    refs = refs[11:]
+    keys, vals, q_all, d_all, probs_t, dscores_t, ds_p, ds_c, dk_acc, dv_acc = refs[:10]
+    all_scores, all_dprobs = refs[10:14], refs[14:18]
+    refs = refs[18:]
     step = pl.program_id(0) * PAIRS + pl.program_id(1)
     if carried:
         net = Net()
         pieces = list(zip(halves_of(grads[0]), halves_of(shares[0])))
         pieces.append((grads[1], shares[1]))
         one, two, proj = (
-            reduce_stages(net, src, dst, refs[10 * i : 10 * i + 10])
+            reduce_stages(net, src, dst, refs[11 * i : 11 * i + 11])
             for i, (src, dst) in enumerate(pieces)
         )
         hosted([(0, net.greet)], step)
@@ -821,7 +829,8 @@
     delta_x = deltas(dx[...], full_x[...])
     delta_x = jnp.concatenate([delta_x[0:1], delta_x[1:2]], axis=1)
 
-    def block_back(first, plan, at_col, halves):
+    def block_back(which, first, plan, at_col, halves):
+        scores, dprobs = all_scores[which], all_dprobs[which]
         count = len(plan)
         width = 128 * len(halves)
         span = slice(first, first + 128 * count)
@@ -878,7 +887,7 @@
         for offset in (1 - side, side):
             key = plength + 2 * (row + 128 * b) + offset
             plan.append((near_index(pos - key), key < lim_c))
-    for _ in block_back(0, plan, x_at, [((tab_a, tab_b), 6, delta_x)]):
+    for _ in block_back(3, 0, plan, x_at, [((tab_a, tab_b), 6, delta_x)]):
         pass
 
     def spread_block(head, key_at, content_at):
@@ -898,7 +907,7 @@
         d = base + col - (row + 128 * b)
         plan.append((near_index(d), d >= 0))
     halves = [((tab_a,), 0, delta_p[0:1]), ((tab_b,), 3, delta_p[1:2])]
-    for half, at, ds in block_back(0, plan, p_at, halves):
+    for half, at, ds in block_back(0, 0, plan, p_at, halves):
         ds_p[128 * at : 128 * at + 128, 128 * half : 128 * half + 128] = ds
     before = jnp.maximum(base - 128, 0)
     base_at = pl.multiple_of(base, 128)
@@ -930,7 +939,7 @@
     near_sum = {}
     own_sum = {}
     last_key = 2 * plength - 128
-    for half, at, ds in block_back(plength, plan_0, c0_at, halves):
+    for half, at, ds in block_back(1, plength, plan_0, c0_at, halves):
         if at == blocks - 1:
             ds = ds + spread_block(half, last_key, PD)
             ds = jnp.where(col < 64, ds, 0.0)
@@ -943,24 +952,24 @@
             own_sum[half] = jnp.where(col >= row, ds, 0.0)
     for half in range(2):
         lane = slice(128 * half, 128 * half + 128)
-        ds_p[0:128, lane] = near_sum[half]
-        ds_p[128:256, lane] = own_sum[half]
+        ds_c[0:128, lane] = near_sum[half]
+        ds_c[128:256, lane] = own_sum[half]
     halves = [((tab_a,), 2, delta_1[0:1]), ((tab_b,), 5, delta_1[1:2])]
-    for half, at, ds in block_back(plength, plan_1, c1_at, halves):
+    for half, at, ds in block_back(2, plength, plan_1, c1_at, halves):
         lane = slice(128 * half, 128 * half + 128)
         if at == blocks:
             ds = ds + spread_block(half, 2 * plength, PD + 128)
-            ds_p[0:128, lane] = ds_p[0:128, lane] + jnp.where(col < row, ds, 0.0)
+            ds_c[0:128, lane] = ds_c[0:128, lane] + jnp.where(col < row, ds, 0.0)
         if at == blocks + 1:
             ds = ds + spread_block(half, 2 * plength + 128, PD + 128)
-            ds_p[128:256, lane] = ds_p[128:256, lane] + jnp.where(col < row, ds, 0.0)
+            ds_c[128:256, lane] = ds_c[128:256, lane] + jnp.where(col < row, ds, 0.0)
         if at == blocks + 2:
             ds = ds + spread_block(half, at_k1, PD + 128)
-            ds = ds_p[0:128, lane] + jnp.where(col >= row, ds, 0.0)
+            ds = ds_c[0:128, lane] + jnp.where(col >= row, ds, 0.0)
             hist[0, 0, 32 * half + 16 : 32 * half + 24] = fold(lookup(ds, turn))
         if at == blocks + 3:
             ds = ds + spread_block(half, at_k1 + 128, PD + 128)
-            ds = ds_p[128:256, lane] + jnp.where(col >= row, ds, 0.0)
+            ds = ds_c[128:256, lane] + jnp.where(col >= row, ds, 0.0)
             hist[0, 0, 32 * half + 24 : 32 * half + 32] = fold(lookup(ds, turn))
 
     own = slice(0, plength)
@@ -1005,9 +1014,10 @@
         part, width = grads[0].shape[3:]
         tall, narrow = grads[1].shape[3:]
         sizes = [(4 * part, width // 2)] * 2 + [(4 * tall, narrow)]
-        kept = [jax.ShapeDtypeStruct((4,) + grad.shape[3:], jnp.bfloat16) for grad in grads]
+        kept = [jax.ShapeDtypeStruct((4,) + grad.shape[3:], jnp.float32) for grad in grads]
     n_keys = k_rows.shape[0] // MICRO
     plength = (n_keys - 2 * CH) // 2
+    groups = [(plength, 256), (plength + 256, 256), (plength + 512, 256), (n_keys, 128)]
     content = pl.BlockSpec((TD, LANES), pair_column())
     extra = pl.BlockSpec((QP, LANES), pair_column())
     own_row = plength + 2 * CH
@@ -1045,14 +1055,14 @@
                 pltpu.VMEM((n_keys, LANES), jnp.bfloat16),
                 pltpu.VMEM((896, LANES), jnp.bfloat16),
                 pltpu.VMEM((896, LANES), jnp.bfloat16),
-                pltpu.VMEM((n_keys, 256), jnp.float32),
-                pltpu.VMEM((n_keys, 256), jnp.float32),
                 pltpu.VMEM((n_keys, 896), jnp.bfloat16),
                 pltpu.VMEM((n_keys, 896), jnp.bfloat16),
                 pltpu.VMEM((plength, 256), jnp.float32),
+                pltpu.VMEM((256, 256), jnp.float32),
                 pltpu.VMEM((n_keys, LANES), jnp.float32),
                 pltpu.VMEM((n_keys, LANES), jnp.float32),
             ]
+            + [pltpu.VMEM(group, jnp.float32) for group in groups] * 2
             + [buffer for size in sizes for buffer in reduce_buffers(*size)],
         ),
         out_shape=[
@@ -1122,9 +1132,12 @@
 
 
 def middle_kernel(
-    x,
-    ctx,
-    cot,
+    x_c,
+    x_x,
+    ctx_c,
+    ctx_x,
+    cot_c,
+    cot_x,
     w_out,
     w_up_ref,
     w_down_ref,
@@ -1154,11 +1167,20 @@
     sems,
     w_up,
     w_down,
+    x,
+    ctx,
+    cot,
     load_sems,
 ):
     step = pl.program_id(0)
     load_up = pltpu.make_async_copy(w_up_ref, w_up, load_sems.at[0])
     load_down = pltpu.make_async_copy(w_down_ref, w_down, load_sems.at[1])
+    loads = []
+    for content, extra, rows in ((x_c, x_x, x), (ctx_c, ctx_x, ctx), (cot_c, cot_x, cot)):
+        size = content.shape[0]
+        for source, at in ((content, pl.ds(0, size)), (extra, pl.ds(size, 2 * QP))):
+            sem = load_sems.at[2 + len(loads)]
+            loads.append(pltpu.make_async_copy(source, rows.at[at], sem))
     width = w_up.shape[1]
     rows_c = out_c.shape[0]
     tiles = x.shape[0] // TILE
@@ -1173,7 +1195,10 @@
         [
             (outs.at[pl.ds(TILE, split)], out_c.at[pl.ds(TILE, split)]),
             (dctx.at[pl.ds(TILE, split)], dctx_c.at[pl.ds(TILE, split)]),
-            (outs.at[pl.ds(rows_c, 2 * QP)], out_x),
+            *[
+                (outs.at[pl.ds(rows_c + QP * m, out_x.shape[1])], out_x.at[m])
+                for m in range(MICRO)
+            ],
             (dctx.at[pl.ds(rows_c, 2 * QP)], dctx_x),
         ],
     ]
@@ -1188,8 +1213,12 @@
 
     @pl.when(step == 0)
     def _():
+        start(loads[2:4] + loads[0:2])
         load_up.start()
+        start(loads[4:6])
         load_down.start()
+        for copy in loads[0:4]:
+            copy.wait()
         sums[...] = jnp.zeros_like(sums)
 
     @pl.when(step < tiles)
@@ -1229,6 +1258,8 @@
         @pl.when(step == 0)
         def _():
             load_down.wait()
+            for copy in loads[4:6]:
+                copy.wait()
 
         work[...] = dot_nn(act[rows], w_down[...])
 
@@ -1299,9 +1330,11 @@
                 copy.wait()
 
 
-def middle(x, ctx, cot, w_out, w_up, w_down, vec, up_bias):
-    rows = x.shape[0]
-    rows_c = MICRO * TD
+def middle(
+    x_c, x_x, ctx_c, ctx_x, cot_c, cot_x, w_out, w_up, w_down, vec, up_bias, extra_rows
+):
+    rows_c = x_c.shape[0]
+    rows = rows_c + x_x.shape[0]
     width = w_up.shape[1]
     tiles = rows // TILE
     quarter = width // 4
@@ -1314,9 +1347,7 @@
         name="middle",
         grid=(tiles + GRAD_STEPS,),
         in_specs=[
-            once(x),
-            once(ctx),
-            once(cot),
+            *[ANY_SPEC] * 6,
             once(w_out),
             ANY_SPEC,
             ANY_SPEC,
@@ -1336,7 +1367,7 @@
         ],
         out_shape=[
             jax.ShapeDtypeStruct((rows_c, D), f32),
-            jax.ShapeDtypeStruct((rows - rows_c, D), f32),
+            jax.ShapeDtypeStruct((MICRO, extra_rows, D), f32),
             jax.ShapeDtypeStruct((rows, D), f32),
             jax.ShapeDtypeStruct((rows_c, D), bf),
             jax.ShapeDtypeStruct((rows - rows_c, D), bf),
@@ -1358,10 +1389,13 @@
             pltpu.VMEM((rows, D), f32),
             pltpu.VMEM((rows, D), bf),
             pltpu.VMEM((56, width), f32),
-            pltpu.SemaphoreType.DMA((6,)),
+            pltpu.SemaphoreType.DMA((7,)),
             pltpu.VMEM(w_up.shape, bf),
             pltpu.VMEM(w_down.shape, bf),
-            pltpu.SemaphoreType.DMA((2,)),
+            pltpu.VMEM((rows, D), bf),
+            pltpu.VMEM((rows, D), bf),
+            pltpu.VMEM((rows, D), bf),
+            pltpu.SemaphoreType.DMA((8,)),
         ],
         compiler_params=pltpu.CompilerParams(vmem_limit_bytes=60 * 1024 * 1024),
         cost_estimate=pl.CostEstimate(
@@ -1369,7 +1403,7 @@
             bytes_accessed=40 * 1024 * 1024,
             transcendentals=2 * rows * width,
         ),
-    )(x, ctx, cot, w_out, w_up, w_down, vec, up_bias)
+    )(x_c, x_x, ctx_c, ctx_x, cot_c, cot_x, w_out, w_up, w_down, vec, up_bias)
 
 
 SMALL_ROWS = 32
@@ -1426,18 +1460,18 @@
 
 
 def finish_kernel(
-    dq_c,
+    dq_c_ref,
     dq_x,
-    dk,
-    dv,
-    keys_0,
-    keys_1,
-    x_c,
+    dk_ref,
+    dv_ref,
+    keys_0_ref,
+    keys_1_ref,
+    x_c_ref,
     x_q,
     w_q,
     w_k,
     w_v,
-    dres,
+    dres_ref,
     hist,
     buckets_of,
     sums,
@@ -1451,8 +1485,8 @@
     grad_q,
     *scratch,
 ):
-    shares = (q_share, k_share, v_share, d_share)
-    buffers = [scratch[10 * i : 10 * i + 10] for i in range(4)]
+    shares = [q_share, k_share, v_share] + halves_of(d_share)
+    buffers = [scratch[11 * i : 11 * i + 11] for i in range(5)]
     (
         grads,
         prompts,
@@ -1468,14 +1502,38 @@
         sm_s,
         sm_r,
         sem,
-    ) = scratch[40:]
+        dq_c,
+        dk,
+        dv,
+        keys_0,
+        keys_1,
+        x_c,
+        load_sem,
+    ) = scratch[55:]
     net = Net()
     net.greet()
-    sources = [grads.at[i] for i in range(3)] + [d_ref]
-    one, two, three, down = (
-        reduce_stages(net, sources[i], shares[i], buffers[i]) for i in range(4)
-    )
+    sources = [grads.at[i] for i in range(3)] + halves_of(d_ref)
+    one, two, three, down, rest = (
+        reduce_stages(net, sources[i], shares[i], buffers[i]) for i in range(5)
+    )
+    n_keys = dk.shape[0] // MICRO
+    halves = [pl.ds(m * n_keys, n_keys) for m in range(MICRO)]
+    moves = []
+    for half in halves:
+        moves += [(dk_ref.at[half], dk.at[half]), (dv_ref.at[half], dv.at[half])]
+    moves += [(x_c_ref, x_c), (dq_c_ref, dq_c), (keys_0_ref, keys_0), (keys_1_ref, keys_1)]
+    moves.append((dres_ref, out_c))
+    loads = [
+        pltpu.make_async_copy(src, dst, load_sem.at[i]) for i, (src, dst) in enumerate(moves)
+    ]
+    start(loads)
+
+    def loaded(first, last):
+        for copy in loads[first:last]:
+            copy.wait()
+
     down[0]()
+    rest[0]()
     copies = Copies(x_s, x_r)
     to_mate = [
         copies.to(net.to_mate, prompts.at[m, :, 1 - net.c], theirs.at[m]) for m in range(MICRO)
@@ -1503,7 +1561,6 @@
         if i + 1 < len(butterfly):
             butterfly[i + 1].start()
 
-    n_keys = dk.shape[0] // MICRO
     n_prompt = n_keys - 2 * CH
 
     def put(value, which):
@@ -1532,7 +1589,7 @@
         prompts[m, net.z_of[1], net.c] = prompts[m, net.z_of[1], net.c] + along[0, m]
         relay[m].start()
 
-    for m in range(MICRO):
+    def prompt_back(m):
         for part in range(n_prompt // 512):
             value = back(slice(m * n_keys + 512 * part, m * n_keys + 512 * part + 512))
             for i in range(4):
@@ -1541,21 +1598,37 @@
                     jnp.bfloat16
                 )
         to_mate[m].start()
-        if m == 0:
-            down[1]()
+
+    loaded(0, 2)
+    prompt_back(0)
+    down[1]()
+    rest[1]()
+    loaded(2, 4)
+    prompt_back(1)
+    onward(0)
+    loaded(4, 6)
     put(dot_tn(x_c[...], dq_c[...]) + dot_tn(x_q[...], dq_x[...]), 0)
     one[0]()
-    onward(0)
+    onward(1)
+    loaded(6, 8)
     put(dot_tn(keys_0[...], dk[:n_keys]) + dot_tn(keys_1[...], dk[n_keys:]), 1)
     two[0]()
-    onward(1)
     one[1]()
+    down[2]()
     put(dot_tn(keys_0[...], dv[:n_keys]) + dot_tn(keys_1[...], dv[n_keys:]), 2)
     three[0]()
     two[1]()
+    rest[2]()
     onto(0)
-    down[2]()
-
+    three[1]()
+    down[3]()
+    one[2]()
+    for m in range(MICRO):
+        value = back(slice(m * n_keys + n_prompt, (m + 1) * n_keys))
+        for i in range(2):
+            nears[m, i] = value[256 * i : 256 * i + 128].astype(jnp.bfloat16)
+            owns[m, i] = value[256 * i + 128 : 256 * i + 256]
+    swap.start()
     small[0] = jnp.zeros_like(small[0])
     sum_q = jnp.sum(dq_c[...].astype(jnp.float32), axis=0, keepdims=True)
     sum_q = sum_q + jnp.sum(dq_x[...].astype(jnp.float32), axis=0, keepdims=True)
@@ -1567,39 +1640,38 @@
         small[0, 8 + i : 9 + i] = sums[6:7, D * i : D * i + D]
     small[0, 16:32, 0:LANES] = table_rows(hist, buckets_of, net.c)
     butterfly[0].start()
-    three[1]()
-    one[2]()
-    for m in range(MICRO):
-        value = back(slice(m * n_keys + n_prompt, (m + 1) * n_keys))
-        for i in range(2):
-            nears[m, i] = value[256 * i : 256 * i + 128].astype(jnp.bfloat16)
-            owns[m, i] = value[256 * i + 128 : 256 * i + 256]
-    swap.start()
+    rest[3]()
     onto(1)
     two[2]()
+    down[4]()
+    one[3]()
     hop(0)
+    three[2]()
+    rest[4]()
+    loaded(8, 9)
     rows_c = x_c.shape[0]
-    out_c[0:rows_c] = dres[0:rows_c] + dot_nt(dq_c[...], w_q[...])
-    out_c[rows_c:] = dres[rows_c:] + dot_nt(dq_x[...], w_q[...])
-    down[3]()
-    one[3]()
-    three[2]()
+    out_c[0:rows_c] = out_c[0:rows_c] + dot_nt(dq_c[...], w_q[...])
+    out_c[rows_c:] = out_c[rows_c:] + dot_nt(dq_x[...], w_q[...])
+    two[3]()
+    down[5]()
+    one[4]()
     hop(1)
-    two[3]()
-    one[4]()
+    three[3]()
+    rest[5]()
+    two[4]()
     swap.wait_recv()
     for m in range(MICRO):
         for i in range(2):
             rows = slice(m * TD + PD + 128 * i, m * TD + PD + 128 * i + 128)
             out_c[rows] = out_c[rows] + owns[m, i] + near_got[m, i].astype(jnp.float32)
-    three[3]()
+    down[6]()
+    one[5]()
     hop(2)
-    two[4]()
-    down[4]()
-    one[5]()
+    three[4]()
+    rest[6]()
+    two[5]()
     hop(3)
-    three[4]()
-    two[5]()
+    down[7]()
     for m in range(MICRO):
         arrive([third[m][1], relay[m]])
         total = prompts[m, net.z, net.c].astype(jnp.float32)
@@ -1609,21 +1681,21 @@
         out_c[rows] = out_c[rows] + total
     stores = [
         pltpu.make_async_copy(out_c.at[pl.ds(0, rows_c)], grad_c, sem.at[0]),
-        pltpu.make_async_copy(out_c.at[pl.ds(rows_c, 2 * QP)], grad_q, sem.at[1]),
     ]
+    for m in range(MICRO):
+        rows = out_c.at[pl.ds(rows_c + QP * m, grad_q.shape[1])]
+        stores.append(pltpu.make_async_copy(rows, grad_q.at[m], sem.at[1 + m]))
     start(stores)
     one[6]()
-    down[5]()
     three[5]()
+    rest[7]()
     hop(4)
-    keep = pltpu.make_async_copy(small.at[5], small_out, sem.at[2])
+    keep = pltpu.make_async_copy(small.at[5], small_out, sem.at[3])
     keep.start()
     two[6]()
     one[7]()
-    down[6]()
     three[6]()
     two[7]()
-    down[7]()
     three[7]()
     for copy in stores + [keep]:
         copy.wait()
@@ -1645,6 +1717,7 @@
     buckets_of,
     sums,
     down_grad,
+    extra_rows,
 ):
     whole = pl.BlockSpec(memory_space=pltpu.VMEM)
     bf, f32 = jnp.bfloat16, jnp.float32
@@ -1653,19 +1726,24 @@
     return pl.pallas_call(
         finish_kernel,
         name="finish",
-        in_specs=[whole] * 15 + [ANY_SPEC],
+        in_specs=[ANY_SPEC, whole]
+        + [ANY_SPEC] * 5
+        + [whole] * 4
+        + [ANY_SPEC]
+        + [whole] * 3
+        + [ANY_SPEC],
         out_specs=[ANY_SPEC] * 7,
         out_shape=[
-            jax.ShapeDtypeStruct((4, part, D), bf),
-            jax.ShapeDtypeStruct((4, part, D), bf),
-            jax.ShapeDtypeStruct((4, part, D), bf),
-            jax.ShapeDtypeStruct((4, tall, D), bf),
+            jax.ShapeDtypeStruct((4, part, D), f32),
+            jax.ShapeDtypeStruct((4, part, D), f32),
+            jax.ShapeDtypeStruct((4, part, D), f32),
+            jax.ShapeDtypeStruct((4, tall, D), f32),
             jax.ShapeDtypeStruct((SMALL_ROWS, D), f32),
             jax.ShapeDtypeStruct((rows_c, D), f32),
-            jax.ShapeDtypeStruct((rows_x, D), f32),
+            jax.ShapeDtypeStruct((MICRO, extra_rows, D), f32),
         ],
         scratch_shapes=reduce_buffers(4 * part, D) * 3
-        + reduce_buffers(4 * tall, D)
+        + reduce_buffers(2 * tall, D) * 2
         + [
             pltpu.VMEM((3, 4, 2, 4, part, D), bf),
             pltpu.VMEM((MICRO, 4, 2, PD, D), bf),
@@ -1680,8 +1758,13 @@
             pltpu.SemaphoreType.DMA((9,)),
             pltpu.SemaphoreType.DMA((5,)),
             pltpu.SemaphoreType.DMA((5,)),
-            pltpu.SemaphoreType.DMA((3,)),
-        ],
+            pltpu.SemaphoreType.DMA((4,)),
+        ]
+        + [
+            pltpu.VMEM(kept.shape, kept.dtype)
+            for kept in (dq_c, dk, dv, *keys_x, x_c)
+        ]
+        + [pltpu.SemaphoreType.DMA((9,))],
         compiler_params=pltpu.CompilerParams(
             collective_id=4, has_side_effects=True, vmem_limit_bytes=60 * 1024 * 1024
         ),
@@ -1834,7 +1917,6 @@
     dist = dist - dist[:, LANES - 1 :]
     table = jnp.pad(dist.reshape(PAIRS, 2, LANES), ((0, 0), (0, 6), (0, 0)))
 
-    x_all = jnp.concatenate([tokens_x, extra_x])
     bias = jnp.pad(jnp.stack([query_bias, value_bias]), ((0, 6), (0, 0)))
     ctx_c, ctx_x, full_c, full_x, lse, queries, extra_q, k_rows, v_rows, *gathered = attend(
         meta, tokens_x, extra_x, qkv_weights, bias, table, xcol, first_rows, other, carried
@@ -1846,8 +1928,6 @@
             entry.reshape(-1, entry.shape[2]) for entry in gathered[1:]
         )
     rows_c = MICRO * TD
-    context = jnp.concatenate([ctx_c, ctx_x])
-    upstream = jnp.concatenate([cot_content.reshape(rows_c, D), pad_rows(cot_query)])
     vec = jnp.stack([out_bias, gain_one, shift_one, down_bias, gain_two, shift_two])
     (
         out_content,
@@ -1860,10 +1940,20 @@
         dweight_out,
         sums,
     ) = middle(
-        x_all, context, upstream, out_weight, up_weight, down_weight, vec, up_bias[None]
+        tokens_x,
+        extra_x,
+        ctx_c,
+        ctx_x,
+        cot_content.reshape(rows_c, D),
+        pad_rows(cot_query),
+        out_weight,
+        up_weight,
+        down_weight,
+        vec,
+        up_bias[None],
+        extra_rows,
     )
     out_content = out_content.reshape(MICRO, TD, D)
-    out_query = out_query.reshape(MICRO, QP, D)[:, :extra_rows]
 
     def by_quarter(grad):
         grad = grad.astype(jnp.bfloat16)
@@ -1903,13 +1993,13 @@
             jnp.broadcast_to(rel_bucket[None], (8, LANES)),
             sums,
             by_quarter(dweight_down),
+            extra_rows,
         )
         grad_content = grad_content.reshape(MICRO, TD, D)
-        grad_query = grad_query.reshape(MICRO, QP, D)[:, :extra_rows]
         t_up, t_out = reduced
         shares = (t_down, t_up, t_out, *t_qkv)
         t_down, t_up, t_out, *t_qkv = [
-            entry.reshape(-1, entry.shape[-1]).astype(jnp.float32) for entry in shares
+            entry.reshape(-1, entry.shape[-1]) for entry in shares
         ]
         pieces = lax.dynamic_slice_in_dim(small[:8], own_rank * shard, shard, 1)
         t_bup = lax.dynamic_index_in_dim(
@@ -1955,7 +2045,7 @@
         dcont = dkeys_x[:, 2 * plength :].reshape(MICRO, 2, 2, 128, D)
         dnear = dcont[:, :, 0].astype(jnp.bfloat16)
         dweight_qkv = jnp.concatenate(
-            [dot_tn(x_all, dq_all), dot_tn(keys_x, dkv_rows)], axis=1
+            [dot_tn(jnp.concatenate([tokens_x, extra_x]), dq_all), dot_tn(keys_x, dkv_rows)], axis=1
         )
 
         def scatter(piece, dimension=0):

time: 363 us -> 353 us (0.972)
  other arithmetic: 15.5 us -> 5.53 us
  local copies, waits for them, and re-layouts: 16.4 us -> 23.8 us
  Pallas kernels: 323 us -> 316 us
    unnamed x40 -> x37, local copies, waits for them, and re-layouts: 2.17 us -> 9.67 us
    pallas_call x1, Pallas kernels: 79.3 us -> 72.7 us  [finish(): pl.pallas_call(finish_kernel, name='finish', in_specs=[ANY_SPEC, whole] +...]
    convert_element_type x6 -> x0, other arithmetic: 6.35 us -> none  [on_device(): entry.reshape(-1, entry.shape[-1]).astype(jnp.float32)]
    concatenate x2 -> x0, other arithmetic: 4.37 us -> none  [the longest x1 3.19 us: on_device(): x_all = jnp.concatenate([tokens_x, extra_x])]
where the time goes in v6:
time: 353 us; the launch traced here: 347 us
  Pallas kernels  316 us (90%)
  local copies, waits for them, and re-layouts  23.8 us (7%)
  other arithmetic  5.53 us (2%)
    pallas_call x1, Pallas kernels, middle(): pl.pallas_call(middle_kernel, name='middle', grid=(tiles + GRAD_STEPS,),...  72.9 us
    pallas_call x1, Pallas kernels, finish(): pl.pallas_call(finish_kernel, name='finish', in_specs=[ANY_SPEC, whole] +...  72.7 us
    pallas_call x1, Pallas kernels, attend(): pl.pallas_call(functools.partial(attend_kernel, plength, carried), name='...  69 us
    pallas_call x1, Pallas kernels, attend_back(): pl.pallas_call(functools.partial(attend_back_kernel, plength, carried), n...  62 us
    pallas_call x1, Pallas kernels, gather_first(): pl.pallas_call(gather_first_kernel, name='gather_first', in_specs=[ANY_SP...  39.5 us
    unnamed x37, local copies, waits for them, and re-layouts  9.67 us

profile of v6, /device:TPU:0, one launch (start us, length us, event | category | flops | bytes accessed | tf_op | source)
XLA Modules:
  0.0 346.6 jit_solution(14761049288867256726)
XLA Ops:
  0.7 0.0 copy-start.7
  0.7 0.7 and_select_fusion.1
  1.4 0.7 and_select_fusion
  2.1 0.1 add_add_fusion
  2.2 0.6 fusion.5
  2.8 0.8 copy.94.refs_8_.refs_6_
  3.6 1.3 select_reduce_fusion.refs_0_
  4.9 0.9 slice_bitcast_fusion.8
  5.8 0.8 stack.83
  6.6 0.6 pad_bitcast_fusion.refs_3_
  7.2 39.5 %gather_first.1 = (bf16[32,24,768]{2,1,0:T(8,128)(2,1)}, bf16[32,24,768]{2,1,0:T(8,128)(2,1)}, bf16[32,24,768]{2,1,0:T(8,128)(2,1)}, bf16[32,8,256]{2,1,0:T(8,128)(2,1)}, bf16[1536,768]{1,0:T(8,128)(2,1)}) custom-call(bf16[4,24,768]{2,1,0:T(8,128)(2,1)} %bitcast.119, bf16[4,24,768]{2,1,0:T(8,128)(2,1)} %bitcast.120, bf16[4,24,768]{2,1,0:T(8,128)(2,1)} %bitcast.121, ...), custom_call_target="tpu_custom_call" | custom-call | tf_op jit(solution)/shard_map/gather_first/pallas_call | solution.py:408
  46.8 1.3 fusion.4
  48.1 0.1 convert_element_type.113
  48.1 0.1 convert_element_type.114
  48.2 0.6 fusion.3.refs_6_
  48.9 0.8 copy.88
  49.6 0.7 compare_select_fusion
  50.3 0.6 gather_fusion
  50.9 0.1 copy.89
  51.0 0.2 slice_reduce_fusion
  51.2 0.1 broadcast_subtract_fusion
  51.3 0.6 pad.33.refs_7_.refs_5_
  51.9 0.0 copy-done.7
  51.9 0.7 pad.29
  52.6 69.0 %attend.1 = (bf16[768,768]{1,0:T(8,128)(2,1)}, bf16[128,768]{1,0:T(8,128)(2,1)}, f32[768,768]{1,0:T(8,128)}, f32[128,768]{1,0:T(8,128)}, f32[2,6,8,128]{3,2,1,0:...) custom-call(s32[2]{0:T(128)} %select_reduce_fusion.refs_0_, ...), custom_call_target="tpu_custom_call" | custom-call | flops 5234491392 | bytes 16777216 | tf_op jit(solution)/shard_map/attend/pallas_call | solution.py:662
  121.6 0.1 convert_element_type.116
  121.7 0.1 convert_element_type.117
  121.8 0.1 convert_element_type.118
  121.9 0.1 convert_element_type.119
  122.0 0.1 convert_element_type.120
  122.1 0.1 convert_element_type.121
  122.2 0.6 stack.91.vec
  122.8 0.7 slice_convert_fusion
  123.5 0.7 reshape.279.up_bias
  124.2 0.0 copy-done.8
  124.2 0.7 pad.36
  124.9 72.9 %middle.1 = (f32[768,768]{1,0:T(8,128)}, f32[2,56,768]{2,1,0:T(8,128)}, f32[896,768]{1,0:T(8,128)}, bf16[768,768]{1,0:T(8,128)(2,1)}, bf16[128,768]{1,0:T(8,128)...) custom-call(bf16[768,768]{1,0:T(8,128)(2,1)} %bitcast.99, ...), custom_call_target="tpu_custom_call" | custom-call | flops 28538044416 | bytes 41943040 | tf_op jit(solution)/shard_map/middle/pallas_call | solution.py:1345
  197.9 0.0 copy-start.9
  197.9 62.0 %attend_back.1 = (bf16[768,768]{1,0:T(8,128)(2,1)}, bf16[128,768]{1,0:T(8,128)(2,1)}, bf16[3072,768]{1,0:T(8,128)(2,1)}, bf16[3072,768]{1,0:T(8,128)(2,1)}, f32[...) custom-call(s32[2]{0:T(128)} %select_reduce_fusion.refs_0_, ...), custom_call_target="tpu_custom_call" | custom-call | flops 13086228480 | bytes 33554432 | tf_op jit(solution)/shard_map/attend_back/pallas_call | solution.py:1025
  259.9 0.0 copy-done.9
  259.9 0.6 broadcast_in_dim.32.buckets_of
  260.5 72.7 %finish.1 = (f32[4,24,768]{2,1,0:T(8,128)}, f32[4,24,768]{2,1,0:T(8,128)}, f32[4,24,768]{2,1,0:T(8,128)}, f32[4,96,768]{2,1,0:T(8,128)}, f32[32,768]{1,0:T(8,128...) custom-call(bf16[768,768]{1,0:T(8,128)(2,1)} %get-tuple-element.84.dq_c_ref, bf16[128,768]{1,0:T(8,128)(2,1)} %get-tuple-element.85.dq_x, ...), custom_call_target="tpu_custom_call" | custom-call | tf_op jit(solution)/shard_map/finish/pallas_call | solution.py:1726
  333.2 0.7 slice.99
  334.0 0.1 constant_dynamic-slice_fusion
  334.0 0.5 slice_bitcast_fusion
  334.6 0.7 slice.105
  335.3 0.6 dynamic-slice_reduce_fusion
  335.9 0.7 slice.109
  336.6 0.1 dynamic-slice_bitcast_fusion
  336.7 0.7 copy.102
  337.4 3.3 copy.119
  340.7 0.0 copy-done.2
  340.7 0.7 copy.120
  341.5 0.0 copy-done.6
  341.5 0.7 copy.121
  342.2 0.0 copy-done.5
  342.2 0.7 copy.122
  342.9 0.0 copy-done.4
  342.9 0.7 copy.123
  343.6 0.0 copy-done.3
  343.6 0.7 copy.124
  344.3 0.0 copy-done
  344.3 1.0 copy.125
  345.3 1.0 copy.126
  (22 shorter events, 0.1 us)
Async XLA Ops:
  0.7 51.3 %copy-start.7 = (bf16[2,56,768]{2,1,0:T(8,128)(2,1)S(1)}, bf16[2,56,768]{2,1,0:T(8,128)(2,1)}, u32[]{:S(2)}) copy-start(bf16[2,56,768]{2,1,0:T(8,128)(2,1)} %param.24) | copy-start | bytes 516100
  52.6 71.6 %copy-start.8 = (bf16[2,56,768]{2,1,0:T(8,128)(2,1)S(1)}, bf16[2,56,768]{2,1,0:T(8,128)(2,1)}, u32[]{:S(2)}) copy-start(bf16[2,56,768]{2,1,0:T(8,128)(2,1)} %param.45) | copy-start | bytes 516100
  197.9 62.1 %copy-start.9 = (s32[128]{0:T(128)S(1)}, s32[128]{0:T(128)}, u32[]{:S(2)}) copy-start(s32[128]{0:T(128)} %param.27) | copy-start | bytes 1540
  337.4 3.3 copy-start.2
  337.4 4.1 %copy-start.6 = (f32[4,24,768]{2,1,0:T(8,128)S(1)}, f32[4,24,768]{2,1,0:T(8,128)}, u32[]{:S(2)}) copy-start(f32[4,24,768]{2,1,0:T(8,128)} %get-tuple-element.95) | copy-start | bytes 884740
  337.4 4.8 %copy-start.5 = (f32[4,24,768]{2,1,0:T(8,128)S(1)}, f32[4,24,768]{2,1,0:T(8,128)}, u32[]{:S(2)}) copy-start(f32[4,24,768]{2,1,0:T(8,128)} %get-tuple-element.97) | copy-start | bytes 884740
  337.4 5.5 %copy-start.4 = (f32[4,24,768]{2,1,0:T(8,128)S(1)}, f32[4,24,768]{2,1,0:T(8,128)}, u32[]{:S(2)}) copy-start(f32[4,24,768]{2,1,0:T(8,128)} %get-tuple-element.98) | copy-start | bytes 884740
  340.7 2.9 copy-start.3
  340.7 3.6 %copy-start = (f32[4,24,3072]{2,1,0:T(8,128)S(1)}, f32[4,24,3072]{2,1,0:T(8,128)}, u32[]{:S(2)}) copy-start(f32[4,24,3072]{2,1,0:T(8,128)} %get-tuple-element.100) | copy-start | bytes 3538948
  341.5 3.9 %copy-start.1 = (f32[4,96,768]{2,1,0:T(8,128)S(1)}, f32[4,96,768]{2,1,0:T(8,128)}, u32[]{:S(2)}) copy-start(f32[4,96,768]{2,1,0:T(8,128)} %get-tuple-element.101) | copy-start | bytes 3538948

commit v7 on v6

--- a/solution.py
+++ b/solution.py
@@ -92,12 +92,13 @@
         self.f_of = [2 * other + self.c for other in self.z_of]
         self.to_x = (self.gx, self.f)
         self.to_y = (self.gy, self.f)
+        self.to_corner = (3 - self.g, self.f)
         self.to_mate = (self.g, self.mate)
         self.to_z = [(self.g, other) for other in self.f_of]
 
     def greet(self):
         barrier = pltpu.get_barrier_semaphore()
-        everyone = [self.to_x, self.to_y, self.to_mate] + self.to_z
+        everyone = [self.to_x, self.to_y, self.to_corner, self.to_mate] + self.to_z
         for device in everyone:
             pl.semaphore_signal(barrier, inc=1, device_id=device, device_id_type=MESH)
         pl.semaphore_wait(barrier, len(everyone))
@@ -242,13 +243,11 @@
         third.append(copies.to(net.to_z[0], line.at[h, net.z_of[2]], along.at[h, 0]))
         third.append(copies.to(net.to_z[0], line.at[h, net.z_of[0]], along.at[h, 1]))
     relay = [copies.to(net.to_z[1], line.at[h, net.z_of[1]], along.at[h, 2]) for h in range(2)]
-    fourth = []
-    fifth = []
-    for h in range(2):
-        fourth.append(copies.to(net.to_x, done.at[h, net.g], done.at[h, net.g]))
-        fourth.append(copies.to(net.to_y, done.at[h, net.g], done.at[h, net.g]))
-    fifth.append(copies.to(net.to_y, done.at[0, net.gx], done.at[0, net.gx]))
-    fifth.append(copies.to(net.to_x, done.at[1, net.gy], done.at[1, net.gy]))
+    fourth = [
+        copies.to(device, done.at[h, net.g], done.at[h, net.g])
+        for h in range(2)
+        for device in (net.to_corner, net.to_x, net.to_y)
+    ]
     store = pltpu.make_async_copy(wide, share, local_sem.at[1])
 
     def begin():
@@ -310,10 +309,8 @@
 
     def corners():
         arrive(fourth)
-        start(fifth)
 
     def end():
-        arrive(fifth)
 
         @pl.loop(0, 4)
         def _(qi):

time: 353 us -> 353 us (level)
  no operation moved by 1% of the time
where the time goes in v7:
time: 353 us; the launch traced here: 347 us
  Pallas kernels  317 us (90%)
  local copies, waits for them, and re-layouts  23.8 us (7%)
  other arithmetic  5.53 us (2%)
    pallas_call x1, Pallas kernels, middle(): pl.pallas_call(middle_kernel, name='middle', grid=(tiles + GRAD_STEPS,),...  72.9 us
    pallas_call x1, Pallas kernels, finish(): pl.pallas_call(finish_kernel, name='finish', in_specs=[ANY_SPEC, whole] +...  72.5 us
    pallas_call x1, Pallas kernels, attend(): pl.pallas_call(functools.partial(attend_kernel, plength, carried), name='...  69.3 us
    pallas_call x1, Pallas kernels, attend_back(): pl.pallas_call(functools.partial(attend_back_kernel, plength, carried), n...  62.6 us
    pallas_call x1, Pallas kernels, gather_first(): pl.pallas_call(gather_first_kernel, name='gather_first', in_specs=[ANY_SP...  39.5 us
    unnamed x37, local copies, waits for them, and re-layouts  9.67 us

profile of v7, /device:TPU:0, one launch (start us, length us, event | category | flops | bytes accessed | tf_op | source)
XLA Modules:
  0.0 347.3 jit_solution(14538365756909208225)
XLA Ops:
  0.7 0.0 copy-start.7
  0.7 0.7 and_select_fusion.1
  1.4 0.7 and_select_fusion
  2.1 0.1 add_add_fusion
  2.2 0.6 fusion.5
  2.8 0.8 copy.94.refs_8_.refs_6_
  3.6 1.3 select_reduce_fusion.refs_0_
  4.9 0.9 slice_bitcast_fusion.8
  5.8 0.8 stack.83
  6.6 0.6 pad_bitcast_fusion.refs_3_
  7.2 39.5 %gather_first.1 = (bf16[32,24,768]{2,1,0:T(8,128)(2,1)}, bf16[32,24,768]{2,1,0:T(8,128)(2,1)}, bf16[32,24,768]{2,1,0:T(8,128)(2,1)}, bf16[32,8,256]{2,1,0:T(8,128)(2,1)}, bf16[1536,768]{1,0:T(8,128)(2,1)}) custom-call(bf16[4,24,768]{2,1,0:T(8,128)(2,1)} %bitcast.119, bf16[4,24,768]{2,1,0:T(8,128)(2,1)} %bitcast.120, bf16[4,24,768]{2,1,0:T(8,128)(2,1)} %bitcast.121, ...), custom_call_target="tpu_custom_call" | custom-call | tf_op jit(solution)/shard_map/gather_first/pallas_call | solution.py:405
  46.8 1.3 fusion.4
  48.1 0.1 convert_element_type.113
  48.1 0.1 convert_element_type.114
  48.2 0.6 fusion.3.refs_6_
  48.9 0.8 copy.88
  49.6 0.7 compare_select_fusion
  50.3 0.6 gather_fusion
  50.9 0.1 copy.89
  51.0 0.2 slice_reduce_fusion
  51.2 0.1 broadcast_subtract_fusion
  51.3 0.6 pad.33.refs_7_.refs_5_
  51.9 0.0 copy-done.7
  51.9 0.7 pad.29
  52.6 69.3 %attend.1 = (bf16[768,768]{1,0:T(8,128)(2,1)}, bf16[128,768]{1,0:T(8,128)(2,1)}, f32[768,768]{1,0:T(8,128)}, f32[128,768]{1,0:T(8,128)}, f32[2,6,8,128]{3,2,1,0:...) custom-call(s32[2]{0:T(128)} %select_reduce_fusion.refs_0_, ...), custom_call_target="tpu_custom_call" | custom-call | flops 5234491392 | bytes 16777216 | tf_op jit(solution)/shard_map/attend/pallas_call | solution.py:659
  121.9 0.1 convert_element_type.116
  122.0 0.1 convert_element_type.117
  122.1 0.1 convert_element_type.118
  122.2 0.1 convert_element_type.119
  122.3 0.1 convert_element_type.120
  122.4 0.1 convert_element_type.121
  122.5 0.6 stack.91.vec
  123.2 0.7 slice_convert_fusion
  123.9 0.7 reshape.279.up_bias
  124.6 0.0 copy-done.8
  124.6 0.7 pad.36
  125.3 72.9 %middle.1 = (f32[768,768]{1,0:T(8,128)}, f32[2,56,768]{2,1,0:T(8,128)}, f32[896,768]{1,0:T(8,128)}, bf16[768,768]{1,0:T(8,128)(2,1)}, bf16[128,768]{1,0:T(8,128)...) custom-call(bf16[768,768]{1,0:T(8,128)(2,1)} %bitcast.99, ...), custom_call_target="tpu_custom_call" | custom-call | flops 28538044416 | bytes 41943040 | tf_op jit(solution)/shard_map/middle/pallas_call | solution.py:1342
  198.2 0.0 copy-start.9
  198.2 62.6 %attend_back.1 = (bf16[768,768]{1,0:T(8,128)(2,1)}, bf16[128,768]{1,0:T(8,128)(2,1)}, bf16[3072,768]{1,0:T(8,128)(2,1)}, bf16[3072,768]{1,0:T(8,128)(2,1)}, f32[...) custom-call(s32[2]{0:T(128)} %select_reduce_fusion.refs_0_, ...), custom_call_target="tpu_custom_call" | custom-call | flops 13086228480 | bytes 33554432 | tf_op jit(solution)/shard_map/attend_back/pallas_call | solution.py:1022
  260.9 0.0 copy-done.9
  260.9 0.6 broadcast_in_dim.32.buckets_of
  261.5 72.5 %finish.1 = (f32[4,24,768]{2,1,0:T(8,128)}, f32[4,24,768]{2,1,0:T(8,128)}, f32[4,24,768]{2,1,0:T(8,128)}, f32[4,96,768]{2,1,0:T(8,128)}, f32[32,768]{1,0:T(8,128...) custom-call(bf16[768,768]{1,0:T(8,128)(2,1)} %get-tuple-element.84.dq_c_ref, bf16[128,768]{1,0:T(8,128)(2,1)} %get-tuple-element.85.dq_x, ...), custom_call_target="tpu_custom_call" | custom-call | tf_op jit(solution)/shard_map/finish/pallas_call | solution.py:1723
  333.9 0.7 slice.99
  334.7 0.1 constant_dynamic-slice_fusion
  334.8 0.5 slice_bitcast_fusion
  335.3 0.7 slice.105
  336.1 0.6 dynamic-slice_reduce_fusion
  336.7 0.7 slice.109
  337.4 0.1 dynamic-slice_bitcast_fusion
  337.4 0.7 copy.102
  338.1 3.3 copy.119
  341.4 0.0 copy-done.2
  341.4 0.7 copy.120
  342.2 0.0 copy-done.6
  342.2 0.7 copy.121
  342.9 0.0 copy-done.5
  342.9 0.7 copy.122
  343.6 0.0 copy-done.4
  343.6 0.7 copy.123
  344.3 0.0 copy-done.3
  344.3 0.7 copy.124
  345.0 0.0 copy-done
  345.0 1.0 copy.125
  346.1 1.0 copy.126
  (22 shorter events, 0.1 us)
Async XLA Ops:
  0.7 51.3 %copy-start.7 = (bf16[2,56,768]{2,1,0:T(8,128)(2,1)S(1)}, bf16[2,56,768]{2,1,0:T(8,128)(2,1)}, u32[]{:S(2)}) copy-start(bf16[2,56,768]{2,1,0:T(8,128)(2,1)} %param.24) | copy-start | bytes 516100
  52.6 72.0 %copy-start.8 = (bf16[2,56,768]{2,1,0:T(8,128)(2,1)S(1)}, bf16[2,56,768]{2,1,0:T(8,128)(2,1)}, u32[]{:S(2)}) copy-start(bf16[2,56,768]{2,1,0:T(8,128)(2,1)} %param.45) | copy-start | bytes 516100
  198.2 62.7 %copy-start.9 = (s32[128]{0:T(128)S(1)}, s32[128]{0:T(128)}, u32[]{:S(2)}) copy-start(s32[128]{0:T(128)} %param.27) | copy-start | bytes 1540
  338.1 3.3 copy-start.2
  338.1 4.1 %copy-start.6 = (f32[4,24,768]{2,1,0:T(8,128)S(1)}, f32[4,24,768]{2,1,0:T(8,128)}, u32[]{:S(2)}) copy-start(f32[4,24,768]{2,1,0:T(8,128)} %get-tuple-element.95) | copy-start | bytes 884740
  338.1 4.8 %copy-start.5 = (f32[4,24,768]{2,1,0:T(8,128)S(1)}, f32[4,24,768]{2,1,0:T(8,128)}, u32[]{:S(2)}) copy-start(f32[4,24,768]{2,1,0:T(8,128)} %get-tuple-element.97) | copy-start | bytes 884740
  338.1 5.5 %copy-start.4 = (f32[4,24,768]{2,1,0:T(8,128)S(1)}, f32[4,24,768]{2,1,0:T(8,128)}, u32[]{:S(2)}) copy-start(f32[4,24,768]{2,1,0:T(8,128)} %get-tuple-element.98) | copy-start | bytes 884740
  341.4 2.9 copy-start.3
  341.4 3.6 %copy-start = (f32[4,24,3072]{2,1,0:T(8,128)S(1)}, f32[4,24,3072]{2,1,0:T(8,128)}, u32[]{:S(2)}) copy-start(f32[4,24,3072]{2,1,0:T(8,128)} %get-tuple-element.100) | copy-start | bytes 3538948
  342.2 3.9 %copy-start.1 = (f32[4,96,768]{2,1,0:T(8,128)S(1)}, f32[4,96,768]{2,1,0:T(8,128)}, u32[]{:S(2)}) copy-start(f32[4,96,768]{2,1,0:T(8,128)} %get-tuple-element.101) | copy-start | bytes 3538948
